TPU v7x, 32 devices: a whole 2x2x4 slice. The times are simulated.
32 devices in a mesh: grp: 4 (over y, core), shard: 8 (over z, x).
Axes of the slice: x: 2, y: 2, z: 4, core: 2. Of those that a mesh axis runs over, the one named last changes fastest.
Arguments:
- tokens: bfloat16 [16384, 768], P(('grp', 'shard')), may hold values from -6 to 6
- cotangent: bfloat16 [16384, 768], P(('grp', 'shard')), may hold values from -6 to 6
- seq_lengths: int32 [4, 8], replicated, may hold values from 1 to 1024, 3840 in all within a row
- seq_order: int32 [4, 8], replicated, may hold values from 0 to 7, each once within a row
- w_project: bfloat16 [2, 768, 2304], P(None, 'shard'), may hold values from -0.21875 to 0.21875
- w_mixer: bfloat16 [2, 768, 768], P(None, 'shard'), may hold values from -4 to 4
- w_expand: bfloat16 [2, 768, 3072], P(None, 'shard'), may hold values from -0.21875 to 0.21875
- w_reduce: bfloat16 [2, 3072, 768], P(None, 'shard'), may hold values from -0.109375 to 0.109375
- biases: bfloat16 [2, 7680], P(None, 'shard'), may hold values from -1.1953125 to 1.1953125
- norm_gains: bfloat16 [2, 1536], P(None, 'shard'), may hold values from 0.5 to 1.5
Outputs:
- activations: bfloat16 [16384, 768], P(('grp', 'shard'))
- input_grad: float32 [16384, 768], P(('grp', 'shard'))
- project_grad: float32 [2, 768, 2304], P(None, 'shard')
- mixer_grad: float32 [2, 768, 768], P(None, 'shard')
- expand_grad: float32 [2, 768, 3072], P(None, 'shard')
- reduce_grad: float32 [2, 3072, 768], P(None, 'shard')
- bias_grad: float32 [2, 7680], P(None, 'shard')
- gain_grad: float32 [2, 1536], P(None, 'shard')
Inputs may be any that keep to these rules, and one draw needn't show every extreme that they name: `seq_lengths`: each row holds the lengths of one group's 8 sequences; they sum to 3840, and the largest of each row is exactly 1024. `seq_order`: each row is a permutation.
All inputs are finite; a program needn't handle non-finite values.
Results may differ from a plain program's by a relative error of at most 0.019.
Values may be sent and summed in bfloat16 or wider, within the bound.
No kernel may reach another device: no remote copies, remote signals or barrier semaphores. Data moves between devices by JAX's collectives and lax.ppermute only.
A program may use at most 320 MiB of HBM per device.

v0:
```python
import jax
import jax.numpy as jnp
from jax import lax
from jax.sharding import PartitionSpec as P

HEADS = 12
LAYERS = 2
SEQ_MAX = 2048


EPSILON = 1e-12
NEGATIVE = -1e30


def passed_along(shard, axis, by):
    size = lax.axis_size(axis)
    pairs = [(i, i + by) for i in range(size) if 0 <= i + by < size]
    return lax.ppermute(shard, axis, pairs)


def layer_norm(values, gain, shift):
    middle = jnp.mean(values, axis=-1, keepdims=True)
    centered = values - middle
    spread = jnp.mean(centered * centered, axis=-1, keepdims=True)
    return centered * lax.rsqrt(spread + EPSILON) * gain + shift


def gelu_exact(values):
    return jax.nn.gelu(values, approximate=False)


def keep_same(carried):
    return carried


def group_ends(seq_lengths, seq_order, group_index):
    lengths_row = lax.dynamic_index_in_dim(seq_lengths, group_index, 0, keepdims=False)
    order_row = lax.dynamic_index_in_dim(seq_order, group_index, 0, keepdims=False)
    places = jnp.arange(lengths_row.shape[0], dtype=jnp.int32)
    picked = order_row[:, None] == places[None, :]
    placed = jnp.sum(jnp.where(picked, lengths_row[None, :], 0), axis=1, dtype=jnp.int32)
    return jnp.cumsum(placed, dtype=jnp.int32)


def slot_segments(slot_index, seq_ends):
    flattened = slot_index.reshape(-1)
    counted = jnp.sum(
        (seq_ends[None, :] <= flattened[:, None]).astype(jnp.int32), axis=1, dtype=jnp.int32
    )
    return counted.reshape(slot_index.shape)


def unpack_weights(weights, width, hidden_units):
    bias_vec = weights[4].astype(jnp.float32)
    gain_vec = weights[5].astype(jnp.float32)
    piece_lens = [width, width, width, width, hidden_units, width, width]
    bias_list = []
    begin_at = 0
    for piece_len in piece_lens:
        bias_list.append(bias_vec[begin_at : begin_at + piece_len])
        begin_at = begin_at + piece_len
    return (
        weights[0],
        weights[1],
        weights[2],
        weights[3],
        bias_list,
        gain_vec[:width],
        gain_vec[width:],
    )


def block_probs(queries, keys_block, seg_block, own_segment, log_total, score_scale):
    raw_scores = jnp.einsum("qhd,khd->hqk", queries, keys_block, preferred_element_type=jnp.float32)
    allowed = (own_segment[:, None] == seg_block[None, :])[None]
    return jnp.where(allowed, jnp.exp(raw_scores * score_scale - log_total[:, :, None]), 0.0)


def gather_window(key_rows, value_rows, reach_blocks):
    key_list = []
    value_list = []
    for step_offset in range(-reach_blocks, reach_blocks + 1):
        if step_offset == 0:
            moved = (key_rows, value_rows)
        else:
            moved = passed_along((key_rows, value_rows), "shard", -step_offset)
        key_list.append(moved[0])
        value_list.append(moved[1])
    return (jnp.stack(key_list), jnp.stack(value_list))


def return_parts(key_parts, value_parts, reach_blocks):
    key_total = key_parts[reach_blocks]
    value_total = value_parts[reach_blocks]
    for step_offset in range(-reach_blocks, reach_blocks + 1):
        if step_offset != 0:
            arrived = (
                passed_along(
                    key_parts[step_offset + reach_blocks].astype(jnp.bfloat16), "shard", step_offset
                ).astype(jnp.float32),
                passed_along(
                    value_parts[step_offset + reach_blocks].astype(jnp.bfloat16),
                    "shard",
                    step_offset,
                ).astype(jnp.float32),
            )
            key_total = key_total + arrived[0]
            value_total = value_total + arrived[1]
    return (key_total, value_total)


def attend_forward(
    queries, window_keys, window_values, window_segment, live_block, own_segment, score_scale
):
    row_count, head_count, head_dim = queries.shape

    def stats_step(carry, items):
        keys_block, seg_block, alive = items

        def stats_compute(state_pair):
            running_top, running_sum = state_pair
            allowed = (own_segment[:, None] == seg_block[None, :])[None]
            raw_scores = jnp.einsum(
                "qhd,khd->hqk", queries, keys_block, preferred_element_type=jnp.float32
            )
            scores = jnp.where(allowed, raw_scores * score_scale, NEGATIVE)
            new_top = jnp.maximum(running_top, jnp.max(scores, axis=-1))
            weighted = jnp.where(allowed, jnp.exp(scores - new_top[:, :, None]), 0.0)
            return (
                new_top,
                running_sum * jnp.exp(running_top - new_top) + jnp.sum(weighted, axis=-1),
            )

        return (lax.cond(alive, stats_compute, keep_same, carry), None)

    begin_stats = (
        jnp.full((head_count, row_count), NEGATIVE, jnp.float32),
        jnp.zeros((head_count, row_count), jnp.float32),
    )
    (running_top, running_sum), unused = lax.scan(
        stats_step, begin_stats, (window_keys, window_segment, live_block)
    )
    log_total = running_top + jnp.log(running_sum)

    def mix_step(carry, items):
        keys_block, values_block, seg_block, alive = items

        def mix_compute(state_pair):
            mixed, extra = state_pair
            probs = block_probs(queries, keys_block, seg_block, own_segment, log_total, score_scale)
            probs_low = probs.astype(jnp.bfloat16)
            rest_low = (probs - lax.optimization_barrier(probs_low).astype(jnp.float32)).astype(
                jnp.bfloat16
            )
            mixed = mixed + jnp.einsum(
                "hqk,khd->qhd", probs_low, values_block, preferred_element_type=jnp.float32
            )
            extra = extra + jnp.einsum(
                "hqk,khd->qhd", rest_low, values_block, preferred_element_type=jnp.float32
            )
            return (mixed, extra)

        return (lax.cond(alive, mix_compute, keep_same, carry), None)

    zeros_mix = jnp.zeros((row_count, head_count, head_dim), jnp.float32)
    (mixed, extra), unused = lax.scan(
        mix_step, (zeros_mix, zeros_mix), (window_keys, window_values, window_segment, live_block)
    )
    return (log_total, mixed, mixed + extra)


def attend_backward(
    queries,
    window_keys,
    window_values,
    window_segment,
    live_block,
    own_segment,
    log_total,
    delta,
    grad_low,
    score_scale,
):

    def grad_step(query_grad, items):
        keys_block, values_block, seg_block, alive = items

        def grad_compute(carried):
            probs = block_probs(queries, keys_block, seg_block, own_segment, log_total, score_scale)
            prob_grad = jnp.einsum(
                "qhd,khd->hqk", grad_low, values_block, preferred_element_type=jnp.float32
            )
            score_low = (probs * (prob_grad - delta[:, :, None])).astype(jnp.bfloat16)
            carried = carried + jnp.einsum(
                "hqk,khd->qhd", score_low, keys_block, preferred_element_type=jnp.float32
            )
            probs_low = probs.astype(jnp.bfloat16)
            value_part = jnp.einsum(
                "hqk,qhd->khd", probs_low, grad_low, preferred_element_type=jnp.float32
            )
            key_part = jnp.einsum(
                "hqk,qhd->khd", score_low, queries, preferred_element_type=jnp.float32
            )
            return (carried, (key_part, value_part))

        def skipped(carried):
            nothing = jnp.zeros(keys_block.shape, jnp.float32)
            return (carried, (nothing, nothing))

        return lax.cond(alive, grad_compute, skipped, query_grad)

    zero_grad = jnp.zeros(queries.shape, jnp.float32)
    query_grad, key_value = lax.scan(
        grad_step, zero_grad, (window_keys, window_values, window_segment, live_block)
    )
    return (query_grad, key_value)


def on_device(
    tokens,
    cotangent,
    seq_lengths,
    seq_order,
    w_project,
    w_mixer,
    w_expand,
    w_reduce,
    biases,
    norm_gains,
):
    row_count, width = tokens.shape
    shard_count = lax.axis_size("shard")
    shard_index = lax.axis_index("shard")
    group_index = lax.axis_index("grp")
    head_dim = width // HEADS
    hidden_units = w_expand.shape[2]
    score_scale = head_dim ** (-0.5)
    longest = min(SEQ_MAX, row_count * shard_count // 4)
    reach_blocks = longest // row_count
    seq_count = seq_lengths.shape[1]
    seq_ends = group_ends(seq_lengths, seq_order, group_index)
    neighbour = shard_index + jnp.arange(-reach_blocks, reach_blocks + 1, dtype=jnp.int32)
    slot_index = neighbour[:, None] * row_count + jnp.arange(row_count, dtype=jnp.int32)[None, :]
    window_segment = slot_segments(slot_index, seq_ends)
    own_segment = window_segment[reach_blocks]
    inside = (neighbour >= 0) & (neighbour < shard_count)
    live_block = (
        inside
        & (window_segment[:, 0] <= own_segment[row_count - 1])
        & (window_segment[:, row_count - 1] >= own_segment[0])
    )
    valid_rows = (own_segment < seq_count).astype(jnp.float32)[:, None]
    hidden_state = tokens.astype(jnp.float32)
    state_low = tokens
    kept_list = []
    for layer_index in range(LAYERS):
        weights = (
            lax.all_gather(w_project[layer_index], "shard", axis=0, tiled=True),
            lax.all_gather(w_mixer[layer_index], "shard", axis=0, tiled=True),
            lax.all_gather(w_expand[layer_index], "shard", axis=0, tiled=True),
            lax.all_gather(w_reduce[layer_index], "shard", axis=0, tiled=True),
            lax.all_gather(biases[layer_index], "shard", axis=0, tiled=True),
            lax.all_gather(norm_gains[layer_index], "shard", axis=0, tiled=True),
        )
        project, mixing, expand, shrink, bias_list, gain_one, gain_two = unpack_weights(
            weights, width, hidden_units
        )
        bias_q, bias_v, bias_mix, shift_one, bias_in, bias_out, shift_two = bias_list
        projected = jnp.dot(state_low, project, preferred_element_type=jnp.float32)
        projected = projected + jnp.concatenate([bias_q, jnp.zeros_like(bias_q), bias_v])
        projected_low = projected.astype(jnp.bfloat16)
        queries = projected_low[:, :width].reshape(row_count, HEADS, head_dim)
        key_rows = projected_low[:, width : 2 * width].reshape(row_count, HEADS, head_dim)
        value_rows = projected_low[:, 2 * width :].reshape(row_count, HEADS, head_dim)
        window_keys, window_values = gather_window(key_rows, value_rows, reach_blocks)
        log_total, mixed, full_mix = attend_forward(
            queries,
            window_keys,
            window_values,
            window_segment,
            live_block,
            own_segment,
            score_scale,
        )
        mixed_low = mixed.reshape(row_count, width).astype(jnp.bfloat16)
        branch = jnp.dot(mixed_low, mixing, preferred_element_type=jnp.float32) + bias_mix
        summed_one = hidden_state + branch
        normed_one = layer_norm(summed_one, gain_one, shift_one)
        normed_low = normed_one.astype(jnp.bfloat16)
        before = jnp.dot(normed_low, expand, preferred_element_type=jnp.float32) + bias_in
        active_low = gelu_exact(before).astype(jnp.bfloat16)
        feed_out = jnp.dot(active_low, shrink, preferred_element_type=jnp.float32) + bias_out
        summed_two = normed_one + feed_out
        hidden_state = layer_norm(summed_two, gain_two, shift_two)
        kept_list.append(
            (
                state_low,
                queries,
                key_rows,
                value_rows,
                window_keys,
                window_values,
                log_total,
                full_mix,
                mixed_low,
                summed_one,
                normed_low,
                before,
                active_low,
                summed_two,
                weights,
            )
        )
        state_low = hidden_state.astype(jnp.bfloat16)
    activations = (hidden_state * valid_rows).astype(jnp.bfloat16)
    state_grad = cotangent.astype(jnp.float32) * valid_rows
    results = [None] * LAYERS
    for layer_index in reversed(range(LAYERS)):
        (
            layer_low,
            queries,
            key_rows,
            value_rows,
            window_keys,
            window_values,
            log_total,
            full_mix,
            mixed_low,
            summed_one,
            normed_low,
            before,
            active_low,
            summed_two,
            kept_weights,
        ) = kept_list[layer_index]
        weights = (
            lax.all_gather(w_project[layer_index], "shard", axis=0, tiled=True),
            lax.all_gather(w_mixer[layer_index], "shard", axis=0, tiled=True),
            lax.all_gather(w_expand[layer_index], "shard", axis=0, tiled=True),
            lax.all_gather(w_reduce[layer_index], "shard", axis=0, tiled=True),
            lax.all_gather(biases[layer_index], "shard", axis=0, tiled=True),
            lax.all_gather(norm_gains[layer_index], "shard", axis=0, tiled=True),
        )
        project, mixing, expand, shrink, bias_list, gain_one, gain_two = unpack_weights(
            weights, width, hidden_units
        )
        bias_q, bias_v, bias_mix, shift_one, bias_in, bias_out, shift_two = bias_list
        unused_two, norm_pull = jax.vjp(layer_norm, summed_two, gain_two, shift_two)
        sum_two_grad, gain_two_grad, shift_two_grad = norm_pull(state_grad)
        feed_low = sum_two_grad.astype(jnp.bfloat16)
        shrink_grad = jnp.einsum(
            "tf,td->fd", active_low, feed_low, preferred_element_type=jnp.float32
        )
        bias_out_grad = jnp.sum(feed_low, axis=0, dtype=jnp.float32)
        active_grad = jnp.einsum("td,fd->tf", feed_low, shrink, preferred_element_type=jnp.float32)
        unused_gelu, gelu_pull = jax.vjp(gelu_exact, before)
        before_low = gelu_pull(active_grad)[0].astype(jnp.bfloat16)
        expand_grad = jnp.einsum(
            "td,tf->df", normed_low, before_low, preferred_element_type=jnp.float32
        )
        bias_in_grad = jnp.sum(before_low, axis=0, dtype=jnp.float32)
        normed_grad = sum_two_grad + jnp.einsum(
            "tf,df->td", before_low, expand, preferred_element_type=jnp.float32
        )
        unused_one, first_pull = jax.vjp(layer_norm, summed_one, gain_one, shift_one)
        sum_one_grad, gain_one_grad, shift_one_grad = first_pull(normed_grad)
        branch_low = sum_one_grad.astype(jnp.bfloat16)
        mixing_grad = jnp.einsum(
            "td,te->de", mixed_low, branch_low, preferred_element_type=jnp.float32
        )
        bias_mix_grad = jnp.sum(branch_low, axis=0, dtype=jnp.float32)
        mixed_grad = jnp.einsum("te,de->td", branch_low, mixing, preferred_element_type=jnp.float32)
        mixed_grad_low = mixed_grad.astype(jnp.bfloat16).reshape(row_count, HEADS, head_dim)
        delta = jnp.sum(mixed_grad_low.astype(jnp.float32) * full_mix, axis=-1).T
        query_grad, key_value = attend_backward(
            queries,
            window_keys,
            window_values,
            window_segment,
            live_block,
            own_segment,
            log_total,
            delta,
            mixed_grad_low,
            score_scale,
        )
        key_total, value_total = return_parts(key_value[0], key_value[1], reach_blocks)
        projected_grad = jnp.concatenate(
            [
                (query_grad * score_scale).reshape(row_count, width),
                (key_total * score_scale).reshape(row_count, width),
                value_total.reshape(row_count, width),
            ],
            axis=1,
        )
        projected_low = projected_grad.astype(jnp.bfloat16)
        project_grad = jnp.einsum(
            "td,te->de", layer_low, projected_low, preferred_element_type=jnp.float32
        )
        bias_q_grad = jnp.sum(projected_low[:, :width], axis=0, dtype=jnp.float32)
        bias_v_grad = jnp.sum(projected_low[:, 2 * width :], axis=0, dtype=jnp.float32)
        state_grad = sum_one_grad + jnp.einsum(
            "te,de->td", projected_low, project, preferred_element_type=jnp.float32
        )
        bias_all = jnp.concatenate(
            [
                bias_q_grad,
                bias_v_grad,
                bias_mix_grad,
                shift_one_grad,
                bias_in_grad,
                bias_out_grad,
                shift_two_grad,
            ]
        )
        gain_all = jnp.concatenate([gain_one_grad, gain_two_grad])
        shares = (
            lax.psum_scatter(
                project_grad.astype(jnp.bfloat16), "shard", scatter_dimension=0, tiled=True
            ).astype(jnp.float32),
            lax.psum_scatter(
                mixing_grad.astype(jnp.bfloat16), "shard", scatter_dimension=0, tiled=True
            ).astype(jnp.float32),
            lax.psum_scatter(
                expand_grad.astype(jnp.bfloat16), "shard", scatter_dimension=0, tiled=True
            ).astype(jnp.float32),
            lax.psum_scatter(
                shrink_grad.astype(jnp.bfloat16), "shard", scatter_dimension=0, tiled=True
            ).astype(jnp.float32),
            lax.psum_scatter(
                bias_all.astype(jnp.bfloat16), "shard", scatter_dimension=0, tiled=True
            ).astype(jnp.float32),
            lax.psum_scatter(
                gain_all.astype(jnp.bfloat16), "shard", scatter_dimension=0, tiled=True
            ).astype(jnp.float32),
        )
        shares = (
            lax.psum(shares[0].astype(jnp.bfloat16), "grp").astype(jnp.float32),
            lax.psum(shares[1].astype(jnp.bfloat16), "grp").astype(jnp.float32),
            lax.psum(shares[2].astype(jnp.bfloat16), "grp").astype(jnp.float32),
            lax.psum(shares[3].astype(jnp.bfloat16), "grp").astype(jnp.float32),
            lax.psum(shares[4].astype(jnp.bfloat16), "grp").astype(jnp.float32),
            lax.psum(shares[5].astype(jnp.bfloat16), "grp").astype(jnp.float32),
        )
        results[layer_index] = shares
    stacked = [jnp.stack([layer_share[member] for layer_share in results]) for member in range(6)]
    return (
        activations,
        state_grad,
        stacked[0],
        stacked[1],
        stacked[2],
        stacked[3],
        stacked[4],
        stacked[5],
    )


def solution(mesh):
    in_specs = (
        P(("grp", "shard"), None),
        P(("grp", "shard"), None),
        P(),
        P(),
        P(None, "shard", None),
        P(None, "shard", None),
        P(None, "shard", None),
        P(None, "shard", None),
        P(None, "shard"),
        P(None, "shard"),
    )
    out_specs = (
        P(("grp", "shard"), None),
        P(("grp", "shard"), None),
        P(None, "shard", None),
        P(None, "shard", None),
        P(None, "shard", None),
        P(None, "shard", None),
        P(None, "shard"),
        P(None, "shard"),
    )
    return jax.shard_map(
        on_device, mesh=mesh, in_specs=in_specs, out_specs=out_specs, check_vma=False
    )
```

profile of v0, /device:TPU:1, one launch (start us, length us, event | category | flops | bytes accessed | tf_op | source)
XLA Modules:
  0.0 1827.6 jit_solution(12030350499868937481)
XLA Ops:
  19.8 32.9 %all-reduce.9 = (bf16[7680]{0:T(1024)(128)(2,1)S(1)}, bf16[1536]{0:T(1024)(128)(2,1)S(1)}, bf16[7680]{0:T(1024)(128)(2,1)S(1)}, bf16[1536]{0:T(1024)(128)(2,1)}) all-reduce(bf16[7680]{0:T(1024)(128)(2,1)S(1)} %dynamic-update-slice, bf16[1536]{0:T(1024)(128)(2,1)S(1)} %dynamic-update-slice.1, ...), channel_id=3, replica_groups=mesh['grp'=4,'shard'=8] {'shard'}, use_global_device_ids=true, to_apply=%add | all-reduce | flops 18432 | bytes 73728
  56.0 22.2 %all-gather.21.cloned.1.call-done = bf16[1,768,2304]{2,1,0:T(8,128)(2,1)} async-done(((bf16[1,96,2304]{2,1,0:T(8,128)(2,1)}), bf16[1,768,2304]{2,1,0:T(8,128)(2,1)}) %all-gather.21.cloned.1.call-update) | async-done | bytes 3538960 | tf_op jit(solution)/shard_map/all_gather | solution.py:258
  107.5 22.2 %collective-permute-done.1 = bf16[512,12,64]{0,2,1:T(8,128)(2,1)} collective-permute-done((bf16[512,12,64]{0,2,1:T(8,128)(2,1)S(1)}, bf16[512,12,64]{0,2,1:T(8,128)(2,1)}, u32[]{:S(2)}, u32[]{:S(2)}) %collective-permute-start.1) | collective-permute-done | bytes 786464 | tf_op jit(solution)/shard_map/ppermute | solution.py:18
  139.6 19.2 %while.82 = (s32[]{:T(128)}, f32[12,512]{1,0:T(8,128)S(1)}, f32[12,512]{1,0:T(8,128)S(1)}, pred[5]{0:T(512)(128)(4,1)S(1)}, s32[1,512]{1,0:T(1,128)S(1)}, /*inde...) while((s32[]{:T(128)}, f32[12,512]{1,0:T(8,128)S(1)}, ...), condition=%wide.region_8.9_spmd, body=%wide.region_3.8_spmd.sunk | while | flops 428093440 | bytes 27853516 | solution.py:140
  143.0 6.7 conditional.12
  150.9 6.8 conditional.12
  160.0 7.5 collective-permute-done.5
  170.0 23.6 %collective-permute-done.7 = bf16[512,12,64]{0,2,1:T(8,128)(2,1)} collective-permute-done((bf16[512,12,64]{0,2,1:T(8,128)(2,1)S(1)}, bf16[512,12,64]{0,2,1:T(8,128)(2,1)}, u32[]{:S(2)}, u32[]{:S(2)}) %collective-permute-start.7) | collective-permute-done | bytes 786464 | tf_op jit(solution)/shard_map/ppermute | solution.py:18
  197.2 32.7 %while.83 = (s32[]{:T(128)}, f32[512,12,64]{0,2,1:T(8,128)S(1)}, f32[512,12,64]{0,2,1:T(8,128)}, pred[5]{0:T(512)(128)(4,1)S(1)}, s32[1,512]{1,0:T(1,128)S(1)}, ...) while((s32[]{:T(128)}, f32[512,12,64]{0,2,1:T(8,128)S(1)}, ...), condition=%wide.region_12.13_spmd, body=%wide.region_9.12_spmd.sunk | while | flops 1240465408 | bytes 54322924 | solution.py:166
  200.6 13.5 conditional.13
  215.2 13.5 conditional.13
  240.8 21.3 %multiply_convert_fusion.1 = (bf16[512,3072]{1,0:T(8,128)(2,1)}, f32[512,3072]{1,0:T(8,128)}, f32[512,3072]{1,0:T(8,128)}) fusion(f32[3072]{0:T(1024)S(1)} %bitcast.505, bf16[1,768,3072]{2,1,0:T(8,128)(2,1)} %all-gather.25.cloned.1.call-done, f32[512,768]{1,0:T(8,128)} %copy-done.14, f32[768]{0:T(1024)S(1)} %get-tuple-element.956, ...), kind=kOutput, calls=%fused_computation.131 | convolution fusion | flops 2521694208 | bytes 22042624 | tf_op jit(solution)/shard_map/dot_general | solution.py:290
  262.0 59.6 %all-gather.27.cloned.1.call-done = bf16[1,3072,768]{2,1,0:T(8,128)(2,1)} async-done(((bf16[1,384,768]{2,1,0:T(8,128)(2,1)}), bf16[1,3072,768]{2,1,0:T(8,128)(2,1)}) %all-gather.27.cloned.1.call-update) | async-done | bytes 4718608 | tf_op jit(solution)/shard_map/all_gather | solution.py:261
  328.1 58.9 %all-gather.29.cloned.1.call-done = bf16[1,768,2304]{2,1,0:T(8,128)(2,1)} async-done(((bf16[1,96,2304]{2,1,0:T(8,128)(2,1)}), bf16[1,768,2304]{2,1,0:T(8,128)(2,1)}) %all-gather.29.cloned.1.call-update) | async-done | bytes 3538960 | tf_op jit(solution)/shard_map/all_gather | solution.py:258
  421.1 15.9 collective-permute-done.9
  449.7 20.0 %while.84 = (s32[]{:T(128)}, f32[12,512]{1,0:T(8,128)S(1)}, f32[12,512]{1,0:T(8,128)S(1)}, pred[5]{0:T(512)(128)(4,1)S(1)}, s32[1,512]{1,0:T(1,128)S(1)}, /*inde...) while((s32[]{:T(128)}, f32[12,512]{1,0:T(8,128)S(1)}, ...), condition=%wide.region_22.23_spmd, body=%wide.region_17.22_spmd.sunk | while | flops 428093440 | bytes 27853516 | solution.py:140
  453.7 6.7 conditional.14
  461.7 6.7 conditional.14
  474.9 25.8 %collective-permute-done.15 = bf16[512,12,64]{0,2,1:T(8,128)(2,1)} collective-permute-done((bf16[512,12,64]{0,2,1:T(8,128)(2,1)S(1)}, bf16[512,12,64]{0,2,1:T(8,128)(2,1)}, u32[]{:S(2)}, u32[]{:S(2)}) %collective-permute-start.15) | collective-permute-done | bytes 786464 | tf_op jit(solution)/shard_map/ppermute | solution.py:18
  504.3 33.4 %while.85 = (s32[]{:T(128)}, f32[512,12,64]{0,2,1:T(8,128)S(1)}, f32[512,12,64]{0,2,1:T(8,128)}, pred[5]{0:T(512)(128)(4,1)S(1)}, s32[1,512]{1,0:T(1,128)S(1)}, ...) while((s32[]{:T(128)}, f32[512,12,64]{0,2,1:T(8,128)S(1)}, ...), condition=%wide.region_26.27_spmd, body=%wide.region_23.26_spmd.sunk | while | flops 1240465408 | bytes 54322924 | solution.py:166
  508.1 13.5 conditional.15
  522.9 13.5 conditional.15
  546.0 21.2 %multiply_convert_fusion = (bf16[512,3072]{1,0:T(8,128)(2,1)}, f32[512,3072]{1,0:T(8,128)}, f32[512,3072]{1,0:T(8,128)}) fusion(f32[3072]{0:T(1024)S(1)} %bitcast.507, bf16[1,768,3072]{2,1,0:T(8,128)(2,1)} %all-gather.33.cloned.1.call-done, f32[512,768]{1,0:T(8,128)} %copy-done.18, f32[768]{0:T(1024)S(1)} %copy-done.107, f32[768]{0:T(1024)S(1)} %get-tuple-element.963, ...), kind=kOutput, calls=%fused_computation.118 | convolution fusion | flops 2521694208 | bytes 22042624 | tf_op jit(solution)/shard_map/dot_general | solution.py:290
  567.2 59.4 %all-gather.35.cloned.1.call-done = bf16[1,3072,768]{2,1,0:T(8,128)(2,1)} async-done(((bf16[1,384,768]{2,1,0:T(8,128)(2,1)}), bf16[1,3072,768]{2,1,0:T(8,128)(2,1)}) %all-gather.35.cloned.1.call-update) | async-done | bytes 4718608 | tf_op jit(solution)/shard_map/all_gather | solution.py:261
  626.6 6.6 fusion.206
  637.6 9.0 fusion.207
  668.4 68.7 %while.86 = (s32[]{:T(128)}, f32[512,12,64]{0,2,1:T(8,128)}, f32[5,512,12,64]{1,3,2,0:T(8,128)}, f32[5,512,12,64]{1,3,2,0:T(8,128)}, pred[5]{0:T(512)(128)(4,1)S...) while((s32[]{:T(128)}, f32[512,12,64]{0,2,1:T(8,128)}, ...), condition=%wide.region_39.40_spmd, body=%wide.region_36.39_spmd.sunk | while | flops 2045378560 | bytes 88164664 | solution.py:213
  677.1 25.5 %conditional.16 = (f32[512,12,64]{0,2,1:T(8,128)}, f32[1,512,12,64]{1,3,2,0:T(8,128)S(1)}, f32[1,512,12,64]{1,3,2,0:T(8,128)S(1)}) conditional(s32[]{:T(128)} %bitcast.434, f32[512,12,64]{0,2,1:T(8,128)} %get-tuple-element.1789, (s32[1,512]{1,0:T(1,128)S(1)}, s32[5,512]{1,0:T(8,128)S(1)}, s32[]{:T(128)}, bf16[5,512,12,64]{1,3,2,0:T(8,128)(2,1)}, ...), branch_computations={%region_37.37_spmd, %region_38.38_spmd} | conditional | flops 2045378560 | bytes 81872472 | solution.py:210
  677.1 7.6 fusion.50
  684.9 7.4 fusion.40
  705.9 25.5 %conditional.16 = (f32[512,12,64]{0,2,1:T(8,128)}, f32[1,512,12,64]{1,3,2,0:T(8,128)S(1)}, f32[1,512,12,64]{1,3,2,0:T(8,128)S(1)}) conditional(s32[]{:T(128)} %bitcast.434, f32[512,12,64]{0,2,1:T(8,128)} %get-tuple-element.1789, (s32[1,512]{1,0:T(1,128)S(1)}, s32[5,512]{1,0:T(8,128)S(1)}, s32[]{:T(128)}, bf16[5,512,12,64]{1,3,2,0:T(8,128)(2,1)}, ...), branch_computations={%region_37.37_spmd, %region_38.38_spmd} | conditional | flops 2045378560 | bytes 81872472 | solution.py:210
  706.0 7.6 fusion.50
  713.8 7.4 fusion.40
  744.3 53.1 %collective-permute-start.18 = (bf16[512,12,64]{0,2,1:T(8,128)(2,1)S(1)}, bf16[512,12,64]{0,2,1:T(8,128)(2,1)S(1)}, u32[]{:S(2)}, u32[]{:S(2)}) collective-permute-start(bf16[512,12,64]{0,2,1:T(8,128)(2,1)S(1)} %get-tuple-element.1164), channel_id=1, source_target_pairs={{0,1},{1,2},{2,3},{3,4},{4,5},{5,6},{6,7},{8,9},{9,10},{10,11},{11... | collective-permute-start | bytes 2359304 | tf_op jit(solution)/shard_map/ppermute | solution.py:18
  805.2 12.6 collective-permute-start.22
  817.8 16.6 collective-permute-start.23
  837.7 8.5 collective-permute-done.23
  860.4 9.8 fusion.208
  892.7 69.2 %while.87 = (s32[]{:T(128)}, f32[512,12,64]{0,2,1:T(8,128)}, f32[5,512,12,64]{1,3,2,0:T(8,128)}, f32[5,512,12,64]{1,3,2,0:T(8,128)}, pred[5]{0:T(512)(128)(4,1)S...) while((s32[]{:T(128)}, f32[512,12,64]{0,2,1:T(8,128)}, ...), condition=%wide.region_48.49_spmd, body=%wide.region_45.48_spmd.sunk | while | flops 2045378560 | bytes 88164664 | solution.py:213
  901.5 25.7 %conditional.17 = (f32[512,12,64]{0,2,1:T(8,128)}, f32[1,512,12,64]{1,3,2,0:T(8,128)S(1)}, f32[1,512,12,64]{1,3,2,0:T(8,128)S(1)}) conditional(s32[]{:T(128)} %bitcast.435, f32[512,12,64]{0,2,1:T(8,128)} %get-tuple-element.1831, (s32[1,512]{1,0:T(1,128)S(1)}, s32[5,512]{1,0:T(8,128)S(1)}, s32[]{:T(128)}, bf16[5,512,12,64]{1,3,2,0:T(8,128)(2,1)}, ...), branch_computations={%region_46.46_spmd, %region_47.47_spmd} | conditional | flops 2045378560 | bytes 81872472 | solution.py:210
  901.5 7.6 fusion.70
  909.3 7.5 fusion.60
  930.5 25.7 %conditional.17 = (f32[512,12,64]{0,2,1:T(8,128)}, f32[1,512,12,64]{1,3,2,0:T(8,128)S(1)}, f32[1,512,12,64]{1,3,2,0:T(8,128)S(1)}) conditional(s32[]{:T(128)} %bitcast.435, f32[512,12,64]{0,2,1:T(8,128)} %get-tuple-element.1831, (s32[1,512]{1,0:T(1,128)S(1)}, s32[5,512]{1,0:T(8,128)S(1)}, s32[]{:T(128)}, bf16[5,512,12,64]{1,3,2,0:T(8,128)(2,1)}, ...), branch_computations={%region_46.46_spmd, %region_47.47_spmd} | conditional | flops 2045378560 | bytes 81872472 | solution.py:210
  930.5 7.6 fusion.70
  938.3 7.4 fusion.60
  969.0 69.1 %collective-permute-start.26 = (bf16[512,12,64]{0,2,1:T(8,128)(2,1)S(1)}, bf16[512,12,64]{0,2,1:T(8,128)(2,1)S(1)}, u32[]{:S(2)}, u32[]{:S(2)}) collective-permute-start(bf16[512,12,64]{0,2,1:T(8,128)(2,1)S(1)} %get-tuple-element.1156), channel_id=1, source_target_pairs={{0,1},{1,2},{2,3},{3,4},{4,5},{5,6},{6,7},{8,9},{9,10},{10,11},{11... | collective-permute-start | bytes 2359304 | tf_op jit(solution)/shard_map/ppermute | solution.py:18
  1038.1 7.0 collective-permute-start.27
  1048.8 7.1 collective-permute-start.30
  1055.8 23.9 %collective-permute-start.31 = (bf16[512,12,64]{0,2,1:T(8,128)(2,1)S(1)}, bf16[512,12,64]{0,2,1:T(8,128)(2,1)S(1)}, u32[]{:S(2)}, u32[]{:S(2)}) collective-permute-start(bf16[512,12,64]{0,2,1:T(8,128)(2,1)S(1)} %get-tuple-element.1159), channel_id=1, source_target_pairs={{0,2},{1,3},{2,4},{3,5},{4,6},{5,7},{8,10},{9,11},{10,12},{11,13},... | collective-permute-start | bytes 2359304 | tf_op jit(solution)/shard_map/ppermute | solution.py:18
  1081.9 13.1 collective-permute-done.31
  1108.3 6.7 convolution_convert_fusion
  1116.4 6.5 convolution_convert_fusion.2
  1124.4 6.4 convolution_convert_fusion.3
  1132.0 6.7 convolution_convert_fusion.1
  1141.2 57.8 %reduce-scatter.25.cloned.1.call-done = bf16[96,2304]{1,0:T(8,128)(2,1)} async-done(((bf16[768,2304]{1,0:T(8,128)(2,1)}), bf16[96,2304]{1,0:T(8,128)(2,1)}) %reduce-scatter.25.cloned.1.call-update) | async-done | bytes 442384
  1201.1 64.3 %reduce-scatter.15.cloned.1.call-done = bf16[96,768]{1,0:T(8,128)(2,1)} async-done(((bf16[768,768]{1,0:T(8,128)(2,1)}), bf16[96,768]{1,0:T(8,128)(2,1)}) %reduce-scatter.15.cloned.1.call-update) | async-done | bytes 147472 | tf_op jit(solution)/shard_map/reduce_scatter | solution.py:421
  1265.3 66.9 %reduce-scatter.13.cloned.1.call-done = bf16[96,768]{1,0:T(8,128)(2,1)} async-done(((bf16[768,768]{1,0:T(8,128)(2,1)}), bf16[96,768]{1,0:T(8,128)(2,1)}) %reduce-scatter.13.cloned.1.call-update) | async-done | bytes 147472 | tf_op jit(solution)/shard_map/reduce_scatter | solution.py:421
  1332.3 99.5 %reduce-scatter.23.cloned.1.call-done = bf16[384,768]{1,0:T(8,128)(2,1)} async-done(((bf16[3072,768]{1,0:T(8,128)(2,1)}), bf16[384,768]{1,0:T(8,128)(2,1)}) %reduce-scatter.23.cloned.1.call-update) | async-done | bytes 589840 | tf_op jit(solution)/shard_map/reduce_scatter | solution.py:427
  1431.8 98.7 %reduce-scatter.19.cloned.1.call-done = bf16[96,3072]{1,0:T(8,128)(2,1)} async-done(((bf16[768,3072]{1,0:T(8,128)(2,1)}), bf16[96,3072]{1,0:T(8,128)(2,1)}) %reduce-scatter.19.cloned.1.call-update) | async-done | bytes 589840 | tf_op jit(solution)/shard_map/reduce_scatter | solution.py:424
  1530.5 98.7 %reduce-scatter.17.cloned.1.call-done = bf16[96,3072]{1,0:T(8,128)(2,1)} async-done(((bf16[768,3072]{1,0:T(8,128)(2,1)}), bf16[96,3072]{1,0:T(8,128)(2,1)}) %reduce-scatter.17.cloned.1.call-update) | async-done | bytes 589840 | tf_op jit(solution)/shard_map/reduce_scatter | solution.py:424
  1629.2 98.7 %reduce-scatter.21.cloned.1.call-done = bf16[384,768]{1,0:T(8,128)(2,1)} async-done(((bf16[3072,768]{1,0:T(8,128)(2,1)}), bf16[384,768]{1,0:T(8,128)(2,1)}) %reduce-scatter.21.cloned.1.call-update) | async-done | bytes 589840 | tf_op jit(solution)/shard_map/reduce_scatter | solution.py:427
  1732.1 29.4 %all-reduce.8 = (bf16[7680]{0:T(1024)(128)(2,1)S(1)}, bf16[7680]{0:T(1024)(128)(2,1)S(1)}, bf16[1536]{0:T(1024)(128)(2,1)S(1)}, bf16[1536]{0:T(1024)(128)(2,1)S(1)}) all-reduce(bf16[7680]{0:T(1024)(128)(2,1)S(1)} %dynamic-update-slice.10, ...), channel_id=23, replica_groups=mesh['grp'=4,'shard'=8] {'shard'}, use_global_device_ids=true, to_apply=%region_81.82.clone | all-reduce | flops 18432 | bytes 73728
  1761.9 16.6 all-reduce.10
  1785.4 26.5 %all-reduce.14.cloned.1.call-done = (bf16[1,96,2304]{1,2,0:T(8,128)(2,1)}, bf16[1,96,2304]{1,2,0:T(8,128)(2,1)}, bf16[1,96,768]{2,1,0:T(8,128)(2,1)}, bf16[1,96,...) async-done(((bf16[1,96,2304]{1,2,0:T(8,128)(2,1)}, ...) | async-done | bytes 3538960 | tf_op jit(solution)/shard_map/psum | solution.py:438
  (698 shorter events, 440.5 us)
Async XLA Ops:
  7.2 71.0 %all-gather.21.cloned.1.call-start = ((), (), s32[]{:S(2)}) async-start(), calls=%async_computation.14 | async-start | bytes 3981312 | tf_op jit(solution)/shard_map/all_gather | solution.py:258
  9.5 220.6 %all-gather.23.cloned.1.call-start = ((), (), s32[]{:S(2)}) async-start(), calls=%async_computation.15 | async-start | bytes 1327104 | tf_op jit(solution)/shard_map/all_gather | solution.py:259
  11.3 229.4 %all-gather.25.cloned.1.call-start = ((), (), s32[]{:S(2)}) async-start(), calls=%async_computation.16 | async-start | bytes 5308416 | tf_op jit(solution)/shard_map/all_gather | solution.py:260
  13.8 307.9 %all-gather.27.cloned.1.call-start = ((), (), s32[]{:S(2)}) async-start(), calls=%async_computation.17 | async-start | bytes 5308416 | tf_op jit(solution)/shard_map/all_gather | solution.py:261
  14.9 372.1 %all-gather.29.cloned.1.call-start = ((), (), s32[]{:S(2)}) async-start(), calls=%async_computation.18 | async-start | bytes 3981312 | tf_op jit(solution)/shard_map/all_gather | solution.py:258
  15.5 522.3 %all-gather.31.cloned.1.call-start = ((), (), s32[]{:S(2)}) async-start(), calls=%async_computation.19 | async-start | bytes 1327104 | tf_op jit(solution)/shard_map/all_gather | solution.py:259
  16.1 529.9 %all-gather.33.cloned.1.call-start = ((), (), s32[]{:S(2)}) async-start(), calls=%async_computation.20 | async-start | bytes 5308416 | tf_op jit(solution)/shard_map/all_gather | solution.py:260
  16.8 609.7 %all-gather.35.cloned.1.call-start = ((), (), s32[]{:S(2)}) async-start(), calls=%async_computation.21 | async-start | bytes 5308416 | tf_op jit(solution)/shard_map/all_gather | solution.py:261
  82.7 22.3 %collective-permute-start = (bf16[512,12,64]{0,2,1:T(8,128)(2,1)S(1)}, bf16[512,12,64]{0,2,1:T(8,128)(2,1)}, u32[]{:S(2)}, u32[]{:S(2)}) collective-permute-start(bf16[512,12,64]{0,2,1:T(8,128)(2,1)S(1)} %bitcast.452), channel_id=1, source_target_pairs={{0,2},{1,3},{2,4},{3,5},{4,6},{5,7},{8,10},{9,11},{10,12},{11,13},... | collective-permute-start | bytes 2359304 | tf_op jit(solution)/shard_map/ppermute | solution.py:18
  86.8 42.9 %collective-permute-start.1 = (bf16[512,12,64]{0,2,1:T(8,128)(2,1)S(1)}, bf16[512,12,64]{0,2,1:T(8,128)(2,1)}, u32[]{:S(2)}, u32[]{:S(2)}) collective-permute-start(bf16[512,12,64]{0,2,1:T(8,128)(2,1)S(1)} %bitcast.453), channel_id=1, source_target_pairs={{0,1},{1,2},{2,3},{3,4},{4,5},{5,6},{6,7},{8,9},{9,10},{10,11},{11... | collective-permute-start | bytes 2359304 | tf_op jit(solution)/shard_map/ppermute | solution.py:18
  92.0 40.3 %collective-permute-start.2 = (bf16[512,12,64]{0,2,1:T(8,128)(2,1)S(1)}, bf16[512,12,64]{0,2,1:T(8,128)(2,1)}, u32[]{:S(2)}, u32[]{:S(2)}) collective-permute-start(bf16[512,12,64]{0,2,1:T(8,128)(2,1)S(1)} %bitcast.454), channel_id=1, source_target_pairs={{1,0},{2,1},{3,2},{4,3},{5,4},{6,5},{7,6},{9,8},{10,9},{11,10},{12... | collective-permute-start | bytes 2359304 | tf_op jit(solution)/shard_map/ppermute | solution.py:18
  94.2 64.6 %collective-permute-start.4 = (bf16[512,12,64]{0,2,1:T(8,128)(2,1)S(1)}, bf16[512,12,64]{0,2,1:T(8,128)(2,1)}, u32[]{:S(2)}, u32[]{:S(2)}) collective-permute-start(bf16[512,12,64]{0,2,1:T(8,128)(2,1)S(1)} %bitcast.447), channel_id=1, source_target_pairs={{0,2},{1,3},{2,4},{3,5},{4,6},{5,7},{8,10},{9,11},{10,12},{11,13},... | collective-permute-start | bytes 2359304 | tf_op jit(solution)/shard_map/ppermute | solution.py:18
  99.3 68.1 %collective-permute-start.5 = (bf16[512,12,64]{0,2,1:T(8,128)(2,1)S(1)}, bf16[512,12,64]{0,2,1:T(8,128)(2,1)}, u32[]{:S(2)}, u32[]{:S(2)}) collective-permute-start(bf16[512,12,64]{0,2,1:T(8,128)(2,1)S(1)} %bitcast.448), channel_id=1, source_target_pairs={{0,1},{1,2},{2,3},{3,4},{4,5},{5,6},{6,7},{8,9},{9,10},{10,11},{11... | collective-permute-start | bytes 2359304 | tf_op jit(solution)/shard_map/ppermute | solution.py:18
  105.0 32.6 %collective-permute-start.3 = (bf16[512,12,64]{0,2,1:T(8,128)(2,1)S(1)}, bf16[512,12,64]{0,2,1:T(8,128)(2,1)S(1)}, u32[]{:S(2)}, u32[]{:S(2)}) collective-permute-start(bf16[512,12,64]{0,2,1:T(8,128)(2,1)S(1)} %bitcast.455), channel_id=1, source_target_pairs={{2,0},{3,1},{4,2},{5,3},{6,4},{7,5},{10,8},{11,9},{12,10},{13,11},... | collective-permute-start | bytes 2359304 | tf_op jit(solution)/shard_map/ppermute | solution.py:18
  129.6 39.1 %collective-permute-start.6 = (bf16[512,12,64]{0,2,1:T(8,128)(2,1)S(1)}, bf16[512,12,64]{0,2,1:T(8,128)(2,1)}, u32[]{:S(2)}, u32[]{:S(2)}) collective-permute-start(bf16[512,12,64]{0,2,1:T(8,128)(2,1)S(1)} %bitcast.449), channel_id=1, source_target_pairs={{1,0},{2,1},{3,2},{4,3},{5,4},{6,5},{7,6},{9,8},{10,9},{11,10},{12... | collective-permute-start | bytes 2359304 | tf_op jit(solution)/shard_map/ppermute | solution.py:18
  132.2 61.3 %collective-permute-start.7 = (bf16[512,12,64]{0,2,1:T(8,128)(2,1)S(1)}, bf16[512,12,64]{0,2,1:T(8,128)(2,1)}, u32[]{:S(2)}, u32[]{:S(2)}) collective-permute-start(bf16[512,12,64]{0,2,1:T(8,128)(2,1)S(1)} %bitcast.450), channel_id=1, source_target_pairs={{2,0},{3,1},{4,2},{5,3},{6,4},{7,5},{10,8},{11,9},{12,10},{13,11},... | collective-permute-start | bytes 2359304 | tf_op jit(solution)/shard_map/ppermute | solution.py:18
  393.7 25.0 %collective-permute-start.8 = (bf16[512,12,64]{0,2,1:T(8,128)(2,1)S(1)}, bf16[512,12,64]{0,2,1:T(8,128)(2,1)}, u32[]{:S(2)}, u32[]{:S(2)}) collective-permute-start(bf16[512,12,64]{0,2,1:T(8,128)(2,1)S(1)} %bitcast.457), channel_id=1, source_target_pairs={{0,2},{1,3},{2,4},{3,5},{4,6},{5,7},{8,10},{9,11},{10,12},{11,13},... | collective-permute-start | bytes 2359304 | tf_op jit(solution)/shard_map/ppermute | solution.py:18
  397.1 39.9 %collective-permute-start.9 = (bf16[512,12,64]{0,2,1:T(8,128)(2,1)S(1)}, bf16[512,12,64]{0,2,1:T(8,128)(2,1)}, u32[]{:S(2)}, u32[]{:S(2)}) collective-permute-start(bf16[512,12,64]{0,2,1:T(8,128)(2,1)S(1)} %bitcast.458), channel_id=1, source_target_pairs={{0,1},{1,2},{2,3},{3,4},{4,5},{5,6},{6,7},{8,9},{9,10},{10,11},{11... | collective-permute-start | bytes 2359304 | tf_op jit(solution)/shard_map/ppermute | solution.py:18
  400.2 738.7 %reduce-scatter.27.cloned.1.call-start = ((), (), s32[]{:S(2)}) async-start(), calls=%async_computation.23 | async-start | bytes 3981312
  400.3 39.3 %collective-permute-start.10 = (bf16[512,12,64]{0,2,1:T(8,128)(2,1)S(1)}, bf16[512,12,64]{0,2,1:T(8,128)(2,1)}, u32[]{:S(2)}, u32[]{:S(2)}) collective-permute-start(bf16[512,12,64]{0,2,1:T(8,128)(2,1)S(1)} %bitcast.459), channel_id=1, source_target_pairs={{1,0},{2,1},{3,2},{4,3},{5,4},{6,5},{7,6},{9,8},{10,9},{11,10},{12... | collective-permute-start | bytes 2359304 | tf_op jit(solution)/shard_map/ppermute | solution.py:18
  404.5 65.3 %collective-permute-start.12 = (bf16[512,12,64]{0,2,1:T(8,128)(2,1)S(1)}, bf16[512,12,64]{0,2,1:T(8,128)(2,1)}, u32[]{:S(2)}, u32[]{:S(2)}) collective-permute-start(bf16[512,12,64]{0,2,1:T(8,128)(2,1)S(1)} %bitcast.442), channel_id=1, source_target_pairs={{0,2},{1,3},{2,4},{3,5},{4,6},{5,7},{8,10},{9,11},{10,12},{11,13},... | collective-permute-start | bytes 2359304 | tf_op jit(solution)/shard_map/ppermute | solution.py:18
  409.7 62.7 %collective-permute-start.13 = (bf16[512,12,64]{0,2,1:T(8,128)(2,1)S(1)}, bf16[512,12,64]{0,2,1:T(8,128)(2,1)}, u32[]{:S(2)}, u32[]{:S(2)}) collective-permute-start(bf16[512,12,64]{0,2,1:T(8,128)(2,1)S(1)} %bitcast.443), channel_id=1, source_target_pairs={{0,1},{1,2},{2,3},{3,4},{4,5},{5,6},{6,7},{8,9},{9,10},{10,11},{11... | collective-permute-start | bytes 2359304 | tf_op jit(solution)/shard_map/ppermute | solution.py:18
  418.6 29.2 %collective-permute-start.11 = (bf16[512,12,64]{0,2,1:T(8,128)(2,1)S(1)}, bf16[512,12,64]{0,2,1:T(8,128)(2,1)S(1)}, u32[]{:S(2)}, u32[]{:S(2)}) collective-permute-start(bf16[512,12,64]{0,2,1:T(8,128)(2,1)S(1)} %bitcast.460), channel_id=1, source_target_pairs={{2,0},{3,1},{4,2},{5,3},{6,4},{7,5},{10,8},{11,9},{12,10},{13,11},... | collective-permute-start | bytes 2359304 | tf_op jit(solution)/shard_map/ppermute | solution.py:18
  437.0 36.6 %collective-permute-start.14 = (bf16[512,12,64]{0,2,1:T(8,128)(2,1)S(1)}, bf16[512,12,64]{0,2,1:T(8,128)(2,1)}, u32[]{:S(2)}, u32[]{:S(2)}) collective-permute-start(bf16[512,12,64]{0,2,1:T(8,128)(2,1)S(1)} %bitcast.444), channel_id=1, source_target_pairs={{1,0},{2,1},{3,2},{4,3},{5,4},{6,5},{7,6},{9,8},{10,9},{11,10},{12... | collective-permute-start | bytes 2359304 | tf_op jit(solution)/shard_map/ppermute | solution.py:18
  439.6 61.1 %collective-permute-start.15 = (bf16[512,12,64]{0,2,1:T(8,128)(2,1)S(1)}, bf16[512,12,64]{0,2,1:T(8,128)(2,1)}, u32[]{:S(2)}, u32[]{:S(2)}) collective-permute-start(bf16[512,12,64]{0,2,1:T(8,128)(2,1)S(1)} %bitcast.445), channel_id=1, source_target_pairs={{2,0},{3,1},{4,2},{5,3},{6,4},{7,5},{10,8},{11,9},{12,10},{13,11},... | collective-permute-start | bytes 2359304 | tf_op jit(solution)/shard_map/ppermute | solution.py:18
  741.6 62.3 %collective-permute-start.16 = (bf16[512,12,64]{0,2,1:T(8,128)(2,1)S(1)}, bf16[512,12,64]{0,2,1:T(8,128)(2,1)S(1)}, u32[]{:S(2)}, u32[]{:S(2)}) collective-permute-start(bf16[512,12,64]{0,2,1:T(8,128)(2,1)S(1)} %get-tuple-element.1162), channel_id=1, source_target_pairs={{2,0},{3,1},{4,2},{5,3},{6,4},{7,5},{10,8},{11,9},{12,10},{13,11},... | collective-permute-start | bytes 2359304 | tf_op jit(solution)/shard_map/ppermute | solution.py:18
  743.0 62.2 %collective-permute-start.17 = (bf16[512,12,64]{0,2,1:T(8,128)(2,1)S(1)}, bf16[512,12,64]{0,2,1:T(8,128)(2,1)S(1)}, u32[]{:S(2)}, u32[]{:S(2)}) collective-permute-start(bf16[512,12,64]{0,2,1:T(8,128)(2,1)S(1)} %get-tuple-element.1165), channel_id=1, source_target_pairs={{1,0},{2,1},{3,2},{4,3},{5,4},{6,5},{7,6},{9,8},{10,9},{11,10},{12... | collective-permute-start | bytes 2359304 | tf_op jit(solution)/shard_map/ppermute | solution.py:18
  744.3 73.5 %collective-permute-start.18 = (bf16[512,12,64]{0,2,1:T(8,128)(2,1)S(1)}, bf16[512,12,64]{0,2,1:T(8,128)(2,1)S(1)}, u32[]{:S(2)}, u32[]{:S(2)}) collective-permute-start(bf16[512,12,64]{0,2,1:T(8,128)(2,1)S(1)} %get-tuple-element.1164), channel_id=1, source_target_pairs={{0,1},{1,2},{2,3},{3,4},{4,5},{5,6},{6,7},{8,9},{9,10},{10,11},{11... | collective-permute-start | bytes 2359304 | tf_op jit(solution)/shard_map/ppermute | solution.py:18
  797.4 37.8 %collective-permute-start.19 = (bf16[512,12,64]{0,2,1:T(8,128)(2,1)S(1)}, bf16[512,12,64]{0,2,1:T(8,128)(2,1)S(1)}, u32[]{:S(2)}, u32[]{:S(2)}) collective-permute-start(bf16[512,12,64]{0,2,1:T(8,128)(2,1)S(1)} %get-tuple-element.1163), channel_id=1, source_target_pairs={{0,2},{1,3},{2,4},{3,5},{4,6},{5,7},{8,10},{9,11},{10,12},{11,13},... | collective-permute-start | bytes 2359304 | tf_op jit(solution)/shard_map/ppermute | solution.py:18
  802.4 35.2 %collective-permute-start.20 = (bf16[512,12,64]{0,2,1:T(8,128)(2,1)S(1)}, bf16[512,12,64]{0,2,1:T(8,128)(2,1)S(1)}, u32[]{:S(2)}, u32[]{:S(2)}) collective-permute-start(bf16[512,12,64]{0,2,1:T(8,128)(2,1)S(1)} %get-tuple-element.1166), channel_id=1, source_target_pairs={{2,0},{3,1},{4,2},{5,3},{6,4},{7,5},{10,8},{11,9},{12,10},{13,11},... | collective-permute-start | bytes 2359304 | tf_op jit(solution)/shard_map/ppermute | solution.py:18
  803.9 33.8 %collective-permute-start.21 = (bf16[512,12,64]{0,2,1:T(8,128)(2,1)S(1)}, bf16[512,12,64]{0,2,1:T(8,128)(2,1)S(1)}, u32[]{:S(2)}, u32[]{:S(2)}) collective-permute-start(bf16[512,12,64]{0,2,1:T(8,128)(2,1)S(1)} %get-tuple-element.1169), channel_id=1, source_target_pairs={{1,0},{2,1},{3,2},{4,3},{5,4},{6,5},{7,6},{9,8},{10,9},{11,10},{12... | collective-permute-start | bytes 2359304 | tf_op jit(solution)/shard_map/ppermute | solution.py:18
  805.2 32.5 %collective-permute-start.22 = (bf16[512,12,64]{0,2,1:T(8,128)(2,1)S(1)}, bf16[512,12,64]{0,2,1:T(8,128)(2,1)S(1)}, u32[]{:S(2)}, u32[]{:S(2)}) collective-permute-start(bf16[512,12,64]{0,2,1:T(8,128)(2,1)S(1)} %get-tuple-element.1168), channel_id=1, source_target_pairs={{0,1},{1,2},{2,3},{3,4},{4,5},{5,6},{6,7},{8,9},{9,10},{10,11},{11... | collective-permute-start | bytes 2359304 | tf_op jit(solution)/shard_map/ppermute | solution.py:18
  817.8 28.4 %collective-permute-start.23 = (bf16[512,12,64]{0,2,1:T(8,128)(2,1)S(1)}, bf16[512,12,64]{0,2,1:T(8,128)(2,1)S(1)}, u32[]{:S(2)}, u32[]{:S(2)}) collective-permute-start(bf16[512,12,64]{0,2,1:T(8,128)(2,1)S(1)} %get-tuple-element.1167), channel_id=1, source_target_pairs={{0,2},{1,3},{2,4},{3,5},{4,6},{5,7},{8,10},{9,11},{10,12},{11,13},... | collective-permute-start | bytes 2359304 | tf_op jit(solution)/shard_map/ppermute | solution.py:18
  859.1 339.9 %reduce-scatter.25.cloned.1.call-start = ((), (), s32[]{:S(2)}) async-start(), calls=%async_computation.22 | async-start | bytes 3981312
  966.2 81.2 %collective-permute-start.24 = (bf16[512,12,64]{0,2,1:T(8,128)(2,1)S(1)}, bf16[512,12,64]{0,2,1:T(8,128)(2,1)S(1)}, u32[]{:S(2)}, u32[]{:S(2)}) collective-permute-start(bf16[512,12,64]{0,2,1:T(8,128)(2,1)S(1)} %get-tuple-element.1154), channel_id=1, source_target_pairs={{2,0},{3,1},{4,2},{5,3},{6,4},{7,5},{10,8},{11,9},{12,10},{13,11},... | collective-permute-start | bytes 2359304 | tf_op jit(solution)/shard_map/ppermute | solution.py:18
  967.7 81.1 %collective-permute-start.25 = (bf16[512,12,64]{0,2,1:T(8,128)(2,1)S(1)}, bf16[512,12,64]{0,2,1:T(8,128)(2,1)S(1)}, u32[]{:S(2)}, u32[]{:S(2)}) collective-permute-start(bf16[512,12,64]{0,2,1:T(8,128)(2,1)S(1)} %get-tuple-element.1157), channel_id=1, source_target_pairs={{1,0},{2,1},{3,2},{4,3},{5,4},{6,5},{7,6},{9,8},{10,9},{11,10},{12... | collective-permute-start | bytes 2359304 | tf_op jit(solution)/shard_map/ppermute | solution.py:18
  969.0 86.9 %collective-permute-start.26 = (bf16[512,12,64]{0,2,1:T(8,128)(2,1)S(1)}, bf16[512,12,64]{0,2,1:T(8,128)(2,1)S(1)}, u32[]{:S(2)}, u32[]{:S(2)}) collective-permute-start(bf16[512,12,64]{0,2,1:T(8,128)(2,1)S(1)} %get-tuple-element.1156), channel_id=1, source_target_pairs={{0,1},{1,2},{2,3},{3,4},{4,5},{5,6},{6,7},{8,9},{9,10},{10,11},{11... | collective-permute-start | bytes 2359304 | tf_op jit(solution)/shard_map/ppermute | solution.py:18
  1038.1 41.7 %collective-permute-start.27 = (bf16[512,12,64]{0,2,1:T(8,128)(2,1)S(1)}, bf16[512,12,64]{0,2,1:T(8,128)(2,1)S(1)}, u32[]{:S(2)}, u32[]{:S(2)}) collective-permute-start(bf16[512,12,64]{0,2,1:T(8,128)(2,1)S(1)} %get-tuple-element.1155), channel_id=1, source_target_pairs={{0,2},{1,3},{2,4},{3,5},{4,6},{5,7},{8,10},{9,11},{10,12},{11,13},... | collective-permute-start | bytes 2359304 | tf_op jit(solution)/shard_map/ppermute | solution.py:18
  1046.0 35.9 %collective-permute-start.28 = (bf16[512,12,64]{0,2,1:T(8,128)(2,1)S(1)}, bf16[512,12,64]{0,2,1:T(8,128)(2,1)S(1)}, u32[]{:S(2)}, u32[]{:S(2)}) collective-permute-start(bf16[512,12,64]{0,2,1:T(8,128)(2,1)S(1)} %get-tuple-element.1158), channel_id=1, source_target_pairs={{2,0},{3,1},{4,2},{5,3},{6,4},{7,5},{10,8},{11,9},{12,10},{13,11},... | collective-permute-start | bytes 2359304 | tf_op jit(solution)/shard_map/ppermute | solution.py:18
  1047.4 34.5 %collective-permute-start.29 = (bf16[512,12,64]{0,2,1:T(8,128)(2,1)S(1)}, bf16[512,12,64]{0,2,1:T(8,128)(2,1)S(1)}, u32[]{:S(2)}, u32[]{:S(2)}) collective-permute-start(bf16[512,12,64]{0,2,1:T(8,128)(2,1)S(1)} %get-tuple-element.1161), channel_id=1, source_target_pairs={{1,0},{2,1},{3,2},{4,3},{5,4},{6,5},{7,6},{9,8},{10,9},{11,10},{12... | collective-permute-start | bytes 2359304 | tf_op jit(solution)/shard_map/ppermute | solution.py:18
  1048.8 33.2 %collective-permute-start.30 = (bf16[512,12,64]{0,2,1:T(8,128)(2,1)S(1)}, bf16[512,12,64]{0,2,1:T(8,128)(2,1)S(1)}, u32[]{:S(2)}, u32[]{:S(2)}) collective-permute-start(bf16[512,12,64]{0,2,1:T(8,128)(2,1)S(1)} %get-tuple-element.1160), channel_id=1, source_target_pairs={{0,1},{1,2},{2,3},{3,4},{4,5},{5,6},{6,7},{8,9},{9,10},{10,11},{11... | collective-permute-start | bytes 2359304 | tf_op jit(solution)/shard_map/ppermute | solution.py:18
  1055.8 39.1 %collective-permute-start.31 = (bf16[512,12,64]{0,2,1:T(8,128)(2,1)S(1)}, bf16[512,12,64]{0,2,1:T(8,128)(2,1)S(1)}, u32[]{:S(2)}, u32[]{:S(2)}) collective-permute-start(bf16[512,12,64]{0,2,1:T(8,128)(2,1)S(1)} %get-tuple-element.1159), channel_id=1, source_target_pairs={{0,2},{1,3},{2,4},{3,5},{4,6},{5,7},{8,10},{9,11},{10,12},{11,13},... | collective-permute-start | bytes 2359304 | tf_op jit(solution)/shard_map/ppermute | solution.py:18
  1103.0 162.4 %reduce-scatter.15.cloned.1.call-start = ((), (), s32[]{:S(2)}) async-start(), calls=%async_computation.9 | async-start | bytes 1327104 | tf_op jit(solution)/shard_map/reduce_scatter | solution.py:421
  1106.3 225.9 %reduce-scatter.13.cloned.1.call-start = ((), (), s32[]{:S(2)}) async-start(), calls=%async_computation.8 | async-start | bytes 1327104 | tf_op jit(solution)/shard_map/reduce_scatter | solution.py:421
  1108.2 323.6 %reduce-scatter.23.cloned.1.call-start = ((), (), s32[]{:S(2)}) async-start(), calls=%async_computation.13 | async-start | bytes 5308416 | tf_op jit(solution)/shard_map/reduce_scatter | solution.py:427
  1115.1 415.5 %reduce-scatter.19.cloned.1.call-start = ((), (), s32[]{:S(2)}) async-start(), calls=%async_computation.11 | async-start | bytes 5308416 | tf_op jit(solution)/shard_map/reduce_scatter | solution.py:424
  1123.0 506.2 %reduce-scatter.17.cloned.1.call-start = ((), (), s32[]{:S(2)}) async-start(), calls=%async_computation.10 | async-start | bytes 5308416 | tf_op jit(solution)/shard_map/reduce_scatter | solution.py:424
  1130.8 597.1 %reduce-scatter.21.cloned.1.call-start = ((), (), s32[]{:S(2)}) async-start(), calls=%async_computation.12 | async-start | bytes 5308416 | tf_op jit(solution)/shard_map/reduce_scatter | solution.py:427
  1138.7 591.5 %copy-start.101 = (bf16[3072]{0:T(1024)(128)(2,1)S(1)}, bf16[3072]{0:T(1024)(128)(2,1)}, u32[]{:S(2)}) copy-start(bf16[3072]{0:T(1024)(128)(2,1)} %get-tuple-element.1204) | copy-start | bytes 18436
  1138.7 591.7 %copy-start.95 = (bf16[768]{0:T(1024)(128)(2,1)S(1)}, bf16[768]{0:T(1024)(128)(2,1)}, u32[]{:S(2)}) copy-start(bf16[768]{0:T(1024)(128)(2,1)} %get-tuple-element.947) | copy-start | bytes 4612
  1138.7 591.9 %copy-start.100 = (bf16[768]{0:T(1024)(128)(2,1)S(1)}, bf16[768]{0:T(1024)(128)(2,1)}, u32[]{:S(2)}) copy-start(bf16[768]{0:T(1024)(128)(2,1)} %get-tuple-element.942) | copy-start | bytes 4612
  1138.7 591.9 %copy-start.118 = (bf16[768]{0:T(1024)(128)(2,1)S(1)}, bf16[768]{0:T(1024)(128)(2,1)}, u32[]{:S(2)}) copy-start(bf16[768]{0:T(1024)(128)(2,1)} %get-tuple-element.940) | copy-start | bytes 4612
  1138.8 591.9 %copy-start.119 = (bf16[768]{0:T(1024)(128)(2,1)S(1)}, bf16[768]{0:T(1024)(128)(2,1)}, u32[]{:S(2)}) copy-start(bf16[768]{0:T(1024)(128)(2,1)} %get-tuple-element.938) | copy-start | bytes 4612
  1138.8 591.9 %copy-start.120 = (bf16[768]{0:T(1024)(128)(2,1)S(1)}, bf16[768]{0:T(1024)(128)(2,1)}, u32[]{:S(2)}) copy-start(bf16[768]{0:T(1024)(128)(2,1)} %get-tuple-element.936) | copy-start | bytes 4612
  1138.8 592.5 %copy-start.99 = (bf16[768]{0:T(1024)(128)(2,1)S(1)}, bf16[768]{0:T(1024)(128)(2,1)}, u32[]{:S(2)}) copy-start(bf16[768]{0:T(1024)(128)(2,1)} %get-tuple-element.1116) | copy-start | bytes 4612
  1138.8 592.7 %copy-start.117 = (bf16[768]{0:T(1024)(128)(2,1)S(1)}, bf16[768]{0:T(1024)(128)(2,1)}, u32[]{:S(2)}) copy-start(bf16[768]{0:T(1024)(128)(2,1)} %get-tuple-element.944) | copy-start | bytes 4612
  1138.8 592.9 %copy-start.102 = (bf16[3072]{0:T(1024)(128)(2,1)S(1)}, bf16[3072]{0:T(1024)(128)(2,1)}, u32[]{:S(2)}) copy-start(bf16[3072]{0:T(1024)(128)(2,1)} %get-tuple-element.1206) | copy-start | bytes 18436
  1138.8 592.9 %copy-start.98 = (bf16[768]{0:T(1024)(128)(2,1)S(1)}, bf16[768]{0:T(1024)(128)(2,1)}, u32[]{:S(2)}) copy-start(bf16[768]{0:T(1024)(128)(2,1)} %get-tuple-element.1114) | copy-start | bytes 4612
  1138.8 593.1 %copy-start.116 = (bf16[768]{0:T(1024)(128)(2,1)S(1)}, bf16[768]{0:T(1024)(128)(2,1)}, u32[]{:S(2)}) copy-start(bf16[768]{0:T(1024)(128)(2,1)} %get-tuple-element.945) | copy-start | bytes 4612
  1138.8 640.9 %copy-start.24 = (f32[512,768]{1,0:T(8,128)S(1)}, f32[512,768]{1,0:T(8,128)}, u32[]{:S(2)}) copy-start(f32[512,768]{1,0:T(8,128)} %copy-done.23) | copy-start | bytes 4718596
  1138.8 640.9 %copy-start.36 = (bf16[512,12,64]{0,2,1:T(8,128)(2,1)S(1)}, bf16[512,12,64]{0,2,1:T(8,128)(2,1)}, u32[]{:S(2)}) copy-start(bf16[512,12,64]{0,2,1:T(8,128)(2,1)} %copy-done.35) | copy-start | bytes 2359300
  1138.8 640.9 %copy-start.38 = (bf16[512,12,64]{0,2,1:T(8,128)(2,1)S(1)}, bf16[512,12,64]{0,2,1:T(8,128)(2,1)}, u32[]{:S(2)}) copy-start(bf16[512,12,64]{0,2,1:T(8,128)(2,1)} %copy-done.37) | copy-start | bytes 2359300
  1138.9 640.8 %copy-start.94 = (f32[512]{0:T(512)S(1)}, f32[512]{0:T(512)}, u32[]{:S(2)}) copy-start(f32[512]{0:T(512)} %copy-done.93) | copy-start | bytes 6148
  1138.9 673.0 %all-reduce.14.cloned.1.call-start = ((), (), s32[]{:S(2)}) async-start(), calls=%async_computation.24 | async-start | bytes 7667712 | tf_op jit(solution)/shard_map/psum | solution.py:438
  (125 other events, 6278.0 us)
Sparse Core Ops, SparseCore 0:
  10.8 67.3 all-gather.20
  81.0 62.4 all-gather.22
  146.2 94.5 all-gather.24
  243.4 78.2 all-gather.26
  323.7 63.3 all-gather.28
  389.1 60.7 all-gather.30
  452.1 93.8 all-gather.32
  548.2 78.3 all-gather.34
  859.2 99.6 reduce-scatter.26
  1103.1 95.8 reduce-scatter.24
  1203.0 62.3 reduce-scatter.14
  1269.2 63.0 reduce-scatter.12
  1335.9 95.8 reduce-scatter.22
  1435.3 95.1 reduce-scatter.18
  1534.0 95.1 reduce-scatter.16
  1632.7 95.1 reduce-scatter.20
  1731.2 80.5 all-reduce.13
where the time goes:
time: 1840 us; the launch traced here: 1830 us
  waiting for transfers between devices  957 us (52%)
  matrix products  316 us (17%)
  starting transfers between devices  245 us (13%)
  local copies, waits for them, and re-layouts  135 us (7%)
  blocking collectives  78.9 us (4%)
  other arithmetic  56.8 us (3%)
  loops' own time  20.4 us (1%)
  between operations  19 us (1%)
    ppermute x32, starting transfers between devices, passed_along(): return lax.ppermute(shard, axis, pairs)  244 us
    reduce_scatter x2, waiting for transfers between devices, on_device(): lax.psum_scatter(shrink_grad.astype(jnp.bfloat16), 'shard', scatter_dimen...  198 us
    reduce_scatter x2, waiting for transfers between devices, on_device(): lax.psum_scatter(expand_grad.astype(jnp.bfloat16), 'shard', scatter_dimen...  197 us
    ppermute x32, waiting for transfers between devices, passed_along(): return lax.ppermute(shard, axis, pairs)  135 us
    reduce_scatter x2, waiting for transfers between devices, on_device(): lax.psum_scatter(mixing_grad.astype(jnp.bfloat16), 'shard', scatter_dimen...  131 us
    all_gather x2, waiting for transfers between devices, on_device(): lax.all_gather(w_reduce[layer_index], 'shard', axis=0, tiled=True)  119 us
    all_gather x2, waiting for transfers between devices, on_device(): lax.all_gather(w_project[layer_index], 'shard', axis=0, tiled=True)  81.1 us
    unnamed x2, blocking collectives  62.3 us
  transfers between devices with their start and end apart: 49, of which 26 were waited for; matrix products, arithmetic and copies ran while one was open for 20% of the time, Pallas kernels for 0%

commit v1 on v0

--- a/solution.py
+++ b/solution.py
@@ -1,6 +1,8 @@
 import jax
 import jax.numpy as jnp
 from jax import lax
+from jax.experimental import pallas as pl
+from jax.experimental.pallas import tpu as pltpu
 from jax.sharding import PartitionSpec as P
 
 HEADS = 12
@@ -456,6 +458,599 @@
     )
 
 
+Q_TILE = 256
+K_TILE = 256
+
+
+def fold_lanes(values, combine):
+    total = values[:, :128]
+    for begin_at in range(128, values.shape[1], 128):
+        total = combine(total, values[:, begin_at : begin_at + 128])
+    return total
+
+
+def halves_of(block):
+    lane = lax.broadcasted_iota(jnp.int32, block.shape, 1)
+    nothing = jnp.zeros_like(block)
+    return (jnp.where(lane < 64, block, nothing), jnp.where(lane < 64, nothing, block))
+
+
+def flash_forward_kernel(
+    bounds, q_ref, k_ref, v_ref, low_ref, high_ref, mix_ref, lse_ref, score_scr
+):
+    rows = q_ref.shape[0]
+    for tile in range(rows // Q_TILE):
+        span = pl.ds(tile * Q_TILE, Q_TILE)
+        heads = halves_of(q_ref[span, :] * jnp.bfloat16(0.125))
+        low = low_ref[span, 0:1]
+        high = high_ref[span, 0:1]
+        first = bounds[2 * tile]
+        last = bounds[2 * tile + 1]
+
+        def score_step(key_tile, tops):
+            begin_at = pl.multiple_of(key_tile * K_TILE, K_TILE)
+            keys = k_ref[pl.ds(begin_at, K_TILE), :]
+            place = lax.broadcasted_iota(jnp.int32, (Q_TILE, K_TILE), 1) + begin_at
+            allowed = (place >= low) & (place < high)
+            out = []
+            for head in range(2):
+                scores = lax.dot_general(
+                    heads[head], keys, (((1,), (1,)), ((), ())), preferred_element_type=jnp.float32
+                )
+                scores = jnp.where(allowed, scores, NEGATIVE)
+                score_scr[head, key_tile] = scores
+                out.append(jnp.maximum(tops[head], fold_lanes(scores, jnp.maximum)))
+            return tuple(out)
+
+        floor = jnp.full((Q_TILE, 128), NEGATIVE, jnp.float32)
+        tops = lax.fori_loop(first, last, score_step, (floor, floor))
+        tops = [jnp.max(top, axis=1, keepdims=True) for top in tops]
+
+        def mix_step(key_tile, carry):
+            begin_at = pl.multiple_of(key_tile * K_TILE, K_TILE)
+            values = v_ref[pl.ds(begin_at, K_TILE), :]
+            out = []
+            for head in range(2):
+                total, mixed = carry[head]
+                weight = jnp.exp(score_scr[head, key_tile] - tops[head])
+                total = total + fold_lanes(weight, jnp.add)
+                mixed = mixed + jnp.dot(
+                    weight.astype(jnp.bfloat16), values, preferred_element_type=jnp.float32
+                )
+                out.append((total, mixed))
+            return tuple(out)
+
+        zero = jnp.zeros((Q_TILE, 128), jnp.float32)
+        carry = lax.fori_loop(first, last, mix_step, ((zero, zero), (zero, zero)))
+        totals = [jnp.sum(total, axis=1, keepdims=True) for total, mixed in carry]
+        lane = lax.broadcasted_iota(jnp.int32, (Q_TILE, 128), 1)
+        mix_ref[span, :] = jnp.where(
+            lane < 64, carry[0][1] / totals[0], carry[1][1] / totals[1]
+        ).astype(jnp.bfloat16)
+        lse_ref[span, :] = jnp.where(
+            lane < 64, tops[0] + jnp.log(totals[0]), tops[1] + jnp.log(totals[1])
+        )
+
+
+def flash_backward_kernel(
+    bounds,
+    q_ref,
+    k_ref,
+    v_ref,
+    grad_ref,
+    lse_ref,
+    low_ref,
+    high_ref,
+    q_grad_ref,
+    k_grad_ref,
+    v_grad_ref,
+    prob_scr,
+    slope_scr,
+    k_acc,
+    v_acc,
+):
+    rows = q_ref.shape[0]
+    k_acc[...] = jnp.zeros_like(k_acc)
+    v_acc[...] = jnp.zeros_like(v_acc)
+    for tile in range(rows // Q_TILE):
+        span = pl.ds(tile * Q_TILE, Q_TILE)
+        heads = halves_of(q_ref[span, :] * jnp.bfloat16(0.125))
+        grads = halves_of(grad_ref[span, :])
+        lse_turned = lse_ref[span, :].T
+        lse = (lse_turned[0:1, :], lse_turned[64:65, :])
+        low = low_ref[0:1, span]
+        high = high_ref[0:1, span]
+        first = bounds[2 * tile]
+        last = bounds[2 * tile + 1]
+
+        def prob_step(key_tile, deltas):
+            begin_at = pl.multiple_of(key_tile * K_TILE, K_TILE)
+            keys = k_ref[pl.ds(begin_at, K_TILE), :]
+            values = v_ref[pl.ds(begin_at, K_TILE), :]
+            place = lax.broadcasted_iota(jnp.int32, (K_TILE, Q_TILE), 0) + begin_at
+            allowed = (place >= low) & (place < high)
+            out = []
+            for head in range(2):
+                scores = lax.dot_general(
+                    keys, heads[head], (((1,), (1,)), ((), ())), preferred_element_type=jnp.float32
+                )
+                probs = jnp.where(allowed, jnp.exp(scores - lse[head]), 0.0)
+                slope = lax.dot_general(
+                    values, grads[head], (((1,), (1,)), ((), ())), preferred_element_type=jnp.float32
+                )
+                prob_scr[head, key_tile] = probs
+                slope_scr[head, key_tile] = slope
+                out.append(
+                    deltas[head]
+                    + jnp.sum((probs * slope).reshape(K_TILE // 8, 8, Q_TILE), axis=0)
+                )
+            return tuple(out)
+
+        zero = jnp.zeros((8, Q_TILE), jnp.float32)
+        deltas = lax.fori_loop(first, last, prob_step, (zero, zero))
+        deltas = [jnp.sum(delta, axis=0, keepdims=True) for delta in deltas]
+
+        def grad_step(key_tile, carry):
+            begin_at = pl.multiple_of(key_tile * K_TILE, K_TILE)
+            key_span = pl.ds(begin_at, K_TILE)
+            keys = k_ref[key_span, :]
+            out = []
+            k_part = None
+            for head in range(2):
+                probs = prob_scr[head, key_tile]
+                low_slope = (probs * (slope_scr[head, key_tile] - deltas[head])).astype(jnp.bfloat16)
+                v_term = jnp.dot(
+                    probs.astype(jnp.bfloat16), grads[head], preferred_element_type=jnp.float32
+                )
+                k_term = jnp.dot(low_slope, heads[head], preferred_element_type=jnp.float32)
+                out.append(
+                    carry[head]
+                    + lax.dot_general(
+                        low_slope, keys, (((0,), (0,)), ((), ())), preferred_element_type=jnp.float32
+                    )
+                )
+                v_part = v_term if head == 0 else v_part + v_term
+                k_part = k_term if head == 0 else k_part + k_term
+            k_acc[key_span, :] += k_part
+            v_acc[key_span, :] += v_part
+            return tuple(out)
+
+        zero = jnp.zeros((Q_TILE, 128), jnp.float32)
+        q_parts = lax.fori_loop(first, last, grad_step, (zero, zero))
+        lane = lax.broadcasted_iota(jnp.int32, (Q_TILE, 128), 1)
+        q_grad_ref[span, :] = (jnp.where(lane < 64, q_parts[0], q_parts[1]) * 0.125).astype(
+            jnp.bfloat16
+        )
+    k_grad_ref[...] = k_acc[...].astype(jnp.bfloat16)
+    v_grad_ref[...] = v_acc[...].astype(jnp.bfloat16)
+
+
+def flash_forward(bounds, queries, key_value, low, high):
+    rows, width = queries.shape
+    window = key_value.shape[0]
+    pairs = width // 128
+    tiles = window // K_TILE
+    return pl.pallas_call(
+        flash_forward_kernel,
+        out_shape=(
+            jax.ShapeDtypeStruct((rows, width), jnp.bfloat16),
+            jax.ShapeDtypeStruct((rows, width), jnp.float32),
+        ),
+        grid_spec=pltpu.PrefetchScalarGridSpec(
+            num_scalar_prefetch=1,
+            grid=(pairs,),
+            in_specs=[
+                pl.BlockSpec((rows, 128), lambda i, b: (0, i)),
+                pl.BlockSpec((window, 128), lambda i, b: (0, i)),
+                pl.BlockSpec((window, 128), lambda i, b: (0, i + pairs)),
+                pl.BlockSpec((rows, 128), lambda i, b: (0, 0)),
+                pl.BlockSpec((rows, 128), lambda i, b: (0, 0)),
+            ],
+            out_specs=[
+                pl.BlockSpec((rows, 128), lambda i, b: (0, i)),
+                pl.BlockSpec((rows, 128), lambda i, b: (0, i)),
+            ],
+            scratch_shapes=[pltpu.VMEM((2, tiles, Q_TILE, K_TILE), jnp.float32)],
+        ),
+        compiler_params=pltpu.CompilerParams(vmem_limit_bytes=40 * 2**20),
+        cost_estimate=pl.CostEstimate(
+            flops=4 * rows * width * 1536, bytes_accessed=8 * 2**20, transcendentals=rows * 12 * 1536
+        ),
+        name="flash_forward",
+    )(bounds, queries, key_value, key_value, low, high)
+
+
+def flash_backward(bounds, queries, key_value, grad_low, lse, low, high):
+    rows, width = queries.shape
+    window = key_value.shape[0]
+    pairs = width // 128
+    tiles = window // K_TILE
+    own = pl.BlockSpec((rows, 128), lambda i, b: (0, i))
+    wide = pl.BlockSpec((window, 128), lambda i, b: (0, i))
+    line = pl.BlockSpec((8, rows), lambda i, b: (0, 0))
+    return pl.pallas_call(
+        flash_backward_kernel,
+        out_shape=(
+            jax.ShapeDtypeStruct((rows, width), jnp.bfloat16),
+            jax.ShapeDtypeStruct((window, width), jnp.bfloat16),
+            jax.ShapeDtypeStruct((window, width), jnp.bfloat16),
+        ),
+        grid_spec=pltpu.PrefetchScalarGridSpec(
+            num_scalar_prefetch=1,
+            grid=(pairs,),
+            in_specs=[
+                own,
+                wide,
+                pl.BlockSpec((window, 128), lambda i, b: (0, i + pairs)),
+                own,
+                own,
+                line,
+                line,
+            ],
+            out_specs=[own, wide, wide],
+            scratch_shapes=[
+                pltpu.VMEM((2, tiles, K_TILE, Q_TILE), jnp.float32),
+                pltpu.VMEM((2, tiles, K_TILE, Q_TILE), jnp.float32),
+                pltpu.VMEM((window, 128), jnp.float32),
+                pltpu.VMEM((window, 128), jnp.float32),
+            ],
+        ),
+        compiler_params=pltpu.CompilerParams(vmem_limit_bytes=48 * 2**20),
+        cost_estimate=pl.CostEstimate(
+            flops=10 * rows * width * 1536,
+            bytes_accessed=16 * 2**20,
+            transcendentals=rows * 12 * 1536,
+        ),
+        name="flash_backward",
+    )(bounds, queries, key_value, key_value, grad_low, lse, low, high)
+
+
+GRP_Y, GRP_CORE, SHARD_Z, SHARD_X = 2, 2, 4, 2
+BOTH = ("grp", "shard")
+
+
+def device_pairs(place):
+    pairs = []
+    for y in range(GRP_Y):
+        for core in range(GRP_CORE):
+            for z in range(SHARD_Z):
+                for x in range(SHARD_X):
+                    target = place(y, core, z, x)
+                    if target is not None:
+                        ty, tcore, tz, tx = target
+                        pairs.append(
+                            (
+                                (y * GRP_CORE + core) * SHARD_Z * SHARD_X + z * SHARD_X + x,
+                                (ty * GRP_CORE + tcore) * SHARD_Z * SHARD_X + tz * SHARD_X + tx,
+                            )
+                        )
+    return pairs
+
+
+def send(values, place):
+    return lax.ppermute(values, BOTH, device_pairs(place))
+
+
+def turn_rows(values):
+    return send(values, lambda y, core, z, x: (y, x, z, core))
+
+
+def swap_core(values):
+    return send(values, lambda y, core, z, x: (y, 1 - core, z, x))
+
+
+def send_up(values):
+    return send(values, lambda y, core, z, x: (y, core, z + 1, x) if z + 1 < SHARD_Z else None)
+
+
+def send_down(values):
+    return send(values, lambda y, core, z, x: (y, core, z - 1, x) if z > 0 else None)
+
+
+def window_of(rows, core):
+    from_below = send_up(rows)
+    from_above = send_down(rows)
+    other = swap_core(jnp.concatenate([rows, jnp.where(core == 1, from_below, from_above)]))
+    count = rows.shape[0]
+    other_own, other_far = other[:count], other[count:]
+    return jnp.concatenate(
+        [
+            from_below,
+            jnp.where(core == 0, other_far, other_own),
+            rows,
+            jnp.where(core == 0, other_own, other_far),
+            from_above,
+        ]
+    )
+
+
+def window_back(parts, core, count):
+    low = parts.astype(jnp.bfloat16)
+    block = [low[i * count : (i + 1) * count] for i in range(5)]
+    near = jnp.where(core == 0, block[3], block[1])
+    far = jnp.where(core == 0, block[1], block[3])
+    other = swap_core(jnp.concatenate([near, far])).astype(jnp.float32)
+    other_near, other_far = other[:count], other[count:]
+    below = block[0].astype(jnp.float32)
+    above = block[4].astype(jnp.float32)
+    below = jnp.where(core == 1, below + other_far, below).astype(jnp.bfloat16)
+    above = jnp.where(core == 0, above + other_far, above).astype(jnp.bfloat16)
+    from_above = send_down(below).astype(jnp.float32)
+    from_below = send_up(above).astype(jnp.float32)
+    return parts[2 * count : 3 * count] + other_near + from_above + from_below
+
+
+def quarter_rows(shard, quarter):
+    count = shard.shape[0] // 4
+    return lax.dynamic_slice_in_dim(shard, quarter * count, count, 0)
+
+
+def split_columns(rows, width):
+    return jnp.concatenate(
+        [rows[:, i : i + width] for i in range(0, rows.shape[1], width)], axis=0
+    )
+
+
+def gather_layer(project, mixer, expand, reduce, small, quarter, width):
+    local = jnp.concatenate(
+        [
+            split_columns(quarter_rows(project, quarter), width),
+            quarter_rows(mixer, quarter),
+            split_columns(quarter_rows(expand, quarter), width),
+            quarter_rows(reduce, quarter),
+            small,
+        ]
+    )
+    return lax.all_gather(local, BOTH, axis=0, tiled=False)
+
+
+def joined(pieces, begin_at, count, columns):
+    width = pieces.shape[2]
+    part = pieces[:, begin_at : begin_at + count * columns]
+    part = part.reshape(4, 8, columns, count, width).transpose(1, 0, 3, 2, 4)
+    return part.reshape(32 * count, columns * width)
+
+
+def parted(grad, columns):
+    rows = grad.shape[0] // 32
+    width = grad.shape[1] // columns
+    part = grad.reshape(8, 4, rows, columns, width).transpose(1, 0, 3, 2, 4)
+    return part.reshape(32, columns * rows, width)
+
+
+def on_device_turned(
+    tokens,
+    cotangent,
+    seq_lengths,
+    seq_order,
+    w_project,
+    w_mixer,
+    w_expand,
+    w_reduce,
+    biases,
+    norm_gains,
+):
+    row_count, width = tokens.shape
+    shard_index = lax.axis_index("shard")
+    quarter = lax.axis_index("grp")
+    z, x = shard_index // SHARD_X, shard_index % SHARD_X
+    y, core = quarter // GRP_CORE, quarter % GRP_CORE
+    hidden_units = w_expand.shape[2]
+    group_slots = row_count * 8
+    seq_count = seq_lengths.shape[1]
+    seq_ends = group_ends(seq_lengths, seq_order, y * GRP_CORE + x)
+    block_index = z * GRP_CORE + core
+    slot_index = block_index * row_count + jnp.arange(row_count, dtype=jnp.int32)
+    before_slot = seq_ends[None, :] <= slot_index[:, None]
+    own_segment = jnp.sum(before_slot.astype(jnp.int32), axis=1, dtype=jnp.int32)
+    starts = jnp.max(jnp.where(before_slot, seq_ends[None, :], 0), axis=1)
+    stops = jnp.min(jnp.where(before_slot, group_slots, seq_ends[None, :]), axis=1)
+    window_begin = (block_index - 2) * row_count
+    low = starts - window_begin
+    high = stops - window_begin
+    low_wide = jnp.broadcast_to(low[:, None], (row_count, 128))
+    high_wide = jnp.broadcast_to(high[:, None], (row_count, 128))
+    low_line = jnp.broadcast_to(low[None, :], (8, row_count))
+    high_line = jnp.broadcast_to(high[None, :], (8, row_count))
+    bounds = jnp.stack(
+        [low[0::Q_TILE] // K_TILE, (high[Q_TILE - 1 :: Q_TILE] + K_TILE - 1) // K_TILE], axis=1
+    ).reshape(-1)
+    valid_rows = (own_segment < seq_count).astype(jnp.float32)[:, None]
+
+    small = jnp.concatenate(
+        [jnp.concatenate([biases[i], norm_gains[i]]) for i in range(LAYERS)]
+    ).reshape(-1, width)
+    small = jnp.concatenate([small, jnp.zeros((8 - small.shape[0], width), small.dtype)])
+    gathered = [
+        gather_layer(
+            w_project[i], w_mixer[i], w_expand[i], w_reduce[i], small, quarter, width
+        )
+        for i in range(LAYERS)
+    ]
+    state_low = turn_rows(tokens)
+    state_grad = turn_rows(cotangent)
+    share = w_project.shape[1] // 4
+    deep = w_reduce.shape[1] // 4
+    counts = [share * 3, share, share * (hidden_units // width), deep]
+    small_at = sum(counts)
+    small_all = gathered[0][:8, small_at : small_at + 3].reshape(8, LAYERS, -1)
+    bias_count = biases.shape[1]
+    weights = []
+    for layer_index in range(LAYERS):
+        pieces = gathered[layer_index]
+        begin_at = 0
+        whole = []
+        for count, columns in zip(counts, (3, 1, hidden_units // width, 1)):
+            whole.append(joined(pieces, begin_at, count // columns, columns))
+            begin_at += count
+        bias_vec = small_all[:, layer_index, :bias_count].reshape(-1)
+        gain_vec = small_all[:, layer_index, bias_count:].reshape(-1)
+        weights.append(unpack_weights(whole + [bias_vec, gain_vec], width, hidden_units))
+
+    hidden_state = state_low.astype(jnp.float32)
+    kept_list = []
+    for layer_index in range(LAYERS):
+        project, mixing, expand, shrink, bias_list, gain_one, gain_two = weights[layer_index]
+        bias_q, bias_v, bias_mix, shift_one, bias_in, bias_out, shift_two = bias_list
+        state_window = window_of(state_low, core)
+        queries = (
+            jnp.dot(state_low, project[:, :width], preferred_element_type=jnp.float32) + bias_q
+        ).astype(jnp.bfloat16)
+        key_value = (
+            jnp.dot(state_window, project[:, width:], preferred_element_type=jnp.float32)
+            + jnp.concatenate([jnp.zeros_like(bias_v), bias_v])
+        ).astype(jnp.bfloat16)
+        mixed_low, lse = flash_forward(bounds, queries, key_value, low_wide, high_wide)
+        branch = jnp.dot(mixed_low, mixing, preferred_element_type=jnp.float32) + bias_mix
+        summed_one = hidden_state + branch
+        normed_one = layer_norm(summed_one, gain_one, shift_one)
+        normed_low = normed_one.astype(jnp.bfloat16)
+        before = jnp.dot(normed_low, expand, preferred_element_type=jnp.float32) + bias_in
+        active_low = gelu_exact(before).astype(jnp.bfloat16)
+        feed_out = jnp.dot(active_low, shrink, preferred_element_type=jnp.float32) + bias_out
+        summed_two = normed_one + feed_out
+        hidden_state = layer_norm(summed_two, gain_two, shift_two)
+        kept_list.append(
+            (
+                state_low,
+                state_window,
+                queries,
+                key_value,
+                lse,
+                mixed_low,
+                summed_one,
+                normed_low,
+                before,
+                active_low,
+                summed_two,
+            )
+        )
+        state_low = hidden_state.astype(jnp.bfloat16)
+    activations = turn_rows((hidden_state * valid_rows).astype(jnp.bfloat16))
+    state_grad = state_grad.astype(jnp.float32) * valid_rows
+    results = [None] * LAYERS
+    for layer_index in reversed(range(LAYERS)):
+        (
+            layer_low,
+            state_window,
+            queries,
+            key_value,
+            lse,
+            mixed_low,
+            summed_one,
+            normed_low,
+            before,
+            active_low,
+            summed_two,
+        ) = kept_list[layer_index]
+        project, mixing, expand, shrink, bias_list, gain_one, gain_two = weights[layer_index]
+        bias_q, bias_v, bias_mix, shift_one, bias_in, bias_out, shift_two = bias_list
+        unused_two, norm_pull = jax.vjp(layer_norm, summed_two, gain_two, shift_two)
+        sum_two_grad, gain_two_grad, shift_two_grad = norm_pull(state_grad)
+        feed_low = sum_two_grad.astype(jnp.bfloat16)
+        shrink_grad = jnp.einsum(
+            "tf,td->fd", active_low, feed_low, preferred_element_type=jnp.float32
+        )
+        bias_out_grad = jnp.sum(feed_low, axis=0, dtype=jnp.float32)
+        active_grad = jnp.einsum("td,fd->tf", feed_low, shrink, preferred_element_type=jnp.float32)
+        unused_gelu, gelu_pull = jax.vjp(gelu_exact, before)
+        before_low = gelu_pull(active_grad)[0].astype(jnp.bfloat16)
+        expand_grad = jnp.einsum(
+            "td,tf->df", normed_low, before_low, preferred_element_type=jnp.float32
+        )
+        bias_in_grad = jnp.sum(before_low, axis=0, dtype=jnp.float32)
+        normed_grad = sum_two_grad + jnp.einsum(
+            "tf,df->td", before_low, expand, preferred_element_type=jnp.float32
+        )
+        unused_one, first_pull = jax.vjp(layer_norm, summed_one, gain_one, shift_one)
+        sum_one_grad, gain_one_grad, shift_one_grad = first_pull(normed_grad)
+        branch_low = sum_one_grad.astype(jnp.bfloat16)
+        mixing_grad = jnp.einsum(
+            "td,te->de", mixed_low, branch_low, preferred_element_type=jnp.float32
+        )
+        bias_mix_grad = jnp.sum(branch_low, axis=0, dtype=jnp.float32)
+        mixed_grad_low = jnp.einsum(
+            "te,de->td", branch_low, mixing, preferred_element_type=jnp.float32
+        ).astype(jnp.bfloat16)
+        query_grad, key_grad, value_grad = flash_backward(
+            bounds, queries, key_value, mixed_grad_low, lse, low_line, high_line
+        )
+        query_term = jnp.einsum(
+            "td,te->de", layer_low, query_grad, preferred_element_type=jnp.float32
+        )
+        key_term = jnp.einsum(
+            "td,te->de", state_window, key_grad, preferred_element_type=jnp.float32
+        )
+        value_term = jnp.einsum(
+            "td,te->de", state_window, value_grad, preferred_element_type=jnp.float32
+        )
+        bias_q_grad = jnp.sum(query_grad, axis=0, dtype=jnp.float32)
+        bias_v_grad = jnp.sum(value_grad, axis=0, dtype=jnp.float32)
+        window_grad = jnp.einsum(
+            "te,de->td", key_grad, project[:, width : 2 * width], preferred_element_type=jnp.float32
+        ) + jnp.einsum(
+            "te,de->td", value_grad, project[:, 2 * width :], preferred_element_type=jnp.float32
+        )
+        state_grad = (
+            sum_one_grad
+            + jnp.einsum(
+                "te,de->td", query_grad, project[:, :width], preferred_element_type=jnp.float32
+            )
+            + window_back(window_grad, core, row_count)
+        )
+        vectors = jnp.concatenate(
+            [
+                bias_q_grad,
+                bias_v_grad,
+                bias_mix_grad,
+                shift_one_grad,
+                bias_in_grad,
+                bias_out_grad,
+                shift_two_grad,
+            ]
+        ).reshape(8, -1)
+        gains = jnp.concatenate([gain_one_grad, gain_two_grad]).reshape(8, -1)
+        vectors = jnp.concatenate([vectors, gains], axis=1).astype(jnp.bfloat16)
+        vectors = vectors.reshape(8, 4, -1).transpose(1, 0, 2).reshape(32, 1, -1)
+        vectors = jnp.pad(vectors, ((0, 0), (0, 7), (0, width - vectors.shape[2])))
+        pieces = jnp.concatenate(
+            [
+                parted(query_term.astype(jnp.bfloat16), 1),
+                parted(key_term.astype(jnp.bfloat16), 1),
+                parted(value_term.astype(jnp.bfloat16), 1),
+                parted(mixing_grad.astype(jnp.bfloat16), 1),
+                parted(expand_grad.astype(jnp.bfloat16), hidden_units // width),
+                parted(shrink_grad.astype(jnp.bfloat16), 1),
+                vectors,
+            ],
+            axis=1,
+        )
+        results[layer_index] = lax.psum_scatter(pieces, BOTH, scatter_dimension=0, tiled=True)[0]
+    both = jnp.concatenate(results)
+    both = lax.all_gather(both, "grp", axis=0, tiled=False)
+    both = both.reshape(4, LAYERS, -1, width).transpose(1, 0, 2, 3).astype(jnp.float32)
+    outs = []
+    begin_at = 0
+    for count, columns in zip(counts, (3, 1, hidden_units // width, 1)):
+        part = both[:, :, begin_at : begin_at + count]
+        part = part.reshape(LAYERS, 4, columns, count // columns, width).transpose(0, 1, 3, 2, 4)
+        outs.append(part.reshape(LAYERS, 4 * count // columns, columns * width))
+        begin_at += count
+    quarter_len = (bias_count + norm_gains.shape[1]) // 4
+    vectors = both[:, :, begin_at, :quarter_len].reshape(LAYERS, -1)
+    input_grad = turn_rows(state_grad.astype(jnp.bfloat16)).astype(jnp.float32)
+    return (
+        activations,
+        input_grad,
+        outs[0],
+        outs[1],
+        outs[2],
+        outs[3],
+        vectors[:, :bias_count],
+        vectors[:, bias_count:],
+    )
+
+
 def solution(mesh):
     in_specs = (
         P(("grp", "shard"), None),
@@ -479,6 +1074,7 @@
         P(None, "shard"),
         P(None, "shard"),
     )
+    body = on_device_turned if mesh.shape["shard"] == 8 and mesh.shape["grp"] == 4 else on_device
     return jax.shard_map(
-        on_device, mesh=mesh, in_specs=in_specs, out_specs=out_specs, check_vma=False
-    )
+        body, mesh=mesh, in_specs=in_specs, out_specs=out_specs, check_vma=False
+    )

time: 1840 us -> 994 us (0.54)
  waiting for transfers between devices: 957 us -> 364 us
  starting transfers between devices: 245 us -> 67.1 us
  Pallas kernels: 0 us -> 149 us
  matrix products: 316 us -> 173 us
  blocking collectives: 78.9 us -> 0 us
  local copies, waits for them, and re-layouts: 135 us -> 186 us
  loops' own time: 20.4 us -> 0 us
    reduce_scatter x6 -> x2, waiting for transfers between devices: 527 us -> 211 us  [on_device_turned(): lax.psum_scatter(pieces, BOTH, scatter_dimension=0, tiled=True)[0]]
    ppermute x32 -> x16, starting transfers between devices: 244 us -> 66.9 us  [send(): return lax.ppermute(values, BOTH, device_pairs(place))]
    all_gather x8 -> x3, waiting for transfers between devices: 209 us -> 43.2 us  [the longest x2 43.2 us: gather_layer(): return lax.all_gather(local, BOTH, axis=0, tiled=False)]
    pallas_call x0 -> x4, Pallas kernels: none -> 149 us  [the longest x2 84 us: flash_backward(): pl.pallas_call(flash_backward_kernel, out_shape=(jax.ShapeDtypeStruct((ro...]
    dot_general x60 -> x34, matrix products: 316 us -> 173 us  [the longest x2 36.9 us: on_device_turned(): jnp.dot(normed_low, expand, preferred_element_type=jnp.float32) + bias_in]
    unnamed x2 -> x0, blocking collectives: 62.3 us -> none
    unnamed x19 -> x5, waiting for transfers between devices: 59.8 us -> 0.08 us
    reshape x1 -> x25, local copies, waits for them, and re-layouts: 0.01 us -> 55.4 us  [the longest x14 45.4 us: parted(): part = grad.reshape(8, 4, rows, columns, width).transpose(1, 0, 3, 2, 4)]
  transfers between devices with their start and end apart: 49 -> 21, of which waited for: 26 -> 16; matrix products, arithmetic and copies ran while one was open for 20% -> 27% of each run, Pallas kernels for 0% -> 11%
where the time goes in v1:
time: 994 us; the launch traced here: 998 us
  waiting for transfers between devices  364 us (37%)
  local copies, waits for them, and re-layouts  186 us (19%)
  matrix products  173 us (17%)
  Pallas kernels  149 us (15%)
  starting transfers between devices  67.1 us (7%)
  other arithmetic  42.5 us (4%)
  between operations  16 us (2%)
    reduce_scatter x2, waiting for transfers between devices, on_device_turned(): lax.psum_scatter(pieces, BOTH, scatter_dimension=0, tiled=True)[0]  211 us
    ppermute x16, waiting for transfers between devices, send(): return lax.ppermute(values, BOTH, device_pairs(place))  110 us
    pallas_call x2, Pallas kernels, flash_backward(): pl.pallas_call(flash_backward_kernel, out_shape=(jax.ShapeDtypeStruct((ro...  84 us
    ppermute x16, starting transfers between devices, send(): return lax.ppermute(values, BOTH, device_pairs(place))  66.9 us
    pallas_call x2, Pallas kernels, flash_forward(): pl.pallas_call(flash_forward_kernel, out_shape=(jax.ShapeDtypeStruct((row...  64.9 us
    reshape x14, local copies, waits for them, and re-layouts, parted(): part = grad.reshape(8, 4, rows, columns, width).transpose(1, 0, 3, 2, 4)  45.4 us
    unnamed x224, local copies, waits for them, and re-layouts  44.9 us
    all_gather x2, waiting for transfers between devices, gather_layer(): return lax.all_gather(local, BOTH, axis=0, tiled=False)  43.2 us
  transfers between devices with their start and end apart: 21, of which 16 were waited for; matrix products, arithmetic and copies ran while one was open for 27% of the time, Pallas kernels for 11%

profile of v1, /device:TPU:1, one launch (start us, length us, event | category | flops | bytes accessed | tf_op | source)
XLA Modules:
  0.0 997.8 jit_solution(13774254847577616295)
XLA Ops:
  14.0 7.0 concatenate.80
  22.0 6.2 concatenate.84
  28.2 4.5 collective-permute-start
  32.7 13.5 %collective-permute-done = bf16[512,768]{1,0:T(8,128)(2,1)S(1)} collective-permute-done((bf16[512,768]{1,0:T(8,128)(2,1)}, bf16[512,768]{1,0:T(8,128)(2,1)S(1)}, u32[]{:S(2)}, u32[]{:S(2)}) %collective-permute-start) | collective-permute-done | bytes 786464 | tf_op jit(solution)/shard_map/ppermute | solution.py:731
  46.3 3.1 collective-permute-start.1
  50.7 20.0 %collective-permute-done.1 = bf16[512,768]{1,0:T(8,128)(2,1)S(1)} collective-permute-done((bf16[512,768]{1,0:T(8,128)(2,1)S(1)}, bf16[512,768]{1,0:T(8,128)(2,1)S(1)}, u32[]{:S(2)}, u32[]{:S(2)}) %collective-permute-start.1) | collective-permute-done | bytes 786464 | tf_op jit(solution)/shard_map/ppermute | solution.py:731
  70.7 11.7 %collective-permute-done.2 = bf16[512,768]{1,0:T(8,128)(2,1)S(1)} collective-permute-done((bf16[512,768]{1,0:T(8,128)(2,1)S(1)}, bf16[512,768]{1,0:T(8,128)(2,1)S(1)}, u32[]{:S(2)}, u32[]{:S(2)}) %collective-permute-start.2) | collective-permute-done | bytes 786464 | tf_op jit(solution)/shard_map/ppermute | solution.py:731
  92.4 43.2 %all-gather.7.cloned.1.call-done = bf16[9472,768]{1,0:T(8,128)(2,1)} async-done(((bf16[296,768]{1,0:T(8,128)(2,1)}), bf16[9472,768]{1,0:T(8,128)(2,1)}) %all-gather.7.cloned.1.call-update) | async-done | bytes 14549008 | tf_op jit(solution)/shard_map/all_gather | solution.py:804
  136.6 4.0 slice.393
  142.2 6.8 fusion.76
  151.5 3.2 copy.109
  160.9 5.0 copy.81
  168.4 8.7 add_convert_fusion.1.k_ref.v_ref
  177.4 32.5 %flash_forward.2 = (bf16[512,768]{1,0:T(8,128)(2,1)S(1)}, f32[512,768]{1,0:T(8,128)S(1)}) custom-call(s32[4]{0:T(128)S(1)} %reshape.398.bounds, bf16[512,768]{1,0:T(8,128)(2,1)S(1)} %fusion.27.q_ref, bf16[2560,1536]{1,0:T(8,128)(2,1)S(1)} %add_convert_fusion.1.k_ref.v_ref, bf16[2560,1536]{1,0:T(8,128)(2,1)S(1)} %add_convert_fusion.1.k_ref.v_ref, ...), custom_call_target="tpu_custom_call" | custom-call | flops 2415919104 | bytes 8388608 | tf_op jit(solution)/shard_map/flash_forward/pallas_call | solution.py:633
  211.2 18.3 %multiply_convert_fusion.1 = (bf16[512,3072]{1,0:T(8,128)(2,1)S(1)}, f32[512,3072]{1,0:T(8,128)}, f32[512,3072]{1,0:T(8,128)}) fusion(f32[3072]{0:T(1024)S(1)} %slice.408, bf16[768,3072]{1,0:T(8,128)(2,1)S(1)} %bitcast.236, f32[512,768]{1,0:T(8,128)S(1)} %get-tuple-element.134, f32[768]{0:T(1024)S(1)} %get-tuple-element.129, f32[768]{0:T(1024)S(1)} %slice.320, ...), kind=kOutput, calls=%fused_computation.22 | convolution fusion | flops 2521694208 | bytes 22042624 | tf_op jit(solution)/shard_map/dot_general | solution.py:908
  233.1 11.8 %collective-permute-start.4 = (bf16[512,768]{1,0:T(8,128)(2,1)S(1)}, bf16[512,768]{1,0:T(8,128)(2,1)S(1)}, u32[]{:S(2)}, u32[]{:S(2)}) collective-permute-start(bf16[512,768]{1,0:T(8,128)(2,1)S(1)} %fusion.29), channel_id=1, source_target_pairs={{0,2},{1,3},{2,4},{3,5},{4,6},{5,7},{8,10},{9,11},{10,12},{11,13},... | collective-permute-start | bytes 2359304 | tf_op jit(solution)/shard_map/ppermute | solution.py:731
  246.6 7.2 collective-permute-done.4
  253.8 9.5 collective-permute-done.5
  266.6 3.2 collective-permute-start.8
  269.9 4.1 slice.420
  276.4 6.5 fusion.75
  285.4 3.3 copy.111
  294.9 4.9 copy.85
  309.4 9.5 add_convert_fusion.k_ref.v_ref
  318.9 32.5 %flash_forward.3 = (bf16[512,768]{1,0:T(8,128)(2,1)S(1)}, f32[512,768]{1,0:T(8,128)S(1)}) custom-call(s32[4]{0:T(128)S(1)} %reshape.398.bounds, bf16[512,768]{1,0:T(8,128)(2,1)S(1)} %add_convert_fusion.4.q_ref, bf16[2560,1536]{1,0:T(8,128)(2,1)S(1)} %add_convert_fusion.k_ref.v_ref, bf16[2560,1536]{1,0:T(8,128)(2,1)S(1)} %add_convert_fusion.k_ref.v_ref, ...), custom_call_target="tpu_custom_call" | custom-call | flops 2415919104 | bytes 8388608 | tf_op jit(solution)/shard_map/flash_forward/pallas_call | solution.py:633
  352.8 18.6 %multiply_convert_fusion = (bf16[512,3072]{1,0:T(8,128)(2,1)S(1)}, f32[512,3072]{1,0:T(8,128)}, f32[512,3072]{1,0:T(8,128)}) fusion(f32[3072]{0:T(1024)S(1)} %slice.434, bf16[768,3072]{1,0:T(8,128)(2,1)S(1)} %bitcast.246, f32[512,768]{1,0:T(8,128)S(1)} %get-tuple-element.139, f32[768]{0:T(1024)S(1)} %get-tuple-element.123, f32[768]{0:T(1024)S(1)} %slice.352, ...), kind=kOutput, calls=%fused_computation.9 | convolution fusion | flops 2521694208 | bytes 22042624 | tf_op jit(solution)/shard_map/dot_general | solution.py:908
  379.7 10.0 %fusion.66 = (bf16[3072]{0:T(1024)(128)(2,1)S(1)}, bf16[512,3072]{1,0:T(8,128)(2,1)}) fusion(f32[512,3072]{1,0:T(8,128)} %get-tuple-element.75, f32[512,3072]{1,0:T(8,128)} %get-tuple-element.140, f32[3072]{0:T(1024)S(1)} %slice.434, bf16[512,768]{1,0:T(8,128)(2,1)S(1)} %get-tuple-element.60, bf16[3072,768]{1,0:T(8,128)(2,1)} %bitcast.250), kind=kOutput, calls=%fused_computation.240 | convolution fusion | flops 2441081856 | bytes 21252096 | tf_op jit(solution)/shard_map/td,fd->tf/dot_general | solution.py:955
  389.7 5.0 multiply_reduce_fusion.1
  398.7 4.9 convolution_convert_fusion.1
  403.6 4.3 convolution_convert_fusion
  408.0 41.9 %flash_backward.2 = (bf16[512,768]{1,0:T(8,128)(2,1)S(1)}, bf16[2560,768]{1,0:T(8,128)(2,1)}, bf16[2560,768]{1,0:T(8,128)(2,1)}) custom-call(s32[4]{0:T(128)S(1)} %reshape.398.bounds, bf16[512,768]{1,0:T(8,128)(2,1)S(1)} %add_convert_fusion.4.q_ref, bf16[2560,1536]{1,0:T(8,128)(2,1)} %copy-done.3, bf16[2560,1536]{1,0:T(8,128)(2,1)} %copy-done.3, ...), custom_call_target="tpu_custom_call" | custom-call | flops 6039797760 | bytes 16777216 | tf_op jit(solution)/shard_map/flash_backward/pallas_call | solution.py:671
  451.9 7.6 convolution_convert_fusion.5
  465.0 5.5 convolution_convert_fusion.6
  473.9 9.8 reshape.439
  483.6 5.3 copy.98
  489.0 5.0 copy.99
  508.1 6.0 fusion.35
  514.0 6.9 fusion.92
  521.2 3.4 collective-permute-done.9
  526.8 25.6 %collective-permute-start.11 = (bf16[512,768]{1,0:T(8,128)(2,1)}, bf16[512,768]{1,0:T(8,128)(2,1)}, u32[]{:S(2)}, u32[]{:S(2)}) collective-permute-start(bf16[512,768]{1,0:T(8,128)(2,1)} %get-tuple-element.87), channel_id=1, source_target_pairs={{0,2},{1,3},{2,4},{3,5},{4,6},{5,7},{8,10},{9,11},{10,12},{11,13},... | collective-permute-start | bytes 2359304 | tf_op jit(solution)/shard_map/ppermute | solution.py:731
  556.0 12.7 %collective-permute-done.11 = bf16[512,768]{1,0:T(8,128)(2,1)} collective-permute-done((bf16[512,768]{1,0:T(8,128)(2,1)}, bf16[512,768]{1,0:T(8,128)(2,1)}, u32[]{:S(2)}, u32[]{:S(2)}) %collective-permute-start.11) | collective-permute-done | bytes 786464 | tf_op jit(solution)/shard_map/ppermute | solution.py:731
  568.6 4.4 collective-permute-done.10
  573.1 3.8 multiply_reduce_fusion.2
  577.9 10.7 %fusion.63 = (bf16[3072]{0:T(1024)(128)(2,1)S(1)}, bf16[512,3072]{1,0:T(8,128)(2,1)S(1)}) fusion(f32[512,3072]{1,0:T(8,128)} %get-tuple-element.77, f32[512,3072]{1,0:T(8,128)} %get-tuple-element.135, f32[3072]{0:T(1024)S(1)} %copy-done.68, bf16[512,768]{1,0:T(8,128)(2,1)S(1)} %get-tuple-element.54, bf16[3072,768]{1,0:T(8,128)(2,1)} %bitcast.240), kind=kOutput, calls=%fused_computation.237 | convolution fusion | flops 2441081856 | bytes 21252096 | tf_op jit(solution)/shard_map/td,fd->tf/dot_general | solution.py:955
  588.8 3.2 multiply_reduce_fusion.3
  594.6 42.1 %flash_backward.3 = (bf16[512,768]{1,0:T(8,128)(2,1)S(1)}, bf16[2560,768]{1,0:T(8,128)(2,1)}, bf16[2560,768]{1,0:T(8,128)(2,1)}) custom-call(s32[4]{0:T(128)S(1)} %reshape.398.bounds, bf16[512,768]{1,0:T(8,128)(2,1)S(1)} %copy-done.7, bf16[2560,1536]{1,0:T(8,128)(2,1)} %copy-done.2, bf16[2560,1536]{1,0:T(8,128)(2,1)} %copy-done.2, ...), custom_call_target="tpu_custom_call" | custom-call | flops 6039797760 | bytes 16777216 | tf_op jit(solution)/shard_map/flash_backward/pallas_call | solution.py:671
  639.0 5.5 convolution_convert_fusion.10
  647.3 6.9 convolution_convert_fusion.9
  657.3 5.0 convolution_convert_fusion.3
  662.2 10.0 %reshape.425 = bf16[8,4,24,4,768]{4,3,2,1,0:T(4,128)(2,1)} reshape(bf16[768,3072]{1,0:T(8,128)(2,1)} %convolution_convert_fusion.3) | data formatting | bytes 9437184 | tf_op jit(solution)/shard_map/reshape | solution.py:817
  672.3 5.6 copy.90
  689.5 5.5 constant_dynamic-update-slice_fusion.7
  698.5 18.1 %reduce-scatter.5.cloned.1.call-done = bf16[1,296,768]{2,1,0:T(8,128)(2,1)} async-done(((bf16[32,296,768]{2,1,0:T(8,128)(2,1)}), bf16[1,296,768]{2,1,0:T(8,128)(2,1)}) %reduce-scatter.5.cloned.1.call-update) | async-done | bytes 454672 | tf_op jit(solution)/shard_map/reduce_scatter | solution.py:1028
  716.6 192.9 %reduce-scatter.3.cloned.1.call-done = bf16[1,296,768]{2,1,0:T(8,128)(2,1)} async-done(((bf16[32,296,768]{2,1,0:T(8,128)(2,1)}), bf16[1,296,768]{2,1,0:T(8,128)(2,1)}) %reduce-scatter.3.cloned.1.call-update) | async-done | bytes 454672 | tf_op jit(solution)/shard_map/reduce_scatter | solution.py:1028
  911.7 6.0 fusion.32
  917.6 4.6 fusion.93
  924.5 3.0 collective-permute-done.12
  932.2 3.6 collective-permute-start.7
  937.9 9.5 collective-permute-done.14
  947.4 3.8 collective-permute-done.13
  951.7 4.7 collective-permute-start.15
  956.4 9.4 collective-permute-done.15
  971.2 3.2 fusion.77
  986.7 3.3 copy.105
  (432 shorter events, 164.1 us)
Async XLA Ops:
  7.2 77.6 %copy-start = (s32[4,8]{1,0:T(4,128)S(1)}, s32[4,8]{1,0:T(4,128)}, u32[]{:S(2)}) copy-start(s32[4,8]{1,0:T(4,128)} %param.12) | copy-start | bytes 388
  7.2 128.5 %all-gather.7.cloned.1.call-start = ((), (), s32[]{:S(2)}) async-start(), calls=%async_computation.4 | async-start | bytes 15003648 | tf_op jit(solution)/shard_map/all_gather | solution.py:804
  21.0 248.8 %all-gather.9.cloned.1.call-start = ((), (), s32[]{:S(2)}) async-start(), calls=%async_computation.5 | async-start | bytes 15003648 | tf_op jit(solution)/shard_map/all_gather | solution.py:804
  28.2 688.4 %reduce-scatter.5.cloned.1.call-start = ((), (), s32[]{:S(2)}) async-start(), calls=%async_computation.3 | async-start | bytes 15003648 | tf_op jit(solution)/shard_map/reduce_scatter | solution.py:1028
  28.2 18.0 %collective-permute-start = (bf16[512,768]{1,0:T(8,128)(2,1)}, bf16[512,768]{1,0:T(8,128)(2,1)S(1)}, u32[]{:S(2)}, u32[]{:S(2)}) collective-permute-start(bf16[512,768]{1,0:T(8,128)(2,1)} %param.10), channel_id=1, source_target_pairs={{0,0},{1,8},{2,2},{3,10},{4,4},{5,12},{6,6},{7,14},{8,1},{9,9},{10... | collective-permute-start | bytes 2359304 | tf_op jit(solution)/shard_map/ppermute | solution.py:731
  46.3 163.6 %copy-start.30 = (bf16[512,768]{1,0:T(8,128)(2,1)}, bf16[512,768]{1,0:T(8,128)(2,1)S(1)}, u32[]{:S(2)}) copy-start(bf16[512,768]{1,0:T(8,128)(2,1)S(1)} %collective-permute-done) | copy-start | bytes 2359300
  46.3 24.4 %collective-permute-start.1 = (bf16[512,768]{1,0:T(8,128)(2,1)S(1)}, bf16[512,768]{1,0:T(8,128)(2,1)S(1)}, u32[]{:S(2)}, u32[]{:S(2)}) collective-permute-start(bf16[512,768]{1,0:T(8,128)(2,1)S(1)} %collective-permute-done), channel_id=1, source_target_pairs={{0,2},{1,3},{2,4},{3,5},{4,6},{5,7},{8,10},{9,11},{10,12},{11,13},... | collective-permute-start | bytes 2359304 | tf_op jit(solution)/shard_map/ppermute | solution.py:731
  49.4 33.0 %collective-permute-start.2 = (bf16[512,768]{1,0:T(8,128)(2,1)S(1)}, bf16[512,768]{1,0:T(8,128)(2,1)S(1)}, u32[]{:S(2)}, u32[]{:S(2)}) collective-permute-start(bf16[512,768]{1,0:T(8,128)(2,1)S(1)} %collective-permute-done), channel_id=1, source_target_pairs={{2,0},{3,1},{4,2},{5,3},{6,4},{7,5},{10,8},{11,9},{12,10},{13,11},... | collective-permute-start | bytes 2359304 | tf_op jit(solution)/shard_map/ppermute | solution.py:731
  84.7 3.6 collective-permute-start.3
  85.9 91.3 %copy-start.59 = (s32[512]{0:T(512)}, s32[512]{0:T(512)S(1)}, u32[]{:S(2)}) copy-start(s32[512]{0:T(512)S(1)} %broadcast_subtract_fusion) | copy-start | bytes 6148
  86.0 91.0 %copy-start.61 = (s32[512]{0:T(512)}, s32[512]{0:T(512)S(1)}, u32[]{:S(2)}) copy-start(s32[512]{0:T(512)S(1)} %broadcast_subtract_fusion.1) | copy-start | bytes 6148
  142.2 69.0 %copy-start.67 = (f32[3072]{0:T(1024)}, f32[3072]{0:T(1024)S(1)}, u32[]{:S(2)}) copy-start(f32[3072]{0:T(1024)S(1)} %slice.408) | copy-start | bytes 36868
  160.9 68.7 %copy-start.65 = (f32[768]{0:T(1024)}, f32[768]{0:T(1024)S(1)}, u32[]{:S(2)}) copy-start(f32[768]{0:T(1024)S(1)} %slice.320) | copy-start | bytes 9220
  165.9 63.6 %copy-start.71 = (f32[768]{0:T(1024)}, f32[768]{0:T(1024)S(1)}, u32[]{:S(2)}) copy-start(f32[768]{0:T(1024)S(1)} %get-tuple-element.129) | copy-start | bytes 9220
  168.4 9.0 copy-start.6
  177.1 32.8 %copy-start.2 = (bf16[2560,1536]{1,0:T(8,128)(2,1)}, bf16[2560,1536]{1,0:T(8,128)(2,1)S(1)}, u32[]{:S(2)}) copy-start(bf16[2560,1536]{1,0:T(8,128)(2,1)S(1)} %add_convert_fusion.1.k_ref.v_ref) | copy-start | bytes 23592964
  177.2 33.9 %slice-start.5 = ((s8[4718592]{0:T(1024)(128)(4,1)}), s8[4194304]{0:T(1024)(128)(4,1)S(1)}, s32[]{:S(2)}) async-start(s8[4718592]{0:T(1024)(128)(4,1)} %bitcast.234), calls=%async_computation.12 | async-start | bytes 8388608
  177.4 32.5 %copy-start.35 = (bf16[8,4,24,1,768]{4,2,1,0,3:T(8,128)(2,1)S(1)}, bf16[8,4,24,1,768]{4,2,1,0,3:T(8,128)(2,1)}, u32[]{:S(2)}) copy-start(bf16[8,4,24,1,768]{4,2,1,0,3:T(8,128)(2,1)} %copy.79) | copy-start | bytes 3538948
  177.4 33.8 %slice-start.6 = ((s8[4718592]{0:T(1024)(128)(4,1)}), s8[524288]{0:T(1024)(128)(4,1)S(1)}, s32[]{:S(2)}) async-start(s8[4718592]{0:T(1024)(128)(4,1)} %bitcast.234), calls=%async_computation.13 | async-start | bytes 1048576
  209.9 19.6 %copy-start.4 = (bf16[512,768]{1,0:T(8,128)(2,1)}, bf16[512,768]{1,0:T(8,128)(2,1)S(1)}, u32[]{:S(2)}) copy-start(bf16[512,768]{1,0:T(8,128)(2,1)S(1)} %get-tuple-element.18) | copy-start | bytes 2359300
  209.9 19.7 %slice-start.9 = ((s8[4718592]{0:T(1024)(128)(4,1)}), s8[4194304]{0:T(1024)(128)(4,1)S(1)}, s32[]{:S(2)}) async-start(s8[4718592]{0:T(1024)(128)(4,1)} %bitcast.241), calls=%async_computation.16 | async-start | bytes 8388608
  210.8 18.8 %copy-start.23 = (f32[512,768]{1,0:T(8,128)}, f32[512,768]{1,0:T(8,128)S(1)}, u32[]{:S(2)}) copy-start(f32[512,768]{1,0:T(8,128)S(1)} %get-tuple-element.134) | copy-start | bytes 4718596
  210.8 18.7 %copy-start.53 = (f32[512]{0:T(512)}, f32[512]{0:T(512)S(1)}, u32[]{:S(2)}) copy-start(f32[512]{0:T(512)S(1)} %broadcast_multiply_fusion.3) | copy-start | bytes 6148
  211.1 18.4 %copy-start.55 = (f32[512]{0:T(512)}, f32[512]{0:T(512)S(1)}, u32[]{:S(2)}) copy-start(f32[512]{0:T(512)S(1)} %multiply_reduce_fusion.11) | copy-start | bytes 6148
  211.2 18.4 %copy-start.69 = (f32[512]{0:T(512)}, f32[512]{0:T(512)S(1)}, u32[]{:S(2)}) copy-start(f32[512]{0:T(512)S(1)} %fusion.48) | copy-start | bytes 6148
  211.2 18.4 %slice-start.10 = ((s8[4718592]{0:T(1024)(128)(4,1)}), s8[524288]{0:T(1024)(128)(4,1)S(1)}, s32[]{:S(2)}) async-start(s8[4718592]{0:T(1024)(128)(4,1)} %bitcast.241), calls=%async_computation.17 | async-start | bytes 1048576
  232.4 32.9 %copy-start.8 = (f32[512,768]{1,0:T(8,128)}, f32[512,768]{1,0:T(8,128)S(1)}, u32[]{:S(2)}) copy-start(f32[512,768]{1,0:T(8,128)S(1)} %get-tuple-element.137) | copy-start | bytes 4718596
  232.7 33.8 %copy-start.57 = (f32[512]{0:T(512)}, f32[512]{0:T(512)S(1)}, u32[]{:S(2)}) copy-start(f32[512]{0:T(512)S(1)} %multiply_reduce_fusion.10) | copy-start | bytes 6148
  233.1 20.7 %collective-permute-start.4 = (bf16[512,768]{1,0:T(8,128)(2,1)S(1)}, bf16[512,768]{1,0:T(8,128)(2,1)S(1)}, u32[]{:S(2)}, u32[]{:S(2)}) collective-permute-start(bf16[512,768]{1,0:T(8,128)(2,1)S(1)} %fusion.29), channel_id=1, source_target_pairs={{0,2},{1,3},{2,4},{3,5},{4,6},{5,7},{8,10},{9,11},{10,12},{11,13},... | collective-permute-start | bytes 2359304 | tf_op jit(solution)/shard_map/ppermute | solution.py:731
  244.9 18.4 %collective-permute-start.5 = (bf16[512,768]{1,0:T(8,128)(2,1)S(1)}, bf16[512,768]{1,0:T(8,128)(2,1)S(1)}, u32[]{:S(2)}, u32[]{:S(2)}) collective-permute-start(bf16[512,768]{1,0:T(8,128)(2,1)S(1)} %fusion.29), channel_id=1, source_target_pairs={{2,0},{3,1},{4,2},{5,3},{6,4},{7,5},{10,8},{11,9},{12,10},{13,11},... | collective-permute-start | bytes 2359304 | tf_op jit(solution)/shard_map/ppermute | solution.py:731
  266.6 35.5 %collective-permute-start.6 = (bf16[1024,768]{1,0:T(8,128)(2,1)}, bf16[1024,768]{1,0:T(8,128)(2,1)}, u32[]{:S(2)}, u32[]{:S(2)}) collective-permute-start(bf16[1024,768]{1,0:T(8,128)(2,1)} %pad_maximum_fusion.1), channel_id=1, source_target_pairs={{0,8},{1,9},{2,10},{3,11},{4,12},{5,13},{6,14},{7,15},{8,0},{9,1},... | collective-permute-start | bytes 4718600 | tf_op jit(solution)/shard_map/ppermute | solution.py:731
  266.6 108.0 %collective-permute-start.8 = (bf16[512,768]{1,0:T(8,128)(2,1)}, bf16[512,768]{1,0:T(8,128)(2,1)}, u32[]{:S(2)}, u32[]{:S(2)}) collective-permute-start(bf16[512,768]{1,0:T(8,128)(2,1)} %param.11), channel_id=1, source_target_pairs={{0,0},{1,8},{2,2},{3,10},{4,4},{5,12},{6,6},{7,14},{8,1},{9,9},{10... | collective-permute-start | bytes 2359304 | tf_op jit(solution)/shard_map/ppermute | solution.py:731
  308.4 44.3 %slice-start.11 = ((s8[4718592]{0:T(1024)(128)(4,1)}), s8[4194304]{0:T(1024)(128)(4,1)S(1)}, s32[]{:S(2)}) async-start(s8[4718592]{0:T(1024)(128)(4,1)} %bitcast.244), calls=%async_computation.18 | async-start | bytes 8388608
  309.4 43.4 %slice-start.12 = ((s8[4718592]{0:T(1024)(128)(4,1)}), s8[524288]{0:T(1024)(128)(4,1)S(1)}, s32[]{:S(2)}) async-start(s8[4718592]{0:T(1024)(128)(4,1)} %bitcast.244), calls=%async_computation.19 | async-start | bytes 1048576
  318.9 32.5 %copy-start.3 = (bf16[2560,1536]{1,0:T(8,128)(2,1)}, bf16[2560,1536]{1,0:T(8,128)(2,1)S(1)}, u32[]{:S(2)}) copy-start(bf16[2560,1536]{1,0:T(8,128)(2,1)S(1)} %add_convert_fusion.k_ref.v_ref) | copy-start | bytes 23592964
  318.9 32.5 %copy-start.37 = (bf16[8,4,24,1,768]{4,2,1,0,3:T(8,128)(2,1)S(1)}, bf16[8,4,24,1,768]{4,2,1,0,3:T(8,128)(2,1)}, u32[]{:S(2)}) copy-start(bf16[8,4,24,1,768]{4,2,1,0,3:T(8,128)(2,1)} %copy.83) | copy-start | bytes 3538948
  351.4 20.0 %slice-start.15 = ((s8[4718592]{0:T(1024)(128)(4,1)}), s8[4194304]{0:T(1024)(128)(4,1)S(1)}, s32[]{:S(2)}) async-start(s8[4718592]{0:T(1024)(128)(4,1)} %bitcast.251), calls=%async_computation.22 | async-start | bytes 8388608
  352.8 18.6 %slice-start.16 = ((s8[4718592]{0:T(1024)(128)(4,1)}), s8[524288]{0:T(1024)(128)(4,1)S(1)}, s32[]{:S(2)}) async-start(s8[4718592]{0:T(1024)(128)(4,1)} %bitcast.251), calls=%async_computation.23 | async-start | bytes 1048576
  376.5 13.2 %slice-start.13 = ((s8[4718592]{0:T(1024)(128)(4,1)}), s8[4194304]{0:T(1024)(128)(4,1)S(1)}, s32[]{:S(2)}) async-start(s8[4718592]{0:T(1024)(128)(4,1)} %bitcast.247), calls=%async_computation.20 | async-start | bytes 8388608
  379.7 10.0 %copy-start.45 = (bf16[512,768]{1,0:T(8,128)(2,1)}, bf16[512,768]{1,0:T(8,128)(2,1)S(1)}, u32[]{:S(2)}) copy-start(bf16[512,768]{1,0:T(8,128)(2,1)S(1)} %get-tuple-element.60) | copy-start | bytes 2359300
  379.7 10.0 %slice-start.14 = ((s8[4718592]{0:T(1024)(128)(4,1)}), s8[524288]{0:T(1024)(128)(4,1)S(1)}, s32[]{:S(2)}) async-start(s8[4718592]{0:T(1024)(128)(4,1)} %bitcast.247), calls=%async_computation.21 | async-start | bytes 1048576
  508.0 401.5 %reduce-scatter.3.cloned.1.call-start = ((), (), s32[]{:S(2)}) async-start(), calls=%async_computation.2 | async-start | bytes 15003648 | tf_op jit(solution)/shard_map/reduce_scatter | solution.py:1028
  521.2 3.5 collective-permute-start.9
  526.8 41.8 %collective-permute-start.11 = (bf16[512,768]{1,0:T(8,128)(2,1)}, bf16[512,768]{1,0:T(8,128)(2,1)}, u32[]{:S(2)}, u32[]{:S(2)}) collective-permute-start(bf16[512,768]{1,0:T(8,128)(2,1)} %get-tuple-element.87), channel_id=1, source_target_pairs={{0,2},{1,3},{2,4},{3,5},{4,6},{5,7},{8,10},{9,11},{10,12},{11,13},... | collective-permute-start | bytes 2359304 | tf_op jit(solution)/shard_map/ppermute | solution.py:731
  552.4 20.7 %collective-permute-start.10 = (bf16[512,768]{1,0:T(8,128)(2,1)S(1)}, bf16[512,768]{1,0:T(8,128)(2,1)}, u32[]{:S(2)}, u32[]{:S(2)}) collective-permute-start(bf16[512,768]{1,0:T(8,128)(2,1)S(1)} %get-tuple-element.86), channel_id=1, source_target_pairs={{2,0},{3,1},{4,2},{5,3},{6,4},{7,5},{10,8},{11,9},{12,10},{13,11},... | collective-permute-start | bytes 2359304 | tf_op jit(solution)/shard_map/ppermute | solution.py:731
  553.7 19.4 %copy-start.10 = (f32[512,768]{1,0:T(8,128)S(1)}, f32[512,768]{1,0:T(8,128)}, u32[]{:S(2)}) copy-start(f32[512,768]{1,0:T(8,128)} %copy-done.8) | copy-start | bytes 4718596
  553.7 19.4 %copy-start.20 = (f32[512,768]{1,0:T(8,128)S(1)}, f32[512,768]{1,0:T(8,128)}, u32[]{:S(2)}) copy-start(f32[512,768]{1,0:T(8,128)} %copy-done.19) | copy-start | bytes 4718596
  577.0 11.7 %slice-start.7 = ((s8[4718592]{0:T(1024)(128)(4,1)}), s8[4194304]{0:T(1024)(128)(4,1)S(1)}, s32[]{:S(2)}) async-start(s8[4718592]{0:T(1024)(128)(4,1)} %bitcast.237), calls=%async_computation.14 | async-start | bytes 8388608
  577.9 10.8 %copy-start.43 = (bf16[512,768]{1,0:T(8,128)(2,1)}, bf16[512,768]{1,0:T(8,128)(2,1)S(1)}, u32[]{:S(2)}) copy-start(bf16[512,768]{1,0:T(8,128)(2,1)S(1)} %get-tuple-element.54) | copy-start | bytes 2359300
  577.9 10.8 %copy-start.24 = (f32[512,768]{1,0:T(8,128)S(1)}, f32[512,768]{1,0:T(8,128)}, u32[]{:S(2)}) copy-start(f32[512,768]{1,0:T(8,128)} %copy-done.23) | copy-start | bytes 4718596
  577.9 10.8 %slice-start.8 = ((s8[4718592]{0:T(1024)(128)(4,1)}), s8[524288]{0:T(1024)(128)(4,1)S(1)}, s32[]{:S(2)}) async-start(s8[4718592]{0:T(1024)(128)(4,1)} %bitcast.237), calls=%async_computation.15 | async-start | bytes 1048576
  577.9 10.8 %copy-start.54 = (f32[512]{0:T(512)S(1)}, f32[512]{0:T(512)}, u32[]{:S(2)}) copy-start(f32[512]{0:T(512)} %copy-done.53) | copy-start | bytes 6148
  577.9 10.8 %copy-start.66 = (f32[768]{0:T(1024)S(1)}, f32[768]{0:T(1024)}, u32[]{:S(2)}) copy-start(f32[768]{0:T(1024)} %copy-done.65) | copy-start | bytes 9220
  577.9 10.8 %copy-start.70 = (f32[512]{0:T(512)S(1)}, f32[512]{0:T(512)}, u32[]{:S(2)}) copy-start(f32[512]{0:T(512)} %copy-done.69) | copy-start | bytes 6148
  593.8 42.9 %copy-start.47 = (bf16[512,768]{1,0:T(8,128)(2,1)}, bf16[512,768]{1,0:T(8,128)(2,1)S(1)}, u32[]{:S(2)}) copy-start(bf16[512,768]{1,0:T(8,128)(2,1)S(1)} %get-tuple-element.58) | copy-start | bytes 2359300
  594.6 42.2 %copy-start.31 = (bf16[512,768]{1,0:T(8,128)(2,1)S(1)}, bf16[512,768]{1,0:T(8,128)(2,1)}, u32[]{:S(2)}) copy-start(bf16[512,768]{1,0:T(8,128)(2,1)} %copy-done.30) | copy-start | bytes 2359300
  698.4 268.7 %all-gather.11.cloned.1.call-start = ((), (), s32[]{:S(2)}) async-start(), calls=%async_computation.6 | async-start | bytes 4546560 | tf_op jit(solution)/shard_map/all_gather | solution.py:1030
  922.5 5.0 collective-permute-start.12
  927.8 23.4 %copy-start.18 = (f32[512,768]{1,0:T(8,128)S(1)}, f32[512,768]{1,0:T(8,128)}, u32[]{:S(2)}) copy-start(f32[512,768]{1,0:T(8,128)} %copy-done.17) | copy-start | bytes 4718596
  928.2 19.2 %collective-permute-start.14 = (bf16[512,768]{1,0:T(8,128)(2,1)S(1)}, bf16[512,768]{1,0:T(8,128)(2,1)S(1)}, u32[]{:S(2)}, u32[]{:S(2)}) collective-permute-start(bf16[512,768]{1,0:T(8,128)(2,1)S(1)} %get-tuple-element.85), channel_id=1, source_target_pairs={{0,2},{1,3},{2,4},{3,5},{4,6},{5,7},{8,10},{9,11},{10,12},{11,13},... | collective-permute-start | bytes 2359304 | tf_op jit(solution)/shard_map/ppermute | solution.py:731
  930.9 20.3 %collective-permute-start.13 = (bf16[512,768]{1,0:T(8,128)(2,1)S(1)}, bf16[512,768]{1,0:T(8,128)(2,1)S(1)}, u32[]{:S(2)}, u32[]{:S(2)}) collective-permute-start(bf16[512,768]{1,0:T(8,128)(2,1)S(1)} %get-tuple-element.84), channel_id=1, source_target_pairs={{2,0},{3,1},{4,2},{5,3},{6,4},{7,5},{10,8},{11,9},{12,10},{13,11},... | collective-permute-start | bytes 2359304 | tf_op jit(solution)/shard_map/ppermute | solution.py:731
  932.2 24.2 %collective-permute-start.7 = (bf16[512,768]{1,0:T(8,128)(2,1)S(1)}, bf16[512,768]{1,0:T(8,128)(2,1)S(1)}, u32[]{:S(2)}, u32[]{:S(2)}) collective-permute-start(bf16[512,768]{1,0:T(8,128)(2,1)S(1)} %copy-done.49), channel_id=1, source_target_pairs={{0,0},{1,8},{2,2},{3,10},{4,4},{5,12},{6,6},{7,14},{8,1},{9,9},{10... | collective-permute-start | bytes 2359304 | tf_op jit(solution)/shard_map/ppermute | solution.py:731
  951.7 14.1 %collective-permute-start.15 = (bf16[512,768]{1,0:T(8,128)(2,1)S(1)}, bf16[512,768]{1,0:T(8,128)(2,1)S(1)}, u32[]{:S(2)}, u32[]{:S(2)}) collective-permute-start(bf16[512,768]{1,0:T(8,128)(2,1)S(1)} %fusion.21), channel_id=1, source_target_pairs={{0,0},{1,8},{2,2},{3,10},{4,4},{5,12},{6,6},{7,14},{8,1},{9,9},{10... | collective-permute-start | bytes 2359304 | tf_op jit(solution)/shard_map/ppermute | solution.py:731
  956.4 9.4 copy-start.41
  (55 other events, 221.2 us)
Sparse Core Ops, SparseCore 0:
  21.2 114.4 all-gather.6
  138.6 103.1 all-gather.8
  508.1 208.4 reduce-scatter.4
  722.5 186.9 reduce-scatter.2
  911.8 31.7 all-gather.10

commit v2 on v0

--- a/solution.py
+++ b/solution.py
@@ -1,6 +1,10 @@
+import functools
+
 import jax
 import jax.numpy as jnp
 from jax import lax
+from jax.experimental import pallas as pl
+from jax.experimental.pallas import tpu as pltpu
 from jax.sharding import PartitionSpec as P
 
 HEADS = 12
@@ -456,6 +460,1236 @@
     )
 
 
+HEAD_SCALE = 0.125
+
+
+def fold_rows(values, combine):
+    total = values[:8]
+    for begin_at in range(8, values.shape[0], 8):
+        total = combine(total, values[begin_at : begin_at + 8])
+    return total
+
+
+def halves_of(block):
+    lane = lax.broadcasted_iota(jnp.int32, block.shape, 1)
+    nothing = jnp.zeros_like(block)
+    return (jnp.where(lane < 64, block, nothing), jnp.where(lane < 64, nothing, block))
+
+
+def turned_dot(keys, queries):
+    return lax.dot_general(
+        keys, queries, (((1,), (1,)), ((), ())), preferred_element_type=jnp.float32
+    )
+
+
+def across_dot(weight, values):
+    return lax.dot_general(
+        weight, values, (((0,), (0,)), ((), ())), preferred_element_type=jnp.float32
+    )
+
+
+KEY_ROWS = 512
+KEY_TILES = 5
+
+
+def key_rows(tile):
+    return pl.ds(pl.multiple_of(tile * KEY_ROWS, KEY_ROWS), KEY_ROWS)
+
+
+def fill_mask(first, last, low, high, mask_scr, index):
+    def mask_step(key_tile, carry):
+        shape = (KEY_ROWS, low.shape[1])
+        place = lax.broadcasted_iota(jnp.int32, shape, 0) + key_tile * KEY_ROWS
+        allowed = (place >= low) & (place < high)
+        mask_scr[index, key_rows(key_tile - first), :] = jnp.where(allowed, 0.0, NEGATIVE)
+        return carry
+
+    lax.fori_loop(first, last, mask_step, 0)
+
+
+def flash_forward_kernel(
+    bounds,
+    a_ref,
+    b_ref,
+    kv_ref,
+    low_ref,
+    high_ref,
+    a_mix,
+    b_mix,
+    a_wide,
+    b_wide,
+    lse_ref,
+    mask_scr,
+    score_scr,
+):
+    rows, width = a_ref.shape
+    pairs = width // 128
+    for index in range(2):
+        span = slice(index * rows, (index + 1) * rows)
+        fill_mask(
+            bounds[2 * index],
+            bounds[2 * index + 1],
+            low_ref[0:1, span],
+            high_ref[0:1, span],
+            mask_scr,
+            index,
+        )
+
+    def pair_step(pair, unused):
+        lanes = pl.ds(pl.multiple_of(pair * 128, 128), 128)
+        value_lanes = pl.ds(pl.multiple_of(pair * 128 + width, 128), 128)
+        for index, (q_ref, mix_ref, wide_ref) in enumerate(
+            ((a_ref, a_mix, a_wide), (b_ref, b_mix, b_wide))
+        ):
+            first, last = bounds[2 * index], bounds[2 * index + 1]
+            heads = halves_of(q_ref[:, lanes] * jnp.bfloat16(HEAD_SCALE))
+
+            def score_step(key_tile, tops, index=index, heads=heads, first=first):
+                keys = kv_ref[key_rows(bounds[4 + key_tile]), lanes]
+                place = key_rows(key_tile - first)
+                mask = mask_scr[index, place, :]
+                out = []
+                for head in range(2):
+                    scores = turned_dot(keys, heads[head]) + mask
+                    score_scr[head, place, :] = scores
+                    out.append(jnp.maximum(tops[head], fold_rows(scores, jnp.maximum)))
+                return tuple(out)
+
+            floor = jnp.full((8, rows), NEGATIVE, jnp.float32)
+            tops = lax.fori_loop(first, last, score_step, (floor, floor))
+            tops = [jnp.max(top, axis=0, keepdims=True) for top in tops]
+
+            def mix_step(key_tile, carry, tops=tops, first=first):
+                values = kv_ref[key_rows(bounds[4 + key_tile]), value_lanes].T
+                totals, mixed = [], []
+                for head in range(2):
+                    weight = jnp.exp(score_scr[head, key_rows(key_tile - first), :] - tops[head])
+                    totals.append(carry[head] + fold_rows(weight, jnp.add))
+                    mixed.append(
+                        carry[2 + head]
+                        + jnp.dot(
+                            values[head * 64 : (head + 1) * 64],
+                            weight.astype(jnp.bfloat16),
+                            preferred_element_type=jnp.float32,
+                        )
+                    )
+                return (totals[0], totals[1], mixed[0], mixed[1])
+
+            zero = jnp.zeros((8, rows), jnp.float32)
+            nothing = jnp.zeros((64, rows), jnp.float32)
+            carry = lax.fori_loop(first, last, mix_step, (zero, zero, nothing, nothing))
+            totals = [jnp.sum(total, axis=0, keepdims=True) for total in carry[:2]]
+            mixed = jnp.concatenate(
+                [carry[2] * (1.0 / totals[0]), carry[3] * (1.0 / totals[1])], axis=0
+            ).T
+            wide_ref[:, lanes] = mixed
+            mix_ref[:, lanes] = mixed.astype(jnp.bfloat16)
+            lse_rows = [tops[head] + jnp.log(totals[head]) for head in range(2)]
+            lse_ref[
+                pl.ds(pl.multiple_of(pair * 8, 8), 8), index * rows : (index + 1) * rows
+            ] = jnp.concatenate([jnp.broadcast_to(line, (4, rows)) for line in lse_rows])
+        return unused
+
+    lax.fori_loop(0, pairs, pair_step, 0)
+
+
+def flash_backward_kernel(
+    bounds,
+    a_ref,
+    b_ref,
+    kv_ref,
+    a_grad_ref,
+    b_grad_ref,
+    a_wide,
+    b_wide,
+    lse_ref,
+    low_ref,
+    high_ref,
+    a_out,
+    b_out,
+    kv_out,
+    mask_scr,
+    k_acc,
+    v_acc,
+):
+    rows, width = a_ref.shape
+    pairs = width // 128
+    tiles = kv_ref.shape[0] // KEY_ROWS
+    for index in range(2):
+        span = slice(index * rows, (index + 1) * rows)
+        fill_mask(
+            bounds[2 * index],
+            bounds[2 * index + 1],
+            low_ref[0:1, span],
+            high_ref[0:1, span],
+            mask_scr,
+            index,
+        )
+
+    def pair_step(pair, unused):
+        lanes = pl.ds(pl.multiple_of(pair * 128, 128), 128)
+        value_lanes = pl.ds(pl.multiple_of(pair * 128 + width, 128), 128)
+        lse_rows = lse_ref[pl.ds(pl.multiple_of(pair * 8, 8), 8), :]
+        k_acc[...] = jnp.zeros_like(k_acc)
+        v_acc[...] = jnp.zeros_like(v_acc)
+        ways = (((1,), (1,)), ((), ()))
+        for index, (q_ref, grad_ref, wide_ref, q_out) in enumerate(
+            ((a_ref, a_grad_ref, a_wide, a_out), (b_ref, b_grad_ref, b_wide, b_out))
+        ):
+            first, last = bounds[2 * index], bounds[2 * index + 1]
+            heads = halves_of(q_ref[:, lanes] * jnp.bfloat16(HEAD_SCALE))
+            grads = halves_of(grad_ref[:, lanes])
+            turned_q = (q_ref[:, lanes] * jnp.bfloat16(HEAD_SCALE)).T
+            turned_grad = grad_ref[:, lanes].T
+            span = slice(index * rows, (index + 1) * rows)
+            lse = (lse_rows[0:1, span], lse_rows[4:5, span])
+
+            product = (grad_ref[:, lanes].astype(jnp.float32) * wide_ref[:, lanes]).T
+            deltas = (
+                jnp.sum(product[:64], axis=0, keepdims=True),
+                jnp.sum(product[64:], axis=0, keepdims=True),
+            )
+
+            def grad_step(
+                key_tile,
+                q_sum,
+                index=index,
+                heads=heads,
+                grads=grads,
+                lse=lse,
+                deltas=deltas,
+                first=first,
+                turned_q=turned_q,
+                turned_grad=turned_grad,
+            ):
+                source = key_rows(bounds[4 + key_tile])
+                columns = key_rows(bounds[4 + key_tile])
+                keys = kv_ref[source, lanes]
+                turned_keys = keys.T
+                values = kv_ref[source, value_lanes]
+                mask = mask_scr[index, key_rows(key_tile - first), :]
+                out = []
+                for head in range(2):
+                    part = slice(head * 64, (head + 1) * 64)
+                    scores = turned_dot(keys, heads[head])
+                    slope = turned_dot(values, grads[head])
+                    probs = jnp.exp((scores - lse[head]) + mask)
+                    low_slope = (probs * (slope - deltas[head])).astype(jnp.bfloat16)
+                    v_acc[part, columns] += lax.dot_general(
+                        turned_grad[part],
+                        probs.astype(jnp.bfloat16),
+                        ways,
+                        preferred_element_type=jnp.float32,
+                    )
+                    k_acc[part, columns] += lax.dot_general(
+                        turned_q[part], low_slope, ways, preferred_element_type=jnp.float32
+                    )
+                    out.append(
+                        q_sum[head]
+                        + jnp.dot(turned_keys[part], low_slope, preferred_element_type=jnp.float32)
+                    )
+                return tuple(out)
+
+            nothing = jnp.zeros((64, rows), jnp.float32)
+            q_parts = lax.fori_loop(first, last, grad_step, (nothing, nothing))
+            q_part = jnp.concatenate(q_parts, axis=0).T
+            q_out[:, lanes] = (q_part * HEAD_SCALE).astype(jnp.bfloat16)
+
+        def store_step(tile, carry):
+            source = key_rows(tile)
+            kv_out[source, lanes] = k_acc[:, source].T.astype(jnp.bfloat16)
+            kv_out[source, value_lanes] = v_acc[:, source].T.astype(jnp.bfloat16)
+            return carry
+
+        lax.fori_loop(0, tiles, store_step, 0)
+        return unused
+
+    lax.fori_loop(0, pairs, pair_step, 0)
+
+
+def whole_block(shape):
+    return pl.BlockSpec(shape, lambda i, b: (0,) * len(shape), pipeline_mode=pl.Buffered(1))
+
+
+def flash_forward(bounds, queries, key_value, low, high):
+    rows, width = queries[0].shape
+    window = key_value.shape[0]
+    pairs = width // 128
+    own = whole_block((rows, width))
+    line = whole_block((8, 2 * rows))
+    return pl.pallas_call(
+        flash_forward_kernel,
+        out_shape=(
+            jax.ShapeDtypeStruct((rows, width), jnp.bfloat16),
+            jax.ShapeDtypeStruct((rows, width), jnp.bfloat16),
+            jax.ShapeDtypeStruct((rows, width), jnp.float32),
+            jax.ShapeDtypeStruct((rows, width), jnp.float32),
+            jax.ShapeDtypeStruct((pairs * 8, 2 * rows), jnp.float32),
+        ),
+        grid_spec=pltpu.PrefetchScalarGridSpec(
+            num_scalar_prefetch=1,
+            grid=(1,),
+            in_specs=[own, own, whole_block((window, 2 * width)), line, line],
+            out_specs=[own, own, own, own, whole_block((pairs * 8, 2 * rows))],
+            scratch_shapes=[
+                pltpu.VMEM((2, KEY_TILES * KEY_ROWS, rows), jnp.float32),
+                pltpu.VMEM((2, KEY_TILES * KEY_ROWS, rows), jnp.float32),
+            ],
+        ),
+        compiler_params=pltpu.CompilerParams(vmem_limit_bytes=44 * 2**20),
+        cost_estimate=pl.CostEstimate(
+            flops=8 * rows * width * 2560, bytes_accessed=12 * 2**20, transcendentals=rows * 12 * 2560
+        ),
+        name="flash_forward",
+    )(bounds, queries[0], queries[1], key_value, low, high)
+
+
+def flash_backward(bounds, queries, key_value, grads, wides, lse, low, high):
+    rows, width = queries[0].shape
+    window = key_value.shape[0]
+    pairs = width // 128
+    own = whole_block((rows, width))
+    wide = whole_block((window, 2 * width))
+    line = whole_block((8, 2 * rows))
+    return pl.pallas_call(
+        flash_backward_kernel,
+        out_shape=(
+            jax.ShapeDtypeStruct((rows, width), jnp.bfloat16),
+            jax.ShapeDtypeStruct((rows, width), jnp.bfloat16),
+            jax.ShapeDtypeStruct((window, 2 * width), jnp.bfloat16),
+        ),
+        grid_spec=pltpu.PrefetchScalarGridSpec(
+            num_scalar_prefetch=1,
+            grid=(1,),
+            in_specs=[own, own, wide] + [own] * 4 + [whole_block((pairs * 8, 2 * rows)), line, line],
+            out_specs=[own, own, wide],
+            scratch_shapes=[
+                pltpu.VMEM((2, KEY_TILES * KEY_ROWS, rows), jnp.float32),
+                pltpu.VMEM((128, window), jnp.float32),
+                pltpu.VMEM((128, window), jnp.float32),
+            ],
+        ),
+        compiler_params=pltpu.CompilerParams(vmem_limit_bytes=56 * 2**20),
+        cost_estimate=pl.CostEstimate(
+            flops=20 * rows * width * 2560,
+            bytes_accessed=20 * 2**20,
+            transcendentals=rows * 12 * 2560,
+        ),
+        name="flash_backward",
+    )(bounds, *queries, key_value, *grads, *wides, lse, low, high)
+
+
+GRP_Y, GRP_CORE, SHARD_Z, SHARD_X = 2, 2, 4, 2
+BOTH = ("grp", "shard")
+
+
+def device_pairs(place):
+    pairs = []
+    for y in range(GRP_Y):
+        for core in range(GRP_CORE):
+            for z in range(SHARD_Z):
+                for x in range(SHARD_X):
+                    target = place(y, core, z, x)
+                    if target is not None:
+                        ty, tcore, tz, tx = target
+                        pairs.append(
+                            (
+                                (y * GRP_CORE + core) * SHARD_Z * SHARD_X + z * SHARD_X + x,
+                                (ty * GRP_CORE + tcore) * SHARD_Z * SHARD_X + tz * SHARD_X + tx,
+                            )
+                        )
+    return pairs
+
+
+def send(values, place):
+    return lax.ppermute(values, BOTH, device_pairs(place))
+
+
+def turn_rows(values):
+    return send(values, lambda y, core, z, x: (y, x, z, core))
+
+
+def swap_core(values):
+    return send(values, lambda y, core, z, x: (y, 1 - core, z, x))
+
+
+def send_up(values):
+    return send(values, lambda y, core, z, x: (y, core, z + 1, x) if z + 1 < SHARD_Z else None)
+
+
+def send_down(values):
+    return send(values, lambda y, core, z, x: (y, core, z - 1, x) if z > 0 else None)
+
+
+def window_of(rows):
+    near = jnp.concatenate([rows, send_up(rows), send_down(rows)])
+    return jnp.concatenate([near, swap_core(near)])
+
+
+def window_back(near, far, count):
+    total = near + swap_core(far.astype(jnp.bfloat16)).astype(jnp.float32)
+    below = total[count : 2 * count].astype(jnp.bfloat16)
+    above = total[2 * count :].astype(jnp.bfloat16)
+    return (
+        total[:count]
+        + send_down(below).astype(jnp.float32)
+        + send_up(above).astype(jnp.float32)
+    )
+
+
+def half_of(values, axis, index):
+    count = values.shape[axis] // 2
+    return lax.dynamic_slice_in_dim(values, index * count, count, axis)
+
+
+def unpack_kernel(kinds, in_ref, *outs):
+    width = in_ref.shape[-1]
+    share = in_ref.shape[3]
+    place = 0
+    for kind, ref in zip(kinds, outs):
+        if kind == "columns":
+            for column in range(ref.shape[-1] // width):
+                ref[:, 0, :, column * width : (column + 1) * width] = in_ref[0, :, place]
+                place += 1
+        else:
+            for piece in range(ref.shape[2] // share):
+                ref[:, 0, piece * share : (piece + 1) * share, :] = in_ref[0, :, place]
+                place += 1
+
+
+def unpack_weights_of(pieces, begin_at, places, kinds, shapes):
+    quarters, shards, unused, share, width = pieces.shape
+    outs = pl.pallas_call(
+        functools.partial(unpack_kernel, kinds),
+        out_shape=[
+            jax.ShapeDtypeStruct((shards, quarters, rows, wide), pieces.dtype)
+            for rows, wide in shapes
+        ],
+        grid=(quarters,),
+        in_specs=[
+            pl.BlockSpec(
+                (1, shards, places, share, width), lambda q: (q, 0, begin_at // places, 0, 0)
+            )
+        ],
+        out_specs=[
+            pl.BlockSpec((shards, 1, rows, wide), lambda q: (0, q, 0, 0)) for rows, wide in shapes
+        ],
+        compiler_params=pltpu.CompilerParams(vmem_limit_bytes=32 * 2**20),
+        cost_estimate=pl.CostEstimate(
+            flops=0, bytes_accessed=128 * places * share * width, transcendentals=0
+        ),
+        name="unpack_weights",
+    )(pieces)
+    return [out.reshape(-1, out.shape[-1]) for out in outs]
+
+
+def pick_kernel(
+    me, near_ref, project_ref, mixer_ref, expand_ref, reduce_ref, small_ref, a_out, b_out, c_out
+):
+    part, half = a_out.shape[-2:]
+    for column in range(3):
+        begin_at = pl.multiple_of(column * 2 * half + me[1] * half, 128)
+        a_out[column] = near_ref[0, :, pl.ds(begin_at, half)]
+    a_out[3] = jnp.zeros((part, half), a_out.dtype)
+    a_out[3, 0:8, :] = small_ref[:, :half]
+    a_out[3, 8:16, :] = small_ref[:, half:]
+    share, width = b_out.shape[-2:]
+    wide = expand_ref.shape[-1] // width
+    for layer, ref in enumerate((b_out, c_out)):
+        ref[0] = mixer_ref[layer]
+        for column in range(wide):
+            ref[1 + column] = expand_ref[layer, :, column * width : (column + 1) * width]
+        for piece in range(reduce_ref.shape[1] // share):
+            ref[1 + wide + piece] = reduce_ref[layer, piece * share : (piece + 1) * share, :]
+    far = c_out.shape[0]
+    for column in range(3):
+        b_out[far + column] = project_ref[0, :, column * width : (column + 1) * width]
+
+
+def pick_quarters(me, project, mixer, expand, reduce, small):
+    share, width = mixer.shape[1] // 4, mixer.shape[2]
+    far = 1 + expand.shape[2] // width + reduce.shape[1] // 4 // share
+
+    def quarter_spec(array):
+        return pl.BlockSpec(
+            (LAYERS, array.shape[1] // 4, array.shape[2]),
+            lambda i, me: (0, me[0] * GRP_CORE + me[1], 0),
+        )
+
+    shapes = [(4, 2 * share, width // 2), (far + 3, share, width), (far, share, width)]
+    return pl.pallas_call(
+        pick_kernel,
+        out_shape=[jax.ShapeDtypeStruct(shape, jnp.bfloat16) for shape in shapes],
+        grid_spec=pltpu.PrefetchScalarGridSpec(
+            num_scalar_prefetch=1,
+            grid=(1,),
+            in_specs=[
+                pl.BlockSpec((1, 2 * share, project.shape[2]), lambda i, me: (0, me[0], 0)),
+                pl.BlockSpec(
+                    (1, share, project.shape[2]), lambda i, me: (1, me[0] * GRP_CORE + me[1], 0)
+                ),
+            ]
+            + [quarter_spec(array) for array in (mixer, expand, reduce)]
+            + [pl.BlockSpec(small.shape, lambda i, me: (0, 0))],
+            out_specs=[pl.BlockSpec(shape, lambda i, me: (0, 0, 0)) for shape in shapes],
+        ),
+        name="pick_quarters",
+    )(me, project, project, mixer, expand, reduce, small)
+
+
+def pack_kernel(kinds, *refs):
+    ins, vector_ref, out_ref = refs[:-2], refs[-2], refs[-1]
+    width = out_ref.shape[-1]
+    share = out_ref.shape[3]
+    place = 0
+    for kind, ref in zip(kinds, ins):
+        if kind == "columns":
+            for column in range(ref.shape[-1] // width):
+                out_ref[0, :, place] = ref[:, 0, :, column * width : (column + 1) * width]
+                place += 1
+        else:
+            for piece in range(ref.shape[2] // share):
+                out_ref[0, :, place] = ref[:, 0, piece * share : (piece + 1) * share, :]
+                place += 1
+    out_ref[0, :, place] = jnp.zeros_like(out_ref[0, :, place])
+    out_ref[0, :, place, 0:8, :] = vector_ref[0]
+
+
+def pack_terms(terms, kinds, share, width, vectors):
+    places = sum(t.size for t in terms) // (32 * share * width) + 1
+    views = [t.reshape(8, 4, -1, t.shape[1]) for t in terms]
+    return pl.pallas_call(
+        functools.partial(pack_kernel, kinds),
+        out_shape=jax.ShapeDtypeStruct((4, 8, places, share, width), jnp.bfloat16),
+        grid=(4,),
+        in_specs=[pl.BlockSpec((8, 1) + view.shape[2:], lambda q: (0, q, 0, 0)) for view in views]
+        + [pl.BlockSpec((1,) + vectors.shape[1:], lambda q: (q, 0, 0, 0))],
+        out_specs=pl.BlockSpec((1, 8, places, share, width), lambda q: (q, 0, 0, 0, 0)),
+        compiler_params=pltpu.CompilerParams(vmem_limit_bytes=32 * 2**20),
+        cost_estimate=pl.CostEstimate(
+            flops=0, bytes_accessed=4 * 32 * places * share * width, transcendentals=0
+        ),
+        name="pack_terms",
+    )(*views, vectors)
+
+
+def swap_y(values):
+    return send(values, lambda y, core, z, x: (1 - y, core, z, x))
+
+
+def swap_x(values):
+    return send(values, lambda y, core, z, x: (y, core, z, 1 - x))
+
+
+def swap_z(values, bit):
+    return send(values, lambda y, core, z, x: (y, core, z ^ bit, x))
+
+
+def spread_kernel(me, q_ref, kv_ref, vector_ref, out_ref):
+    part, half = out_ref.shape[-2:]
+    for x_bit in range(SHARD_X):
+        for z_bits in range(SHARD_Z):
+            shard = (z_bits ^ me[3]) * SHARD_X + (x_bit ^ me[2])
+            out_ref[0, x_bit, z_bits, 0] = q_ref[shard, 0]
+            out_ref[0, x_bit, z_bits, 1] = kv_ref[shard, 0, :, :half]
+            out_ref[0, x_bit, z_bits, 2] = kv_ref[shard, 0, :, half:]
+            out_ref[0, x_bit, z_bits, 3] = jnp.zeros((part, half), jnp.bfloat16)
+            out_ref[0, x_bit, z_bits, 3, 0:8, :] = vector_ref[0, shard]
+
+
+def spread_terms(me, query_term, key_value_term, vectors):
+    half = query_term.shape[1]
+    part = query_term.shape[0] // 16
+    shape = (GRP_Y, SHARD_X, SHARD_Z, 4, part, half)
+
+    def rows_spec(columns):
+        return pl.BlockSpec((8, 1, part, columns), lambda j, me: (0, j ^ me[0], 0, 0))
+
+    return pl.pallas_call(
+        spread_kernel,
+        out_shape=jax.ShapeDtypeStruct(shape, jnp.bfloat16),
+        grid_spec=pltpu.PrefetchScalarGridSpec(
+            num_scalar_prefetch=1,
+            grid=(2,),
+            in_specs=[
+                rows_spec(half),
+                rows_spec(2 * half),
+                pl.BlockSpec((1,) + vectors.shape[1:], lambda j, me: (j ^ me[0], 0, 0, 0)),
+            ],
+            out_specs=pl.BlockSpec((1,) + shape[1:], lambda j, me: (j, 0, 0, 0, 0, 0)),
+        ),
+        name="spread_terms",
+    )(
+        me,
+        query_term.reshape(8, 2, part, half),
+        key_value_term.reshape(8, 2, part, 2 * half),
+        vectors,
+    )
+
+
+def summed(one, other):
+    return (one.astype(jnp.float32) + other.astype(jnp.float32)).astype(jnp.bfloat16)
+
+
+def scatter_terms(me, query_term, key_value_term, vectors):
+    spread = spread_terms(me, query_term, key_value_term, vectors)
+    a_part, b_part = spread[:, :, :, :2], spread[:, :, :, 2:]
+    a_next = swap_y(a_part[1])
+    b_next = swap_x(b_part[:, 1])
+    a_last = swap_x(summed(a_part[0, 1], a_next[1]))
+    b_last = swap_y(summed(b_part[1, 0], b_next[1]))
+    a_keep = summed(a_part[0, 0], a_next[0])
+    b_keep = summed(b_part[0, 0], b_next[0])
+    whole = jnp.concatenate([a_keep, b_keep], axis=1)
+    come = jnp.concatenate([a_last, b_last], axis=1)
+    far = swap_z(summed(whole[2:], come[2:]), 2)
+    whole = summed(whole[:2], come[:2])
+    near = swap_z(summed(whole[1], far[1]), 1)
+    return summed(summed(whole[0], far[0]), near)
+
+
+def gather_quarters(piece):
+    pair = jnp.stack([piece, swap_y(piece)])
+    return jnp.stack([pair, swap_core(pair)])
+
+
+def finish_kernel(me, *refs):
+    layers = len(refs) // 2 - 3
+    outs = refs[2 * layers :]
+
+    def fill(near_ref, far_ref):
+        part, half = near_ref.shape[-2:]
+        share, width = far_ref.shape[-2:]
+        for y_bit in range(GRP_Y):
+            for core_bit in range(GRP_CORE):
+                y = y_bit ^ me[0]
+                core = core_bit ^ me[1]
+                quarter = y * GRP_CORE + core
+                for column in range(3):
+                    lanes = pl.ds(pl.multiple_of(column * 2 * half + core * half, 128), half)
+                    outs[0][0, y, :, lanes] = near_ref[core_bit, y_bit, column].astype(jnp.float32)
+                outs[4][0, quarter] = near_ref[core_bit, y_bit, 3, 0:8, :].astype(jnp.float32)
+                outs[1][0, quarter] = far_ref[core_bit, y_bit, 0].astype(jnp.float32)
+                place = 1
+                for column in range(outs[2].shape[-1] // width):
+                    lanes = slice(column * width, (column + 1) * width)
+                    outs[2][0, quarter, :, lanes] = far_ref[core_bit, y_bit, place].astype(
+                        jnp.float32
+                    )
+                    place += 1
+                for piece in range(outs[3].shape[2] // share):
+                    rows = slice(piece * share, (piece + 1) * share)
+                    outs[3][0, quarter, rows, :] = far_ref[core_bit, y_bit, place].astype(
+                        jnp.float32
+                    )
+                    place += 1
+                outs[5][0, quarter] = far_ref[core_bit, y_bit, place, 0:8, :].astype(jnp.float32)
+
+    for layer in range(layers):
+        pl.when(pl.program_id(0) == layer)(
+            functools.partial(fill, refs[2 * layer], refs[2 * layer + 1])
+        )
+
+
+def finish_shares(me, shares, hidden_units, deep):
+    layers = len(shares)
+    part, half = shares[0][0].shape[-2:]
+    share, width = shares[0][1].shape[-2:]
+    shapes = [
+        (2, part, 3 * width),
+        (4, share, width),
+        (4, share, hidden_units),
+        (4, deep, width),
+        (4, 8, half),
+        (4, 8, width),
+    ]
+    flat = [array for pair in shares for array in pair]
+    outs = pl.pallas_call(
+        finish_kernel,
+        out_shape=[jax.ShapeDtypeStruct((layers,) + shape, jnp.float32) for shape in shapes],
+        grid_spec=pltpu.PrefetchScalarGridSpec(
+            num_scalar_prefetch=1,
+            grid=(layers,),
+            in_specs=[whole_block(array.shape) for array in flat],
+            out_specs=[
+                pl.BlockSpec((1,) + shape, lambda i, me: (i, 0, 0, 0)) for shape in shapes
+            ],
+        ),
+        compiler_params=pltpu.CompilerParams(vmem_limit_bytes=32 * 2**20),
+        name="finish_shares",
+    )(me, *flat)
+    return [out.reshape(layers, -1, out.shape[-1]) for out in outs[:4]] + list(outs[4:])
+
+
+def row_mean(values):
+    return jnp.mean(values, axis=1, keepdims=True)
+
+
+def column_sum(values):
+    return jnp.sum(values, axis=0, keepdims=True)
+
+
+def standardized(values):
+    centered = values - row_mean(values)
+    scale = lax.rsqrt(row_mean(centered * centered) + EPSILON)
+    return centered * scale, scale
+
+
+def standard_back(grad, norm, scale, gain):
+    weighted = grad * gain
+    return (weighted - row_mean(weighted) - norm * row_mean(weighted * norm)) * scale
+
+
+def tail_forward_kernel(
+    me,
+    own_ref,
+    far_ref,
+    state_ref,
+    mixer_ref,
+    expand_ref,
+    reduce_ref,
+    bias_in_ref,
+    vector_ref,
+    mix_out,
+    norm_one_out,
+    scale_one_out,
+    low_out,
+    active_out,
+    slope_out,
+    norm_two_out,
+    scale_two_out,
+    state_out,
+    state_low_out,
+    wide_scr,
+    total_scr,
+):
+    step = pl.program_id(0)
+    half = own_ref.shape[1]
+
+    @pl.when(step == 0)
+    def begin():
+        mix_out[:, pl.ds(pl.multiple_of(me[1] * half, 128), half)] = own_ref[...]
+        mix_out[:, pl.ds(pl.multiple_of((1 - me[1]) * half, 128), half)] = far_ref[...]
+        branch = jnp.dot(mix_out[...], mixer_ref[...], preferred_element_type=jnp.float32)
+        norm, scale = standardized(state_ref[...].astype(jnp.float32) + (branch + vector_ref[0:1]))
+        norm_one_out[...] = norm
+        scale_one_out[...] = jnp.broadcast_to(scale, scale_one_out.shape)
+        wide = norm * vector_ref[1:2] + vector_ref[2:3]
+        wide_scr[...] = wide
+        low_out[...] = wide.astype(jnp.bfloat16)
+        total_scr[...] = jnp.zeros_like(total_scr)
+
+    before = (
+        jnp.dot(low_out[...], expand_ref[...], preferred_element_type=jnp.float32)
+        + bias_in_ref[...]
+    )
+    normal = 0.5 * (1.0 + lax.erf(before * 0.7071067811865476))
+    density = jnp.exp(before * before * -0.5) * 0.3989422804014327
+    active = (before * normal).astype(jnp.bfloat16)
+    active_out[...] = active
+    slope_out[...] = normal + before * density
+    total_scr[...] += jnp.dot(active, reduce_ref[...], preferred_element_type=jnp.float32)
+
+    @pl.when(step == pl.num_programs(0) - 1)
+    def end():
+        norm, scale = standardized(wide_scr[...] + (total_scr[...] + vector_ref[3:4]))
+        norm_two_out[...] = norm
+        scale_two_out[...] = jnp.broadcast_to(scale, scale_two_out.shape)
+        state = norm * vector_ref[4:5] + vector_ref[5:6]
+        state_out[...] = state
+        state_low_out[...] = state.astype(jnp.bfloat16)
+
+
+FEED_TILE = 512
+
+
+def tail_forward(me, own_mix, far_mix, state, mixer, expand, reduce, bias_in, vectors):
+    rows, width = state.shape
+    hidden_units = expand.shape[1]
+    steps = hidden_units // FEED_TILE
+    whole = whole_block((rows, width))
+    halves = whole_block((rows, width // 2))
+    scale = whole_block((rows, 128))
+    tile = pl.BlockSpec((rows, FEED_TILE), lambda j, me: (0, j))
+
+    def shaped(columns, kind):
+        return jax.ShapeDtypeStruct((rows, columns), kind)
+
+    return pl.pallas_call(
+        tail_forward_kernel,
+        out_shape=[
+            shaped(width, jnp.bfloat16),
+            shaped(width, jnp.float32),
+            shaped(128, jnp.float32),
+            shaped(width, jnp.bfloat16),
+            shaped(hidden_units, jnp.bfloat16),
+            shaped(hidden_units, jnp.float32),
+            shaped(width, jnp.float32),
+            shaped(128, jnp.float32),
+            shaped(width, jnp.float32),
+            shaped(width, jnp.bfloat16),
+        ],
+        grid_spec=pltpu.PrefetchScalarGridSpec(
+            num_scalar_prefetch=1,
+            grid=(steps,),
+            in_specs=[
+                halves,
+                halves,
+                whole,
+                whole_block((width, width)),
+                pl.BlockSpec((width, FEED_TILE), lambda j, me: (0, j)),
+                pl.BlockSpec((FEED_TILE, width), lambda j, me: (j, 0)),
+                pl.BlockSpec((1, FEED_TILE), lambda j, me: (0, j)),
+                whole_block((8, width)),
+            ],
+            out_specs=[whole, whole, scale, whole, tile, tile, whole, scale, whole, whole],
+            scratch_shapes=[
+                pltpu.VMEM((rows, width), jnp.float32),
+                pltpu.VMEM((rows, width), jnp.float32),
+            ],
+        ),
+        compiler_params=pltpu.CompilerParams(vmem_limit_bytes=44 * 2**20),
+        cost_estimate=pl.CostEstimate(
+            flops=2 * rows * width * (width + 2 * hidden_units),
+            bytes_accessed=32 * 2**20,
+            transcendentals=2 * rows * hidden_units,
+        ),
+        name="tail_forward",
+    )(me, own_mix, far_mix, state, mixer, expand, reduce, bias_in, vectors)
+
+
+def tail_backward_kernel(
+    me,
+    grad_ref,
+    norm_two_ref,
+    scale_two_ref,
+    norm_one_ref,
+    scale_one_ref,
+    low_ref,
+    mix_ref,
+    slope_ref,
+    active_ref,
+    expand_ref,
+    reduce_ref,
+    mixer_ref,
+    vector_ref,
+    sum_out,
+    own_out,
+    far_out,
+    mixer_out,
+    expand_out,
+    reduce_out,
+    bias_in_out,
+    vector_out,
+    wide_scr,
+    feed_scr,
+    total_scr,
+):
+    step = pl.program_id(0)
+    half = own_out.shape[1]
+
+    @pl.when(step == 0)
+    def begin():
+        grad = grad_ref[...]
+        norm = norm_two_ref[...]
+        wide = standard_back(grad, norm, scale_two_ref[:, 0:1], vector_ref[4:5])
+        wide_scr[...] = wide
+        feed = wide.astype(jnp.bfloat16)
+        feed_scr[...] = feed
+        vector_out[...] = jnp.zeros_like(vector_out)
+        vector_out[3:4] = column_sum(feed.astype(jnp.float32))
+        vector_out[4:5] = column_sum(grad * norm)
+        vector_out[5:6] = column_sum(grad)
+        total_scr[...] = jnp.zeros_like(total_scr)
+
+    feed = feed_scr[...]
+    active_grad = turned_dot(feed, reduce_ref[...])
+    before = (active_grad * slope_ref[...]).astype(jnp.bfloat16)
+    bias_in_out[...] = column_sum(before.astype(jnp.float32))
+    reduce_out[...] = across_dot(active_ref[...], feed).astype(jnp.bfloat16)
+    expand_out[...] = across_dot(low_ref[...], before).astype(jnp.bfloat16)
+    total_scr[...] += turned_dot(before, expand_ref[...])
+
+    @pl.when(step == pl.num_programs(0) - 1)
+    def end():
+        grad = wide_scr[...] + total_scr[...]
+        norm = norm_one_ref[...]
+        wide = standard_back(grad, norm, scale_one_ref[:, 0:1], vector_ref[1:2])
+        sum_out[...] = wide
+        branch = wide.astype(jnp.bfloat16)
+        vector_out[0:1] = column_sum(branch.astype(jnp.float32))
+        vector_out[1:2] = column_sum(grad * norm)
+        vector_out[2:3] = column_sum(grad)
+        mixer_out[...] = across_dot(mix_ref[...], branch).astype(jnp.bfloat16)
+        mixed = turned_dot(branch, mixer_ref[...]).astype(jnp.bfloat16)
+        total_scr[...] = mixed.astype(jnp.float32)
+        own = total_scr[:, pl.ds(pl.multiple_of(me[1] * half, 128), half)]
+        far = total_scr[:, pl.ds(pl.multiple_of((1 - me[1]) * half, 128), half)]
+        own_out[...] = own.astype(jnp.bfloat16)
+        far_out[...] = far.astype(jnp.bfloat16)
+
+
+def tail_backward(me, grad, kept, weights, vectors):
+    norm_two, scale_two, norm_one, scale_one, low, mixed, slope, active = kept
+    mixer, expand, reduce = weights
+    rows, width = grad.shape
+    hidden_units = expand.shape[1]
+    steps = hidden_units // FEED_TILE
+    whole = whole_block((rows, width))
+    halves = whole_block((rows, width // 2))
+    scale = whole_block((rows, 128))
+    square = whole_block((width, width))
+    tile = pl.BlockSpec((rows, FEED_TILE), lambda j, me: (0, j))
+    across = pl.BlockSpec((width, FEED_TILE), lambda j, me: (0, j))
+    down = pl.BlockSpec((FEED_TILE, width), lambda j, me: (j, 0))
+    line = pl.BlockSpec((1, FEED_TILE), lambda j, me: (0, j))
+
+    def shaped(rows, columns, kind):
+        return jax.ShapeDtypeStruct((rows, columns), kind)
+
+    return pl.pallas_call(
+        tail_backward_kernel,
+        out_shape=[
+            shaped(rows, width, jnp.float32),
+            shaped(rows, width // 2, jnp.bfloat16),
+            shaped(rows, width // 2, jnp.bfloat16),
+            shaped(width, width, jnp.bfloat16),
+            shaped(width, hidden_units, jnp.bfloat16),
+            shaped(hidden_units, width, jnp.bfloat16),
+            shaped(1, hidden_units, jnp.float32),
+            shaped(8, width, jnp.float32),
+        ],
+        grid_spec=pltpu.PrefetchScalarGridSpec(
+            num_scalar_prefetch=1,
+            grid=(steps,),
+            in_specs=[whole, whole, scale, whole, scale, whole, whole, tile, tile, across, down]
+            + [square, whole_block((8, width))],
+            out_specs=[whole, halves, halves, square, across, down, line, whole_block((8, width))],
+            scratch_shapes=[
+                pltpu.VMEM((rows, width), jnp.float32),
+                pltpu.VMEM((rows, width), jnp.bfloat16),
+                pltpu.VMEM((rows, width), jnp.float32),
+            ],
+        ),
+        compiler_params=pltpu.CompilerParams(vmem_limit_bytes=48 * 2**20),
+        cost_estimate=pl.CostEstimate(
+            flops=2 * rows * width * (2 * width + 4 * hidden_units),
+            bytes_accessed=40 * 2**20,
+            transcendentals=0,
+        ),
+        name="tail_backward",
+    )(
+        me,
+        grad,
+        norm_two,
+        scale_two,
+        norm_one,
+        scale_one,
+        low,
+        mixed,
+        slope,
+        active,
+        expand,
+        reduce,
+        mixer,
+        vectors,
+    )
+
+
+def gather_all(local):
+    places, share, width = local.shape
+    gathered = lax.all_gather(local.reshape(-1, width), BOTH, axis=0, tiled=False)
+    return gathered.reshape(4, 8, places, share, width)
+
+
+def join_kernel(me, a_ref, b_ref, project_ref, small_ref):
+    half = a_ref.shape[-1]
+    for y_bit in range(GRP_Y):
+        y = y_bit ^ me[0]
+        for x_bit in range(SHARD_X):
+            for z_bits in range(SHARD_Z):
+                shard = (z_bits ^ me[3]) * SHARD_X + (x_bit ^ me[2])
+                project_ref[shard, y, :, :half] = a_ref[y_bit, x_bit, z_bits, 0]
+                project_ref[shard, y, :, half : 2 * half] = a_ref[y_bit, x_bit, z_bits, 1]
+                project_ref[shard, y, :, 2 * half :] = b_ref[x_bit, y_bit, z_bits, 0]
+                if y_bit == 0:
+                    small_ref[shard, :, :half] = b_ref[x_bit, y_bit, z_bits, 1, 0:8, :]
+                    small_ref[shard, :, half:] = b_ref[x_bit, y_bit, z_bits, 1, 8:16, :]
+
+
+def gather_first(me, local, rows):
+    part, half = local.shape[1:]
+    pair = jnp.stack([local, swap_z(local, 1)])
+    pair, rows = lax.optimization_barrier((pair, rows))
+    window = window_of(rows)
+    four = jnp.concatenate([pair, swap_z(pair, 2)])
+    a_part, b_part = four[:, :2], four[:, 2:]
+    a_two = jnp.stack([a_part, swap_x(a_part)])
+    b_two = jnp.stack([b_part, swap_y(b_part)])
+    a_four = jnp.stack([a_two, swap_y(a_two)])
+    b_four = jnp.stack([b_two, swap_x(b_two)])
+    project, small = pl.pallas_call(
+        join_kernel,
+        out_shape=[
+            jax.ShapeDtypeStruct((8, 2, part, 3 * half), local.dtype),
+            jax.ShapeDtypeStruct((8, 8, 2 * half), local.dtype),
+        ],
+        grid_spec=pltpu.PrefetchScalarGridSpec(
+            num_scalar_prefetch=1,
+            grid=(1,),
+            in_specs=[whole_block(a_four.shape)] * 2,
+            out_specs=[whole_block((8, 2, part, 3 * half)), whole_block((8, 8, 2 * half))],
+        ),
+        compiler_params=pltpu.CompilerParams(vmem_limit_bytes=24 * 2**20),
+        name="join_projection",
+    )(me, a_four, b_four)
+    return project.reshape(-1, 3 * half), small, four, rows, window
+
+
+def on_device_turned(
+    tokens,
+    cotangent,
+    seq_lengths,
+    seq_order,
+    w_project,
+    w_mixer,
+    w_expand,
+    w_reduce,
+    biases,
+    norm_gains,
+):
+    row_count, width = tokens.shape
+    shard_index = lax.axis_index("shard")
+    quarter = lax.axis_index("grp")
+    z, x = shard_index // SHARD_X, shard_index % SHARD_X
+    y, core = quarter // GRP_CORE, quarter % GRP_CORE
+    me = jnp.stack([y, core, x, z]).astype(jnp.int32)
+    hidden_units = w_expand.shape[2]
+    group_slots = row_count * 8
+    seq_count = seq_lengths.shape[1]
+    seq_ends = group_ends(seq_lengths, seq_order, y * GRP_CORE + x)
+    block_index = z * GRP_CORE + jnp.stack([core, 1 - core])
+    slot_index = block_index[:, None] * row_count + jnp.arange(row_count, dtype=jnp.int32)[None, :]
+    slot_index = slot_index.reshape(-1)
+    before_slot = seq_ends[None, :] <= slot_index[:, None]
+    own_segment = jnp.sum(before_slot[:row_count].astype(jnp.int32), axis=1, dtype=jnp.int32)
+    starts = jnp.max(jnp.where(before_slot, seq_ends[None, :], 0), axis=1)
+    stops = jnp.min(jnp.where(before_slot, group_slots, seq_ends[None, :]), axis=1)
+    window_begin = (z - 1) * GRP_CORE * row_count
+    low = starts - window_begin
+    high = stops - window_begin
+    low_line = jnp.broadcast_to(low[None, :], (8, 2 * row_count))
+    high_line = jnp.broadcast_to(high[None, :], (8, 2 * row_count))
+    places = [(1, 0, 2)[t // 2] + ((t % 2) ^ core) * 3 for t in range(6)]
+    bounds = jnp.stack(
+        [
+            low[0] // KEY_ROWS,
+            (high[row_count - 1] + KEY_ROWS - 1) // KEY_ROWS,
+            low[row_count] // KEY_ROWS,
+            (high[2 * row_count - 1] + KEY_ROWS - 1) // KEY_ROWS,
+        ]
+        + places
+    ).astype(jnp.int32)
+    valid_rows = (own_segment < seq_count).astype(jnp.float32)[:, None]
+
+    small = jnp.concatenate(
+        [jnp.concatenate([biases[i], norm_gains[i]]) for i in range(LAYERS)]
+    ).reshape(-1, width)
+    share = w_project.shape[1] // 4
+    deep = w_reduce.shape[1] // 4
+    bias_count = biases.shape[1]
+    small_rows = small.shape[0]
+    small = jnp.concatenate([small, jnp.zeros((8 - small_rows, width), small.dtype)])
+    near_first, far_first, far_last = pick_quarters(
+        me, w_project, w_mixer, w_expand, w_reduce, small
+    )
+    state_low = turn_rows(tokens)
+    state_grad = turn_rows(cotangent)
+    project_first, small_all, arrived, state_low, first_window = gather_first(
+        me, near_first, state_low
+    )
+    far_first, arrived = lax.optimization_barrier((far_first, arrived))
+    far_kinds = ("columns", "columns", "rows")
+    far_shapes = [(share, width), (share, hidden_units), (deep, width)]
+    far_count = far_last.shape[0]
+    pieces = gather_all(far_first)
+    first_whole = [project_first] + unpack_weights_of(pieces, 0, far_count, far_kinds, far_shapes)
+    project_last = unpack_weights_of(pieces, far_count, 3, ("columns",), [(share, 3 * width)])[0]
+    project_last = jnp.concatenate(
+        [half_of(project_last[:, i * width : (i + 1) * width], 1, core) for i in range(3)], axis=1
+    )
+    last_whole = [project_last] + unpack_weights_of(
+        gather_all(far_last), 0, far_count, far_kinds, far_shapes
+    )
+    small_all = small_all[:, :small_rows].reshape(8, LAYERS, -1)
+    weights = []
+    for layer_index, whole in enumerate([first_whole, last_whole]):
+        bias_vec = small_all[:, layer_index, :bias_count].reshape(-1)
+        gain_vec = small_all[:, layer_index, bias_count:].reshape(-1)
+        weights.append(unpack_weights(whole + [bias_vec, gain_vec], width, hidden_units))
+
+    hidden_state = state_low.astype(jnp.float32)
+    kept_list = []
+    for layer_index in range(LAYERS):
+        project, mixing, expand, shrink, bias_list, gain_one, gain_two = weights[layer_index]
+        bias_q, bias_v, bias_mix, shift_one, bias_in, bias_out, shift_two = bias_list
+        state_window = first_window if layer_index == 0 else window_of(state_low)
+        half = width // 2
+        far_begin = 3 * row_count
+        queries = [
+            (
+                jnp.dot(
+                    state_window[begin_at : begin_at + row_count],
+                    project[:, :half],
+                    preferred_element_type=jnp.float32,
+                )
+                + half_of(bias_q, 0, core)
+            ).astype(jnp.bfloat16)
+            for begin_at in (0, far_begin)
+        ]
+        key_value = (
+            jnp.dot(state_window, project[:, half:], preferred_element_type=jnp.float32)
+            + jnp.concatenate([jnp.zeros((half,), jnp.float32), half_of(bias_v, 0, core)])
+        ).astype(jnp.bfloat16)
+        own_mix, far_mix, own_wide, far_wide, lse = flash_forward(bounds, queries, key_value, low_line, high_line)
+        far_mix = swap_core(far_mix)
+        tail_vectors = jnp.stack(
+            [bias_mix, gain_one, shift_one, bias_out, gain_two, shift_two, bias_mix, bias_mix]
+        )
+        (
+            mixed_low,
+            norm_one,
+            scale_one,
+            normed_low,
+            active_low,
+            slope,
+            norm_two,
+            scale_two,
+            hidden_state,
+            next_low,
+        ) = tail_forward(
+            me, own_mix, far_mix, hidden_state, mixing, expand, shrink, bias_in[None], tail_vectors
+        )
+        kept_list.append(
+            (
+                state_low,
+                state_window,
+                queries,
+                key_value,
+                (own_wide, far_wide),
+                lse,
+                (norm_two, scale_two, norm_one, scale_one, normed_low, mixed_low, slope, active_low),
+                tail_vectors,
+            )
+        )
+        state_low = next_low
+    activations = turn_rows((hidden_state * valid_rows).astype(jnp.bfloat16))
+    state_grad = state_grad.astype(jnp.float32) * valid_rows
+    results = [None] * LAYERS
+    for layer_index in reversed(range(LAYERS)):
+        layer_low, state_window, queries, key_value, wides, lse, kept, tail_vectors = kept_list[
+            layer_index
+        ]
+        project, mixing, expand, shrink, *unused = weights[layer_index]
+        (
+            sum_one_grad,
+            own_mix_grad,
+            far_mix_grad,
+            mixing_grad,
+            expand_grad,
+            shrink_grad,
+            bias_in_grad,
+            vector_grads,
+        ) = tail_backward(me, state_grad, kept, (mixing, expand, shrink), tail_vectors)
+        bias_mix_grad, gain_one_grad, shift_one_grad, bias_out_grad, gain_two_grad, shift_two_grad = [
+            vector_grads[i] for i in range(6)
+        ]
+        mixed_grads = (own_mix_grad, swap_core(far_mix_grad))
+        own_grad, far_grad, key_value_grad = flash_backward(
+            bounds, queries, key_value, mixed_grads, wides, lse, low_line, high_line
+        )
+        query_term = jnp.einsum(
+            "td,te->de", layer_low, own_grad, preferred_element_type=jnp.float32
+        ) + jnp.einsum(
+            "td,te->de",
+            state_window[far_begin : far_begin + row_count],
+            far_grad,
+            preferred_element_type=jnp.float32,
+        )
+        key_value_term = jnp.einsum(
+            "td,te->de", state_window, key_value_grad, preferred_element_type=jnp.float32
+        )
+        bias_q_grad = jnp.sum(own_grad, axis=0, dtype=jnp.float32) + jnp.sum(
+            far_grad, axis=0, dtype=jnp.float32
+        )
+        bias_v_grad = jnp.sum(key_value_grad[:, half:], axis=0, dtype=jnp.float32)
+        window_grad = jnp.einsum(
+            "te,de->td", key_value_grad, project[:, half:], preferred_element_type=jnp.float32
+        )
+        own_part = jnp.einsum(
+            "te,de->td", own_grad, project[:, :half], preferred_element_type=jnp.float32
+        )
+        far_part = jnp.einsum(
+            "te,de->td", far_grad, project[:, :half], preferred_element_type=jnp.float32
+        )
+        near_terms = jnp.concatenate(
+            [window_grad[:row_count] + own_part, window_grad[row_count:far_begin]]
+        )
+        far_terms = jnp.concatenate(
+            [
+                window_grad[far_begin : far_begin + row_count] + far_part,
+                window_grad[far_begin + row_count :],
+            ]
+        )
+        state_grad = sum_one_grad + window_back(near_terms, far_terms, row_count)
+        zeros_two = jnp.zeros((2 * width,), jnp.float32)
+        vectors = jnp.concatenate(
+            [
+                zeros_two,
+                bias_mix_grad,
+                shift_one_grad,
+                bias_in_grad[0],
+                bias_out_grad,
+                shift_two_grad,
+            ]
+        ).reshape(8, -1)
+        gains = jnp.concatenate([gain_one_grad, gain_two_grad]).reshape(8, -1)
+        vectors = jnp.concatenate([vectors, gains], axis=1).astype(jnp.bfloat16)
+        vectors = vectors.reshape(8, 4, 1, -1).transpose(1, 0, 2, 3)
+        vectors = jnp.pad(vectors, ((0, 0), (0, 0), (0, 7), (0, width - vectors.shape[3])))
+        terms = (mixing_grad, expand_grad, shrink_grad)
+        pieces = pack_terms(terms, far_kinds, share, width, vectors)
+        fed = lax.psum_scatter(
+            pieces.reshape(32, -1, width), BOTH, scatter_dimension=0, tiled=True
+        ).reshape(-1, share, width)
+        lines = jnp.zeros((8 * bias_count,), jnp.float32)
+        lines = lax.dynamic_update_slice(lines, bias_q_grad, (core * half,))
+        lines = lax.dynamic_update_slice(lines, bias_v_grad, (width + core * half,))
+        lines = lines.reshape(8, 2, -1).transpose(1, 0, 2).astype(jnp.bfloat16)
+        lines = jnp.pad(lines, ((0, 0), (0, 0), (0, width - lines.shape[2])))
+        lines = jnp.pad(lines.reshape(2, 8, 2, half), ((0, 0), (0, 0), (0, 6), (0, 0)))
+        attended = scatter_terms(
+            me, query_term.astype(jnp.bfloat16), key_value_term.astype(jnp.bfloat16), lines
+        )
+        results[layer_index] = (gather_quarters(attended), gather_quarters(fed))
+    outs = finish_shares(me, results, hidden_units, deep)
+    quarter_len = (bias_count + norm_gains.shape[1]) // 4
+    vectors = outs[5][:, :, 0, :quarter_len].reshape(LAYERS, -1)
+    lines = outs[4][:, :, :2].reshape(LAYERS, GRP_Y, GRP_CORE, width)[..., : bias_count // 2]
+    lines = jnp.sum(lines, axis=2).reshape(LAYERS, bias_count)
+    input_grad = turn_rows(state_grad.astype(jnp.bfloat16)).astype(jnp.float32)
+    return (
+        activations,
+        input_grad,
+        outs[0],
+        outs[1],
+        outs[2],
+        outs[3],
+        vectors[:, :bias_count] + lines,
+        vectors[:, bias_count:],
+    )
+
+
 def solution(mesh):
     in_specs = (
         P(("grp", "shard"), None),
@@ -479,6 +1713,7 @@
         P(None, "shard"),
         P(None, "shard"),
     )
+    body = on_device_turned if mesh.shape["shard"] == 8 and mesh.shape["grp"] == 4 else on_device
     return jax.shard_map(
-        on_device, mesh=mesh, in_specs=in_specs, out_specs=out_specs, check_vma=False
-    )
+        body, mesh=mesh, in_specs=in_specs, out_specs=out_specs, check_vma=False
+    )

time: 1840 us -> 743 us (0.40)
  waiting for transfers between devices: 957 us -> 210 us
  matrix products: 316 us -> 57.7 us
  Pallas kernels: 0 us -> 202 us
  starting transfers between devices: 245 us -> 114 us
  blocking collectives: 78.9 us -> 0 us
  local copies, waits for them, and re-layouts: 135 us -> 91.9 us
  loops' own time: 20.4 us -> 0 us
  other arithmetic: 56.8 us -> 38.2 us
    reduce_scatter x6 -> x2, waiting for transfers between devices: 527 us -> 0.01 us  [on_device_turned(): lax.psum_scatter(pieces.reshape(32, -1, width), BOTH, scatter_dimension=0...]
    dot_general x60 -> x18, matrix products: 316 us -> 57.7 us  [the longest x2 17.6 us: on_device_turned(): jnp.einsum('td,te->de', state_window, key_value_grad, preferred_element_t...]
    pallas_call x0 -> x18, Pallas kernels: none -> 202 us  [the longest x2 69.3 us: flash_backward(): pl.pallas_call(flash_backward_kernel, out_shape=(jax.ShapeDtypeStruct((ro...]
    all_gather x8 -> x2, waiting for transfers between devices: 209 us -> 15.4 us  [gather_all(): lax.all_gather(local.reshape(-1, width), BOTH, axis=0, tiled=False)]
    ppermute x32 -> x46, starting transfers between devices: 244 us -> 114 us  [send(): return lax.ppermute(values, BOTH, device_pairs(place))]
    unnamed x2 -> x0, blocking collectives: 62.3 us -> none
    unnamed x19 -> x4, waiting for transfers between devices: 59.8 us -> 0.75 us
    ppermute x32 -> x46, waiting for transfers between devices: 135 us -> 193 us  [send(): return lax.ppermute(values, BOTH, device_pairs(place))]
  transfers between devices with their start and end apart: 49 -> 50, of which waited for: 26 -> 23; matrix products, arithmetic and copies ran while one was open for 20% -> 17% of each run, Pallas kernels for 0% -> 24%
where the time goes in v2:
time: 743 us; the launch traced here: 736 us
  waiting for transfers between devices  210 us (28%)
  Pallas kernels  202 us (27%)
  starting transfers between devices  114 us (15%)
  local copies, waits for them, and re-layouts  91.9 us (12%)
  matrix products  57.7 us (8%)
  other arithmetic  38.2 us (5%)
  between operations  22 us (3%)
    ppermute x46, waiting for transfers between devices, send(): return lax.ppermute(values, BOTH, device_pairs(place))  193 us
    ppermute x46, starting transfers between devices, send(): return lax.ppermute(values, BOTH, device_pairs(place))  114 us
    pallas_call x2, Pallas kernels, flash_backward(): pl.pallas_call(flash_backward_kernel, out_shape=(jax.ShapeDtypeStruct((ro...  69.3 us
    unnamed x188, local copies, waits for them, and re-layouts  58.7 us
    pallas_call x2, Pallas kernels, tail_backward(): pl.pallas_call(tail_backward_kernel, out_shape=[shaped(rows, width, jnp.f...  43.5 us
    pallas_call x2, Pallas kernels, flash_forward(): pl.pallas_call(flash_forward_kernel, out_shape=(jax.ShapeDtypeStruct((row...  34.3 us
    pallas_call x2, Pallas kernels, tail_forward(): pl.pallas_call(tail_forward_kernel, out_shape=[shaped(width, jnp.bfloat16...  30.3 us
    dot_general x2, matrix products, on_device_turned(): jnp.einsum('td,te->de', state_window, key_value_grad, preferred_element_t...  17.6 us
  transfers between devices with their start and end apart: 50, of which 23 were waited for; matrix products, arithmetic and copies ran while one was open for 17% of the time, Pallas kernels for 24%

profile of v2, /device:TPU:1, one launch (start us, length us, event | category | flops | bytes accessed | tf_op | source)
XLA Modules:
  0.0 736.0 jit_solution(11946091373283653808)
XLA Ops:
  7.2 4.5 collective-permute-start.1
  14.7 2.9 pick_quarters.1
  18.8 3.2 collective-permute-done
  23.1 2.8 collective-permute-start.2
  25.9 13.8 %collective-permute-done.2 = bf16[2,4,48,384]{3,2,1,0:T(8,128)(2,1)S(1)} collective-permute-done((bf16[2,4,48,384]{3,2,1,0:T(8,128)(2,1)S(1)}, bf16[2,4,48,384]{3,2,1,0:T(8,128)(2,1)S(1)}, u32[]{:S(2)}, u32[]{:S(2)}) %collective-permute-start.2) | collective-permute-done | bytes 294944 | tf_op jit(solution)/shard_map/ppermute | solution.py:805
  41.9 4.0 collective-permute-start.7
  47.2 23.4 %collective-permute-done.8 = bf16[512,768]{1,0:T(8,128)(2,1)S(1)} collective-permute-done((bf16[512,768]{1,0:T(8,128)(2,1)S(1)}, bf16[512,768]{1,0:T(8,128)(2,1)S(1)}, u32[]{:S(2)}, u32[]{:S(2)}) %collective-permute-start.8) | collective-permute-done | bytes 786464 | tf_op jit(solution)/shard_map/ppermute | solution.py:805
  84.6 6.2 collective-permute-done.3
  94.9 11.2 %collective-permute-done.4 = bf16[2,4,2,48,384]{4,3,2,1,0:T(8,128)(2,1)S(1)} collective-permute-done((bf16[2,4,2,48,384]{4,3,2,1,0:T(8,128)(2,1)S(1)}, bf16[2,4,2,48,384]{4,3,2,1,0:T(8,128)(2,1)S(1)}, u32[]{:S(2)}, u32[]{:S(2)}) %collective-permute-start.4) | collective-permute-done | bytes 589856 | tf_op jit(solution)/shard_map/ppermute | solution.py:805
  106.2 2.4 collective-permute-done.6
  110.7 2.8 fusion.10.b_ref
  116.0 4.1 add_convert_fusion.1.kv_ref
  120.1 17.0 %flash_forward.2 = (bf16[512,384]{1,0:T(8,128)(2,1)S(1)}, bf16[512,384]{1,0:T(8,128)(2,1)S(1)}, f32[512,384]{1,0:T(8,128)S(1)}, f32[512,384]{1,0:T(8,128)S(1)}, f32[24,1024]{1,0:T(8,128)S(1)}) custom-call(s32[10]{0:T(128)S(1)} %stack.229.bounds, bf16[512,384]{1,0:T(8,128)(2,1)S(1)} %fusion.9.a_ref, bf16[512,384]{1,0:T(8,128)(2,1)S(1)} %fusion.10.b_ref, ...), custom_call_target="tpu_custom_call" | custom-call | flops 4026531840 | bytes 12582912 | tf_op jit(solution)/shard_map/flash_forward/pallas_call | solution.py:720
  142.3 15.4 %all-gather.3.cloned.1.call-done = bf16[32,288,768]{2,1,0:T(8,128)(2,1)} async-done(((bf16[1,288,768]{2,1,0:T(8,128)(2,1)}), bf16[32,288,768]{2,1,0:T(8,128)(2,1)}) %all-gather.3.cloned.1.call-update) | async-done | bytes 14155792 | tf_op jit(solution)/shard_map/all_gather | solution.py:1401
  157.7 5.3 unpack_weights.3
  167.4 15.1 %tail_forward.2 = (bf16[512,768]{1,0:T(8,128)(2,1)S(1)}, f32[512,768]{1,0:T(8,128)S(1)}, f32[512,128]{1,0:T(8,128)S(1)}, bf16[512,768]{1,0:T(8,128)(2,1)S(1)}, b...) custom-call(s32[4]{0:T(128)S(1)} %copy-done.12, ...), custom_call_target="tpu_custom_call" | custom-call | flops 5435817984 | bytes 33554432 | tf_op jit(solution)/shard_map/tail_forward/pallas_call | solution.py:1218
  186.2 4.0 collective-permute-start.11
  190.2 29.4 %collective-permute-done.12 = bf16[512,768]{1,0:T(8,128)(2,1)S(1)} collective-permute-done((bf16[512,768]{1,0:T(8,128)(2,1)S(1)}, bf16[512,768]{1,0:T(8,128)(2,1)S(1)}, u32[]{:S(2)}, u32[]{:S(2)}) %collective-permute-start.12) | collective-permute-done | bytes 786464 | tf_op jit(solution)/shard_map/ppermute | solution.py:805
  221.9 3.0 collective-permute-start.16
  225.8 5.1 copy-done
  237.6 4.1 add_convert_fusion.kv_ref
  241.7 17.3 %flash_forward.3 = (bf16[512,384]{1,0:T(8,128)(2,1)S(1)}, bf16[512,384]{1,0:T(8,128)(2,1)S(1)}, f32[512,384]{1,0:T(8,128)S(1)}, f32[512,384]{1,0:T(8,128)S(1)}, f32[24,1024]{1,0:T(8,128)S(1)}) custom-call(s32[10]{0:T(128)S(1)} %stack.229.bounds, bf16[512,384]{1,0:T(8,128)(2,1)S(1)} %fusion.11.a_ref, bf16[512,384]{1,0:T(8,128)(2,1)S(1)} %fusion.12.b_ref, ...), custom_call_target="tpu_custom_call" | custom-call | flops 4026531840 | bytes 12582912 | tf_op jit(solution)/shard_map/flash_forward/pallas_call | solution.py:720
  261.4 4.5 collective-permute-start.14
  268.6 4.0 copy-done.3
  278.4 15.2 %tail_forward.3 = (bf16[512,768]{1,0:T(8,128)(2,1)S(1)}, f32[512,768]{1,0:T(8,128)S(1)}, f32[512,128]{1,0:T(8,128)S(1)}, bf16[512,768]{1,0:T(8,128)(2,1)S(1)}, b...) custom-call(s32[4]{0:T(128)S(1)} %copy-done.12, ...), custom_call_target="tpu_custom_call" | custom-call | flops 5435817984 | bytes 33554432 | tf_op jit(solution)/shard_map/tail_forward/pallas_call | solution.py:1218
  293.6 3.4 convert_multiply_fusion
  297.0 21.5 %tail_backward.2 = (f32[512,768]{1,0:T(8,128)}, bf16[512,384]{1,0:T(8,128)(2,1)S(1)}, bf16[512,384]{1,0:T(8,128)(2,1)S(1)}, bf16[768,768]{1,0:T(8,128)(2,1)S(1)}...) custom-call(s32[4]{0:T(128)S(1)} %copy-done.12, ...), custom_call_target="tpu_custom_call" | custom-call | flops 10871635968 | bytes 41943040 | tf_op jit(solution)/shard_map/tail_backward/pallas_call | solution.py:1350
  321.6 2.3 copy-done.6
  323.9 2.3 copy-done.7
  327.9 4.3 copy-done.1
  335.6 34.4 %flash_backward.2 = (bf16[512,384]{1,0:T(8,128)(2,1)}, bf16[512,384]{1,0:T(8,128)(2,1)}, bf16[3072,768]{1,0:T(8,128)(2,1)}) custom-call(s32[10]{0:T(128)} %copy-done.14, bf16[512,384]{1,0:T(8,128)(2,1)} %copy-done.23, bf16[512,384]{1,0:T(8,128)(2,1)} %copy-done.25, bf16[3072,768]{1,0:T(8,128)(2,1)} %copy-done.32, bf16[512,384]{1,0:T(8,128)(2,1)} %copy-done.43, ...), custom_call_target="tpu_custom_call" | custom-call | flops 10066329600 | bytes 20971520 | tf_op jit(solution)/shard_map/flash_backward/pallas_call | solution.py:754
  370.0 6.0 fusion.16
  379.8 3.5 collective-permute-done.18
  383.3 2.7 fusion.77
  387.2 17.4 %collective-permute-start.20 = (bf16[512,768]{1,0:T(8,128)(2,1)}, bf16[512,768]{1,0:T(8,128)(2,1)S(1)}, u32[]{:S(2)}, u32[]{:S(2)}) collective-permute-start(bf16[512,768]{1,0:T(8,128)(2,1)} %get-tuple-element.196), channel_id=1, source_target_pairs={{0,2},{1,3},{2,4},{3,5},{4,6},{5,7},{8,10},{9,11},{10,12},{11,13},... | collective-permute-start | bytes 2359304 | tf_op jit(solution)/shard_map/ppermute | solution.py:805
  406.3 32.6 %collective-permute-done.20 = bf16[512,768]{1,0:T(8,128)(2,1)S(1)} collective-permute-done((bf16[512,768]{1,0:T(8,128)(2,1)}, bf16[512,768]{1,0:T(8,128)(2,1)S(1)}, u32[]{:S(2)}, u32[]{:S(2)}) %collective-permute-start.20) | collective-permute-done | bytes 786464 | tf_op jit(solution)/shard_map/ppermute | solution.py:805
  438.9 7.7 %collective-permute-done.19 = bf16[512,768]{1,0:T(8,128)(2,1)} collective-permute-done((bf16[512,768]{1,0:T(8,128)(2,1)}, bf16[512,768]{1,0:T(8,128)(2,1)}, u32[]{:S(2)}, u32[]{:S(2)}) %collective-permute-start.19) | collective-permute-done | bytes 786464 | tf_op jit(solution)/shard_map/ppermute | solution.py:805
  446.6 3.6 fusion.5.grad_ref
  450.2 22.0 %tail_backward.3 = (f32[512,768]{1,0:T(8,128)}, bf16[512,384]{1,0:T(8,128)(2,1)S(1)}, bf16[512,384]{1,0:T(8,128)(2,1)S(1)}, bf16[768,768]{1,0:T(8,128)(2,1)S(1)}...) custom-call(s32[4]{0:T(128)S(1)} %copy-done.12, ...), custom_call_target="tpu_custom_call" | custom-call | flops 10871635968 | bytes 41943040 | tf_op jit(solution)/shard_map/tail_backward/pallas_call | solution.py:1350
  475.3 2.3 copy-done.4
  477.6 2.5 copy-done.5
  481.7 4.2 copy-done.2
  494.1 8.7 %convolution_convert_fusion = bf16[768,768]{1,0:T(8,128)(2,1)} fusion(bf16[3072,768]{1,0:T(8,128)(2,1)} %copy-done.72, bf16[3072,768]{1,0:T(8,128)(2,1)} %get-tuple-element.114), kind=kOutput, calls=%fused_computation.27 | convolution fusion | flops 3624468480 | bytes 10616832 | tf_op jit(solution)/shard_map/td,te->de/dot_general | solution.py:1619
  502.8 3.5 spread_terms.3
  512.2 11.3 %collective-permute-done.36 = bf16[2,4,2,48,384]{4,3,2,1,0:T(8,128)(2,1)S(1)} collective-permute-done((bf16[2,4,2,48,384]{4,3,2,1,0:T(8,128)(2,1)S(1)}, bf16[2,4,2,48,384]{4,3,2,1,0:T(8,128)(2,1)S(1)}, u32[]{:S(2)}, u32[]{:S(2)}) %collective-permute-start.36) | collective-permute-done | bytes 589856 | tf_op jit(solution)/shard_map/ppermute | solution.py:805
  527.6 34.9 %flash_backward.3 = (bf16[512,384]{1,0:T(8,128)(2,1)}, bf16[512,384]{1,0:T(8,128)(2,1)}, bf16[3072,768]{1,0:T(8,128)(2,1)}) custom-call(s32[10]{0:T(128)} %copy-done.14, bf16[512,384]{1,0:T(8,128)(2,1)} %copy-done.24, bf16[512,384]{1,0:T(8,128)(2,1)} %copy-done.26, bf16[3072,768]{1,0:T(8,128)(2,1)} %copy-done.37, bf16[512,384]{1,0:T(8,128)(2,1)} %copy-done.42, ...), custom_call_target="tpu_custom_call" | custom-call | flops 10066329600 | bytes 20971520 | tf_op jit(solution)/shard_map/flash_backward/pallas_call | solution.py:754
  562.5 8.7 %fusion.13 = f32[3072,768]{1,0:T(8,128)} fusion(bf16[3072,768]{1,0:T(8,128)(2,1)} %get-tuple-element.131, bf16[768,1152]{1,0:T(8,128)(2,1)S(1)} %bitcast.247), kind=kOutput, calls=%fused_computation.46 | convolution fusion | flops 3623878656 | bytes 15335424 | tf_op jit(solution)/shard_map/te,de->td/dot_general | solution.py:1626
  577.2 2.3 collective-permute-start.22
  583.3 8.9 %convolution_convert_fusion.1 = bf16[768,768]{1,0:T(8,128)(2,1)} fusion(bf16[3072,768]{1,0:T(8,128)(2,1)} %copy-done.75, bf16[3072,768]{1,0:T(8,128)(2,1)} %get-tuple-element.131), kind=kOutput, calls=%fused_computation.28 | convolution fusion | flops 3624468480 | bytes 10616832 | tf_op jit(solution)/shard_map/td,te->de/dot_general | solution.py:1619
  593.6 3.4 spread_terms.2
  599.3 6.2 collective-permute-start.27
  609.7 9.6 %collective-permute-start.40 = (bf16[2,4,48,384]{3,2,1,0:T(8,128)(2,1)S(1)}, bf16[2,4,48,384]{3,2,1,0:T(8,128)(2,1)S(1)}, u32[]{:S(2)}, u32[]{:S(2)}) collective-permute-start(bf16[2,4,48,384]{3,2,1,0:T(8,128)(2,1)S(1)} %get-tuple-element.198), channel_id=1, source_target_pairs={{0,4},{1,5},{2,6},{3,7},{4,0},{5,1},{6,2},{7,3},{8,12},{9,13},{10,... | collective-permute-start | bytes 884744 | tf_op jit(solution)/shard_map/ppermute | solution.py:805
  619.3 3.8 slice.527
  623.3 5.6 collective-permute-start.28
  632.4 6.3 collective-permute-done.28
  640.5 8.1 %collective-permute-start.30 = (bf16[2,4,48,384]{3,2,1,0:T(8,128)(2,1)S(1)}, bf16[2,4,48,384]{3,2,1,0:T(8,128)(2,1)S(1)}, u32[]{:S(2)}, u32[]{:S(2)}) collective-permute-start(bf16[2,4,48,384]{3,2,1,0:T(8,128)(2,1)S(1)} %get-tuple-element.200), channel_id=1, source_target_pairs={{0,4},{1,5},{2,6},{3,7},{4,0},{5,1},{6,2},{7,3},{8,12},{9,13},{10,... | collective-permute-start | bytes 884744 | tf_op jit(solution)/shard_map/ppermute | solution.py:805
  648.6 5.3 fusion.76
  654.9 3.5 collective-permute-start.24
  661.9 2.8 collective-permute-start.31
  664.7 25.4 %collective-permute-done.41 = bf16[4,48,384]{2,1,0:T(8,128)(2,1)S(1)} collective-permute-done((bf16[4,48,384]{2,1,0:T(8,128)(2,1)S(1)}, bf16[4,48,384]{2,1,0:T(8,128)(2,1)S(1)}, u32[]{:S(2)}, u32[]{:S(2)}) %collective-permute-start.41) | collective-permute-done | bytes 147488 | tf_op jit(solution)/shard_map/ppermute | solution.py:805
  699.5 3.5 collective-permute-done.44
  703.0 5.7 collective-permute-start.25
  708.8 5.2 collective-permute-done.34
  721.9 3.8 finish_shares.1
  (425 shorter events, 144.5 us)
Async XLA Ops:
  7.2 150.6 %all-gather.3.cloned.1.call-start = ((), (), s32[]{:S(2)}) async-start(), calls=%async_computation.2 | async-start | bytes 14598144 | tf_op jit(solution)/shard_map/all_gather | solution.py:1401
  7.2 15.8 %collective-permute-start.1 = (bf16[512,768]{1,0:T(8,128)(2,1)}, bf16[512,768]{1,0:T(8,128)(2,1)S(1)}, u32[]{:S(2)}, u32[]{:S(2)}) collective-permute-start(bf16[512,768]{1,0:T(8,128)(2,1)} %param.10), channel_id=1, source_target_pairs={{0,0},{1,8},{2,2},{3,10},{4,4},{5,12},{6,6},{7,14},{8,1},{9,9},{10... | collective-permute-start | bytes 2359304 | tf_op jit(solution)/shard_map/ppermute | solution.py:805
  17.6 4.5 collective-permute-start
  23.1 87.0 %copy-start.52 = (bf16[512,768]{1,0:T(8,128)(2,1)}, bf16[512,768]{1,0:T(8,128)(2,1)S(1)}, u32[]{:S(2)}) copy-start(bf16[512,768]{1,0:T(8,128)(2,1)S(1)} %collective-permute-done.1) | copy-start | bytes 2359300
  23.1 16.6 %collective-permute-start.2 = (bf16[2,4,48,384]{3,2,1,0:T(8,128)(2,1)S(1)}, bf16[2,4,48,384]{3,2,1,0:T(8,128)(2,1)S(1)}, u32[]{:S(2)}, u32[]{:S(2)}) collective-permute-start(bf16[2,4,48,384]{3,2,1,0:T(8,128)(2,1)S(1)} %pad_maximum_fusion.19), channel_id=1, source_target_pairs={{0,4},{1,5},{2,6},{3,7},{4,0},{5,1},{6,2},{7,3},{8,12},{9,13},{10,... | collective-permute-start | bytes 884744 | tf_op jit(solution)/shard_map/ppermute | solution.py:805
  39.7 228.9 %all-gather.5.cloned.1.call-start = ((), (), s32[]{:S(2)}) async-start(), calls=%async_computation.3 | async-start | bytes 10948608 | tf_op jit(solution)/shard_map/all_gather | solution.py:1401
  40.5 652.9 %reduce-scatter.5.cloned.1.call-start = ((), (), s32[]{:S(2)}) async-start(), calls=%async_computation.5 | async-start | bytes 12165120 | tf_op jit(solution)/shard_map/reduce_scatter | solution.py:1662
  40.6 30.0 %collective-permute-start.8 = (bf16[512,768]{1,0:T(8,128)(2,1)S(1)}, bf16[512,768]{1,0:T(8,128)(2,1)S(1)}, u32[]{:S(2)}, u32[]{:S(2)}) collective-permute-start(bf16[512,768]{1,0:T(8,128)(2,1)S(1)} %collective-permute-done.1), channel_id=1, source_target_pairs={{2,0},{3,1},{4,2},{5,3},{6,4},{7,5},{10,8},{11,9},{12,10},{13,11},... | collective-permute-start | bytes 2359304 | tf_op jit(solution)/shard_map/ppermute | solution.py:805
  41.9 29.5 %collective-permute-start.7 = (bf16[512,768]{1,0:T(8,128)(2,1)S(1)}, bf16[512,768]{1,0:T(8,128)(2,1)S(1)}, u32[]{:S(2)}, u32[]{:S(2)}) collective-permute-start(bf16[512,768]{1,0:T(8,128)(2,1)S(1)} %collective-permute-done.1), channel_id=1, source_target_pairs={{0,2},{1,3},{2,4},{3,5},{4,6},{5,7},{8,10},{9,11},{10,12},{11,13},... | collective-permute-start | bytes 2359304 | tf_op jit(solution)/shard_map/ppermute | solution.py:805
  47.1 25.9 %copy-start.78 = (s32[8,1]{0,1:T(1,128)}, s32[8,1]{0,1:T(1,128)S(1)}, u32[]{:S(2)}) copy-start(s32[8,1]{0,1:T(1,128)S(1)} %reduce-window.8) | copy-start | bytes 100
  73.0 37.6 %collective-permute-start.9 = (bf16[1536,768]{1,0:T(8,128)(2,1)}, bf16[1536,768]{1,0:T(8,128)(2,1)}, u32[]{:S(2)}, u32[]{:S(2)}) collective-permute-start(bf16[1536,768]{1,0:T(8,128)(2,1)} %pad_maximum_fusion), channel_id=1, source_target_pairs={{0,8},{1,9},{2,10},{3,11},{4,12},{5,13},{6,14},{7,15},{8,0},{9,1},... | collective-permute-start | bytes 7077896 | tf_op jit(solution)/shard_map/ppermute | solution.py:805
  75.6 15.1 %collective-permute-start.3 = (bf16[4,2,48,384]{3,2,1,0:T(8,128)(2,1)}, bf16[4,2,48,384]{3,2,1,0:T(8,128)(2,1)S(1)}, u32[]{:S(2)}, u32[]{:S(2)}) collective-permute-start(bf16[4,2,48,384]{3,2,1,0:T(8,128)(2,1)} %get-tuple-element.212), channel_id=1, source_target_pairs={{0,1},{1,0},{2,3},{3,2},{4,5},{5,4},{6,7},{7,6},{8,9},{9,8},{10,11... | collective-permute-start | bytes 884744 | tf_op jit(solution)/shard_map/ppermute | solution.py:805
  75.7 17.3 %collective-permute-start.5 = (bf16[4,2,48,384]{3,2,1,0:T(8,128)(2,1)}, bf16[4,2,48,384]{3,2,1,0:T(8,128)(2,1)S(1)}, u32[]{:S(2)}, u32[]{:S(2)}) collective-permute-start(bf16[4,2,48,384]{3,2,1,0:T(8,128)(2,1)} %get-tuple-element.211), channel_id=1, source_target_pairs={{0,16},{1,17},{2,18},{3,19},{4,20},{5,21},{6,22},{7,23},{8,24},{9,... | collective-permute-start | bytes 884744 | tf_op jit(solution)/shard_map/ppermute | solution.py:805
  84.6 157.0 %copy-start.14 = (s32[10]{0:T(128)}, s32[10]{0:T(128)S(1)}, u32[]{:S(2)}) copy-start(s32[10]{0:T(128)S(1)} %stack.229.bounds) | copy-start | bytes 124
  91.8 14.3 %collective-permute-start.4 = (bf16[2,4,2,48,384]{4,3,2,1,0:T(8,128)(2,1)S(1)}, bf16[2,4,2,48,384]{4,3,2,1,0:T(8,128)(2,1)S(1)}, u32[]{:S(2)}, u32[]{:S(2)}) collective-permute-start(bf16[2,4,2,48,384]{4,3,2,1,0:T(8,128)(2,1)S(1)} %get-tuple-element.214), channel_id=1, source_target_pairs={{0,16},{1,17},{2,18},{3,19},{4,20},{5,21},{6,22},{7,23},{8,24},{9,... | collective-permute-start | bytes 1769480 | tf_op jit(solution)/shard_map/ppermute | solution.py:805
  93.1 15.6 %collective-permute-start.6 = (bf16[2,4,2,48,384]{4,3,2,1,0:T(8,128)(2,1)S(1)}, bf16[2,4,2,48,384]{4,3,2,1,0:T(8,128)(2,1)S(1)}, u32[]{:S(2)}, u32[]{:S(2)}) collective-permute-start(bf16[2,4,2,48,384]{4,3,2,1,0:T(8,128)(2,1)S(1)} %get-tuple-element.208), channel_id=1, source_target_pairs={{0,1},{1,0},{2,3},{3,2},{4,5},{5,4},{6,7},{7,6},{8,9},{9,8},{10,11... | collective-permute-start | bytes 1769480 | tf_op jit(solution)/shard_map/ppermute | solution.py:805
  120.1 121.6 %copy-start.10 = (s32[8,1024]{1,0:T(8,128)}, s32[8,1024]{1,0:T(8,128)S(1)}, u32[]{:S(2)}) copy-start(s32[8,1024]{1,0:T(8,128)S(1)} %broadcast_in_dim.47.low_ref) | copy-start | bytes 98308
  120.1 121.5 %copy-start.11 = (s32[8,1024]{1,0:T(8,128)}, s32[8,1024]{1,0:T(8,128)S(1)}, u32[]{:S(2)}) copy-start(s32[8,1024]{1,0:T(8,128)S(1)} %broadcast_in_dim.48.high_ref) | copy-start | bytes 98308
  139.7 23.2 %copy-start.48 = (f32[24,1024]{1,0:T(8,128)}, f32[24,1024]{1,0:T(8,128)S(1)}, u32[]{:S(2)}) copy-start(f32[24,1024]{1,0:T(8,128)S(1)} %get-tuple-element.130.lse_ref) | copy-start | bytes 294916
  139.7 27.6 %collective-permute-start.10 = (bf16[512,384]{1,0:T(8,128)(2,1)S(1)}, bf16[512,384]{1,0:T(8,128)(2,1)S(1)}, u32[]{:S(2)}, u32[]{:S(2)}) collective-permute-start(bf16[512,384]{1,0:T(8,128)(2,1)S(1)} %get-tuple-element.85), channel_id=1, source_target_pairs={{0,8},{1,9},{2,10},{3,11},{4,12},{5,13},{6,14},{7,15},{8,0},{9,1},... | collective-permute-start | bytes 1179656 | tf_op jit(solution)/shard_map/ppermute | solution.py:805
  184.9 36.4 %copy-start.27 = (f32[512,768]{1,0:T(8,128)}, f32[512,768]{1,0:T(8,128)S(1)}, u32[]{:S(2)}) copy-start(f32[512,768]{1,0:T(8,128)S(1)} %get-tuple-element.119.norm_one_ref) | copy-start | bytes 4718596
  184.9 36.4 %copy-start.28 = (f32[512,768]{1,0:T(8,128)}, f32[512,768]{1,0:T(8,128)S(1)}, u32[]{:S(2)}) copy-start(f32[512,768]{1,0:T(8,128)S(1)} %get-tuple-element.117.norm_two_ref) | copy-start | bytes 4718596
  184.9 36.4 %copy-start.29 = (f32[512,768]{1,0:T(8,128)}, f32[512,768]{1,0:T(8,128)S(1)}, u32[]{:S(2)}) copy-start(f32[512,768]{1,0:T(8,128)S(1)} %get-tuple-element.94.state_ref) | copy-start | bytes 4718596
  184.9 34.7 %collective-permute-start.12 = (bf16[512,768]{1,0:T(8,128)(2,1)S(1)}, bf16[512,768]{1,0:T(8,128)(2,1)S(1)}, u32[]{:S(2)}, u32[]{:S(2)}) collective-permute-start(bf16[512,768]{1,0:T(8,128)(2,1)S(1)} %get-tuple-element.91), channel_id=1, source_target_pairs={{2,0},{3,1},{4,2},{5,3},{6,4},{7,5},{10,8},{11,9},{12,10},{13,11},... | collective-permute-start | bytes 2359304 | tf_op jit(solution)/shard_map/ppermute | solution.py:805
  186.2 33.4 %collective-permute-start.11 = (bf16[512,768]{1,0:T(8,128)(2,1)S(1)}, bf16[512,768]{1,0:T(8,128)(2,1)S(1)}, u32[]{:S(2)}, u32[]{:S(2)}) collective-permute-start(bf16[512,768]{1,0:T(8,128)(2,1)S(1)} %get-tuple-element.91), channel_id=1, source_target_pairs={{0,2},{1,3},{2,4},{3,5},{4,6},{5,7},{8,10},{9,11},{10,12},{11,13},... | collective-permute-start | bytes 2359304 | tf_op jit(solution)/shard_map/ppermute | solution.py:805
  221.3 12.5 %collective-permute-start.13 = (bf16[1536,768]{1,0:T(8,128)(2,1)}, bf16[1536,768]{1,0:T(8,128)(2,1)}, u32[]{:S(2)}, u32[]{:S(2)}) collective-permute-start(bf16[1536,768]{1,0:T(8,128)(2,1)} %pad_maximum_fusion.1), channel_id=1, source_target_pairs={{0,8},{1,9},{2,10},{3,11},{4,12},{5,13},{6,14},{7,15},{8,0},{9,1},... | collective-permute-start | bytes 7077896 | tf_op jit(solution)/shard_map/ppermute | solution.py:805
  221.9 71.6 %collective-permute-start.16 = (bf16[512,768]{1,0:T(8,128)(2,1)}, bf16[512,768]{1,0:T(8,128)(2,1)}, u32[]{:S(2)}, u32[]{:S(2)}) collective-permute-start(bf16[512,768]{1,0:T(8,128)(2,1)} %param.11), channel_id=1, source_target_pairs={{0,0},{1,8},{2,2},{3,10},{4,4},{5,12},{6,6},{7,14},{8,1},{9,9},{10... | collective-permute-start | bytes 2359304 | tf_op jit(solution)/shard_map/ppermute | solution.py:805
  241.7 24.2 %copy-start.79 = (s32[8,1]{0,1:T(1,128)S(1)}, s32[8,1]{0,1:T(1,128)}, u32[]{:S(2)}) copy-start(s32[8,1]{0,1:T(1,128)} %copy-done.78) | copy-start | bytes 100
  261.4 17.0 %collective-permute-start.14 = (bf16[512,384]{1,0:T(8,128)(2,1)S(1)}, bf16[512,384]{1,0:T(8,128)(2,1)S(1)}, u32[]{:S(2)}, u32[]{:S(2)}) collective-permute-start(bf16[512,384]{1,0:T(8,128)(2,1)S(1)} %get-tuple-element.93), channel_id=1, source_target_pairs={{0,8},{1,9},{2,10},{3,11},{4,12},{5,13},{6,14},{7,15},{8,0},{9,1},... | collective-permute-start | bytes 1179656 | tf_op jit(solution)/shard_map/ppermute | solution.py:805
  332.2 363.8 %reduce-scatter.3.cloned.1.call-start = ((), (), s32[]{:S(2)}) async-start(), calls=%async_computation.4 | async-start | bytes 12165120 | tf_op jit(solution)/shard_map/reduce_scatter | solution.py:1662
  333.1 1.7 collective-permute-start.17
  335.6 34.4 %copy-start.66 = (bf16[768,384]{1,0:T(8,128)(2,1)S(1)}, bf16[768,384]{1,0:T(8,128)(2,1)}, u32[]{:S(2)}) copy-start(bf16[768,384]{1,0:T(8,128)(2,1)} %copy-done.65) | copy-start | bytes 1769476
  335.6 34.4 %copy-start.68 = (bf16[768,384]{1,0:T(8,128)(2,1)S(1)}, bf16[768,384]{1,0:T(8,128)(2,1)}, u32[]{:S(2)}) copy-start(bf16[768,384]{1,0:T(8,128)(2,1)} %copy-done.67) | copy-start | bytes 1769476
  378.2 5.1 collective-permute-start.18
  387.2 51.7 %collective-permute-start.20 = (bf16[512,768]{1,0:T(8,128)(2,1)}, bf16[512,768]{1,0:T(8,128)(2,1)S(1)}, u32[]{:S(2)}, u32[]{:S(2)}) collective-permute-start(bf16[512,768]{1,0:T(8,128)(2,1)} %get-tuple-element.196), channel_id=1, source_target_pairs={{0,2},{1,3},{2,4},{3,5},{4,6},{5,7},{8,10},{9,11},{10,12},{11,13},... | collective-permute-start | bytes 2359304 | tf_op jit(solution)/shard_map/ppermute | solution.py:805
  404.6 41.9 %collective-permute-start.19 = (bf16[512,768]{1,0:T(8,128)(2,1)}, bf16[512,768]{1,0:T(8,128)(2,1)}, u32[]{:S(2)}, u32[]{:S(2)}) collective-permute-start(bf16[512,768]{1,0:T(8,128)(2,1)} %get-tuple-element.195), channel_id=1, source_target_pairs={{2,0},{3,1},{4,2},{5,3},{6,4},{7,5},{10,8},{11,9},{12,10},{13,11},... | collective-permute-start | bytes 2359304 | tf_op jit(solution)/shard_map/ppermute | solution.py:805
  508.7 14.8 %collective-permute-start.36 = (bf16[2,4,2,48,384]{4,3,2,1,0:T(8,128)(2,1)S(1)}, bf16[2,4,2,48,384]{4,3,2,1,0:T(8,128)(2,1)S(1)}, u32[]{:S(2)}, u32[]{:S(2)}) collective-permute-start(bf16[2,4,2,48,384]{4,3,2,1,0:T(8,128)(2,1)S(1)} %slice_bitcast_fusion.1), channel_id=1, source_target_pairs={{0,16},{1,17},{2,18},{3,19},{4,20},{5,21},{6,22},{7,23},{8,24},{9,... | collective-permute-start | bytes 1769480 | tf_op jit(solution)/shard_map/ppermute | solution.py:805
  510.1 14.3 %collective-permute-start.37 = (bf16[2,4,2,48,384]{4,3,2,1,0:T(8,128)(2,1)S(1)}, bf16[2,4,2,48,384]{4,3,2,1,0:T(8,128)(2,1)S(1)}, u32[]{:S(2)}, u32[]{:S(2)}) collective-permute-start(bf16[2,4,2,48,384]{4,3,2,1,0:T(8,128)(2,1)S(1)} %slice_bitcast_fusion), channel_id=1, source_target_pairs={{0,1},{1,0},{2,3},{3,2},{4,5},{5,4},{6,7},{7,6},{8,9},{9,8},{10,11... | collective-permute-start | bytes 1769480 | tf_op jit(solution)/shard_map/ppermute | solution.py:805
  511.1 15.7 %collective-permute-start.21 = (bf16[512,384]{1,0:T(8,128)(2,1)S(1)}, bf16[512,384]{1,0:T(8,128)(2,1)S(1)}, u32[]{:S(2)}, u32[]{:S(2)}) collective-permute-start(bf16[512,384]{1,0:T(8,128)(2,1)S(1)} %copy-done.20), channel_id=1, source_target_pairs={{0,8},{1,9},{2,10},{3,11},{4,12},{5,13},{6,14},{7,15},{8,0},{9,1},... | collective-permute-start | bytes 1179656 | tf_op jit(solution)/shard_map/ppermute | solution.py:805
  525.4 80.1 %collective-permute-start.38 = (bf16[4,2,48,384]{3,2,1,0:T(8,128)(2,1)}, bf16[4,2,48,384]{3,2,1,0:T(8,128)(2,1)}, u32[]{:S(2)}, u32[]{:S(2)}) collective-permute-start(bf16[4,2,48,384]{3,2,1,0:T(8,128)(2,1)} %get-tuple-element.182), channel_id=1, source_target_pairs={{0,1},{1,0},{2,3},{3,2},{4,5},{5,4},{6,7},{7,6},{8,9},{9,8},{10,11... | collective-permute-start | bytes 884744 | tf_op jit(solution)/shard_map/ppermute | solution.py:805
  526.2 82.3 %collective-permute-start.39 = (bf16[4,2,48,384]{3,2,1,0:T(8,128)(2,1)S(1)}, bf16[4,2,48,384]{3,2,1,0:T(8,128)(2,1)}, u32[]{:S(2)}, u32[]{:S(2)}) collective-permute-start(bf16[4,2,48,384]{3,2,1,0:T(8,128)(2,1)S(1)} %get-tuple-element.189), channel_id=1, source_target_pairs={{0,16},{1,17},{2,18},{3,19},{4,20},{5,21},{6,22},{7,23},{8,24},{9,... | collective-permute-start | bytes 884744 | tf_op jit(solution)/shard_map/ppermute | solution.py:805
  527.6 35.0 %copy-start.9 = (bf16[8,2,48,1152]{3,2,1,0:T(8,128)(2,1)S(1)}, bf16[8,2,48,1152]{3,2,1,0:T(8,128)(2,1)}, u32[]{:S(2)}) copy-start(bf16[8,2,48,1152]{3,2,1,0:T(8,128)(2,1)} %copy-done.8) | copy-start | bytes 5308420
  577.2 71.4 %collective-permute-start.22 = (bf16[1536,768]{1,0:T(8,128)(2,1)}, bf16[1536,768]{1,0:T(8,128)(2,1)}, u32[]{:S(2)}, u32[]{:S(2)}) collective-permute-start(bf16[1536,768]{1,0:T(8,128)(2,1)} %pad_maximum_fusion.3), channel_id=1, source_target_pairs={{0,8},{1,9},{2,10},{3,11},{4,12},{5,13},{6,14},{7,15},{8,0},{9,1},... | collective-permute-start | bytes 7077896 | tf_op jit(solution)/shard_map/ppermute | solution.py:805
  599.2 23.8 %collective-permute-start.26 = (bf16[2,4,2,48,384]{4,3,2,1,0:T(8,128)(2,1)S(1)}, bf16[2,4,2,48,384]{4,3,2,1,0:T(8,128)(2,1)S(1)}, u32[]{:S(2)}, u32[]{:S(2)}) collective-permute-start(bf16[2,4,2,48,384]{4,3,2,1,0:T(8,128)(2,1)S(1)} %slice_bitcast_fusion.3), channel_id=1, source_target_pairs={{0,16},{1,17},{2,18},{3,19},{4,20},{5,21},{6,22},{7,23},{8,24},{9,... | collective-permute-start | bytes 1769480 | tf_op jit(solution)/shard_map/ppermute | solution.py:805
  599.3 23.7 %collective-permute-start.27 = (bf16[2,4,2,48,384]{4,3,2,1,0:T(8,128)(2,1)S(1)}, bf16[2,4,2,48,384]{4,3,2,1,0:T(8,128)(2,1)S(1)}, u32[]{:S(2)}, u32[]{:S(2)}) collective-permute-start(bf16[2,4,2,48,384]{4,3,2,1,0:T(8,128)(2,1)S(1)} %slice_bitcast_fusion.2), channel_id=1, source_target_pairs={{0,1},{1,0},{2,3},{3,2},{4,5},{5,4},{6,7},{7,6},{8,9},{9,8},{10,11... | collective-permute-start | bytes 1769480 | tf_op jit(solution)/shard_map/ppermute | solution.py:805
  605.5 112.8 %collective-permute-start.15 = (bf16[512,768]{1,0:T(8,128)(2,1)}, bf16[512,768]{1,0:T(8,128)(2,1)}, u32[]{:S(2)}, u32[]{:S(2)}) collective-permute-start(bf16[512,768]{1,0:T(8,128)(2,1)} %get-tuple-element.238), channel_id=1, source_target_pairs={{0,0},{1,8},{2,2},{3,10},{4,4},{5,12},{6,6},{7,14},{8,1},{9,9},{10... | collective-permute-start | bytes 2359304 | tf_op jit(solution)/shard_map/ppermute | solution.py:805
  609.7 49.9 %collective-permute-start.40 = (bf16[2,4,48,384]{3,2,1,0:T(8,128)(2,1)S(1)}, bf16[2,4,48,384]{3,2,1,0:T(8,128)(2,1)S(1)}, u32[]{:S(2)}, u32[]{:S(2)}) collective-permute-start(bf16[2,4,48,384]{3,2,1,0:T(8,128)(2,1)S(1)} %get-tuple-element.198), channel_id=1, source_target_pairs={{0,4},{1,5},{2,6},{3,7},{4,0},{5,1},{6,2},{7,3},{8,12},{9,13},{10,... | collective-permute-start | bytes 884744 | tf_op jit(solution)/shard_map/ppermute | solution.py:805
  623.3 15.3 %collective-permute-start.28 = (bf16[4,2,48,384]{3,2,1,0:T(8,128)(2,1)S(1)}, bf16[4,2,48,384]{3,2,1,0:T(8,128)(2,1)S(1)}, u32[]{:S(2)}, u32[]{:S(2)}) collective-permute-start(bf16[4,2,48,384]{3,2,1,0:T(8,128)(2,1)S(1)} %get-tuple-element.186), channel_id=1, source_target_pairs={{0,1},{1,0},{2,3},{3,2},{4,5},{5,4},{6,7},{7,6},{8,9},{9,8},{10,11... | collective-permute-start | bytes 884744 | tf_op jit(solution)/shard_map/ppermute | solution.py:805
  629.0 11.3 %collective-permute-start.29 = (bf16[4,2,48,384]{3,2,1,0:T(8,128)(2,1)S(1)}, bf16[4,2,48,384]{3,2,1,0:T(8,128)(2,1)S(1)}, u32[]{:S(2)}, u32[]{:S(2)}) collective-permute-start(bf16[4,2,48,384]{3,2,1,0:T(8,128)(2,1)S(1)} %get-tuple-element.191), channel_id=1, source_target_pairs={{0,16},{1,17},{2,18},{3,19},{4,20},{5,21},{6,22},{7,23},{8,24},{9,... | collective-permute-start | bytes 884744 | tf_op jit(solution)/shard_map/ppermute | solution.py:805
  640.5 21.4 %collective-permute-start.30 = (bf16[2,4,48,384]{3,2,1,0:T(8,128)(2,1)S(1)}, bf16[2,4,48,384]{3,2,1,0:T(8,128)(2,1)S(1)}, u32[]{:S(2)}, u32[]{:S(2)}) collective-permute-start(bf16[2,4,48,384]{3,2,1,0:T(8,128)(2,1)S(1)} %get-tuple-element.200), channel_id=1, source_target_pairs={{0,4},{1,5},{2,6},{3,7},{4,0},{5,1},{6,2},{7,3},{8,12},{9,13},{10,... | collective-permute-start | bytes 884744 | tf_op jit(solution)/shard_map/ppermute | solution.py:805
  653.9 43.3 %copy-start.64 = (f32[512,768]{1,0:T(8,128)S(1)}, f32[512,768]{1,0:T(8,128)}, u32[]{:S(2)}) copy-start(f32[512,768]{1,0:T(8,128)} %get-tuple-element.125) | copy-start | bytes 4718596
  654.9 40.8 %collective-permute-start.24 = (bf16[512,768]{1,0:T(8,128)(2,1)}, bf16[512,768]{1,0:T(8,128)(2,1)}, u32[]{:S(2)}, u32[]{:S(2)}) collective-permute-start(bf16[512,768]{1,0:T(8,128)(2,1)} %get-tuple-element.194), channel_id=1, source_target_pairs={{0,2},{1,3},{2,4},{3,5},{4,6},{5,7},{8,10},{9,11},{10,12},{11,13},... | collective-permute-start | bytes 2359304 | tf_op jit(solution)/shard_map/ppermute | solution.py:805
  658.4 37.6 %collective-permute-start.23 = (bf16[512,768]{1,0:T(8,128)(2,1)S(1)}, bf16[512,768]{1,0:T(8,128)(2,1)}, u32[]{:S(2)}, u32[]{:S(2)}) collective-permute-start(bf16[512,768]{1,0:T(8,128)(2,1)S(1)} %get-tuple-element.193), channel_id=1, source_target_pairs={{2,0},{3,1},{4,2},{5,3},{6,4},{7,5},{10,8},{11,9},{12,10},{13,11},... | collective-permute-start | bytes 2359304 | tf_op jit(solution)/shard_map/ppermute | solution.py:805
  659.7 30.4 %collective-permute-start.41 = (bf16[4,48,384]{2,1,0:T(8,128)(2,1)S(1)}, bf16[4,48,384]{2,1,0:T(8,128)(2,1)S(1)}, u32[]{:S(2)}, u32[]{:S(2)}) collective-permute-start(bf16[4,48,384]{2,1,0:T(8,128)(2,1)S(1)} %fusion.58), channel_id=1, source_target_pairs={{0,2},{1,3},{2,0},{3,1},{4,6},{5,7},{6,4},{7,5},{8,10},{9,11},{10,... | collective-permute-start | bytes 442376 | tf_op jit(solution)/shard_map/ppermute | solution.py:805
  661.9 31.4 %collective-permute-start.31 = (bf16[4,48,384]{2,1,0:T(8,128)(2,1)S(1)}, bf16[4,48,384]{2,1,0:T(8,128)(2,1)}, u32[]{:S(2)}, u32[]{:S(2)}) collective-permute-start(bf16[4,48,384]{2,1,0:T(8,128)(2,1)S(1)} %fusion.56), channel_id=1, source_target_pairs={{0,2},{1,3},{2,0},{3,1},{4,6},{5,7},{6,4},{7,5},{8,10},{9,11},{10,... | collective-permute-start | bytes 442376 | tf_op jit(solution)/shard_map/ppermute | solution.py:805
  690.1 25.6 %collective-permute-start.42 = (bf16[4,48,384]{2,1,0:T(8,128)(2,1)S(1)}, bf16[4,48,384]{2,1,0:T(8,128)(2,1)}, u32[]{:S(2)}, u32[]{:S(2)}) collective-permute-start(bf16[4,48,384]{2,1,0:T(8,128)(2,1)S(1)} %fusion.53), channel_id=1, source_target_pairs={{0,16},{1,17},{2,18},{3,19},{4,20},{5,21},{6,22},{7,23},{8,24},{9,... | collective-permute-start | bytes 442376 | tf_op jit(solution)/shard_map/ppermute | solution.py:805
  693.4 9.6 %collective-permute-start.44 = (bf16[10,24,768]{2,1,0:T(8,128)(2,1)}, bf16[10,24,768]{2,1,0:T(8,128)(2,1)S(1)}, u32[]{:S(2)}, u32[]{:S(2)}) collective-permute-start(bf16[10,24,768]{2,1,0:T(8,128)(2,1)} %bitcast.277), channel_id=1, source_target_pairs={{0,16},{1,17},{2,18},{3,19},{4,20},{5,21},{6,22},{7,23},{8,24},{9,... | collective-permute-start | bytes 1105928 | tf_op jit(solution)/shard_map/ppermute | solution.py:805
  695.7 21.1 %collective-permute-start.32 = (bf16[4,48,384]{2,1,0:T(8,128)(2,1)S(1)}, bf16[4,48,384]{2,1,0:T(8,128)(2,1)}, u32[]{:S(2)}, u32[]{:S(2)}) collective-permute-start(bf16[4,48,384]{2,1,0:T(8,128)(2,1)S(1)} %fusion.54), channel_id=1, source_target_pairs={{0,16},{1,17},{2,18},{3,19},{4,20},{5,21},{6,22},{7,23},{8,24},{9,... | collective-permute-start | bytes 442376 | tf_op jit(solution)/shard_map/ppermute | solution.py:805
  695.9 18.1 %collective-permute-start.34 = (bf16[10,24,768]{2,1,0:T(8,128)(2,1)}, bf16[10,24,768]{2,1,0:T(8,128)(2,1)S(1)}, u32[]{:S(2)}, u32[]{:S(2)}) collective-permute-start(bf16[10,24,768]{2,1,0:T(8,128)(2,1)} %bitcast.279), channel_id=1, source_target_pairs={{0,16},{1,17},{2,18},{3,19},{4,20},{5,21},{6,22},{7,23},{8,24},{9,... | collective-permute-start | bytes 1105928 | tf_op jit(solution)/shard_map/ppermute | solution.py:805
  703.0 17.1 %collective-permute-start.25 = (bf16[512,768]{1,0:T(8,128)(2,1)S(1)}, bf16[512,768]{1,0:T(8,128)(2,1)S(1)}, u32[]{:S(2)}, u32[]{:S(2)}) collective-permute-start(bf16[512,768]{1,0:T(8,128)(2,1)S(1)} %fusion.2), channel_id=1, source_target_pairs={{0,0},{1,8},{2,2},{3,10},{4,4},{5,12},{6,6},{7,14},{8,1},{9,9},{10... | collective-permute-start | bytes 2359304 | tf_op jit(solution)/shard_map/ppermute | solution.py:805
  714.0 7.3 collective-permute-start.45
  715.7 5.7 collective-permute-start.35
  716.8 2.1 collective-permute-start.43
  718.3 1.6 collective-permute-start.33
  (70 other events, 324.3 us)
Sparse Core Ops, SparseCore 0:
  39.9 117.8 all-gather.2
  161.3 106.6 all-gather.4
  332.3 172.9 reduce-scatter.4
  512.3 164.3 reduce-scatter.2

commit v3 on v2

--- a/solution.py
+++ b/solution.py
@@ -461,6 +461,10 @@
 
 
 HEAD_SCALE = 0.125
+
+
+def in_main(array):
+    return pltpu.with_memory_space_constraint(array, pltpu.HBM)
 
 
 def fold_rows(values, combine):
@@ -862,8 +866,7 @@
     outs = pl.pallas_call(
         functools.partial(unpack_kernel, kinds),
         out_shape=[
-            jax.ShapeDtypeStruct((shards, quarters, rows, wide), pieces.dtype)
-            for rows, wide in shapes
+            pltpu.HBM((shards, quarters, rows, wide), pieces.dtype) for rows, wide in shapes
         ],
         grid=(quarters,),
         in_specs=[
@@ -879,7 +882,7 @@
             flops=0, bytes_accessed=128 * places * share * width, transcendentals=0
         ),
         name="unpack_weights",
-    )(pieces)
+    )(in_main(pieces))
     return [out.reshape(-1, out.shape[-1]) for out in outs]
 
 
@@ -940,37 +943,36 @@
 def pack_kernel(kinds, *refs):
     ins, vector_ref, out_ref = refs[:-2], refs[-2], refs[-1]
     width = out_ref.shape[-1]
-    share = out_ref.shape[3]
-    place = 0
+    share = ins[0].shape[2]
+    begin_at = 0
     for kind, ref in zip(kinds, ins):
         if kind == "columns":
             for column in range(ref.shape[-1] // width):
-                out_ref[0, :, place] = ref[:, 0, :, column * width : (column + 1) * width]
-                place += 1
+                lanes = slice(column * width, (column + 1) * width)
+                out_ref[0, :, begin_at : begin_at + share, :] = ref[:, 0, :, lanes]
+                begin_at += share
         else:
-            for piece in range(ref.shape[2] // share):
-                out_ref[0, :, place] = ref[:, 0, piece * share : (piece + 1) * share, :]
-                place += 1
-    out_ref[0, :, place] = jnp.zeros_like(out_ref[0, :, place])
-    out_ref[0, :, place, 0:8, :] = vector_ref[0]
-
-
-def pack_terms(terms, kinds, share, width, vectors):
-    places = sum(t.size for t in terms) // (32 * share * width) + 1
+            out_ref[0, :, begin_at : begin_at + ref.shape[2], :] = ref[:, 0]
+            begin_at += ref.shape[2]
+    out_ref[0, :, begin_at : begin_at + 8, :] = vector_ref[0]
+
+
+def pack_terms(terms, kinds, width, vectors):
+    rows = sum(t.size for t in terms) // (32 * width) + 8
     views = [t.reshape(8, 4, -1, t.shape[1]) for t in terms]
     return pl.pallas_call(
         functools.partial(pack_kernel, kinds),
-        out_shape=jax.ShapeDtypeStruct((4, 8, places, share, width), jnp.bfloat16),
+        out_shape=pltpu.HBM((4, 8, rows, width), jnp.bfloat16),
         grid=(4,),
         in_specs=[pl.BlockSpec((8, 1) + view.shape[2:], lambda q: (0, q, 0, 0)) for view in views]
         + [pl.BlockSpec((1,) + vectors.shape[1:], lambda q: (q, 0, 0, 0))],
-        out_specs=pl.BlockSpec((1, 8, places, share, width), lambda q: (q, 0, 0, 0, 0)),
+        out_specs=pl.BlockSpec((1, 8, rows, width), lambda q: (q, 0, 0, 0)),
         compiler_params=pltpu.CompilerParams(vmem_limit_bytes=32 * 2**20),
         cost_estimate=pl.CostEstimate(
-            flops=0, bytes_accessed=4 * 32 * places * share * width, transcendentals=0
+            flops=0, bytes_accessed=128 * rows * width, transcendentals=0
         ),
         name="pack_terms",
-    )(*views, vectors)
+    )(*[in_main(view) for view in views], vectors)
 
 
 def swap_y(values):
@@ -1031,11 +1033,8 @@
     return (one.astype(jnp.float32) + other.astype(jnp.float32)).astype(jnp.bfloat16)
 
 
-def scatter_terms(me, query_term, key_value_term, vectors):
-    spread = spread_terms(me, query_term, key_value_term, vectors)
-    a_part, b_part = spread[:, :, :, :2], spread[:, :, :, 2:]
+def scatter_terms(a_part, b_part, b_next):
     a_next = swap_y(a_part[1])
-    b_next = swap_x(b_part[:, 1])
     a_last = swap_x(summed(a_part[0, 1], a_next[1]))
     b_last = swap_y(summed(b_part[1, 0], b_next[1]))
     a_keep = summed(a_part[0, 0], a_next[0])
@@ -1059,7 +1058,7 @@
 
     def fill(near_ref, far_ref):
         part, half = near_ref.shape[-2:]
-        share, width = far_ref.shape[-2:]
+        share, width = part // 2, 2 * half
         for y_bit in range(GRP_Y):
             for core_bit in range(GRP_CORE):
                 y = y_bit ^ me[0]
@@ -1069,21 +1068,18 @@
                     lanes = pl.ds(pl.multiple_of(column * 2 * half + core * half, 128), half)
                     outs[0][0, y, :, lanes] = near_ref[core_bit, y_bit, column].astype(jnp.float32)
                 outs[4][0, quarter] = near_ref[core_bit, y_bit, 3, 0:8, :].astype(jnp.float32)
-                outs[1][0, quarter] = far_ref[core_bit, y_bit, 0].astype(jnp.float32)
-                place = 1
+                pieces = far_ref.at[core_bit, y_bit]
+                outs[1][0, quarter] = pieces[:share, :].astype(jnp.float32)
+                begin_at = share
                 for column in range(outs[2].shape[-1] // width):
                     lanes = slice(column * width, (column + 1) * width)
-                    outs[2][0, quarter, :, lanes] = far_ref[core_bit, y_bit, place].astype(
-                        jnp.float32
-                    )
-                    place += 1
-                for piece in range(outs[3].shape[2] // share):
-                    rows = slice(piece * share, (piece + 1) * share)
-                    outs[3][0, quarter, rows, :] = far_ref[core_bit, y_bit, place].astype(
-                        jnp.float32
-                    )
-                    place += 1
-                outs[5][0, quarter] = far_ref[core_bit, y_bit, place, 0:8, :].astype(jnp.float32)
+                    rows = slice(begin_at, begin_at + share)
+                    outs[2][0, quarter, :, lanes] = pieces[rows, :].astype(jnp.float32)
+                    begin_at += share
+                deep = outs[3].shape[2]
+                outs[3][0, quarter] = pieces[begin_at : begin_at + deep, :].astype(jnp.float32)
+                begin_at += deep
+                outs[5][0, quarter] = pieces[begin_at : begin_at + 8, :].astype(jnp.float32)
 
     for layer in range(layers):
         pl.when(pl.program_id(0) == layer)(
@@ -1094,7 +1090,7 @@
 def finish_shares(me, shares, hidden_units, deep):
     layers = len(shares)
     part, half = shares[0][0].shape[-2:]
-    share, width = shares[0][1].shape[-2:]
+    share, width = part // 2, 2 * half
     shapes = [
         (2, part, 3 * width),
         (4, share, width),
@@ -1586,6 +1582,7 @@
     activations = turn_rows((hidden_state * valid_rows).astype(jnp.bfloat16))
     state_grad = state_grad.astype(jnp.float32) * valid_rows
     results = [None] * LAYERS
+    spreads = [None] * LAYERS
     for layer_index in reversed(range(LAYERS)):
         layer_low, state_window, queries, key_value, wides, lse, kept, tail_vectors = kept_list[
             layer_index
@@ -1608,6 +1605,8 @@
         own_grad, far_grad, key_value_grad = flash_backward(
             bounds, queries, key_value, mixed_grads, wides, lse, low_line, high_line
         )
+        if layer_index == 0:
+            key_value_grad, started = lax.optimization_barrier((key_value_grad, started))
         query_term = jnp.einsum(
             "td,te->de", layer_low, own_grad, preferred_element_type=jnp.float32
         ) + jnp.einsum(
@@ -1658,20 +1657,31 @@
         vectors = vectors.reshape(8, 4, 1, -1).transpose(1, 0, 2, 3)
         vectors = jnp.pad(vectors, ((0, 0), (0, 0), (0, 7), (0, width - vectors.shape[3])))
         terms = (mixing_grad, expand_grad, shrink_grad)
-        pieces = pack_terms(terms, far_kinds, share, width, vectors)
+        pieces = pack_terms(terms, far_kinds, width, vectors)
         fed = lax.psum_scatter(
             pieces.reshape(32, -1, width), BOTH, scatter_dimension=0, tiled=True
-        ).reshape(-1, share, width)
+        )[0]
         lines = jnp.zeros((8 * bias_count,), jnp.float32)
         lines = lax.dynamic_update_slice(lines, bias_q_grad, (core * half,))
         lines = lax.dynamic_update_slice(lines, bias_v_grad, (width + core * half,))
         lines = lines.reshape(8, 2, -1).transpose(1, 0, 2).astype(jnp.bfloat16)
         lines = jnp.pad(lines, ((0, 0), (0, 0), (0, width - lines.shape[2])))
         lines = jnp.pad(lines.reshape(2, 8, 2, half), ((0, 0), (0, 0), (0, 6), (0, 0)))
-        attended = scatter_terms(
-            me, query_term.astype(jnp.bfloat16), key_value_term.astype(jnp.bfloat16), lines
-        )
-        results[layer_index] = (gather_quarters(attended), gather_quarters(fed))
+        query_term = query_term.astype(jnp.bfloat16)
+        key_value_term = key_value_term.astype(jnp.bfloat16)
+        if layer_index > 0:
+            state_grad, query_term, key_value_term = lax.optimization_barrier(
+                (state_grad, query_term, key_value_term)
+            )
+        spreads[layer_index] = spread_terms(me, query_term, key_value_term, lines)
+        if layer_index > 0:
+            started = swap_x(spreads[layer_index][:, 1])
+        results[layer_index] = gather_quarters(fed)
+    attended = gather_quarters(scatter_terms(*spreads, started))
+    results = [
+        (attended[:, :, 4 * layer_index : 4 * (layer_index + 1)], results[layer_index])
+        for layer_index in range(LAYERS)
+    ]
     outs = finish_shares(me, results, hidden_units, deep)
     quarter_len = (bias_count + norm_gains.shape[1]) // 4
     vectors = outs[5][:, :, 0, :quarter_len].reshape(LAYERS, -1)

time: 743 us -> 726 us (0.977)
  local copies, waits for them, and re-layouts: 91.9 us -> 51.6 us
  Pallas kernels: 202 us -> 230 us
  starting transfers between devices: 114 us -> 87.9 us
  waiting for transfers between devices: 210 us -> 235 us
    unnamed x188 -> x161, local copies, waits for them, and re-layouts: 58.7 us -> 28.4 us
    pallas_call x5, Pallas kernels: 10.6 us -> 38.3 us  [the longest x3 21.1 us: unpack_weights_of(): pl.pallas_call(functools.partial(unpack_kernel, kinds), out_shape=[pltpu....]
    ppermute x46 -> x38, starting transfers between devices: 114 us -> 87.7 us  [send(): return lax.ppermute(values, BOTH, device_pairs(place))]
    ppermute x46 -> x38, waiting for transfers between devices: 193 us -> 220 us  [send(): return lax.ppermute(values, BOTH, device_pairs(place))]
  transfers between devices with their start and end apart: 50 -> 42, of which waited for: 23 -> 19; matrix products, arithmetic and copies ran while one was open for 17% -> 15% of each run, Pallas kernels for 24% -> 27%
where the time goes in v3:
time: 726 us; the launch traced here: 717 us
  waiting for transfers between devices  235 us (32%)
  Pallas kernels  230 us (32%)
  starting transfers between devices  87.9 us (12%)
  matrix products  55.1 us (8%)
  local copies, waits for them, and re-layouts  51.6 us (7%)
  other arithmetic  35.6 us (5%)
  between operations  21.7 us (3%)
    ppermute x38, waiting for transfers between devices, send(): return lax.ppermute(values, BOTH, device_pairs(place))  220 us
    ppermute x38, starting transfers between devices, send(): return lax.ppermute(values, BOTH, device_pairs(place))  87.7 us
    pallas_call x2, Pallas kernels, flash_backward(): pl.pallas_call(flash_backward_kernel, out_shape=(jax.ShapeDtypeStruct((ro...  68.9 us
    pallas_call x2, Pallas kernels, tail_backward(): pl.pallas_call(tail_backward_kernel, out_shape=[shaped(rows, width, jnp.f...  43.5 us
    pallas_call x2, Pallas kernels, flash_forward(): pl.pallas_call(flash_forward_kernel, out_shape=(jax.ShapeDtypeStruct((row...  34.4 us
    pallas_call x2, Pallas kernels, tail_forward(): pl.pallas_call(tail_forward_kernel, out_shape=[shaped(width, jnp.bfloat16...  30.3 us
    unnamed x161, local copies, waits for them, and re-layouts  28.4 us
    pallas_call x3, Pallas kernels, unpack_weights_of(): pl.pallas_call(functools.partial(unpack_kernel, kinds), out_shape=[pltpu....  21.1 us
  transfers between devices with their start and end apart: 42, of which 19 were waited for; matrix products, arithmetic and copies ran while one was open for 15% of the time, Pallas kernels for 27%

profile of v3, /device:TPU:1, one launch (start us, length us, event | category | flops | bytes accessed | tf_op | source)
XLA Modules:
  0.0 716.5 jit_solution(4952795648645645801)
XLA Ops:
  7.2 4.5 collective-permute-start.1
  14.7 2.9 pick_quarters.1
  18.9 3.2 collective-permute-done
  23.1 2.8 collective-permute-start.2
  26.0 13.8 %collective-permute-done.2 = bf16[2,4,48,384]{3,2,1,0:T(8,128)(2,1)S(1)} collective-permute-done((bf16[2,4,48,384]{3,2,1,0:T(8,128)(2,1)S(1)}, bf16[2,4,48,384]{3,2,1,0:T(8,128)(2,1)S(1)}, u32[]{:S(2)}, u32[]{:S(2)}) %collective-permute-start.2) | collective-permute-done | bytes 294944 | tf_op jit(solution)/shard_map/ppermute | solution.py:809
  42.0 4.0 collective-permute-start.7
  47.3 23.4 %collective-permute-done.8 = bf16[512,768]{1,0:T(8,128)(2,1)S(1)} collective-permute-done((bf16[512,768]{1,0:T(8,128)(2,1)S(1)}, bf16[512,768]{1,0:T(8,128)(2,1)S(1)}, u32[]{:S(2)}, u32[]{:S(2)}) %collective-permute-start.8) | collective-permute-done | bytes 786464 | tf_op jit(solution)/shard_map/ppermute | solution.py:809
  84.5 6.4 collective-permute-done.3
  96.8 10.1 %collective-permute-done.4 = bf16[2,4,2,48,384]{4,3,2,1,0:T(8,128)(2,1)S(1)} collective-permute-done((bf16[2,4,2,48,384]{4,3,2,1,0:T(8,128)(2,1)S(1)}, bf16[2,4,2,48,384]{4,3,2,1,0:T(8,128)(2,1)S(1)}, u32[]{:S(2)}, u32[]{:S(2)}) %collective-permute-start.4) | collective-permute-done | bytes 589856 | tf_op jit(solution)/shard_map/ppermute | solution.py:809
  110.2 2.1 fusion.9.a_ref
  112.3 3.3 fusion.10.b_ref
  115.6 2.0 constant_dynamic-update-slice_fusion.2
  117.6 4.1 add_convert_fusion.1.kv_ref
  121.8 17.4 %flash_forward.2 = (bf16[512,384]{1,0:T(8,128)(2,1)S(1)}, bf16[512,384]{1,0:T(8,128)(2,1)S(1)}, f32[512,384]{1,0:T(8,128)S(1)}, f32[512,384]{1,0:T(8,128)S(1)}, f32[24,1024]{1,0:T(8,128)S(1)}) custom-call(s32[10]{0:T(128)S(1)} %stack.211.bounds, bf16[512,384]{1,0:T(8,128)(2,1)S(1)} %fusion.9.a_ref, bf16[512,384]{1,0:T(8,128)(2,1)S(1)} %fusion.10.b_ref, ...), custom_call_target="tpu_custom_call" | custom-call | flops 4026531840 | bytes 12582912 | tf_op jit(solution)/shard_map/flash_forward/pallas_call | solution.py:724
  142.7 14.3 %all-gather.3.cloned.1.call-done = bf16[32,288,768]{2,1,0:T(8,128)(2,1)} async-done(((bf16[1,288,768]{2,1,0:T(8,128)(2,1)}), bf16[32,288,768]{2,1,0:T(8,128)(2,1)}) %all-gather.3.cloned.1.call-update) | async-done | bytes 14155792 | tf_op jit(solution)/shard_map/all_gather | solution.py:1397
  157.1 8.2 %unpack_weights.3 = (bf16[8,4,24,768]{3,2,1,0:T(8,128)(2,1)}, bf16[8,4,24,3072]{3,2,1,0:T(8,128)(2,1)}, bf16[8,4,96,768]{3,2,1,0:T(8,128)(2,1)}) custom-call(bf16[4,8,12,24,768]{4,3,2,1,0:T(8,128)(2,1)} %bitcast.182), custom_call_target="tpu_custom_call" | custom-call | bytes 21233664 | tf_op jit(solution)/shard_map/unpack_weights/pallas_call | solution.py:866
  166.6 15.1 %tail_forward.2 = (bf16[512,768]{1,0:T(8,128)(2,1)S(1)}, f32[512,768]{1,0:T(8,128)S(1)}, f32[512,128]{1,0:T(8,128)S(1)}, bf16[512,768]{1,0:T(8,128)(2,1)S(1)}, b...) custom-call(s32[4]{0:T(128)S(1)} %copy-done.6, ...), custom_call_target="tpu_custom_call" | custom-call | flops 5435817984 | bytes 33554432 | tf_op jit(solution)/shard_map/tail_forward/pallas_call | solution.py:1214
  185.3 4.0 collective-permute-start.11
  189.4 29.5 %collective-permute-done.12 = bf16[512,768]{1,0:T(8,128)(2,1)S(1)} collective-permute-done((bf16[512,768]{1,0:T(8,128)(2,1)S(1)}, bf16[512,768]{1,0:T(8,128)(2,1)S(1)}, u32[]{:S(2)}, u32[]{:S(2)}) %collective-permute-start.12) | collective-permute-done | bytes 786464 | tf_op jit(solution)/shard_map/ppermute | solution.py:809
  221.1 3.0 collective-permute-start.16
  224.4 4.5 unpack_weights.4
  228.9 2.2 fusion.70
  233.9 2.0 constant_dynamic-update-slice_fusion.6
  235.9 2.2 copy-done.63
  238.1 4.0 add_convert_fusion.kv_ref
  242.2 17.0 %flash_forward.3 = (bf16[512,384]{1,0:T(8,128)(2,1)S(1)}, bf16[512,384]{1,0:T(8,128)(2,1)S(1)}, f32[512,384]{1,0:T(8,128)S(1)}, f32[512,384]{1,0:T(8,128)S(1)}, f32[24,1024]{1,0:T(8,128)S(1)}) custom-call(s32[10]{0:T(128)S(1)} %stack.211.bounds, bf16[512,384]{1,0:T(8,128)(2,1)S(1)} %fusion.11.a_ref, bf16[512,384]{1,0:T(8,128)(2,1)S(1)} %fusion.12.b_ref, ...), custom_call_target="tpu_custom_call" | custom-call | flops 4026531840 | bytes 12582912 | tf_op jit(solution)/shard_map/flash_forward/pallas_call | solution.py:724
  261.8 4.5 collective-permute-start.14
  267.0 8.4 %unpack_weights.5 = (bf16[8,4,24,768]{3,2,1,0:T(8,128)(2,1)}, bf16[8,4,24,3072]{3,2,1,0:T(8,128)(2,1)}, bf16[8,4,96,768]{3,2,1,0:T(8,128)(2,1)}) custom-call(bf16[4,8,9,24,768]{4,3,2,1,0:T(8,128)(2,1)} %bitcast.187), custom_call_target="tpu_custom_call" | custom-call | bytes 21233664 | tf_op jit(solution)/shard_map/unpack_weights/pallas_call | solution.py:866
  276.7 15.2 %tail_forward.3 = (bf16[512,768]{1,0:T(8,128)(2,1)S(1)}, f32[512,768]{1,0:T(8,128)S(1)}, f32[512,128]{1,0:T(8,128)S(1)}, bf16[512,768]{1,0:T(8,128)(2,1)S(1)}, b...) custom-call(s32[4]{0:T(128)S(1)} %copy-done.6, ...), custom_call_target="tpu_custom_call" | custom-call | flops 5435817984 | bytes 33554432 | tf_op jit(solution)/shard_map/tail_forward/pallas_call | solution.py:1214
  293.1 3.4 convert_multiply_fusion
  296.5 21.5 %tail_backward.2 = (f32[512,768]{1,0:T(8,128)}, bf16[512,384]{1,0:T(8,128)(2,1)S(1)}, bf16[512,384]{1,0:T(8,128)(2,1)S(1)}, bf16[768,768]{1,0:T(8,128)(2,1)S(1)}...) custom-call(s32[4]{0:T(128)S(1)} %copy-done.6, ...), custom_call_target="tpu_custom_call" | custom-call | flops 10871635968 | bytes 41943040 | tf_op jit(solution)/shard_map/tail_backward/pallas_call | solution.py:1346
  321.3 8.6 %pack_terms.3 = bf16[4,8,224,768]{3,2,1,0:T(8,128)(2,1)} custom-call(bf16[8,4,24,768]{3,2,1,0:T(8,128)(2,1)} %bitcast.169, bf16[8,4,24,3072]{3,2,1,0:T(8,128)(2,1)} %bitcast.190, bf16[8,4,96,768]{3,2,1,0:T(8,128)(2,1)} %bitcast.191, bf16[4,8,8,768]{3,2,1,0:T(8,128)(2,1)S(1)} %pad.29.refs_3_), custom_call_target="tpu_custom_call" | custom-call | bytes 22020096 | tf_op jit(solution)/shard_map/pack_terms/pallas_call | solution.py:963
  332.6 34.4 %flash_backward.2 = (bf16[512,384]{1,0:T(8,128)(2,1)}, bf16[512,384]{1,0:T(8,128)(2,1)}, bf16[3072,768]{1,0:T(8,128)(2,1)}) custom-call(s32[10]{0:T(128)} %copy-done.8, bf16[512,384]{1,0:T(8,128)(2,1)} %copy-done.13, bf16[512,384]{1,0:T(8,128)(2,1)} %copy-done.15, bf16[3072,768]{1,0:T(8,128)(2,1)} %copy-done.22, bf16[512,384]{1,0:T(8,128)(2,1)} %copy-done.33, ...), custom_call_target="tpu_custom_call" | custom-call | flops 10066329600 | bytes 20971520 | tf_op jit(solution)/shard_map/flash_backward/pallas_call | solution.py:758
  367.0 5.9 fusion.20
  373.1 4.0 copy-done.40
  379.7 1.9 fusion.21
  381.5 3.2 fusion.7
  386.6 3.2 fusion.69
  390.0 17.2 %collective-permute-start.20 = (bf16[512,768]{1,0:T(8,128)(2,1)S(1)}, bf16[512,768]{1,0:T(8,128)(2,1)S(1)}, u32[]{:S(2)}, u32[]{:S(2)}) collective-permute-start(bf16[512,768]{1,0:T(8,128)(2,1)S(1)} %get-tuple-element.200), channel_id=1, source_target_pairs={{0,2},{1,3},{2,4},{3,5},{4,6},{5,7},{8,10},{9,11},{10,12},{11,13},... | collective-permute-start | bytes 2359304 | tf_op jit(solution)/shard_map/ppermute | solution.py:809
  409.2 7.3 %convolution_convert_fusion.1 = bf16[768,768]{1,0:T(8,128)(2,1)} fusion(bf16[3072,768]{1,0:T(8,128)(2,1)} %copy-done.63, bf16[3072,768]{1,0:T(8,128)(2,1)S(1)} %bitcast.196), kind=kOutput, calls=%fused_computation.28 | convolution fusion | flops 3624468480 | bytes 10616832 | tf_op jit(solution)/shard_map/td,te->de/dot_general | solution.py:1618
  416.5 17.8 %collective-permute-done.20 = bf16[512,768]{1,0:T(8,128)(2,1)S(1)} collective-permute-done((bf16[512,768]{1,0:T(8,128)(2,1)S(1)}, bf16[512,768]{1,0:T(8,128)(2,1)S(1)}, u32[]{:S(2)}, u32[]{:S(2)}) %collective-permute-start.20) | collective-permute-done | bytes 786464 | tf_op jit(solution)/shard_map/ppermute | solution.py:809
  438.3 22.0 %tail_backward.3 = (f32[512,768]{1,0:T(8,128)}, bf16[512,384]{1,0:T(8,128)(2,1)S(1)}, bf16[512,384]{1,0:T(8,128)(2,1)S(1)}, bf16[768,768]{1,0:T(8,128)(2,1)S(1)}...) custom-call(s32[4]{0:T(128)S(1)} %copy-done.6, ...), custom_call_target="tpu_custom_call" | custom-call | flops 10871635968 | bytes 41943040 | tf_op jit(solution)/shard_map/tail_backward/pallas_call | solution.py:1346
  462.7 8.5 %pack_terms.2 = bf16[4,8,224,768]{3,2,1,0:T(8,128)(2,1)} custom-call(bf16[8,4,24,768]{3,2,1,0:T(8,128)(2,1)} %bitcast.168, bf16[8,4,24,3072]{3,2,1,0:T(8,128)(2,1)} %bitcast.188, bf16[8,4,96,768]{3,2,1,0:T(8,128)(2,1)} %bitcast.189, bf16[4,8,8,768]{3,2,1,0:T(8,128)(2,1)S(1)} %pad.28.refs_3_), custom_call_target="tpu_custom_call" | custom-call | bytes 22020096 | tf_op jit(solution)/shard_map/pack_terms/pallas_call | solution.py:963
  472.4 2.1 convert_reduce_fusion.1
  476.2 3.4 spread_terms.2
  483.2 34.5 %flash_backward.3 = (bf16[512,384]{1,0:T(8,128)(2,1)}, bf16[512,384]{1,0:T(8,128)(2,1)}, bf16[3072,768]{1,0:T(8,128)(2,1)}) custom-call(s32[10]{0:T(128)} %copy-done.8, bf16[512,384]{1,0:T(8,128)(2,1)} %copy-done.14, bf16[512,384]{1,0:T(8,128)(2,1)} %copy-done.16, bf16[3072,768]{1,0:T(8,128)(2,1)} %copy-done.25, bf16[512,384]{1,0:T(8,128)(2,1)} %copy-done.32, ...), custom_call_target="tpu_custom_call" | custom-call | flops 10066329600 | bytes 20971520 | tf_op jit(solution)/shard_map/flash_backward/pallas_call | solution.py:758
  520.2 2.1 fusion.24
  525.2 9.2 %convolution_convert_fusion = bf16[768,768]{1,0:T(8,128)(2,1)} fusion(bf16[3072,768]{1,0:T(8,128)(2,1)} %copy-done.66, bf16[3072,768]{1,0:T(8,128)(2,1)} %get-tuple-element.140), kind=kOutput, calls=%fused_computation.27 | convolution fusion | flops 3624468480 | bytes 10616832 | tf_op jit(solution)/shard_map/td,te->de/dot_general | solution.py:1618
  534.4 3.5 spread_terms.3
  539.5 5.9 fusion.17
  547.7 28.9 %collective-permute-done.27 = bf16[2,4,4,48,384]{4,3,2,1,0:T(8,128)(2,1)S(1)} collective-permute-done((bf16[2,4,4,48,384]{4,3,2,1,0:T(8,128)(2,1)S(1)}, bf16[2,4,4,48,384]{4,3,2,1,0:T(8,128)(2,1)S(1)}, u32[]{:S(2)}, u32[]{:S(2)}) %collective-permute-start.27) | collective-permute-done | bytes 1179680 | tf_op jit(solution)/shard_map/ppermute | solution.py:809
  576.8 4.7 collective-permute-start.28
  582.3 21.4 %collective-permute-done.28 = bf16[4,4,48,384]{3,2,1,0:T(8,128)(2,1)S(1)} collective-permute-done((bf16[4,4,48,384]{3,2,1,0:T(8,128)(2,1)S(1)}, bf16[4,4,48,384]{3,2,1,0:T(8,128)(2,1)S(1)}, u32[]{:S(2)}, u32[]{:S(2)}) %collective-permute-start.28) | collective-permute-done | bytes 589856 | tf_op jit(solution)/shard_map/ppermute | solution.py:809
  605.2 6.6 collective-permute-start.30
  612.6 40.0 %collective-permute-done.30 = bf16[2,8,48,384]{3,2,1,0:T(8,128)(2,1)S(1)} collective-permute-done((bf16[2,8,48,384]{3,2,1,0:T(8,128)(2,1)S(1)}, bf16[2,8,48,384]{3,2,1,0:T(8,128)(2,1)S(1)}, u32[]{:S(2)}, u32[]{:S(2)}) %collective-permute-start.30) | collective-permute-done | bytes 589856 | tf_op jit(solution)/shard_map/ppermute | solution.py:809
  652.8 2.8 fusion.68
  656.8 4.2 collective-permute-start.25
  662.5 10.2 %collective-permute-start.15 = (bf16[512,768]{1,0:T(8,128)(2,1)}, bf16[512,768]{1,0:T(8,128)(2,1)S(1)}, u32[]{:S(2)}, u32[]{:S(2)}) collective-permute-start(bf16[512,768]{1,0:T(8,128)(2,1)} %get-tuple-element.238), channel_id=1, source_target_pairs={{0,0},{1,8},{2,2},{3,10},{4,4},{5,12},{6,6},{7,14},{8,1},{9,9},{10... | collective-permute-start | bytes 2359304 | tf_op jit(solution)/shard_map/ppermute | solution.py:809
  673.0 10.3 %collective-permute-done.25 = bf16[512,768]{1,0:T(8,128)(2,1)} collective-permute-done((bf16[512,768]{1,0:T(8,128)(2,1)}, bf16[512,768]{1,0:T(8,128)(2,1)}, u32[]{:S(2)}, u32[]{:S(2)}) %collective-permute-start.25) | collective-permute-done | bytes 786464 | tf_op jit(solution)/shard_map/ppermute | solution.py:809
  683.5 2.0 collective-permute-done.24
  685.5 2.2 fusion.2
  687.7 4.3 collective-permute-start.26
  695.4 6.3 collective-permute-done.26
  703.6 3.8 finish_shares.1
  (375 shorter events, 93.5 us)
Async XLA Ops:
  7.2 149.9 %all-gather.3.cloned.1.call-start = ((), (), s32[]{:S(2)}) async-start(), calls=%async_computation.2 | async-start | bytes 14598144 | tf_op jit(solution)/shard_map/all_gather | solution.py:1397
  7.2 15.9 %collective-permute-start.1 = (bf16[512,768]{1,0:T(8,128)(2,1)}, bf16[512,768]{1,0:T(8,128)(2,1)S(1)}, u32[]{:S(2)}, u32[]{:S(2)}) collective-permute-start(bf16[512,768]{1,0:T(8,128)(2,1)} %param.10), channel_id=1, source_target_pairs={{0,0},{1,8},{2,2},{3,10},{4,4},{5,12},{6,6},{7,14},{8,1},{9,9},{10... | collective-permute-start | bytes 2359304 | tf_op jit(solution)/shard_map/ppermute | solution.py:809
  17.6 4.5 collective-permute-start
  23.1 72.3 %copy-start.44 = (bf16[512,768]{1,0:T(8,128)(2,1)}, bf16[512,768]{1,0:T(8,128)(2,1)S(1)}, u32[]{:S(2)}) copy-start(bf16[512,768]{1,0:T(8,128)(2,1)S(1)} %collective-permute-done.1) | copy-start | bytes 2359300
  23.1 16.6 %collective-permute-start.2 = (bf16[2,4,48,384]{3,2,1,0:T(8,128)(2,1)S(1)}, bf16[2,4,48,384]{3,2,1,0:T(8,128)(2,1)S(1)}, u32[]{:S(2)}, u32[]{:S(2)}) collective-permute-start(bf16[2,4,48,384]{3,2,1,0:T(8,128)(2,1)S(1)} %pad_maximum_fusion.18), channel_id=1, source_target_pairs={{0,4},{1,5},{2,6},{3,7},{4,0},{5,1},{6,2},{7,3},{8,12},{9,13},{10,... | collective-permute-start | bytes 884744 | tf_op jit(solution)/shard_map/ppermute | solution.py:809
  39.8 227.2 %all-gather.5.cloned.1.call-start = ((), (), s32[]{:S(2)}) async-start(), calls=%async_computation.3 | async-start | bytes 10948608 | tf_op jit(solution)/shard_map/all_gather | solution.py:1397
  40.6 632.4 %reduce-scatter.5.cloned.1.call-start = ((), (), s32[]{:S(2)}) async-start(), calls=%async_computation.5 | async-start | bytes 11354112 | tf_op jit(solution)/shard_map/reduce_scatter | solution.py:1661
  40.7 30.0 %collective-permute-start.8 = (bf16[512,768]{1,0:T(8,128)(2,1)S(1)}, bf16[512,768]{1,0:T(8,128)(2,1)S(1)}, u32[]{:S(2)}, u32[]{:S(2)}) collective-permute-start(bf16[512,768]{1,0:T(8,128)(2,1)S(1)} %collective-permute-done.1), channel_id=1, source_target_pairs={{2,0},{3,1},{4,2},{5,3},{6,4},{7,5},{10,8},{11,9},{12,10},{13,11},... | collective-permute-start | bytes 2359304 | tf_op jit(solution)/shard_map/ppermute | solution.py:809
  42.0 29.5 %collective-permute-start.7 = (bf16[512,768]{1,0:T(8,128)(2,1)S(1)}, bf16[512,768]{1,0:T(8,128)(2,1)S(1)}, u32[]{:S(2)}, u32[]{:S(2)}) collective-permute-start(bf16[512,768]{1,0:T(8,128)(2,1)S(1)} %collective-permute-done.1), channel_id=1, source_target_pairs={{0,2},{1,3},{2,4},{3,5},{4,6},{5,7},{8,10},{9,11},{10,12},{11,13},... | collective-permute-start | bytes 2359304 | tf_op jit(solution)/shard_map/ppermute | solution.py:809
  73.1 39.2 %collective-permute-start.9 = (bf16[1536,768]{1,0:T(8,128)(2,1)}, bf16[1536,768]{1,0:T(8,128)(2,1)}, u32[]{:S(2)}, u32[]{:S(2)}) collective-permute-start(bf16[1536,768]{1,0:T(8,128)(2,1)} %pad_maximum_fusion), channel_id=1, source_target_pairs={{0,8},{1,9},{2,10},{3,11},{4,12},{5,13},{6,14},{7,15},{8,0},{9,1},... | collective-permute-start | bytes 7077896 | tf_op jit(solution)/shard_map/ppermute | solution.py:809
  75.7 15.1 %collective-permute-start.3 = (bf16[4,2,48,384]{3,2,1,0:T(8,128)(2,1)}, bf16[4,2,48,384]{3,2,1,0:T(8,128)(2,1)S(1)}, u32[]{:S(2)}, u32[]{:S(2)}) collective-permute-start(bf16[4,2,48,384]{3,2,1,0:T(8,128)(2,1)} %get-tuple-element.216), channel_id=1, source_target_pairs={{0,1},{1,0},{2,3},{3,2},{4,5},{5,4},{6,7},{7,6},{8,9},{9,8},{10,11... | collective-permute-start | bytes 884744 | tf_op jit(solution)/shard_map/ppermute | solution.py:809
  75.7 18.2 %collective-permute-start.5 = (bf16[4,2,48,384]{3,2,1,0:T(8,128)(2,1)}, bf16[4,2,48,384]{3,2,1,0:T(8,128)(2,1)}, u32[]{:S(2)}, u32[]{:S(2)}) collective-permute-start(bf16[4,2,48,384]{3,2,1,0:T(8,128)(2,1)} %get-tuple-element.215), channel_id=1, source_target_pairs={{0,16},{1,17},{2,18},{3,19},{4,20},{5,21},{6,22},{7,23},{8,24},{9,... | collective-permute-start | bytes 884744 | tf_op jit(solution)/shard_map/ppermute | solution.py:809
  84.5 157.7 %copy-start.8 = (s32[10]{0:T(128)}, s32[10]{0:T(128)S(1)}, u32[]{:S(2)}) copy-start(s32[10]{0:T(128)S(1)} %stack.211.bounds) | copy-start | bytes 124
  92.7 14.2 %collective-permute-start.4 = (bf16[2,4,2,48,384]{4,3,2,1,0:T(8,128)(2,1)S(1)}, bf16[2,4,2,48,384]{4,3,2,1,0:T(8,128)(2,1)S(1)}, u32[]{:S(2)}, u32[]{:S(2)}) collective-permute-start(bf16[2,4,2,48,384]{4,3,2,1,0:T(8,128)(2,1)S(1)} %get-tuple-element.218), channel_id=1, source_target_pairs={{0,16},{1,17},{2,18},{3,19},{4,20},{5,21},{6,22},{7,23},{8,24},{9,... | collective-permute-start | bytes 1769480 | tf_op jit(solution)/shard_map/ppermute | solution.py:809
  94.9 13.9 %collective-permute-start.6 = (bf16[2,4,2,48,384]{4,3,2,1,0:T(8,128)(2,1)S(1)}, bf16[2,4,2,48,384]{4,3,2,1,0:T(8,128)(2,1)S(1)}, u32[]{:S(2)}, u32[]{:S(2)}) collective-permute-start(bf16[2,4,2,48,384]{4,3,2,1,0:T(8,128)(2,1)S(1)} %get-tuple-element.212), channel_id=1, source_target_pairs={{0,1},{1,0},{2,3},{3,2},{4,5},{5,4},{6,7},{7,6},{8,9},{9,8},{10,11... | collective-permute-start | bytes 1769480 | tf_op jit(solution)/shard_map/ppermute | solution.py:809
  96.8 12.0 %copy-start.64 = (bf16[3072,768]{1,0:T(8,128)(2,1)}, bf16[3072,768]{1,0:T(8,128)(2,1)S(1)}, u32[]{:S(2)}) copy-start(bf16[3072,768]{1,0:T(8,128)(2,1)S(1)} %constant_dynamic-update-slice_fusion.3) | copy-start | bytes 14155780
  112.3 9.4 %copy-start.14 = (bf16[512,384]{1,0:T(8,128)(2,1)}, bf16[512,384]{1,0:T(8,128)(2,1)S(1)}, u32[]{:S(2)}) copy-start(bf16[512,384]{1,0:T(8,128)(2,1)S(1)} %fusion.9.a_ref) | copy-start | bytes 1179652
  121.7 17.5 %copy-start.25 = (bf16[3072,768]{1,0:T(8,128)(2,1)}, bf16[3072,768]{1,0:T(8,128)(2,1)S(1)}, u32[]{:S(2)}) copy-start(bf16[3072,768]{1,0:T(8,128)(2,1)S(1)} %add_convert_fusion.1.kv_ref) | copy-start | bytes 14155780
  121.7 120.5 %copy-start.4 = (s32[8,1024]{1,0:T(8,128)}, s32[8,1024]{1,0:T(8,128)S(1)}, u32[]{:S(2)}) copy-start(s32[8,1024]{1,0:T(8,128)S(1)} %broadcast_in_dim.47.low_ref) | copy-start | bytes 98308
  121.7 120.4 %copy-start.5 = (s32[8,1024]{1,0:T(8,128)}, s32[8,1024]{1,0:T(8,128)S(1)}, u32[]{:S(2)}) copy-start(s32[8,1024]{1,0:T(8,128)S(1)} %broadcast_in_dim.48.high_ref) | copy-start | bytes 98308
  141.6 23.7 %collective-permute-start.10 = (bf16[512,384]{1,0:T(8,128)(2,1)S(1)}, bf16[512,384]{1,0:T(8,128)(2,1)S(1)}, u32[]{:S(2)}, u32[]{:S(2)}) collective-permute-start(bf16[512,384]{1,0:T(8,128)(2,1)S(1)} %get-tuple-element.90), channel_id=1, source_target_pairs={{0,8},{1,9},{2,10},{3,11},{4,12},{5,13},{6,14},{7,15},{8,0},{9,1},... | collective-permute-start | bytes 1179656 | tf_op jit(solution)/shard_map/ppermute | solution.py:809
  184.0 36.4 %copy-start.17 = (f32[512,768]{1,0:T(8,128)}, f32[512,768]{1,0:T(8,128)S(1)}, u32[]{:S(2)}) copy-start(f32[512,768]{1,0:T(8,128)S(1)} %get-tuple-element.125.norm_one_ref) | copy-start | bytes 4718596
  184.0 36.4 %copy-start.18 = (f32[512,768]{1,0:T(8,128)}, f32[512,768]{1,0:T(8,128)S(1)}, u32[]{:S(2)}) copy-start(f32[512,768]{1,0:T(8,128)S(1)} %get-tuple-element.123.norm_two_ref) | copy-start | bytes 4718596
  184.0 36.4 %copy-start.19 = (f32[512,768]{1,0:T(8,128)}, f32[512,768]{1,0:T(8,128)S(1)}, u32[]{:S(2)}) copy-start(f32[512,768]{1,0:T(8,128)S(1)} %get-tuple-element.99.state_ref) | copy-start | bytes 4718596
  184.0 34.8 %collective-permute-start.12 = (bf16[512,768]{1,0:T(8,128)(2,1)S(1)}, bf16[512,768]{1,0:T(8,128)(2,1)S(1)}, u32[]{:S(2)}, u32[]{:S(2)}) collective-permute-start(bf16[512,768]{1,0:T(8,128)(2,1)S(1)} %get-tuple-element.96), channel_id=1, source_target_pairs={{2,0},{3,1},{4,2},{5,3},{6,4},{7,5},{10,8},{11,9},{12,10},{13,11},... | collective-permute-start | bytes 2359304 | tf_op jit(solution)/shard_map/ppermute | solution.py:809
  185.3 33.5 %collective-permute-start.11 = (bf16[512,768]{1,0:T(8,128)(2,1)S(1)}, bf16[512,768]{1,0:T(8,128)(2,1)S(1)}, u32[]{:S(2)}, u32[]{:S(2)}) collective-permute-start(bf16[512,768]{1,0:T(8,128)(2,1)S(1)} %get-tuple-element.96), channel_id=1, source_target_pairs={{0,2},{1,3},{2,4},{3,5},{4,6},{5,7},{8,10},{9,11},{10,12},{11,13},... | collective-permute-start | bytes 2359304 | tf_op jit(solution)/shard_map/ppermute | solution.py:809
  220.4 11.6 %collective-permute-start.13 = (bf16[1536,768]{1,0:T(8,128)(2,1)}, bf16[1536,768]{1,0:T(8,128)(2,1)}, u32[]{:S(2)}, u32[]{:S(2)}) collective-permute-start(bf16[1536,768]{1,0:T(8,128)(2,1)} %pad_maximum_fusion.1), channel_id=1, source_target_pairs={{0,8},{1,9},{2,10},{3,11},{4,12},{5,13},{6,14},{7,15},{8,0},{9,1},... | collective-permute-start | bytes 7077896 | tf_op jit(solution)/shard_map/ppermute | solution.py:809
  221.1 72.0 %collective-permute-start.16 = (bf16[512,768]{1,0:T(8,128)(2,1)}, bf16[512,768]{1,0:T(8,128)(2,1)}, u32[]{:S(2)}, u32[]{:S(2)}) collective-permute-start(bf16[512,768]{1,0:T(8,128)(2,1)} %param.11), channel_id=1, source_target_pairs={{0,0},{1,8},{2,2},{3,10},{4,4},{5,12},{6,6},{7,14},{8,1},{9,9},{10... | collective-permute-start | bytes 2359304 | tf_op jit(solution)/shard_map/ppermute | solution.py:809
  231.9 10.3 %copy-start.13 = (bf16[512,384]{1,0:T(8,128)(2,1)}, bf16[512,384]{1,0:T(8,128)(2,1)S(1)}, u32[]{:S(2)}) copy-start(bf16[512,384]{1,0:T(8,128)(2,1)S(1)} %fusion.11.a_ref) | copy-start | bytes 1179652
  242.2 17.0 %copy-start.22 = (bf16[3072,768]{1,0:T(8,128)(2,1)}, bf16[3072,768]{1,0:T(8,128)(2,1)S(1)}, u32[]{:S(2)}) copy-start(bf16[3072,768]{1,0:T(8,128)(2,1)S(1)} %add_convert_fusion.kv_ref) | copy-start | bytes 14155780
  261.8 13.7 %copy-start.39 = (f32[24,1024]{1,0:T(8,128)}, f32[24,1024]{1,0:T(8,128)S(1)}, u32[]{:S(2)}) copy-start(f32[24,1024]{1,0:T(8,128)S(1)} %get-tuple-element.118.lse_ref) | copy-start | bytes 294916
  261.8 13.7 %collective-permute-start.14 = (bf16[512,384]{1,0:T(8,128)(2,1)S(1)}, bf16[512,384]{1,0:T(8,128)(2,1)S(1)}, u32[]{:S(2)}, u32[]{:S(2)}) collective-permute-start(bf16[512,384]{1,0:T(8,128)(2,1)S(1)} %get-tuple-element.98), channel_id=1, source_target_pairs={{0,8},{1,9},{2,10},{3,11},{4,12},{5,13},{6,14},{7,15},{8,0},{9,1},... | collective-permute-start | bytes 1179656 | tf_op jit(solution)/shard_map/ppermute | solution.py:809
  330.0 353.3 %reduce-scatter.3.cloned.1.call-start = ((), (), s32[]{:S(2)}) async-start(), calls=%async_computation.4 | async-start | bytes 11354112 | tf_op jit(solution)/shard_map/reduce_scatter | solution.py:1661
  330.0 1.8 collective-permute-start.17
  332.6 34.4 %copy-start.57 = (bf16[768,384]{1,0:T(8,128)(2,1)S(1)}, bf16[768,384]{1,0:T(8,128)(2,1)}, u32[]{:S(2)}) copy-start(bf16[768,384]{1,0:T(8,128)(2,1)} %copy-done.56) | copy-start | bytes 1769476
  332.6 34.4 %copy-start.59 = (bf16[768,384]{1,0:T(8,128)(2,1)S(1)}, bf16[768,384]{1,0:T(8,128)(2,1)}, u32[]{:S(2)}) copy-start(bf16[768,384]{1,0:T(8,128)(2,1)} %copy-done.58) | copy-start | bytes 1769476
  379.2 6.1 collective-permute-start.18
  384.7 24.4 %slice-start.1 = ((s8[4718592]{0:T(1024)(128)(4,1)}), s8[524288]{0:T(1024)(128)(4,1)S(1)}, s32[]{:S(2)}) async-start(s8[4718592]{0:T(1024)(128)(4,1)} %bitcast.195), calls=%async_computation.7 | async-start | bytes 1048576
  385.4 23.8 %slice-start.2 = ((s8[4718592]{0:T(1024)(128)(4,1)}), s8[4194304]{0:T(1024)(128)(4,1)S(1)}, s32[]{:S(2)}) async-start(s8[4718592]{0:T(1024)(128)(4,1)} %bitcast.195), calls=%async_computation.8 | async-start | bytes 8388608
  390.0 44.3 %collective-permute-start.20 = (bf16[512,768]{1,0:T(8,128)(2,1)S(1)}, bf16[512,768]{1,0:T(8,128)(2,1)S(1)}, u32[]{:S(2)}, u32[]{:S(2)}) collective-permute-start(bf16[512,768]{1,0:T(8,128)(2,1)S(1)} %get-tuple-element.200), channel_id=1, source_target_pairs={{0,2},{1,3},{2,4},{3,5},{4,6},{5,7},{8,10},{9,11},{10,12},{11,13},... | collective-permute-start | bytes 2359304 | tf_op jit(solution)/shard_map/ppermute | solution.py:809
  407.2 28.8 %copy-start.54 = (f32[512,768]{1,0:T(8,128)S(1)}, f32[512,768]{1,0:T(8,128)}, u32[]{:S(2)}) copy-start(f32[512,768]{1,0:T(8,128)} %get-tuple-element.113) | copy-start | bytes 4718596
  407.2 28.8 %collective-permute-start.19 = (bf16[512,768]{1,0:T(8,128)(2,1)S(1)}, bf16[512,768]{1,0:T(8,128)(2,1)S(1)}, u32[]{:S(2)}, u32[]{:S(2)}) collective-permute-start(bf16[512,768]{1,0:T(8,128)(2,1)S(1)} %get-tuple-element.199), channel_id=1, source_target_pairs={{2,0},{3,1},{4,2},{5,3},{6,4},{7,5},{10,8},{11,9},{12,10},{13,11},... | collective-permute-start | bytes 2359304 | tf_op jit(solution)/shard_map/ppermute | solution.py:809
  461.2 10.0 %copy-start.32 = (bf16[512,384]{1,0:T(8,128)(2,1)}, bf16[512,384]{1,0:T(8,128)(2,1)S(1)}, u32[]{:S(2)}) copy-start(bf16[512,384]{1,0:T(8,128)(2,1)S(1)} %get-tuple-element.132.a_grad_ref) | copy-start | bytes 1179652
  474.5 7.9 %collective-permute-start.21 = (bf16[512,384]{1,0:T(8,128)(2,1)S(1)}, bf16[512,384]{1,0:T(8,128)(2,1)S(1)}, u32[]{:S(2)}, u32[]{:S(2)}) collective-permute-start(bf16[512,384]{1,0:T(8,128)(2,1)S(1)} %get-tuple-element.133), channel_id=1, source_target_pairs={{0,8},{1,9},{2,10},{3,11},{4,12},{5,13},{6,14},{7,15},{8,0},{9,1},... | collective-permute-start | bytes 1179656 | tf_op jit(solution)/shard_map/ppermute | solution.py:809
  481.0 42.7 %collective-permute-start.22 = (bf16[2,4,4,48,384]{4,3,2,1,0:T(8,128)(2,1)S(1)}, bf16[2,4,4,48,384]{4,3,2,1,0:T(8,128)(2,1)S(1)}, u32[]{:S(2)}, u32[]{:S(2)}) collective-permute-start(bf16[2,4,4,48,384]{4,3,2,1,0:T(8,128)(2,1)S(1)} %slice_bitcast_fusion.1), channel_id=1, source_target_pairs={{0,1},{1,0},{2,3},{3,2},{4,5},{5,4},{6,7},{7,6},{8,9},{9,8},{10,11... | collective-permute-start | bytes 3538952 | tf_op jit(solution)/shard_map/ppermute | solution.py:809
  539.4 37.1 %collective-permute-start.27 = (bf16[2,4,4,48,384]{4,3,2,1,0:T(8,128)(2,1)S(1)}, bf16[2,4,4,48,384]{4,3,2,1,0:T(8,128)(2,1)S(1)}, u32[]{:S(2)}, u32[]{:S(2)}) collective-permute-start(bf16[2,4,4,48,384]{4,3,2,1,0:T(8,128)(2,1)S(1)} %slice_bitcast_fusion), channel_id=1, source_target_pairs={{0,16},{1,17},{2,18},{3,19},{4,20},{5,21},{6,22},{7,23},{8,24},{9,... | collective-permute-start | bytes 3538952 | tf_op jit(solution)/shard_map/ppermute | solution.py:809
  547.0 29.5 %copy-start.43 = (bf16[2,2,4,4,48,384]{5,4,3,2,1,0:T(8,128)(2,1)S(1)}, bf16[2,2,4,4,48,384]{5,4,3,2,1,0:T(8,128)(2,1)}, u32[]{:S(2)}) copy-start(bf16[2,2,4,4,48,384]{5,4,3,2,1,0:T(8,128)(2,1)} %spread_terms.3) | copy-start | bytes 7077892
  547.2 34.4 %copy-start.42 = (bf16[2,2,4,4,48,384]{5,4,3,2,1,0:T(8,128)(2,1)S(1)}, bf16[2,2,4,4,48,384]{5,4,3,2,1,0:T(8,128)(2,1)}, u32[]{:S(2)}) copy-start(bf16[2,2,4,4,48,384]{5,4,3,2,1,0:T(8,128)(2,1)} %spread_terms.2) | copy-start | bytes 7077892
  547.2 105.6 %collective-permute-start.23 = (bf16[1536,768]{1,0:T(8,128)(2,1)S(1)}, bf16[1536,768]{1,0:T(8,128)(2,1)S(1)}, u32[]{:S(2)}, u32[]{:S(2)}) collective-permute-start(bf16[1536,768]{1,0:T(8,128)(2,1)S(1)} %pad_maximum_fusion.3), channel_id=1, source_target_pairs={{0,8},{1,9},{2,10},{3,11},{4,12},{5,13},{6,14},{7,15},{8,0},{9,1},... | collective-permute-start | bytes 7077896 | tf_op jit(solution)/shard_map/ppermute | solution.py:809
  576.8 26.9 %collective-permute-start.28 = (bf16[4,4,48,384]{3,2,1,0:T(8,128)(2,1)S(1)}, bf16[4,4,48,384]{3,2,1,0:T(8,128)(2,1)S(1)}, u32[]{:S(2)}, u32[]{:S(2)}) collective-permute-start(bf16[4,4,48,384]{3,2,1,0:T(8,128)(2,1)S(1)} %get-tuple-element.189), channel_id=1, source_target_pairs={{0,1},{1,0},{2,3},{3,2},{4,5},{5,4},{6,7},{7,6},{8,9},{9,8},{10,11... | collective-permute-start | bytes 1769480 | tf_op jit(solution)/shard_map/ppermute | solution.py:809
  581.9 22.9 %collective-permute-start.29 = (bf16[4,4,48,384]{3,2,1,0:T(8,128)(2,1)S(1)}, bf16[4,4,48,384]{3,2,1,0:T(8,128)(2,1)S(1)}, u32[]{:S(2)}, u32[]{:S(2)}) collective-permute-start(bf16[4,4,48,384]{3,2,1,0:T(8,128)(2,1)S(1)} %get-tuple-element.191), channel_id=1, source_target_pairs={{0,16},{1,17},{2,18},{3,19},{4,20},{5,21},{6,22},{7,23},{8,24},{9,... | collective-permute-start | bytes 1769480 | tf_op jit(solution)/shard_map/ppermute | solution.py:809
  605.2 47.4 %collective-permute-start.30 = (bf16[2,8,48,384]{3,2,1,0:T(8,128)(2,1)S(1)}, bf16[2,8,48,384]{3,2,1,0:T(8,128)(2,1)S(1)}, u32[]{:S(2)}, u32[]{:S(2)}) collective-permute-start(bf16[2,8,48,384]{3,2,1,0:T(8,128)(2,1)S(1)} %get-tuple-element.196), channel_id=1, source_target_pairs={{0,4},{1,5},{2,6},{3,7},{4,0},{5,1},{6,2},{7,3},{8,12},{9,13},{10,... | collective-permute-start | bytes 1769480 | tf_op jit(solution)/shard_map/ppermute | solution.py:809
  652.7 9.6 %collective-permute-start.31 = (bf16[8,48,384]{2,1,0:T(8,128)(2,1)S(1)}, bf16[8,48,384]{2,1,0:T(8,128)(2,1)S(1)}, u32[]{:S(2)}, u32[]{:S(2)}) collective-permute-start(bf16[8,48,384]{2,1,0:T(8,128)(2,1)S(1)} %fusion.51), channel_id=1, source_target_pairs={{0,2},{1,3},{2,0},{3,1},{4,6},{5,7},{6,4},{7,5},{8,10},{9,11},{10,... | collective-permute-start | bytes 884744 | tf_op jit(solution)/shard_map/ppermute | solution.py:809
  655.6 29.9 %copy-start.53 = (f32[512,768]{1,0:T(8,128)S(1)}, f32[512,768]{1,0:T(8,128)}, u32[]{:S(2)}) copy-start(f32[512,768]{1,0:T(8,128)} %get-tuple-element.131) | copy-start | bytes 4718596
  656.8 26.5 %collective-permute-start.25 = (bf16[512,768]{1,0:T(8,128)(2,1)}, bf16[512,768]{1,0:T(8,128)(2,1)}, u32[]{:S(2)}, u32[]{:S(2)}) collective-permute-start(bf16[512,768]{1,0:T(8,128)(2,1)} %get-tuple-element.198), channel_id=1, source_target_pairs={{0,2},{1,3},{2,4},{3,5},{4,6},{5,7},{8,10},{9,11},{10,12},{11,13},... | collective-permute-start | bytes 2359304 | tf_op jit(solution)/shard_map/ppermute | solution.py:809
  661.0 24.4 %collective-permute-start.24 = (bf16[512,768]{1,0:T(8,128)(2,1)}, bf16[512,768]{1,0:T(8,128)(2,1)}, u32[]{:S(2)}, u32[]{:S(2)}) collective-permute-start(bf16[512,768]{1,0:T(8,128)(2,1)} %get-tuple-element.197), channel_id=1, source_target_pairs={{2,0},{3,1},{4,2},{5,3},{6,4},{7,5},{10,8},{11,9},{12,10},{13,11},... | collective-permute-start | bytes 2359304 | tf_op jit(solution)/shard_map/ppermute | solution.py:809
  662.5 10.3 %collective-permute-start.32 = (bf16[8,48,384]{2,1,0:T(8,128)(2,1)S(1)}, bf16[8,48,384]{2,1,0:T(8,128)(2,1)S(1)}, u32[]{:S(2)}, u32[]{:S(2)}) collective-permute-start(bf16[8,48,384]{2,1,0:T(8,128)(2,1)S(1)} %fusion.29), channel_id=1, source_target_pairs={{0,16},{1,17},{2,18},{3,19},{4,20},{5,21},{6,22},{7,23},{8,24},{9,... | collective-permute-start | bytes 884744 | tf_op jit(solution)/shard_map/ppermute | solution.py:809
  662.5 31.7 %collective-permute-start.15 = (bf16[512,768]{1,0:T(8,128)(2,1)}, bf16[512,768]{1,0:T(8,128)(2,1)S(1)}, u32[]{:S(2)}, u32[]{:S(2)}) collective-permute-start(bf16[512,768]{1,0:T(8,128)(2,1)} %get-tuple-element.238), channel_id=1, source_target_pairs={{0,0},{1,8},{2,2},{3,10},{4,4},{5,12},{6,6},{7,14},{8,1},{9,9},{10... | collective-permute-start | bytes 2359304 | tf_op jit(solution)/shard_map/ppermute | solution.py:809
  672.8 21.4 %collective-permute-start.33 = (bf16[2,8,48,384]{3,2,1,0:T(8,128)(2,1)S(1)}, bf16[2,8,48,384]{3,2,1,0:T(8,128)(2,1)}, u32[]{:S(2)}, u32[]{:S(2)}) collective-permute-start(bf16[2,8,48,384]{3,2,1,0:T(8,128)(2,1)S(1)} %get-tuple-element.209), channel_id=1, source_target_pairs={{0,8},{1,9},{2,10},{3,11},{4,12},{5,13},{6,14},{7,15},{8,0},{9,1},... | collective-permute-start | bytes 1769480 | tf_op jit(solution)/shard_map/ppermute | solution.py:809
  672.9 19.1 %collective-permute-start.36 = (bf16[224,768]{1,0:T(8,128)(2,1)}, bf16[224,768]{1,0:T(8,128)(2,1)}, u32[]{:S(2)}, u32[]{:S(2)}) collective-permute-start(bf16[224,768]{1,0:T(8,128)(2,1)} %bitcast.204), channel_id=1, source_target_pairs={{0,16},{1,17},{2,18},{3,19},{4,20},{5,21},{6,22},{7,23},{8,24},{9,... | collective-permute-start | bytes 1032200 | tf_op jit(solution)/shard_map/ppermute | solution.py:809
  683.3 9.8 %collective-permute-start.34 = (bf16[224,768]{1,0:T(8,128)(2,1)}, bf16[224,768]{1,0:T(8,128)(2,1)S(1)}, u32[]{:S(2)}, u32[]{:S(2)}) collective-permute-start(bf16[224,768]{1,0:T(8,128)(2,1)} %bitcast.205), channel_id=1, source_target_pairs={{0,16},{1,17},{2,18},{3,19},{4,20},{5,21},{6,22},{7,23},{8,24},{9,... | collective-permute-start | bytes 1032200 | tf_op jit(solution)/shard_map/ppermute | solution.py:809
  687.7 13.9 %collective-permute-start.26 = (bf16[512,768]{1,0:T(8,128)(2,1)S(1)}, bf16[512,768]{1,0:T(8,128)(2,1)S(1)}, u32[]{:S(2)}, u32[]{:S(2)}) collective-permute-start(bf16[512,768]{1,0:T(8,128)(2,1)S(1)} %fusion.2), channel_id=1, source_target_pairs={{0,0},{1,8},{2,2},{3,10},{4,4},{5,12},{6,6},{7,14},{8,1},{9,9},{10... | collective-permute-start | bytes 2359304 | tf_op jit(solution)/shard_map/ppermute | solution.py:809
  693.1 9.8 %collective-permute-start.37 = (bf16[2,224,768]{2,1,0:T(8,128)(2,1)S(1)}, bf16[2,224,768]{2,1,0:T(8,128)(2,1)S(1)}, u32[]{:S(2)}, u32[]{:S(2)}) collective-permute-start(bf16[2,224,768]{2,1,0:T(8,128)(2,1)S(1)} %get-tuple-element.206), channel_id=1, source_target_pairs={{0,8},{1,9},{2,10},{3,11},{4,12},{5,13},{6,14},{7,15},{8,0},{9,1},... | collective-permute-start | bytes 2064392 | tf_op jit(solution)/shard_map/ppermute | solution.py:809
  693.3 9.8 %collective-permute-start.35 = (bf16[2,224,768]{2,1,0:T(8,128)(2,1)S(1)}, bf16[2,224,768]{2,1,0:T(8,128)(2,1)S(1)}, u32[]{:S(2)}, u32[]{:S(2)}) collective-permute-start(bf16[2,224,768]{2,1,0:T(8,128)(2,1)S(1)} %get-tuple-element.208), channel_id=1, source_target_pairs={{0,8},{1,9},{2,10},{3,11},{4,12},{5,13},{6,14},{7,15},{8,0},{9,1},... | collective-permute-start | bytes 2064392 | tf_op jit(solution)/shard_map/ppermute | solution.py:809
  (50 other events, 144.5 us)
Sparse Core Ops, SparseCore 0:
  39.9 117.1 all-gather.2
  160.6 106.3 all-gather.4
  330.1 162.0 reduce-scatter.4
  498.1 174.8 reduce-scatter.2

commit v4 on v3

--- a/solution.py
+++ b/solution.py
@@ -899,11 +899,12 @@
     share, width = b_out.shape[-2:]
     wide = expand_ref.shape[-1] // width
     for layer, ref in enumerate((b_out, c_out)):
-        ref[0] = mixer_ref[layer]
+        deep = reduce_ref.shape[1] // share
+        for piece in range(deep):
+            ref[piece] = reduce_ref[layer, piece * share : (piece + 1) * share, :]
         for column in range(wide):
-            ref[1 + column] = expand_ref[layer, :, column * width : (column + 1) * width]
-        for piece in range(reduce_ref.shape[1] // share):
-            ref[1 + wide + piece] = reduce_ref[layer, piece * share : (piece + 1) * share, :]
+            ref[deep + column] = expand_ref[layer, :, column * width : (column + 1) * width]
+        ref[deep + wide] = mixer_ref[layer]
     far = c_out.shape[0]
     for column in range(3):
         b_out[far + column] = project_ref[0, :, column * width : (column + 1) * width]
@@ -1136,14 +1137,33 @@
     return (weighted - row_mean(weighted) - norm * row_mean(weighted * norm)) * scale
 
 
+def join_rows(ref, whole_scr):
+    quarters, shards, pieces, share, unused = ref.shape
+    for shard in range(shards):
+        for quarter in range(quarters):
+            for piece in range(pieces):
+                begin_at = ((shard * quarters + quarter) * pieces + piece) * share
+                whole_scr[begin_at : begin_at + share, :] = ref[quarter, shard, piece]
+
+
+def piece_specs(pieces, steps):
+    quarters, shards, unused, share, width = pieces.shape
+    deep = steps
+    return [
+        pl.BlockSpec((quarters, shards, 1, share, width), lambda j, me: (0, 0, deep + j, 0, 0)),
+        pl.BlockSpec((quarters, shards // steps, deep, share, width), lambda j, me: (0, j, 0, 0, 0)),
+        pl.BlockSpec((quarters, shards, 1, share, width), lambda j, me: (0, 0, deep + steps, 0, 0)),
+    ]
+
+
 def tail_forward_kernel(
     me,
     own_ref,
     far_ref,
     state_ref,
-    mixer_ref,
     expand_ref,
     reduce_ref,
+    mixer_ref,
     bias_in_ref,
     vector_ref,
     mix_out,
@@ -1158,6 +1178,8 @@
     state_low_out,
     wide_scr,
     total_scr,
+    one_scr,
+    two_scr,
 ):
     step = pl.program_id(0)
     half = own_ref.shape[1]
@@ -1166,17 +1188,20 @@
     def begin():
         mix_out[:, pl.ds(pl.multiple_of(me[1] * half, 128), half)] = own_ref[...]
         mix_out[:, pl.ds(pl.multiple_of((1 - me[1]) * half, 128), half)] = far_ref[...]
-        branch = jnp.dot(mix_out[...], mixer_ref[...], preferred_element_type=jnp.float32)
-        norm, scale = standardized(state_ref[...].astype(jnp.float32) + (branch + vector_ref[0:1]))
+        join_rows(mixer_ref, one_scr)
+        branch = jnp.dot(mix_out[...], one_scr[...], preferred_element_type=jnp.float32)
+        norm, scale = standardized(state_ref[...].astype(jnp.float32) + (branch + vector_ref[2:3]))
         norm_one_out[...] = norm
         scale_one_out[...] = jnp.broadcast_to(scale, scale_one_out.shape)
-        wide = norm * vector_ref[1:2] + vector_ref[2:3]
+        wide = norm * vector_ref[10:11] + vector_ref[3:4]
         wide_scr[...] = wide
         low_out[...] = wide.astype(jnp.bfloat16)
         total_scr[...] = jnp.zeros_like(total_scr)
 
+    join_rows(expand_ref, one_scr)
+    join_rows(reduce_ref, two_scr)
     before = (
-        jnp.dot(low_out[...], expand_ref[...], preferred_element_type=jnp.float32)
+        jnp.dot(low_out[...], one_scr[...], preferred_element_type=jnp.float32)
         + bias_in_ref[...]
     )
     normal = 0.5 * (1.0 + lax.erf(before * 0.7071067811865476))
@@ -1184,29 +1209,26 @@
     active = (before * normal).astype(jnp.bfloat16)
     active_out[...] = active
     slope_out[...] = normal + before * density
-    total_scr[...] += jnp.dot(active, reduce_ref[...], preferred_element_type=jnp.float32)
+    total_scr[...] += jnp.dot(active, two_scr[...], preferred_element_type=jnp.float32)
 
     @pl.when(step == pl.num_programs(0) - 1)
     def end():
-        norm, scale = standardized(wide_scr[...] + (total_scr[...] + vector_ref[3:4]))
+        norm, scale = standardized(wide_scr[...] + (total_scr[...] + vector_ref[8:9]))
         norm_two_out[...] = norm
         scale_two_out[...] = jnp.broadcast_to(scale, scale_two_out.shape)
-        state = norm * vector_ref[4:5] + vector_ref[5:6]
+        state = norm * vector_ref[11:12] + vector_ref[9:10]
         state_out[...] = state
         state_low_out[...] = state.astype(jnp.bfloat16)
 
 
-FEED_TILE = 512
-
-
-def tail_forward(me, own_mix, far_mix, state, mixer, expand, reduce, bias_in, vectors):
+def tail_forward(me, own_mix, far_mix, state, pieces, bias_in, vectors):
     rows, width = state.shape
-    hidden_units = expand.shape[1]
-    steps = hidden_units // FEED_TILE
+    hidden_units = bias_in.shape[1]
+    steps = hidden_units // width
     whole = whole_block((rows, width))
     halves = whole_block((rows, width // 2))
     scale = whole_block((rows, 128))
-    tile = pl.BlockSpec((rows, FEED_TILE), lambda j, me: (0, j))
+    tile = pl.BlockSpec((rows, width), lambda j, me: (0, j))
 
     def shaped(columns, kind):
         return jax.ShapeDtypeStruct((rows, columns), kind)
@@ -1232,16 +1254,15 @@
                 halves,
                 halves,
                 whole,
-                whole_block((width, width)),
-                pl.BlockSpec((width, FEED_TILE), lambda j, me: (0, j)),
-                pl.BlockSpec((FEED_TILE, width), lambda j, me: (j, 0)),
-                pl.BlockSpec((1, FEED_TILE), lambda j, me: (0, j)),
-                whole_block((8, width)),
-            ],
+            ]
+            + piece_specs(pieces, steps)
+            + [pl.BlockSpec((1, width), lambda j, me: (0, j)), whole_block(vectors.shape)],
             out_specs=[whole, whole, scale, whole, tile, tile, whole, scale, whole, whole],
             scratch_shapes=[
                 pltpu.VMEM((rows, width), jnp.float32),
                 pltpu.VMEM((rows, width), jnp.float32),
+                pltpu.VMEM((width, width), jnp.bfloat16),
+                pltpu.VMEM((width, width), jnp.bfloat16),
             ],
         ),
         compiler_params=pltpu.CompilerParams(vmem_limit_bytes=44 * 2**20),
@@ -1251,7 +1272,7 @@
             transcendentals=2 * rows * hidden_units,
         ),
         name="tail_forward",
-    )(me, own_mix, far_mix, state, mixer, expand, reduce, bias_in, vectors)
+    )(me, own_mix, far_mix, state, *[in_main(pieces)] * 3, bias_in, vectors)
 
 
 def tail_backward_kernel(
@@ -1280,6 +1301,8 @@
     wide_scr,
     feed_scr,
     total_scr,
+    one_scr,
+    two_scr,
 ):
     step = pl.program_id(0)
     half = own_out.shape[1]
@@ -1288,7 +1311,7 @@
     def begin():
         grad = grad_ref[...]
         norm = norm_two_ref[...]
-        wide = standard_back(grad, norm, scale_two_ref[:, 0:1], vector_ref[4:5])
+        wide = standard_back(grad, norm, scale_two_ref[:, 0:1], vector_ref[11:12])
         wide_scr[...] = wide
         feed = wide.astype(jnp.bfloat16)
         feed_scr[...] = feed
@@ -1298,26 +1321,29 @@
         vector_out[5:6] = column_sum(grad)
         total_scr[...] = jnp.zeros_like(total_scr)
 
+    join_rows(expand_ref, one_scr)
+    join_rows(reduce_ref, two_scr)
     feed = feed_scr[...]
-    active_grad = turned_dot(feed, reduce_ref[...])
+    active_grad = turned_dot(feed, two_scr[...])
     before = (active_grad * slope_ref[...]).astype(jnp.bfloat16)
     bias_in_out[...] = column_sum(before.astype(jnp.float32))
     reduce_out[...] = across_dot(active_ref[...], feed).astype(jnp.bfloat16)
     expand_out[...] = across_dot(low_ref[...], before).astype(jnp.bfloat16)
-    total_scr[...] += turned_dot(before, expand_ref[...])
+    total_scr[...] += turned_dot(before, one_scr[...])
 
     @pl.when(step == pl.num_programs(0) - 1)
     def end():
         grad = wide_scr[...] + total_scr[...]
         norm = norm_one_ref[...]
-        wide = standard_back(grad, norm, scale_one_ref[:, 0:1], vector_ref[1:2])
+        wide = standard_back(grad, norm, scale_one_ref[:, 0:1], vector_ref[10:11])
         sum_out[...] = wide
         branch = wide.astype(jnp.bfloat16)
         vector_out[0:1] = column_sum(branch.astype(jnp.float32))
         vector_out[1:2] = column_sum(grad * norm)
         vector_out[2:3] = column_sum(grad)
         mixer_out[...] = across_dot(mix_ref[...], branch).astype(jnp.bfloat16)
-        mixed = turned_dot(branch, mixer_ref[...]).astype(jnp.bfloat16)
+        join_rows(mixer_ref, one_scr)
+        mixed = turned_dot(branch, one_scr[...]).astype(jnp.bfloat16)
         total_scr[...] = mixed.astype(jnp.float32)
         own = total_scr[:, pl.ds(pl.multiple_of(me[1] * half, 128), half)]
         far = total_scr[:, pl.ds(pl.multiple_of((1 - me[1]) * half, 128), half)]
@@ -1325,20 +1351,19 @@
         far_out[...] = far.astype(jnp.bfloat16)
 
 
-def tail_backward(me, grad, kept, weights, vectors):
+def tail_backward(me, grad, kept, pieces, vectors):
     norm_two, scale_two, norm_one, scale_one, low, mixed, slope, active = kept
-    mixer, expand, reduce = weights
     rows, width = grad.shape
-    hidden_units = expand.shape[1]
-    steps = hidden_units // FEED_TILE
+    hidden_units = active.shape[1]
+    steps = hidden_units // width
     whole = whole_block((rows, width))
     halves = whole_block((rows, width // 2))
     scale = whole_block((rows, 128))
     square = whole_block((width, width))
-    tile = pl.BlockSpec((rows, FEED_TILE), lambda j, me: (0, j))
-    across = pl.BlockSpec((width, FEED_TILE), lambda j, me: (0, j))
-    down = pl.BlockSpec((FEED_TILE, width), lambda j, me: (j, 0))
-    line = pl.BlockSpec((1, FEED_TILE), lambda j, me: (0, j))
+    tile = pl.BlockSpec((rows, width), lambda j, me: (0, j))
+    across = pl.BlockSpec((width, width), lambda j, me: (0, j))
+    down = pl.BlockSpec((width, width), lambda j, me: (j, 0))
+    line = pl.BlockSpec((1, width), lambda j, me: (0, j))
 
     def shaped(rows, columns, kind):
         return jax.ShapeDtypeStruct((rows, columns), kind)
@@ -1358,13 +1383,16 @@
         grid_spec=pltpu.PrefetchScalarGridSpec(
             num_scalar_prefetch=1,
             grid=(steps,),
-            in_specs=[whole, whole, scale, whole, scale, whole, whole, tile, tile, across, down]
-            + [square, whole_block((8, width))],
+            in_specs=[whole, whole, scale, whole, scale, whole, whole, tile, tile]
+            + piece_specs(pieces, steps)
+            + [whole_block(vectors.shape)],
             out_specs=[whole, halves, halves, square, across, down, line, whole_block((8, width))],
             scratch_shapes=[
                 pltpu.VMEM((rows, width), jnp.float32),
                 pltpu.VMEM((rows, width), jnp.bfloat16),
                 pltpu.VMEM((rows, width), jnp.float32),
+                pltpu.VMEM((width, width), jnp.bfloat16),
+                pltpu.VMEM((width, width), jnp.bfloat16),
             ],
         ),
         compiler_params=pltpu.CompilerParams(vmem_limit_bytes=48 * 2**20),
@@ -1385,9 +1413,7 @@
         mixed,
         slope,
         active,
-        expand,
-        reduce,
-        mixer,
+        *[in_main(pieces)] * 3,
         vectors,
     )
 
@@ -1509,20 +1535,23 @@
     far_shapes = [(share, width), (share, hidden_units), (deep, width)]
     far_count = far_last.shape[0]
     pieces = gather_all(far_first)
-    first_whole = [project_first] + unpack_weights_of(pieces, 0, far_count, far_kinds, far_shapes)
     project_last = unpack_weights_of(pieces, far_count, 3, ("columns",), [(share, 3 * width)])[0]
     project_last = jnp.concatenate(
         [half_of(project_last[:, i * width : (i + 1) * width], 1, core) for i in range(3)], axis=1
     )
-    last_whole = [project_last] + unpack_weights_of(
-        gather_all(far_last), 0, far_count, far_kinds, far_shapes
-    )
+    tail_pieces = [pieces, gather_all(far_last)]
     small_all = small_all[:, :small_rows].reshape(8, LAYERS, -1)
     weights = []
-    for layer_index, whole in enumerate([first_whole, last_whole]):
+    vector_rows = []
+    for layer_index, project in enumerate([project_first, project_last]):
         bias_vec = small_all[:, layer_index, :bias_count].reshape(-1)
         gain_vec = small_all[:, layer_index, bias_count:].reshape(-1)
-        weights.append(unpack_weights(whole + [bias_vec, gain_vec], width, hidden_units))
+        weights.append(
+            unpack_weights((project, None, None, None, bias_vec, gain_vec), width, hidden_units)
+        )
+        vector_rows.append(
+            jnp.concatenate([bias_vec, gain_vec]).astype(jnp.float32).reshape(-1, width)
+        )
 
     hidden_state = state_low.astype(jnp.float32)
     kept_list = []
@@ -1549,9 +1578,7 @@
         ).astype(jnp.bfloat16)
         own_mix, far_mix, own_wide, far_wide, lse = flash_forward(bounds, queries, key_value, low_line, high_line)
         far_mix = swap_core(far_mix)
-        tail_vectors = jnp.stack(
-            [bias_mix, gain_one, shift_one, bias_out, gain_two, shift_two, bias_mix, bias_mix]
-        )
+        tail_vectors = vector_rows[layer_index]
         (
             mixed_low,
             norm_one,
@@ -1564,7 +1591,7 @@
             hidden_state,
             next_low,
         ) = tail_forward(
-            me, own_mix, far_mix, hidden_state, mixing, expand, shrink, bias_in[None], tail_vectors
+            me, own_mix, far_mix, hidden_state, tail_pieces[layer_index], bias_in[None], tail_vectors
         )
         kept_list.append(
             (
@@ -1597,7 +1624,7 @@
             shrink_grad,
             bias_in_grad,
             vector_grads,
-        ) = tail_backward(me, state_grad, kept, (mixing, expand, shrink), tail_vectors)
+        ) = tail_backward(me, state_grad, kept, tail_pieces[layer_index], tail_vectors)
         bias_mix_grad, gain_one_grad, shift_one_grad, bias_out_grad, gain_two_grad, shift_two_grad = [
             vector_grads[i] for i in range(6)
         ]

time: 726 us -> 711 us (0.979)
  waiting for transfers between devices: 235 us -> 226 us
  local copies, waits for them, and re-layouts: 51.6 us -> 59.8 us
    pallas_call x3 -> x1, Pallas kernels: 21.1 us -> 4.69 us  [unpack_weights_of(): pl.pallas_call(functools.partial(unpack_kernel, kinds), out_shape=[pltpu....]
    pallas_call x2, Pallas kernels: 68.9 us -> 78 us  [flash_backward(): pl.pallas_call(flash_backward_kernel, out_shape=(jax.ShapeDtypeStruct((ro...]
    all_gather x2, waiting for transfers between devices: 14.4 us -> 6.74 us  [gather_all(): lax.all_gather(local.reshape(-1, width), BOTH, axis=0, tiled=False)]
    unnamed x161 -> x187, local copies, waits for them, and re-layouts: 28.4 us -> 27.2 us
  transfers between devices with their start and end apart: 42 -> 42, of which waited for: 19 -> 22; matrix products, arithmetic and copies ran while one was open for 15% -> 17% of each run, Pallas kernels for 27% -> 27%
where the time goes in v4:
time: 711 us; the launch traced here: 707 us
  waiting for transfers between devices  226 us (32%)
  Pallas kernels  225 us (32%)
  starting transfers between devices  80.9 us (11%)
  local copies, waits for them, and re-layouts  59.8 us (8%)
  matrix products  58 us (8%)
  other arithmetic  35.3 us (5%)
  between operations  21.8 us (3%)
    ppermute x38, waiting for transfers between devices, send(): return lax.ppermute(values, BOTH, device_pairs(place))  218 us
    ppermute x38, starting transfers between devices, send(): return lax.ppermute(values, BOTH, device_pairs(place))  80.8 us
    pallas_call x2, Pallas kernels, flash_backward(): pl.pallas_call(flash_backward_kernel, out_shape=(jax.ShapeDtypeStruct((ro...  78 us
    pallas_call x2, Pallas kernels, tail_backward(): pl.pallas_call(tail_backward_kernel, out_shape=[shaped(rows, width, jnp.f...  41.5 us
    pallas_call x2, Pallas kernels, flash_forward(): pl.pallas_call(flash_forward_kernel, out_shape=(jax.ShapeDtypeStruct((row...  41 us
    pallas_call x2, Pallas kernels, tail_forward(): pl.pallas_call(tail_forward_kernel, out_shape=[shaped(width, jnp.bfloat16...  29.2 us
    unnamed x187, local copies, waits for them, and re-layouts  27.2 us
    pallas_call x2, Pallas kernels, pack_terms(): pl.pallas_call(functools.partial(pack_kernel, kinds), out_shape=pltpu.HBM...  16.8 us
  transfers between devices with their start and end apart: 42, of which 22 were waited for; matrix products, arithmetic and copies ran while one was open for 17% of the time, Pallas kernels for 27%

profile of v4, /device:TPU:1, one launch (start us, length us, event | category | flops | bytes accessed | tf_op | source)
XLA Modules:
  0.0 706.7 jit_solution(2838800516760200748)
XLA Ops:
  7.2 4.5 collective-permute-start.1
  14.6 2.9 pick_quarters.1
  18.8 3.2 collective-permute-done
  23.1 2.8 collective-permute-start.2
  25.9 13.8 %collective-permute-done.2 = bf16[2,4,48,384]{3,2,1,0:T(8,128)(2,1)S(1)} collective-permute-done((bf16[2,4,48,384]{3,2,1,0:T(8,128)(2,1)S(1)}, bf16[2,4,48,384]{3,2,1,0:T(8,128)(2,1)S(1)}, u32[]{:S(2)}, u32[]{:S(2)}) %collective-permute-start.2) | collective-permute-done | bytes 294944 | tf_op jit(solution)/shard_map/ppermute | solution.py:809
  41.9 4.0 collective-permute-start.7
  47.7 22.9 %collective-permute-done.8 = bf16[512,768]{1,0:T(8,128)(2,1)S(1)} collective-permute-done((bf16[512,768]{1,0:T(8,128)(2,1)S(1)}, bf16[512,768]{1,0:T(8,128)(2,1)S(1)}, u32[]{:S(2)}, u32[]{:S(2)}) %collective-permute-start.8) | collective-permute-done | bytes 786464 | tf_op jit(solution)/shard_map/ppermute | solution.py:809
  84.4 6.3 collective-permute-done.3
  93.3 11.9 %collective-permute-done.4 = bf16[2,4,2,48,384]{4,3,2,1,0:T(8,128)(2,1)S(1)} collective-permute-done((bf16[2,4,2,48,384]{4,3,2,1,0:T(8,128)(2,1)S(1)}, bf16[2,4,2,48,384]{4,3,2,1,0:T(8,128)(2,1)S(1)}, u32[]{:S(2)}, u32[]{:S(2)}) %collective-permute-start.4) | collective-permute-done | bytes 589856 | tf_op jit(solution)/shard_map/ppermute | solution.py:809
  105.3 3.6 collective-permute-done.6
  112.0 2.2 fusion.9.a_ref
  116.3 3.4 constant_dynamic-update-slice_fusion.2
  119.7 6.6 add_convert_fusion.1.kv_ref
  126.3 20.0 %flash_forward.2 = (bf16[512,384]{1,0:T(8,128)(2,1)S(1)}, bf16[512,384]{1,0:T(8,128)(2,1)S(1)}, f32[512,384]{1,0:T(8,128)S(1)}, f32[512,384]{1,0:T(8,128)S(1)}, f32[24,1024]{1,0:T(8,128)S(1)}) custom-call(s32[10]{0:T(128)S(1)} %stack.165.bounds, bf16[512,384]{1,0:T(8,128)(2,1)S(1)} %fusion.9.a_ref, bf16[512,384]{1,0:T(8,128)(2,1)S(1)} %fusion.10.b_ref, ...), custom_call_target="tpu_custom_call" | custom-call | flops 4026531840 | bytes 12582912 | tf_op jit(solution)/shard_map/flash_forward/pallas_call | solution.py:724
  152.0 6.7 all-gather.3.cloned.1.call-done
  160.7 14.5 %tail_forward.2 = (bf16[512,768]{1,0:T(8,128)(2,1)S(1)}, f32[512,768]{1,0:T(8,128)S(1)}, f32[512,128]{1,0:T(8,128)S(1)}, bf16[512,768]{1,0:T(8,128)(2,1)S(1)}, b...) custom-call(s32[4]{0:T(128)S(1)} %copy-done.21, ...), custom_call_target="tpu_custom_call" | custom-call | flops 5435817984 | bytes 33554432 | tf_op jit(solution)/shard_map/tail_forward/pallas_call | solution.py:1236
  178.3 4.0 collective-permute-start.11
  182.3 29.6 %collective-permute-done.12 = bf16[512,768]{1,0:T(8,128)(2,1)S(1)} collective-permute-done((bf16[512,768]{1,0:T(8,128)(2,1)S(1)}, bf16[512,768]{1,0:T(8,128)(2,1)S(1)}, u32[]{:S(2)}, u32[]{:S(2)}) %collective-permute-start.12) | collective-permute-done | bytes 786464 | tf_op jit(solution)/shard_map/ppermute | solution.py:809
  215.2 3.0 collective-permute-start.16
  218.6 4.7 unpack_weights.1
  223.3 2.3 fusion.68
  231.6 2.1 copy-done.70
  233.7 4.0 add_convert_fusion.kv_ref
  237.9 21.0 %flash_forward.3 = (bf16[512,384]{1,0:T(8,128)(2,1)S(1)}, bf16[512,384]{1,0:T(8,128)(2,1)}, f32[512,384]{1,0:T(8,128)S(1)}, f32[512,384]{1,0:T(8,128)S(1)}, f32[24,1024]{1,0:T(8,128)S(1)}) custom-call(s32[10]{0:T(128)S(1)} %stack.165.bounds, bf16[512,384]{1,0:T(8,128)(2,1)S(1)} %fusion.11.a_ref, bf16[512,384]{1,0:T(8,128)(2,1)S(1)} %fusion.12.b_ref, ...), custom_call_target="tpu_custom_call" | custom-call | flops 4026531840 | bytes 12582912 | tf_op jit(solution)/shard_map/flash_forward/pallas_call | solution.py:724
  262.0 4.2 collective-permute-start.14
  270.4 14.7 %tail_forward.3 = (bf16[512,768]{1,0:T(8,128)(2,1)S(1)}, f32[512,768]{1,0:T(8,128)S(1)}, f32[512,128]{1,0:T(8,128)S(1)}, bf16[512,768]{1,0:T(8,128)(2,1)S(1)}, b...) custom-call(s32[4]{0:T(128)S(1)} %copy-done.21, ...), custom_call_target="tpu_custom_call" | custom-call | flops 5435817984 | bytes 33554432 | tf_op jit(solution)/shard_map/tail_forward/pallas_call | solution.py:1236
  285.2 3.4 convert_multiply_fusion
  288.5 20.7 %tail_backward.2 = (f32[512,768]{1,0:T(8,128)S(1)}, bf16[512,384]{1,0:T(8,128)(2,1)S(1)}, bf16[512,384]{1,0:T(8,128)(2,1)S(1)}, bf16[768,768]{1,0:T(8,128)(2,1)S...) custom-call(s32[4]{0:T(128)S(1)} %copy-done.21, ...), custom_call_target="tpu_custom_call" | custom-call | flops 10871635968 | bytes 41943040 | tf_op jit(solution)/shard_map/tail_backward/pallas_call | solution.py:1371
  313.4 8.4 %pack_terms.3 = bf16[4,8,224,768]{3,2,1,0:T(8,128)(2,1)} custom-call(bf16[8,4,24,768]{3,2,1,0:T(8,128)(2,1)} %bitcast.163, bf16[8,4,24,3072]{3,2,1,0:T(8,128)(2,1)} %bitcast.190, bf16[8,4,96,768]{3,2,1,0:T(8,128)(2,1)} %bitcast.191, bf16[4,8,8,768]{3,2,1,0:T(8,128)(2,1)S(1)} %pad.29.refs_3_), custom_call_target="tpu_custom_call" | custom-call | bytes 22020096 | tf_op jit(solution)/shard_map/pack_terms/pallas_call | solution.py:964
  324.6 39.0 %flash_backward.2 = (bf16[512,384]{1,0:T(8,128)(2,1)}, bf16[512,384]{1,0:T(8,128)(2,1)}, bf16[3072,768]{1,0:T(8,128)(2,1)}) custom-call(s32[10]{0:T(128)} %copy-done.25, bf16[512,384]{1,0:T(8,128)(2,1)} %copy-done.29, bf16[512,384]{1,0:T(8,128)(2,1)} %copy-done.31, bf16[3072,768]{1,0:T(8,128)(2,1)} %copy-done.33, bf16[512,384]{1,0:T(8,128)(2,1)} %copy-done.27, ...), custom_call_target="tpu_custom_call" | custom-call | flops 10066329600 | bytes 20971520 | tf_op jit(solution)/shard_map/flash_backward/pallas_call | solution.py:758
  363.6 8.9 %fusion.20 = f32[3072,768]{1,0:T(8,128)} fusion(bf16[3072,768]{1,0:T(8,128)(2,1)} %get-tuple-element.107, bf16[768,384]{1,0:T(8,128)(2,1)S(1)} %copy-done.64, bf16[768,384]{1,0:T(8,128)(2,1)S(1)} %copy-done.66), kind=kOutput, calls=%fused_computation.69 | convolution fusion | flops 3626237952 | bytes 15335424 | tf_op jit(solution)/shard_map/te,de->td/dot_general | solution.py:1652
  372.6 2.2 slice.539
  374.9 2.0 fusion.6
  378.7 4.7 slice.376
  386.8 2.2 slice_add_fusion.5
  389.0 3.4 fusion.67
  392.5 10.6 %collective-permute-start.20 = (bf16[512,768]{1,0:T(8,128)(2,1)S(1)}, bf16[512,768]{1,0:T(8,128)(2,1)S(1)}, u32[]{:S(2)}, u32[]{:S(2)}) collective-permute-start(bf16[512,768]{1,0:T(8,128)(2,1)S(1)} %get-tuple-element.186), channel_id=1, source_target_pairs={{0,2},{1,3},{2,4},{3,5},{4,6},{5,7},{8,10},{9,11},{10,12},{11,13},... | collective-permute-start | bytes 2359304 | tf_op jit(solution)/shard_map/ppermute | solution.py:809
  404.8 4.9 convolution_convert_fusion.1
  409.7 16.1 %collective-permute-done.20 = bf16[512,768]{1,0:T(8,128)(2,1)S(1)} collective-permute-done((bf16[512,768]{1,0:T(8,128)(2,1)S(1)}, bf16[512,768]{1,0:T(8,128)(2,1)S(1)}, u32[]{:S(2)}, u32[]{:S(2)}) %collective-permute-start.20) | collective-permute-done | bytes 786464 | tf_op jit(solution)/shard_map/ppermute | solution.py:809
  429.2 20.8 %tail_backward.3 = (f32[512,768]{1,0:T(8,128)S(1)}, bf16[512,384]{1,0:T(8,128)(2,1)S(1)}, bf16[512,384]{1,0:T(8,128)(2,1)S(1)}, bf16[768,768]{1,0:T(8,128)(2,1)S...) custom-call(s32[4]{0:T(128)S(1)} %copy-done.21, ...), custom_call_target="tpu_custom_call" | custom-call | flops 10871635968 | bytes 41943040 | tf_op jit(solution)/shard_map/tail_backward/pallas_call | solution.py:1371
  452.5 8.5 %pack_terms.2 = bf16[4,8,224,768]{3,2,1,0:T(8,128)(2,1)} custom-call(bf16[8,4,24,768]{3,2,1,0:T(8,128)(2,1)} %bitcast.162, bf16[8,4,24,3072]{3,2,1,0:T(8,128)(2,1)} %bitcast.188, bf16[8,4,96,768]{3,2,1,0:T(8,128)(2,1)} %bitcast.189, bf16[4,8,8,768]{3,2,1,0:T(8,128)(2,1)S(1)} %pad.28.refs_3_), custom_call_target="tpu_custom_call" | custom-call | bytes 22020096 | tf_op jit(solution)/shard_map/pack_terms/pallas_call | solution.py:964
  462.2 2.1 convert_reduce_fusion.1
  466.1 3.4 spread_terms.2
  470.8 6.0 collective-permute-start.22
  477.6 39.0 %flash_backward.3 = (bf16[512,384]{1,0:T(8,128)(2,1)}, bf16[512,384]{1,0:T(8,128)(2,1)}, bf16[3072,768]{1,0:T(8,128)(2,1)}) custom-call(s32[10]{0:T(128)} %copy-done.25, bf16[512,384]{1,0:T(8,128)(2,1)} %copy-done.30, bf16[512,384]{1,0:T(8,128)(2,1)} %copy-done.32, bf16[3072,768]{1,0:T(8,128)(2,1)} %copy-done.34, bf16[512,384]{1,0:T(8,128)(2,1)} %copy-done.26, ...), custom_call_target="tpu_custom_call" | custom-call | flops 10066329600 | bytes 20971520 | tf_op jit(solution)/shard_map/flash_backward/pallas_call | solution.py:758
  519.2 2.1 fusion.24
  524.3 9.2 %convolution_convert_fusion = bf16[768,768]{1,0:T(8,128)(2,1)} fusion(bf16[3072,768]{1,0:T(8,128)(2,1)} %constant_dynamic-update-slice_fusion.2, bf16[3072,768]{1,0:T(8,128)(2,1)} %get-tuple-element.128), kind=kOutput, calls=%fused_computation.27 | convolution fusion | flops 3624468480 | bytes 10616832 | tf_op jit(solution)/shard_map/td,te->de/dot_general | solution.py:1645
  533.4 3.5 spread_terms.3
  538.4 5.8 fusion.17
  546.4 31.9 %collective-permute-done.27 = bf16[2,4,4,48,384]{4,3,2,1,0:T(8,128)(2,1)S(1)} collective-permute-done((bf16[2,4,4,48,384]{4,3,2,1,0:T(8,128)(2,1)S(1)}, bf16[2,4,4,48,384]{4,3,2,1,0:T(8,128)(2,1)S(1)}, u32[]{:S(2)}, u32[]{:S(2)}) %collective-permute-start.27) | collective-permute-done | bytes 1179680 | tf_op jit(solution)/shard_map/ppermute | solution.py:809
  580.3 14.8 %collective-permute-done.28 = bf16[4,4,48,384]{3,2,1,0:T(8,128)(2,1)S(1)} collective-permute-done((bf16[4,4,48,384]{3,2,1,0:T(8,128)(2,1)S(1)}, bf16[4,4,48,384]{3,2,1,0:T(8,128)(2,1)S(1)}, u32[]{:S(2)}, u32[]{:S(2)}) %collective-permute-start.28) | collective-permute-done | bytes 589856 | tf_op jit(solution)/shard_map/ppermute | solution.py:809
  595.1 2.6 collective-permute-done.29
  598.1 4.0 collective-permute-start.30
  602.9 39.9 %collective-permute-done.30 = bf16[2,8,48,384]{3,2,1,0:T(8,128)(2,1)S(1)} collective-permute-done((bf16[2,8,48,384]{3,2,1,0:T(8,128)(2,1)S(1)}, bf16[2,8,48,384]{3,2,1,0:T(8,128)(2,1)S(1)}, u32[]{:S(2)}, u32[]{:S(2)}) %collective-permute-start.30) | collective-permute-done | bytes 589856 | tf_op jit(solution)/shard_map/ppermute | solution.py:809
  642.9 2.8 fusion.66
  647.0 4.2 collective-permute-start.25
  652.5 2.9 collective-permute-done.31
  655.6 8.8 %collective-permute-start.15 = (bf16[512,768]{1,0:T(8,128)(2,1)}, bf16[512,768]{1,0:T(8,128)(2,1)S(1)}, u32[]{:S(2)}, u32[]{:S(2)}) collective-permute-start(bf16[512,768]{1,0:T(8,128)(2,1)} %get-tuple-element.214), channel_id=1, source_target_pairs={{0,0},{1,8},{2,2},{3,10},{4,4},{5,12},{6,6},{7,14},{8,1},{9,9},{10... | collective-permute-start | bytes 2359304 | tf_op jit(solution)/shard_map/ppermute | solution.py:809
  664.5 3.4 collective-permute-start.33
  667.8 5.1 collective-permute-done.25
  675.2 2.2 fusion.2
  677.4 4.8 collective-permute-start.26
  687.3 4.6 collective-permute-done.26
  693.8 3.8 finish_shares.1
  (390 shorter events, 103.7 us)
Async XLA Ops:
  7.2 151.6 %all-gather.3.cloned.1.call-start = ((), (), s32[]{:S(2)}) async-start(), calls=%async_computation.2 | async-start | bytes 14598144 | tf_op jit(solution)/shard_map/all_gather | solution.py:1423
  7.2 15.8 %collective-permute-start.1 = (bf16[512,768]{1,0:T(8,128)(2,1)}, bf16[512,768]{1,0:T(8,128)(2,1)S(1)}, u32[]{:S(2)}, u32[]{:S(2)}) collective-permute-start(bf16[512,768]{1,0:T(8,128)(2,1)} %param.10), channel_id=1, source_target_pairs={{0,0},{1,8},{2,2},{3,10},{4,4},{5,12},{6,6},{7,14},{8,1},{9,9},{10... | collective-permute-start | bytes 2359304 | tf_op jit(solution)/shard_map/ppermute | solution.py:809
  17.5 4.5 collective-permute-start
  23.0 89.0 %copy-start.43 = (bf16[512,768]{1,0:T(8,128)(2,1)}, bf16[512,768]{1,0:T(8,128)(2,1)S(1)}, u32[]{:S(2)}) copy-start(bf16[512,768]{1,0:T(8,128)(2,1)S(1)} %collective-permute-done.1) | copy-start | bytes 2359300
  23.1 16.6 %collective-permute-start.2 = (bf16[2,4,48,384]{3,2,1,0:T(8,128)(2,1)S(1)}, bf16[2,4,48,384]{3,2,1,0:T(8,128)(2,1)S(1)}, u32[]{:S(2)}, u32[]{:S(2)}) collective-permute-start(bf16[2,4,48,384]{3,2,1,0:T(8,128)(2,1)S(1)} %pad_maximum_fusion.18), channel_id=1, source_target_pairs={{0,4},{1,5},{2,6},{3,7},{4,0},{5,1},{6,2},{7,3},{8,12},{9,13},{10,... | collective-permute-start | bytes 884744 | tf_op jit(solution)/shard_map/ppermute | solution.py:809
  39.7 229.7 %all-gather.5.cloned.1.call-start = ((), (), s32[]{:S(2)}) async-start(), calls=%async_computation.3 | async-start | bytes 10948608 | tf_op jit(solution)/shard_map/all_gather | solution.py:1423
  40.5 627.3 %reduce-scatter.5.cloned.1.call-start = ((), (), s32[]{:S(2)}) async-start(), calls=%async_computation.5 | async-start | bytes 11354112 | tf_op jit(solution)/shard_map/reduce_scatter | solution.py:1688
  40.6 30.0 %collective-permute-start.8 = (bf16[512,768]{1,0:T(8,128)(2,1)S(1)}, bf16[512,768]{1,0:T(8,128)(2,1)S(1)}, u32[]{:S(2)}, u32[]{:S(2)}) collective-permute-start(bf16[512,768]{1,0:T(8,128)(2,1)S(1)} %collective-permute-done.1), channel_id=1, source_target_pairs={{2,0},{3,1},{4,2},{5,3},{6,4},{7,5},{10,8},{11,9},{12,10},{13,11},... | collective-permute-start | bytes 2359304 | tf_op jit(solution)/shard_map/ppermute | solution.py:809
  41.9 29.5 %collective-permute-start.7 = (bf16[512,768]{1,0:T(8,128)(2,1)S(1)}, bf16[512,768]{1,0:T(8,128)(2,1)S(1)}, u32[]{:S(2)}, u32[]{:S(2)}) collective-permute-start(bf16[512,768]{1,0:T(8,128)(2,1)S(1)} %collective-permute-done.1), channel_id=1, source_target_pairs={{0,2},{1,3},{2,4},{3,5},{4,6},{5,7},{8,10},{9,11},{10,12},{11,13},... | collective-permute-start | bytes 2359304 | tf_op jit(solution)/shard_map/ppermute | solution.py:809
  46.0 27.1 %copy-start.73 = (s32[1,4,2,128]{3,1,2,0:T(4,128)}, s32[1,4,2,128]{3,1,2,0:T(4,128)S(1)}, u32[]{:S(2)}) copy-start(s32[1,4,2,128]{3,1,2,0:T(4,128)S(1)} %copy.37) | copy-start | bytes 12292
  73.1 41.1 %collective-permute-start.9 = (bf16[1536,768]{1,0:T(8,128)(2,1)}, bf16[1536,768]{1,0:T(8,128)(2,1)}, u32[]{:S(2)}, u32[]{:S(2)}) collective-permute-start(bf16[1536,768]{1,0:T(8,128)(2,1)} %pad_maximum_fusion), channel_id=1, source_target_pairs={{0,8},{1,9},{2,10},{3,11},{4,12},{5,13},{6,14},{7,15},{8,0},{9,1},... | collective-permute-start | bytes 7077896 | tf_op jit(solution)/shard_map/ppermute | solution.py:809
  75.6 15.1 %collective-permute-start.3 = (bf16[4,2,48,384]{3,2,1,0:T(8,128)(2,1)}, bf16[4,2,48,384]{3,2,1,0:T(8,128)(2,1)S(1)}, u32[]{:S(2)}, u32[]{:S(2)}) collective-permute-start(bf16[4,2,48,384]{3,2,1,0:T(8,128)(2,1)} %get-tuple-element.202), channel_id=1, source_target_pairs={{0,1},{1,0},{2,3},{3,2},{4,5},{5,4},{6,7},{7,6},{8,9},{9,8},{10,11... | collective-permute-start | bytes 884744 | tf_op jit(solution)/shard_map/ppermute | solution.py:809
  75.6 16.4 %collective-permute-start.5 = (bf16[4,2,48,384]{3,2,1,0:T(8,128)(2,1)S(1)}, bf16[4,2,48,384]{3,2,1,0:T(8,128)(2,1)S(1)}, u32[]{:S(2)}, u32[]{:S(2)}) collective-permute-start(bf16[4,2,48,384]{3,2,1,0:T(8,128)(2,1)S(1)} %get-tuple-element.201), channel_id=1, source_target_pairs={{0,16},{1,17},{2,18},{3,19},{4,20},{5,21},{6,22},{7,23},{8,24},{9,... | collective-permute-start | bytes 884744 | tf_op jit(solution)/shard_map/ppermute | solution.py:809
  84.4 153.4 %copy-start.25 = (s32[10]{0:T(128)}, s32[10]{0:T(128)S(1)}, u32[]{:S(2)}) copy-start(s32[10]{0:T(128)S(1)} %stack.165.bounds) | copy-start | bytes 124
  90.9 14.3 %collective-permute-start.4 = (bf16[2,4,2,48,384]{4,3,2,1,0:T(8,128)(2,1)S(1)}, bf16[2,4,2,48,384]{4,3,2,1,0:T(8,128)(2,1)S(1)}, u32[]{:S(2)}, u32[]{:S(2)}) collective-permute-start(bf16[2,4,2,48,384]{4,3,2,1,0:T(8,128)(2,1)S(1)} %get-tuple-element.204), channel_id=1, source_target_pairs={{0,16},{1,17},{2,18},{3,19},{4,20},{5,21},{6,22},{7,23},{8,24},{9,... | collective-permute-start | bytes 1769480 | tf_op jit(solution)/shard_map/ppermute | solution.py:809
  92.1 16.8 %collective-permute-start.6 = (bf16[2,4,2,48,384]{4,3,2,1,0:T(8,128)(2,1)S(1)}, bf16[2,4,2,48,384]{4,3,2,1,0:T(8,128)(2,1)S(1)}, u32[]{:S(2)}, u32[]{:S(2)}) collective-permute-start(bf16[2,4,2,48,384]{4,3,2,1,0:T(8,128)(2,1)S(1)} %get-tuple-element.198), channel_id=1, source_target_pairs={{0,1},{1,0},{2,3},{3,2},{4,5},{5,4},{6,7},{7,6},{8,9},{9,8},{10,11... | collective-permute-start | bytes 1769480 | tf_op jit(solution)/shard_map/ppermute | solution.py:809
  126.3 20.1 %copy-start.34 = (bf16[3072,768]{1,0:T(8,128)(2,1)}, bf16[3072,768]{1,0:T(8,128)(2,1)S(1)}, u32[]{:S(2)}) copy-start(bf16[3072,768]{1,0:T(8,128)(2,1)S(1)} %add_convert_fusion.1.kv_ref) | copy-start | bytes 14155780
  126.3 111.5 %copy-start.23 = (s32[8,1024]{1,0:T(8,128)}, s32[8,1024]{1,0:T(8,128)S(1)}, u32[]{:S(2)}) copy-start(s32[8,1024]{1,0:T(8,128)S(1)} %broadcast_in_dim.47.low_ref) | copy-start | bytes 98308
  126.3 111.5 %copy-start.24 = (s32[8,1024]{1,0:T(8,128)}, s32[8,1024]{1,0:T(8,128)S(1)}, u32[]{:S(2)}) copy-start(s32[8,1024]{1,0:T(8,128)S(1)} %broadcast_in_dim.48.high_ref) | copy-start | bytes 98308
  149.0 2.3 collective-permute-start.10
  176.8 36.9 %copy-start = (f32[512,768]{1,0:T(8,128)}, f32[512,768]{1,0:T(8,128)S(1)}, u32[]{:S(2)}) copy-start(f32[512,768]{1,0:T(8,128)S(1)} %get-tuple-element.90.state_ref) | copy-start | bytes 4718596
  176.8 36.9 %copy-start.2 = (f32[512,768]{1,0:T(8,128)}, f32[512,768]{1,0:T(8,128)S(1)}, u32[]{:S(2)}) copy-start(f32[512,768]{1,0:T(8,128)S(1)} %get-tuple-element.113.norm_one_ref) | copy-start | bytes 4718596
  176.8 36.9 %copy-start.3 = (f32[512,768]{1,0:T(8,128)}, f32[512,768]{1,0:T(8,128)S(1)}, u32[]{:S(2)}) copy-start(f32[512,768]{1,0:T(8,128)S(1)} %get-tuple-element.111.norm_two_ref) | copy-start | bytes 4718596
  176.8 41.4 %copy-start.74 = (s32[1,4,2,128]{3,1,2,0:T(4,128)S(1)}, s32[1,4,2,128]{3,1,2,0:T(4,128)}, u32[]{:S(2)}) copy-start(s32[1,4,2,128]{3,1,2,0:T(4,128)} %copy-done.73) | copy-start | bytes 12292
  176.8 41.4 %copy-start.77 = (s32[8,1]{0,1:T(1,128)S(1)}, s32[8,1]{0,1:T(1,128)}, u32[]{:S(2)}) copy-start(s32[8,1]{0,1:T(1,128)} %copy-done.76) | copy-start | bytes 100
  176.9 41.5 %copy-start.72 = (bf16[8,960]{1,0:T(8,128)(2,1)S(1)}, bf16[8,960]{1,0:T(8,128)(2,1)}, u32[]{:S(2)}) copy-start(bf16[8,960]{1,0:T(8,128)(2,1)} %get-tuple-element.150) | copy-start | bytes 46084
  176.9 35.1 %collective-permute-start.12 = (bf16[512,768]{1,0:T(8,128)(2,1)S(1)}, bf16[512,768]{1,0:T(8,128)(2,1)S(1)}, u32[]{:S(2)}, u32[]{:S(2)}) collective-permute-start(bf16[512,768]{1,0:T(8,128)(2,1)S(1)} %get-tuple-element.87), channel_id=1, source_target_pairs={{2,0},{3,1},{4,2},{5,3},{6,4},{7,5},{10,8},{11,9},{12,10},{13,11},... | collective-permute-start | bytes 2359304 | tf_op jit(solution)/shard_map/ppermute | solution.py:809
  178.3 33.6 %collective-permute-start.11 = (bf16[512,768]{1,0:T(8,128)(2,1)S(1)}, bf16[512,768]{1,0:T(8,128)(2,1)S(1)}, u32[]{:S(2)}, u32[]{:S(2)}) collective-permute-start(bf16[512,768]{1,0:T(8,128)(2,1)S(1)} %get-tuple-element.87), channel_id=1, source_target_pairs={{0,2},{1,3},{2,4},{3,5},{4,6},{5,7},{8,10},{9,11},{10,12},{11,13},... | collective-permute-start | bytes 2359304 | tf_op jit(solution)/shard_map/ppermute | solution.py:809
  213.7 14.2 %collective-permute-start.13 = (bf16[1536,768]{1,0:T(8,128)(2,1)}, bf16[1536,768]{1,0:T(8,128)(2,1)}, u32[]{:S(2)}, u32[]{:S(2)}) collective-permute-start(bf16[1536,768]{1,0:T(8,128)(2,1)} %pad_maximum_fusion.1), channel_id=1, source_target_pairs={{0,8},{1,9},{2,10},{3,11},{4,12},{5,13},{6,14},{7,15},{8,0},{9,1},... | collective-permute-start | bytes 7077896 | tf_op jit(solution)/shard_map/ppermute | solution.py:809
  215.2 69.9 %collective-permute-start.16 = (bf16[512,768]{1,0:T(8,128)(2,1)}, bf16[512,768]{1,0:T(8,128)(2,1)}, u32[]{:S(2)}, u32[]{:S(2)}) collective-permute-start(bf16[512,768]{1,0:T(8,128)(2,1)} %param.11), channel_id=1, source_target_pairs={{0,0},{1,8},{2,2},{3,10},{4,4},{5,12},{6,6},{7,14},{8,1},{9,9},{10... | collective-permute-start | bytes 2359304 | tf_op jit(solution)/shard_map/ppermute | solution.py:809
  237.8 21.0 %copy-start.33 = (bf16[3072,768]{1,0:T(8,128)(2,1)}, bf16[3072,768]{1,0:T(8,128)(2,1)S(1)}, u32[]{:S(2)}) copy-start(bf16[3072,768]{1,0:T(8,128)(2,1)S(1)} %add_convert_fusion.kv_ref) | copy-start | bytes 14155780
  237.8 29.4 %copy-start.75 = (bf16[8,192]{1,0:T(8,128)(2,1)S(1)}, bf16[8,192]{1,0:T(8,128)(2,1)}, u32[]{:S(2)}) copy-start(bf16[8,192]{1,0:T(8,128)(2,1)} %get-tuple-element.148) | copy-start | bytes 9220
  237.8 31.6 %copy-start.1 = (f32[512,768]{1,0:T(8,128)S(1)}, f32[512,768]{1,0:T(8,128)}, u32[]{:S(2)}) copy-start(f32[512,768]{1,0:T(8,128)} %copy-done) | copy-start | bytes 4718596
  262.0 7.4 %collective-permute-start.14 = (bf16[512,384]{1,0:T(8,128)(2,1)}, bf16[512,384]{1,0:T(8,128)(2,1)}, u32[]{:S(2)}, u32[]{:S(2)}) collective-permute-start(bf16[512,384]{1,0:T(8,128)(2,1)} %get-tuple-element.89), channel_id=1, source_target_pairs={{0,8},{1,9},{2,10},{3,11},{4,12},{5,13},{6,14},{7,15},{8,0},{9,1},... | collective-permute-start | bytes 1179656 | tf_op jit(solution)/shard_map/ppermute | solution.py:809
  321.8 351.1 %reduce-scatter.3.cloned.1.call-start = ((), (), s32[]{:S(2)}) async-start(), calls=%async_computation.4 | async-start | bytes 11354112 | tf_op jit(solution)/shard_map/reduce_scatter | solution.py:1688
  321.9 2.0 collective-permute-start.17
  324.6 39.0 %copy-start.64 = (bf16[768,384]{1,0:T(8,128)(2,1)S(1)}, bf16[768,384]{1,0:T(8,128)(2,1)}, u32[]{:S(2)}) copy-start(bf16[768,384]{1,0:T(8,128)(2,1)} %copy-done.63) | copy-start | bytes 1769476
  324.6 39.0 %copy-start.66 = (bf16[768,384]{1,0:T(8,128)(2,1)S(1)}, bf16[768,384]{1,0:T(8,128)(2,1)}, u32[]{:S(2)}) copy-start(bf16[768,384]{1,0:T(8,128)(2,1)} %copy-done.65) | copy-start | bytes 1769476
  378.4 10.5 %collective-permute-start.18 = (bf16[1536,768]{1,0:T(8,128)(2,1)}, bf16[1536,768]{1,0:T(8,128)(2,1)}, u32[]{:S(2)}, u32[]{:S(2)}) collective-permute-start(bf16[1536,768]{1,0:T(8,128)(2,1)} %pad_maximum_fusion.2), channel_id=1, source_target_pairs={{0,8},{1,9},{2,10},{3,11},{4,12},{5,13},{6,14},{7,15},{8,0},{9,1},... | collective-permute-start | bytes 7077896 | tf_op jit(solution)/shard_map/ppermute | solution.py:809
  386.8 18.0 %slice-start = ((s8[4718592]{0:T(1024)(128)(4,1)}), s8[524288]{0:T(1024)(128)(4,1)S(1)}, s32[]{:S(2)}) async-start(s8[4718592]{0:T(1024)(128)(4,1)} %bitcast.195), calls=%async_computation.6 | async-start | bytes 1048576
  386.8 18.0 %slice-start.2 = ((s8[4718592]{0:T(1024)(128)(4,1)}), s8[4194304]{0:T(1024)(128)(4,1)S(1)}, s32[]{:S(2)}) async-start(s8[4718592]{0:T(1024)(128)(4,1)} %bitcast.215), calls=%async_computation.8 | async-start | bytes 8388608
  388.9 15.9 %slice-start.1 = ((s8[4718592]{0:T(1024)(128)(4,1)}), s8[4194304]{0:T(1024)(128)(4,1)S(1)}, s32[]{:S(2)}) async-start(s8[4718592]{0:T(1024)(128)(4,1)} %bitcast.195), calls=%async_computation.7 | async-start | bytes 8388608
  392.5 33.4 %collective-permute-start.20 = (bf16[512,768]{1,0:T(8,128)(2,1)S(1)}, bf16[512,768]{1,0:T(8,128)(2,1)S(1)}, u32[]{:S(2)}, u32[]{:S(2)}) collective-permute-start(bf16[512,768]{1,0:T(8,128)(2,1)S(1)} %get-tuple-element.186), channel_id=1, source_target_pairs={{0,2},{1,3},{2,4},{3,5},{4,6},{5,7},{8,10},{9,11},{10,12},{11,13},... | collective-permute-start | bytes 2359304 | tf_op jit(solution)/shard_map/ppermute | solution.py:809
  403.1 24.6 %collective-permute-start.19 = (bf16[512,768]{1,0:T(8,128)(2,1)S(1)}, bf16[512,768]{1,0:T(8,128)(2,1)S(1)}, u32[]{:S(2)}, u32[]{:S(2)}) collective-permute-start(bf16[512,768]{1,0:T(8,128)(2,1)S(1)} %get-tuple-element.185), channel_id=1, source_target_pairs={{2,0},{3,1},{4,2},{5,3},{6,4},{7,5},{10,8},{11,9},{12,10},{13,11},... | collective-permute-start | bytes 2359304 | tf_op jit(solution)/shard_map/ppermute | solution.py:809
  464.3 12.5 %collective-permute-start.21 = (bf16[512,384]{1,0:T(8,128)(2,1)S(1)}, bf16[512,384]{1,0:T(8,128)(2,1)S(1)}, u32[]{:S(2)}, u32[]{:S(2)}) collective-permute-start(bf16[512,384]{1,0:T(8,128)(2,1)S(1)} %get-tuple-element.121), channel_id=1, source_target_pairs={{0,8},{1,9},{2,10},{3,11},{4,12},{5,13},{6,14},{7,15},{8,0},{9,1},... | collective-permute-start | bytes 1179656 | tf_op jit(solution)/shard_map/ppermute | solution.py:809
  470.8 51.9 %collective-permute-start.22 = (bf16[2,4,4,48,384]{4,3,2,1,0:T(8,128)(2,1)S(1)}, bf16[2,4,4,48,384]{4,3,2,1,0:T(8,128)(2,1)}, u32[]{:S(2)}, u32[]{:S(2)}) collective-permute-start(bf16[2,4,4,48,384]{4,3,2,1,0:T(8,128)(2,1)S(1)} %slice_bitcast_fusion.1), channel_id=1, source_target_pairs={{0,1},{1,0},{2,3},{3,2},{4,5},{5,4},{6,7},{7,6},{8,9},{9,8},{10,11... | collective-permute-start | bytes 3538952 | tf_op jit(solution)/shard_map/ppermute | solution.py:809
  538.3 39.9 %collective-permute-start.27 = (bf16[2,4,4,48,384]{4,3,2,1,0:T(8,128)(2,1)S(1)}, bf16[2,4,4,48,384]{4,3,2,1,0:T(8,128)(2,1)S(1)}, u32[]{:S(2)}, u32[]{:S(2)}) collective-permute-start(bf16[2,4,4,48,384]{4,3,2,1,0:T(8,128)(2,1)S(1)} %slice_bitcast_fusion), channel_id=1, source_target_pairs={{0,16},{1,17},{2,18},{3,19},{4,20},{5,21},{6,22},{7,23},{8,24},{9,... | collective-permute-start | bytes 3538952 | tf_op jit(solution)/shard_map/ppermute | solution.py:809
  545.8 32.4 %copy-start.42 = (bf16[2,2,4,4,48,384]{5,4,3,2,1,0:T(8,128)(2,1)S(1)}, bf16[2,2,4,4,48,384]{5,4,3,2,1,0:T(8,128)(2,1)}, u32[]{:S(2)}) copy-start(bf16[2,2,4,4,48,384]{5,4,3,2,1,0:T(8,128)(2,1)} %spread_terms.3) | copy-start | bytes 7077892
  546.0 32.7 %copy-start.41 = (bf16[2,2,4,4,48,384]{5,4,3,2,1,0:T(8,128)(2,1)S(1)}, bf16[2,2,4,4,48,384]{5,4,3,2,1,0:T(8,128)(2,1)}, u32[]{:S(2)}) copy-start(bf16[2,2,4,4,48,384]{5,4,3,2,1,0:T(8,128)(2,1)} %spread_terms.2) | copy-start | bytes 7077892
  546.0 97.0 %collective-permute-start.23 = (bf16[1536,768]{1,0:T(8,128)(2,1)S(1)}, bf16[1536,768]{1,0:T(8,128)(2,1)S(1)}, u32[]{:S(2)}, u32[]{:S(2)}) collective-permute-start(bf16[1536,768]{1,0:T(8,128)(2,1)S(1)} %pad_maximum_fusion.3), channel_id=1, source_target_pairs={{0,8},{1,9},{2,10},{3,11},{4,12},{5,13},{6,14},{7,15},{8,0},{9,1},... | collective-permute-start | bytes 7077896 | tf_op jit(solution)/shard_map/ppermute | solution.py:809
  578.5 16.5 %collective-permute-start.28 = (bf16[4,4,48,384]{3,2,1,0:T(8,128)(2,1)S(1)}, bf16[4,4,48,384]{3,2,1,0:T(8,128)(2,1)S(1)}, u32[]{:S(2)}, u32[]{:S(2)}) collective-permute-start(bf16[4,4,48,384]{3,2,1,0:T(8,128)(2,1)S(1)} %get-tuple-element.175), channel_id=1, source_target_pairs={{0,1},{1,0},{2,3},{3,2},{4,5},{5,4},{6,7},{7,6},{8,9},{9,8},{10,11... | collective-permute-start | bytes 1769480 | tf_op jit(solution)/shard_map/ppermute | solution.py:809
  580.2 17.5 %collective-permute-start.29 = (bf16[4,4,48,384]{3,2,1,0:T(8,128)(2,1)S(1)}, bf16[4,4,48,384]{3,2,1,0:T(8,128)(2,1)S(1)}, u32[]{:S(2)}, u32[]{:S(2)}) collective-permute-start(bf16[4,4,48,384]{3,2,1,0:T(8,128)(2,1)S(1)} %get-tuple-element.177), channel_id=1, source_target_pairs={{0,16},{1,17},{2,18},{3,19},{4,20},{5,21},{6,22},{7,23},{8,24},{9,... | collective-permute-start | bytes 1769480 | tf_op jit(solution)/shard_map/ppermute | solution.py:809
  598.1 44.7 %collective-permute-start.30 = (bf16[2,8,48,384]{3,2,1,0:T(8,128)(2,1)S(1)}, bf16[2,8,48,384]{3,2,1,0:T(8,128)(2,1)S(1)}, u32[]{:S(2)}, u32[]{:S(2)}) collective-permute-start(bf16[2,8,48,384]{3,2,1,0:T(8,128)(2,1)S(1)} %get-tuple-element.182), channel_id=1, source_target_pairs={{0,4},{1,5},{2,6},{3,7},{4,0},{5,1},{6,2},{7,3},{8,12},{9,13},{10,... | collective-permute-start | bytes 1769480 | tf_op jit(solution)/shard_map/ppermute | solution.py:809
  642.9 12.5 %collective-permute-start.31 = (bf16[8,48,384]{2,1,0:T(8,128)(2,1)S(1)}, bf16[8,48,384]{2,1,0:T(8,128)(2,1)S(1)}, u32[]{:S(2)}, u32[]{:S(2)}) collective-permute-start(bf16[8,48,384]{2,1,0:T(8,128)(2,1)S(1)} %fusion.51), channel_id=1, source_target_pairs={{0,2},{1,3},{2,0},{3,1},{4,6},{5,7},{6,4},{7,5},{8,10},{9,11},{10,... | collective-permute-start | bytes 884744 | tf_op jit(solution)/shard_map/ppermute | solution.py:809
  647.0 25.9 %collective-permute-start.25 = (bf16[512,768]{1,0:T(8,128)(2,1)}, bf16[512,768]{1,0:T(8,128)(2,1)}, u32[]{:S(2)}, u32[]{:S(2)}) collective-permute-start(bf16[512,768]{1,0:T(8,128)(2,1)} %get-tuple-element.184), channel_id=1, source_target_pairs={{0,2},{1,3},{2,4},{3,5},{4,6},{5,7},{8,10},{9,11},{10,12},{11,13},... | collective-permute-start | bytes 2359304 | tf_op jit(solution)/shard_map/ppermute | solution.py:809
  651.2 23.9 %collective-permute-start.24 = (bf16[512,768]{1,0:T(8,128)(2,1)}, bf16[512,768]{1,0:T(8,128)(2,1)}, u32[]{:S(2)}, u32[]{:S(2)}) collective-permute-start(bf16[512,768]{1,0:T(8,128)(2,1)} %get-tuple-element.183), channel_id=1, source_target_pairs={{2,0},{3,1},{4,2},{5,3},{6,4},{7,5},{10,8},{11,9},{12,10},{13,11},... | collective-permute-start | bytes 2359304 | tf_op jit(solution)/shard_map/ppermute | solution.py:809
  655.5 8.9 %collective-permute-start.32 = (bf16[8,48,384]{2,1,0:T(8,128)(2,1)S(1)}, bf16[8,48,384]{2,1,0:T(8,128)(2,1)S(1)}, u32[]{:S(2)}, u32[]{:S(2)}) collective-permute-start(bf16[8,48,384]{2,1,0:T(8,128)(2,1)S(1)} %fusion.29), channel_id=1, source_target_pairs={{0,16},{1,17},{2,18},{3,19},{4,20},{5,21},{6,22},{7,23},{8,24},{9,... | collective-permute-start | bytes 884744 | tf_op jit(solution)/shard_map/ppermute | solution.py:809
  655.6 30.5 %collective-permute-start.15 = (bf16[512,768]{1,0:T(8,128)(2,1)}, bf16[512,768]{1,0:T(8,128)(2,1)S(1)}, u32[]{:S(2)}, u32[]{:S(2)}) collective-permute-start(bf16[512,768]{1,0:T(8,128)(2,1)} %get-tuple-element.214), channel_id=1, source_target_pairs={{0,0},{1,8},{2,2},{3,10},{4,4},{5,12},{6,6},{7,14},{8,1},{9,9},{10... | collective-permute-start | bytes 2359304 | tf_op jit(solution)/shard_map/ppermute | solution.py:809
  664.5 21.6 %collective-permute-start.33 = (bf16[2,8,48,384]{3,2,1,0:T(8,128)(2,1)S(1)}, bf16[2,8,48,384]{3,2,1,0:T(8,128)(2,1)}, u32[]{:S(2)}, u32[]{:S(2)}) collective-permute-start(bf16[2,8,48,384]{3,2,1,0:T(8,128)(2,1)S(1)} %get-tuple-element.195), channel_id=1, source_target_pairs={{0,8},{1,9},{2,10},{3,11},{4,12},{5,13},{6,14},{7,15},{8,0},{9,1},... | collective-permute-start | bytes 1769480 | tf_op jit(solution)/shard_map/ppermute | solution.py:809
  667.8 14.4 %collective-permute-start.36 = (bf16[224,768]{1,0:T(8,128)(2,1)}, bf16[224,768]{1,0:T(8,128)(2,1)}, u32[]{:S(2)}, u32[]{:S(2)}) collective-permute-start(bf16[224,768]{1,0:T(8,128)(2,1)} %bitcast.204), channel_id=1, source_target_pairs={{0,16},{1,17},{2,18},{3,19},{4,20},{5,21},{6,22},{7,23},{8,24},{9,... | collective-permute-start | bytes 1032200 | tf_op jit(solution)/shard_map/ppermute | solution.py:809
  672.9 12.1 %collective-permute-start.34 = (bf16[224,768]{1,0:T(8,128)(2,1)}, bf16[224,768]{1,0:T(8,128)(2,1)S(1)}, u32[]{:S(2)}, u32[]{:S(2)}) collective-permute-start(bf16[224,768]{1,0:T(8,128)(2,1)} %bitcast.205), channel_id=1, source_target_pairs={{0,16},{1,17},{2,18},{3,19},{4,20},{5,21},{6,22},{7,23},{8,24},{9,... | collective-permute-start | bytes 1032200 | tf_op jit(solution)/shard_map/ppermute | solution.py:809
  677.4 14.5 %collective-permute-start.26 = (bf16[512,768]{1,0:T(8,128)(2,1)S(1)}, bf16[512,768]{1,0:T(8,128)(2,1)S(1)}, u32[]{:S(2)}, u32[]{:S(2)}) collective-permute-start(bf16[512,768]{1,0:T(8,128)(2,1)S(1)} %fusion.2), channel_id=1, source_target_pairs={{0,0},{1,8},{2,2},{3,10},{4,4},{5,12},{6,6},{7,14},{8,1},{9,9},{10... | collective-permute-start | bytes 2359304 | tf_op jit(solution)/shard_map/ppermute | solution.py:809
  683.3 9.8 %collective-permute-start.37 = (bf16[2,224,768]{2,1,0:T(8,128)(2,1)S(1)}, bf16[2,224,768]{2,1,0:T(8,128)(2,1)S(1)}, u32[]{:S(2)}, u32[]{:S(2)}) collective-permute-start(bf16[2,224,768]{2,1,0:T(8,128)(2,1)S(1)} %get-tuple-element.192), channel_id=1, source_target_pairs={{0,8},{1,9},{2,10},{3,11},{4,12},{5,13},{6,14},{7,15},{8,0},{9,1},... | collective-permute-start | bytes 2064392 | tf_op jit(solution)/shard_map/ppermute | solution.py:809
  685.1 8.2 %collective-permute-start.35 = (bf16[2,224,768]{2,1,0:T(8,128)(2,1)S(1)}, bf16[2,224,768]{2,1,0:T(8,128)(2,1)S(1)}, u32[]{:S(2)}, u32[]{:S(2)}) collective-permute-start(bf16[2,224,768]{2,1,0:T(8,128)(2,1)S(1)} %get-tuple-element.194), channel_id=1, source_target_pairs={{0,8},{1,9},{2,10},{3,11},{4,12},{5,13},{6,14},{7,15},{8,0},{9,1},... | collective-permute-start | bytes 2064392 | tf_op jit(solution)/shard_map/ppermute | solution.py:809
  (62 other events, 220.0 us)
Sparse Core Ops, SparseCore 0:
  39.9 118.8 all-gather.2
  161.7 101.8 all-gather.4
  321.9 158.4 reduce-scatter.4
  486.3 174.2 reduce-scatter.2

commit v5 on v4

--- a/solution.py
+++ b/solution.py
@@ -1697,8 +1697,8 @@
         query_term = query_term.astype(jnp.bfloat16)
         key_value_term = key_value_term.astype(jnp.bfloat16)
         if layer_index > 0:
-            state_grad, query_term, key_value_term = lax.optimization_barrier(
-                (state_grad, query_term, key_value_term)
+            state_grad, query_term, key_value_term, activations = lax.optimization_barrier(
+                (state_grad, query_term, key_value_term, activations)
             )
         spreads[layer_index] = spread_terms(me, query_term, key_value_term, lines)
         if layer_index > 0:

time: 711 us -> 716 us (level)
  waiting for transfers between devices: 226 us -> 239 us
  starting transfers between devices: 80.9 us -> 68.4 us
    ppermute x38, starting transfers between devices: 80.8 us -> 68.3 us  [send(): return lax.ppermute(values, BOTH, device_pairs(place))]
    ppermute x38, waiting for transfers between devices: 218 us -> 229 us  [send(): return lax.ppermute(values, BOTH, device_pairs(place))]
    unnamed x187 -> x181, local copies, waits for them, and re-layouts: 27.2 us -> 26.6 us
  transfers between devices with their start and end apart: 42 -> 42, of which waited for: 22 -> 21; matrix products, arithmetic and copies ran while one was open for 17% -> 17% of each run, Pallas kernels for 27% -> 27%
where the time goes in v5:
time: 716 us; the launch traced here: 708 us
  waiting for transfers between devices  239 us (33%)
  Pallas kernels  225 us (31%)
  starting transfers between devices  68.4 us (10%)
  local copies, waits for them, and re-layouts  60 us (8%)
  matrix products  57.9 us (8%)
  other arithmetic  35.6 us (5%)
  between operations  21.9 us (3%)
    ppermute x38, waiting for transfers between devices, send(): return lax.ppermute(values, BOTH, device_pairs(place))  229 us
    pallas_call x2, Pallas kernels, flash_backward(): pl.pallas_call(flash_backward_kernel, out_shape=(jax.ShapeDtypeStruct((ro...  78.2 us
    ppermute x38, starting transfers between devices, send(): return lax.ppermute(values, BOTH, device_pairs(place))  68.3 us
    pallas_call x2, Pallas kernels, tail_backward(): pl.pallas_call(tail_backward_kernel, out_shape=[shaped(rows, width, jnp.f...  41.5 us
    pallas_call x2, Pallas kernels, flash_forward(): pl.pallas_call(flash_forward_kernel, out_shape=(jax.ShapeDtypeStruct((row...  41 us
    pallas_call x2, Pallas kernels, tail_forward(): pl.pallas_call(tail_forward_kernel, out_shape=[shaped(width, jnp.bfloat16...  29.1 us
    unnamed x181, local copies, waits for them, and re-layouts  26.6 us
    pallas_call x2, Pallas kernels, pack_terms(): pl.pallas_call(functools.partial(pack_kernel, kinds), out_shape=pltpu.HBM...  16.9 us
  transfers between devices with their start and end apart: 42, of which 21 were waited for; matrix products, arithmetic and copies ran while one was open for 17% of the time, Pallas kernels for 27%

profile of v5, /device:TPU:1, one launch (start us, length us, event | category | flops | bytes accessed | tf_op | source)
XLA Modules:
  0.0 707.9 jit_solution(6483443924220569227)
XLA Ops:
  7.2 4.5 collective-permute-start.2
  14.7 2.9 pick_quarters.1
  18.9 3.2 collective-permute-done.1
  23.1 2.8 collective-permute-start.3
  26.0 13.8 %collective-permute-done.3 = bf16[2,4,48,384]{3,2,1,0:T(8,128)(2,1)S(1)} collective-permute-done((bf16[2,4,48,384]{3,2,1,0:T(8,128)(2,1)S(1)}, bf16[2,4,48,384]{3,2,1,0:T(8,128)(2,1)S(1)}, u32[]{:S(2)}, u32[]{:S(2)}) %collective-permute-start.3) | collective-permute-done | bytes 294944 | tf_op jit(solution)/shard_map/ppermute | solution.py:809
  41.3 2.5 collective-permute-start.8
  45.7 23.9 %collective-permute-done.8 = bf16[512,768]{1,0:T(8,128)(2,1)S(1)} collective-permute-done((bf16[512,768]{1,0:T(8,128)(2,1)S(1)}, bf16[512,768]{1,0:T(8,128)(2,1)S(1)}, u32[]{:S(2)}, u32[]{:S(2)}) %collective-permute-start.8) | collective-permute-done | bytes 786464 | tf_op jit(solution)/shard_map/ppermute | solution.py:809
  69.7 3.8 collective-permute-done.9
  86.6 4.9 collective-permute-done.6
  91.7 2.3 collective-permute-done.4
  95.3 15.0 %collective-permute-done.7 = bf16[2,4,2,48,384]{4,3,2,1,0:T(8,128)(2,1)S(1)} collective-permute-done((bf16[2,4,2,48,384]{4,3,2,1,0:T(8,128)(2,1)S(1)}, bf16[2,4,2,48,384]{4,3,2,1,0:T(8,128)(2,1)S(1)}, u32[]{:S(2)}, u32[]{:S(2)}) %collective-permute-start.7) | collective-permute-done | bytes 589856 | tf_op jit(solution)/shard_map/ppermute | solution.py:809
  115.7 2.0 fusion.10.b_ref
  117.8 3.4 constant_dynamic-update-slice_fusion.2
  121.2 6.6 add_convert_fusion.1.kv_ref
  127.9 20.3 %flash_forward.2 = (bf16[512,384]{1,0:T(8,128)(2,1)S(1)}, bf16[512,384]{1,0:T(8,128)(2,1)S(1)}, f32[512,384]{1,0:T(8,128)S(1)}, f32[512,384]{1,0:T(8,128)S(1)}, f32[24,1024]{1,0:T(8,128)S(1)}) custom-call(s32[10]{0:T(128)S(1)} %stack.165.bounds, bf16[512,384]{1,0:T(8,128)(2,1)S(1)} %fusion.9.a_ref, bf16[512,384]{1,0:T(8,128)(2,1)S(1)} %fusion.10.b_ref, ...), custom_call_target="tpu_custom_call" | custom-call | flops 4026531840 | bytes 12582912 | tf_op jit(solution)/shard_map/flash_forward/pallas_call | solution.py:724
  153.5 9.0 %all-gather.3.cloned.1.call-done = bf16[32,288,768]{2,1,0:T(8,128)(2,1)} async-done(((bf16[1,288,768]{2,1,0:T(8,128)(2,1)}), bf16[32,288,768]{2,1,0:T(8,128)(2,1)}) %all-gather.3.cloned.1.call-update) | async-done | bytes 14155792 | tf_op jit(solution)/shard_map/all_gather | solution.py:1423
  164.5 14.4 %tail_forward.2 = (bf16[512,768]{1,0:T(8,128)(2,1)S(1)}, f32[512,768]{1,0:T(8,128)S(1)}, f32[512,128]{1,0:T(8,128)S(1)}, bf16[512,768]{1,0:T(8,128)(2,1)S(1)}, b...) custom-call(s32[4]{0:T(128)S(1)} %copy-done.21, ...), custom_call_target="tpu_custom_call" | custom-call | flops 5435817984 | bytes 33554432 | tf_op jit(solution)/shard_map/tail_forward/pallas_call | solution.py:1236
  180.6 2.3 collective-permute-start.12
  184.2 24.1 %collective-permute-done.12 = bf16[512,768]{1,0:T(8,128)(2,1)S(1)} collective-permute-done((bf16[512,768]{1,0:T(8,128)(2,1)S(1)}, bf16[512,768]{1,0:T(8,128)(2,1)S(1)}, u32[]{:S(2)}, u32[]{:S(2)}) %collective-permute-start.12) | collective-permute-done | bytes 786464 | tf_op jit(solution)/shard_map/ppermute | solution.py:809
  208.3 9.2 %collective-permute-done.13 = bf16[512,768]{1,0:T(8,128)(2,1)S(1)} collective-permute-done((bf16[512,768]{1,0:T(8,128)(2,1)S(1)}, bf16[512,768]{1,0:T(8,128)(2,1)S(1)}, u32[]{:S(2)}, u32[]{:S(2)}) %collective-permute-start.13) | collective-permute-done | bytes 786464 | tf_op jit(solution)/shard_map/ppermute | solution.py:809
  220.7 2.9 collective-permute-start
  226.1 4.5 unpack_weights.1
  230.6 2.3 fusion.68
  238.9 4.1 add_convert_fusion.kv_ref
  243.1 20.8 %flash_forward.3 = (bf16[512,384]{1,0:T(8,128)(2,1)S(1)}, bf16[512,384]{1,0:T(8,128)(2,1)}, f32[512,384]{1,0:T(8,128)S(1)}, f32[512,384]{1,0:T(8,128)S(1)}, f32[24,1024]{1,0:T(8,128)S(1)}) custom-call(s32[10]{0:T(128)S(1)} %stack.165.bounds, bf16[512,384]{1,0:T(8,128)(2,1)S(1)} %fusion.11.a_ref, bf16[512,384]{1,0:T(8,128)(2,1)S(1)} %fusion.12.b_ref, ...), custom_call_target="tpu_custom_call" | custom-call | flops 4026531840 | bytes 12582912 | tf_op jit(solution)/shard_map/flash_forward/pallas_call | solution.py:724
  267.0 4.5 collective-permute-start.15
  275.7 14.7 %tail_forward.3 = (bf16[512,768]{1,0:T(8,128)(2,1)S(1)}, f32[512,768]{1,0:T(8,128)S(1)}, f32[512,128]{1,0:T(8,128)S(1)}, bf16[512,768]{1,0:T(8,128)(2,1)S(1)}, b...) custom-call(s32[4]{0:T(128)S(1)} %copy-done.21, ...), custom_call_target="tpu_custom_call" | custom-call | flops 5435817984 | bytes 33554432 | tf_op jit(solution)/shard_map/tail_forward/pallas_call | solution.py:1236
  290.4 3.4 multiply_convert_fusion
  293.8 20.7 %tail_backward.2 = (f32[512,768]{1,0:T(8,128)S(1)}, bf16[512,384]{1,0:T(8,128)(2,1)S(1)}, bf16[512,384]{1,0:T(8,128)(2,1)S(1)}, bf16[768,768]{1,0:T(8,128)(2,1)S...) custom-call(s32[4]{0:T(128)S(1)} %copy-done.21, ...), custom_call_target="tpu_custom_call" | custom-call | flops 10871635968 | bytes 41943040 | tf_op jit(solution)/shard_map/tail_backward/pallas_call | solution.py:1371
  318.6 8.4 %pack_terms.3 = bf16[4,8,224,768]{3,2,1,0:T(8,128)(2,1)} custom-call(bf16[8,4,24,768]{3,2,1,0:T(8,128)(2,1)} %bitcast.163, bf16[8,4,24,3072]{3,2,1,0:T(8,128)(2,1)} %bitcast.190, bf16[8,4,96,768]{3,2,1,0:T(8,128)(2,1)} %bitcast.191, bf16[4,8,8,768]{3,2,1,0:T(8,128)(2,1)S(1)} %pad.29.refs_3_), custom_call_target="tpu_custom_call" | custom-call | bytes 22020096 | tf_op jit(solution)/shard_map/pack_terms/pallas_call | solution.py:964
  329.8 39.0 %flash_backward.2 = (bf16[512,384]{1,0:T(8,128)(2,1)}, bf16[512,384]{1,0:T(8,128)(2,1)}, bf16[3072,768]{1,0:T(8,128)(2,1)}) custom-call(s32[10]{0:T(128)} %copy-done.25, bf16[512,384]{1,0:T(8,128)(2,1)} %copy-done.29, bf16[512,384]{1,0:T(8,128)(2,1)} %copy-done.31, bf16[3072,768]{1,0:T(8,128)(2,1)} %copy-done.33, bf16[512,384]{1,0:T(8,128)(2,1)} %copy-done.27, ...), custom_call_target="tpu_custom_call" | custom-call | flops 10066329600 | bytes 20971520 | tf_op jit(solution)/shard_map/flash_backward/pallas_call | solution.py:758
  368.8 8.9 %fusion.20 = f32[3072,768]{1,0:T(8,128)} fusion(bf16[3072,768]{1,0:T(8,128)(2,1)} %get-tuple-element.107, bf16[768,384]{1,0:T(8,128)(2,1)S(1)} %copy-done.65, bf16[768,384]{1,0:T(8,128)(2,1)S(1)} %copy-done.67), kind=kOutput, calls=%fused_computation.69 | convolution fusion | flops 3626237952 | bytes 15335424 | tf_op jit(solution)/shard_map/te,de->td/dot_general | solution.py:1652
  377.7 2.2 slice.539
  384.1 3.5 collective-permute-start.20
  387.6 3.8 slice.376
  391.4 2.2 slice_add_fusion.5
  393.6 4.0 fusion.67
  399.0 11.8 %collective-permute-start.19 = (bf16[512,768]{1,0:T(8,128)(2,1)S(1)}, bf16[512,768]{1,0:T(8,128)(2,1)S(1)}, u32[]{:S(2)}, u32[]{:S(2)}) collective-permute-start(bf16[512,768]{1,0:T(8,128)(2,1)S(1)} %get-tuple-element.188), channel_id=1, source_target_pairs={{0,2},{1,3},{2,4},{3,5},{4,6},{5,7},{8,10},{9,11},{10,12},{11,13},... | collective-permute-start | bytes 2359304 | tf_op jit(solution)/shard_map/ppermute | solution.py:809
  410.8 4.9 convolution_convert_fusion.1
  418.9 12.0 %collective-permute-done.18 = bf16[512,768]{1,0:T(8,128)(2,1)S(1)} collective-permute-done((bf16[512,768]{1,0:T(8,128)(2,1)S(1)}, bf16[512,768]{1,0:T(8,128)(2,1)S(1)}, u32[]{:S(2)}, u32[]{:S(2)}) %collective-permute-start.18) | collective-permute-done | bytes 786464 | tf_op jit(solution)/shard_map/ppermute | solution.py:809
  432.4 20.8 %tail_backward.3 = (f32[512,768]{1,0:T(8,128)S(1)}, bf16[512,384]{1,0:T(8,128)(2,1)S(1)}, bf16[512,384]{1,0:T(8,128)(2,1)S(1)}, bf16[768,768]{1,0:T(8,128)(2,1)S...) custom-call(s32[4]{0:T(128)S(1)} %copy-done.21, ...), custom_call_target="tpu_custom_call" | custom-call | flops 10871635968 | bytes 41943040 | tf_op jit(solution)/shard_map/tail_backward/pallas_call | solution.py:1371
  456.6 8.5 %pack_terms.2 = bf16[4,8,224,768]{3,2,1,0:T(8,128)(2,1)} custom-call(bf16[8,4,24,768]{3,2,1,0:T(8,128)(2,1)} %bitcast.162, bf16[8,4,24,3072]{3,2,1,0:T(8,128)(2,1)} %bitcast.188, bf16[8,4,96,768]{3,2,1,0:T(8,128)(2,1)} %bitcast.189, bf16[4,8,8,768]{3,2,1,0:T(8,128)(2,1)S(1)} %pad.28.refs_3_), custom_call_target="tpu_custom_call" | custom-call | bytes 22020096 | tf_op jit(solution)/shard_map/pack_terms/pallas_call | solution.py:964
  466.4 2.1 convert_reduce_fusion.1
  470.3 3.4 spread_terms.2
  476.9 39.2 %flash_backward.3 = (bf16[512,384]{1,0:T(8,128)(2,1)}, bf16[512,384]{1,0:T(8,128)(2,1)}, bf16[3072,768]{1,0:T(8,128)(2,1)}) custom-call(s32[10]{0:T(128)} %copy-done.25, bf16[512,384]{1,0:T(8,128)(2,1)} %copy-done.30, bf16[512,384]{1,0:T(8,128)(2,1)} %copy-done.32, bf16[3072,768]{1,0:T(8,128)(2,1)} %copy-done.34, bf16[512,384]{1,0:T(8,128)(2,1)} %copy-done.26, ...), custom_call_target="tpu_custom_call" | custom-call | flops 10066329600 | bytes 20971520 | tf_op jit(solution)/shard_map/flash_backward/pallas_call | solution.py:758
  518.5 2.1 fusion.24
  523.6 9.2 %convolution_convert_fusion = bf16[768,768]{1,0:T(8,128)(2,1)} fusion(bf16[3072,768]{1,0:T(8,128)(2,1)} %constant_dynamic-update-slice_fusion.2, bf16[3072,768]{1,0:T(8,128)(2,1)} %get-tuple-element.130), kind=kOutput, calls=%fused_computation.27 | convolution fusion | flops 3624468480 | bytes 10616832 | tf_op jit(solution)/shard_map/td,te->de/dot_general | solution.py:1645
  532.8 3.4 spread_terms.3
  537.6 6.2 fusion.17
  546.6 29.5 %collective-permute-done.27 = bf16[2,4,4,48,384]{4,3,2,1,0:T(8,128)(2,1)S(1)} collective-permute-done((bf16[2,4,4,48,384]{4,3,2,1,0:T(8,128)(2,1)S(1)}, bf16[2,4,4,48,384]{4,3,2,1,0:T(8,128)(2,1)S(1)}, u32[]{:S(2)}, u32[]{:S(2)}) %collective-permute-start.27) | collective-permute-done | bytes 1179680 | tf_op jit(solution)/shard_map/ppermute | solution.py:809
  578.2 20.0 %collective-permute-done.28 = bf16[4,4,48,384]{3,2,1,0:T(8,128)(2,1)S(1)} collective-permute-done((bf16[4,4,48,384]{3,2,1,0:T(8,128)(2,1)S(1)}, bf16[4,4,48,384]{3,2,1,0:T(8,128)(2,1)S(1)}, u32[]{:S(2)}, u32[]{:S(2)}) %collective-permute-start.28) | collective-permute-done | bytes 589856 | tf_op jit(solution)/shard_map/ppermute | solution.py:809
  598.8 5.0 collective-permute-start.30
  604.7 40.0 %collective-permute-done.30 = bf16[2,8,48,384]{3,2,1,0:T(8,128)(2,1)S(1)} collective-permute-done((bf16[2,8,48,384]{3,2,1,0:T(8,128)(2,1)S(1)}, bf16[2,8,48,384]{3,2,1,0:T(8,128)(2,1)S(1)}, u32[]{:S(2)}, u32[]{:S(2)}) %collective-permute-start.30) | collective-permute-done | bytes 589856 | tf_op jit(solution)/shard_map/ppermute | solution.py:809
  644.8 2.8 fusion.66
  649.9 4.9 collective-permute-start.25
  654.8 3.8 collective-permute-done.31
  658.8 6.0 collective-permute-done.32
  665.7 3.4 collective-permute-start.33
  670.8 6.8 collective-permute-done.24
  677.6 2.2 fusion.2
  679.8 3.2 collective-permute-start.26
  683.2 3.4 collective-permute-done.34
  688.7 4.4 collective-permute-done.26
  695.0 3.8 finish_shares.1
  (384 shorter events, 102.3 us)
Async XLA Ops:
  7.2 155.4 %all-gather.3.cloned.1.call-start = ((), (), s32[]{:S(2)}) async-start(), calls=%async_computation.2 | async-start | bytes 14598144 | tf_op jit(solution)/shard_map/all_gather | solution.py:1423
  7.2 15.9 %collective-permute-start.2 = (bf16[512,768]{1,0:T(8,128)(2,1)}, bf16[512,768]{1,0:T(8,128)(2,1)S(1)}, u32[]{:S(2)}, u32[]{:S(2)}) collective-permute-start(bf16[512,768]{1,0:T(8,128)(2,1)} %param.10), channel_id=1, source_target_pairs={{0,0},{1,8},{2,2},{3,10},{4,4},{5,12},{6,6},{7,14},{8,1},{9,9},{10... | collective-permute-start | bytes 2359304 | tf_op jit(solution)/shard_map/ppermute | solution.py:809
  17.6 4.5 collective-permute-start.1
  23.1 90.8 %copy-start.43 = (bf16[512,768]{1,0:T(8,128)(2,1)}, bf16[512,768]{1,0:T(8,128)(2,1)S(1)}, u32[]{:S(2)}) copy-start(bf16[512,768]{1,0:T(8,128)(2,1)S(1)} %collective-permute-done.2) | copy-start | bytes 2359300
  23.1 16.6 %collective-permute-start.3 = (bf16[2,4,48,384]{3,2,1,0:T(8,128)(2,1)S(1)}, bf16[2,4,48,384]{3,2,1,0:T(8,128)(2,1)S(1)}, u32[]{:S(2)}, u32[]{:S(2)}) collective-permute-start(bf16[2,4,48,384]{3,2,1,0:T(8,128)(2,1)S(1)} %pad_maximum_fusion.18), channel_id=1, source_target_pairs={{0,4},{1,5},{2,6},{3,7},{4,0},{5,1},{6,2},{7,3},{8,12},{9,13},{10,... | collective-permute-start | bytes 884744 | tf_op jit(solution)/shard_map/ppermute | solution.py:809
  39.8 234.9 %all-gather.5.cloned.1.call-start = ((), (), s32[]{:S(2)}) async-start(), calls=%async_computation.3 | async-start | bytes 10948608 | tf_op jit(solution)/shard_map/all_gather | solution.py:1423
  40.5 628.6 %reduce-scatter.5.cloned.1.call-start = ((), (), s32[]{:S(2)}) async-start(), calls=%async_computation.5 | async-start | bytes 11354112 | tf_op jit(solution)/shard_map/reduce_scatter | solution.py:1688
  41.3 28.4 %collective-permute-start.8 = (bf16[512,768]{1,0:T(8,128)(2,1)S(1)}, bf16[512,768]{1,0:T(8,128)(2,1)S(1)}, u32[]{:S(2)}, u32[]{:S(2)}) collective-permute-start(bf16[512,768]{1,0:T(8,128)(2,1)S(1)} %collective-permute-done.2), channel_id=1, source_target_pairs={{0,2},{1,3},{2,4},{3,5},{4,6},{5,7},{8,10},{9,11},{10,12},{11,13},... | collective-permute-start | bytes 2359304 | tf_op jit(solution)/shard_map/ppermute | solution.py:809
  43.8 29.7 %collective-permute-start.9 = (bf16[512,768]{1,0:T(8,128)(2,1)S(1)}, bf16[512,768]{1,0:T(8,128)(2,1)S(1)}, u32[]{:S(2)}, u32[]{:S(2)}) collective-permute-start(bf16[512,768]{1,0:T(8,128)(2,1)S(1)} %collective-permute-done.2), channel_id=1, source_target_pairs={{2,0},{3,1},{4,2},{5,3},{6,4},{7,5},{10,8},{11,9},{12,10},{13,11},... | collective-permute-start | bytes 2359304 | tf_op jit(solution)/shard_map/ppermute | solution.py:809
  45.5 29.7 %copy-start.73 = (s32[8,1]{0,1:T(1,128)}, s32[8,1]{0,1:T(1,128)S(1)}, u32[]{:S(2)}) copy-start(s32[8,1]{0,1:T(1,128)S(1)} %reduce-window.8) | copy-start | bytes 100
  75.2 40.5 %collective-permute-start.10 = (bf16[1536,768]{1,0:T(8,128)(2,1)}, bf16[1536,768]{1,0:T(8,128)(2,1)}, u32[]{:S(2)}, u32[]{:S(2)}) collective-permute-start(bf16[1536,768]{1,0:T(8,128)(2,1)} %pad_maximum_fusion), channel_id=1, source_target_pairs={{0,8},{1,9},{2,10},{3,11},{4,12},{5,13},{6,14},{7,15},{8,0},{9,1},... | collective-permute-start | bytes 7077896 | tf_op jit(solution)/shard_map/ppermute | solution.py:809
  77.6 13.9 %collective-permute-start.6 = (bf16[4,2,48,384]{3,2,1,0:T(8,128)(2,1)}, bf16[4,2,48,384]{3,2,1,0:T(8,128)(2,1)S(1)}, u32[]{:S(2)}, u32[]{:S(2)}) collective-permute-start(bf16[4,2,48,384]{3,2,1,0:T(8,128)(2,1)} %get-tuple-element.203), channel_id=1, source_target_pairs={{0,16},{1,17},{2,18},{3,19},{4,20},{5,21},{6,22},{7,23},{8,24},{9,... | collective-permute-start | bytes 884744 | tf_op jit(solution)/shard_map/ppermute | solution.py:809
  78.8 15.2 %collective-permute-start.4 = (bf16[4,2,48,384]{3,2,1,0:T(8,128)(2,1)S(1)}, bf16[4,2,48,384]{3,2,1,0:T(8,128)(2,1)S(1)}, u32[]{:S(2)}, u32[]{:S(2)}) collective-permute-start(bf16[4,2,48,384]{3,2,1,0:T(8,128)(2,1)S(1)} %get-tuple-element.204), channel_id=1, source_target_pairs={{0,1},{1,0},{2,3},{3,2},{4,5},{5,4},{6,7},{7,6},{8,9},{9,8},{10,11... | collective-permute-start | bytes 884744 | tf_op jit(solution)/shard_map/ppermute | solution.py:809
  86.6 156.4 %copy-start.25 = (s32[10]{0:T(128)}, s32[10]{0:T(128)S(1)}, u32[]{:S(2)}) copy-start(s32[10]{0:T(128)S(1)} %stack.165.bounds) | copy-start | bytes 124
  91.6 18.7 %collective-permute-start.7 = (bf16[2,4,2,48,384]{4,3,2,1,0:T(8,128)(2,1)S(1)}, bf16[2,4,2,48,384]{4,3,2,1,0:T(8,128)(2,1)S(1)}, u32[]{:S(2)}, u32[]{:S(2)}) collective-permute-start(bf16[2,4,2,48,384]{4,3,2,1,0:T(8,128)(2,1)S(1)} %get-tuple-element.200), channel_id=1, source_target_pairs={{0,1},{1,0},{2,3},{3,2},{4,5},{5,4},{6,7},{7,6},{8,9},{9,8},{10,11... | collective-permute-start | bytes 1769480 | tf_op jit(solution)/shard_map/ppermute | solution.py:809
  94.1 16.3 %collective-permute-start.5 = (bf16[2,4,2,48,384]{4,3,2,1,0:T(8,128)(2,1)S(1)}, bf16[2,4,2,48,384]{4,3,2,1,0:T(8,128)(2,1)S(1)}, u32[]{:S(2)}, u32[]{:S(2)}) collective-permute-start(bf16[2,4,2,48,384]{4,3,2,1,0:T(8,128)(2,1)S(1)} %get-tuple-element.206), channel_id=1, source_target_pairs={{0,16},{1,17},{2,18},{3,19},{4,20},{5,21},{6,22},{7,23},{8,24},{9,... | collective-permute-start | bytes 1769480 | tf_op jit(solution)/shard_map/ppermute | solution.py:809
  127.8 20.4 %copy-start.34 = (bf16[3072,768]{1,0:T(8,128)(2,1)}, bf16[3072,768]{1,0:T(8,128)(2,1)S(1)}, u32[]{:S(2)}) copy-start(bf16[3072,768]{1,0:T(8,128)(2,1)S(1)} %add_convert_fusion.1.kv_ref) | copy-start | bytes 14155780
  127.9 115.2 %copy-start.23 = (s32[8,1024]{1,0:T(8,128)}, s32[8,1024]{1,0:T(8,128)S(1)}, u32[]{:S(2)}) copy-start(s32[8,1024]{1,0:T(8,128)S(1)} %broadcast_in_dim.48.high_ref) | copy-start | bytes 98308
  127.9 115.1 %copy-start.24 = (s32[8,1024]{1,0:T(8,128)}, s32[8,1024]{1,0:T(8,128)S(1)}, u32[]{:S(2)}) copy-start(s32[8,1024]{1,0:T(8,128)S(1)} %broadcast_in_dim.47.low_ref) | copy-start | bytes 98308
  150.8 2.0 collective-permute-start.11
  180.6 38.6 %copy-start = (f32[512,768]{1,0:T(8,128)}, f32[512,768]{1,0:T(8,128)S(1)}, u32[]{:S(2)}) copy-start(f32[512,768]{1,0:T(8,128)S(1)} %get-tuple-element.91.state_ref) | copy-start | bytes 4718596
  180.6 38.6 %copy-start.2 = (f32[512,768]{1,0:T(8,128)}, f32[512,768]{1,0:T(8,128)S(1)}, u32[]{:S(2)}) copy-start(f32[512,768]{1,0:T(8,128)S(1)} %get-tuple-element.115.norm_one_ref) | copy-start | bytes 4718596
  180.6 38.6 %copy-start.3 = (f32[512,768]{1,0:T(8,128)}, f32[512,768]{1,0:T(8,128)S(1)}, u32[]{:S(2)}) copy-start(f32[512,768]{1,0:T(8,128)S(1)} %get-tuple-element.113.norm_two_ref) | copy-start | bytes 4718596
  180.6 43.1 %copy-start.74 = (s32[8,1]{0,1:T(1,128)S(1)}, s32[8,1]{0,1:T(1,128)}, u32[]{:S(2)}) copy-start(s32[8,1]{0,1:T(1,128)} %copy-done.73) | copy-start | bytes 100
  180.6 27.7 %collective-permute-start.12 = (bf16[512,768]{1,0:T(8,128)(2,1)S(1)}, bf16[512,768]{1,0:T(8,128)(2,1)S(1)}, u32[]{:S(2)}, u32[]{:S(2)}) collective-permute-start(bf16[512,768]{1,0:T(8,128)(2,1)S(1)} %get-tuple-element.88), channel_id=1, source_target_pairs={{0,2},{1,3},{2,4},{3,5},{4,6},{5,7},{8,10},{9,11},{10,12},{11,13},... | collective-permute-start | bytes 2359304 | tf_op jit(solution)/shard_map/ppermute | solution.py:809
  182.9 34.6 %collective-permute-start.13 = (bf16[512,768]{1,0:T(8,128)(2,1)S(1)}, bf16[512,768]{1,0:T(8,128)(2,1)S(1)}, u32[]{:S(2)}, u32[]{:S(2)}) collective-permute-start(bf16[512,768]{1,0:T(8,128)(2,1)S(1)} %get-tuple-element.88), channel_id=1, source_target_pairs={{2,0},{3,1},{4,2},{5,3},{6,4},{7,5},{10,8},{11,9},{12,10},{13,11},... | collective-permute-start | bytes 2359304 | tf_op jit(solution)/shard_map/ppermute | solution.py:809
  208.3 22.3 %copy-start.57 = (bf16[512,768]{1,0:T(8,128)(2,1)}, bf16[512,768]{1,0:T(8,128)(2,1)S(1)}, u32[]{:S(2)}) copy-start(bf16[512,768]{1,0:T(8,128)(2,1)S(1)} %collective-permute-done.12) | copy-start | bytes 2359300
  219.2 16.0 %collective-permute-start.14 = (bf16[1536,768]{1,0:T(8,128)(2,1)}, bf16[1536,768]{1,0:T(8,128)(2,1)}, u32[]{:S(2)}, u32[]{:S(2)}) collective-permute-start(bf16[1536,768]{1,0:T(8,128)(2,1)} %pad_maximum_fusion.1), channel_id=1, source_target_pairs={{0,8},{1,9},{2,10},{3,11},{4,12},{5,13},{6,14},{7,15},{8,0},{9,1},... | collective-permute-start | bytes 7077896 | tf_op jit(solution)/shard_map/ppermute | solution.py:809
  220.7 69.7 %collective-permute-start = (bf16[512,768]{1,0:T(8,128)(2,1)}, bf16[512,768]{1,0:T(8,128)(2,1)}, u32[]{:S(2)}, u32[]{:S(2)}) collective-permute-start(bf16[512,768]{1,0:T(8,128)(2,1)} %param.11), channel_id=1, source_target_pairs={{0,0},{1,8},{2,2},{3,10},{4,4},{5,12},{6,6},{7,14},{8,1},{9,9},{10... | collective-permute-start | bytes 2359304 | tf_op jit(solution)/shard_map/ppermute | solution.py:809
  243.1 20.8 %copy-start.33 = (bf16[3072,768]{1,0:T(8,128)(2,1)}, bf16[3072,768]{1,0:T(8,128)(2,1)S(1)}, u32[]{:S(2)}) copy-start(bf16[3072,768]{1,0:T(8,128)(2,1)S(1)} %add_convert_fusion.kv_ref) | copy-start | bytes 14155780
  243.1 29.4 %copy-start.72 = (bf16[8,192]{1,0:T(8,128)(2,1)S(1)}, bf16[8,192]{1,0:T(8,128)(2,1)}, u32[]{:S(2)}) copy-start(bf16[8,192]{1,0:T(8,128)(2,1)} %get-tuple-element.150) | copy-start | bytes 9220
  243.1 31.6 %copy-start.1 = (f32[512,768]{1,0:T(8,128)S(1)}, f32[512,768]{1,0:T(8,128)}, u32[]{:S(2)}) copy-start(f32[512,768]{1,0:T(8,128)} %copy-done) | copy-start | bytes 4718596
  267.0 7.7 %collective-permute-start.15 = (bf16[512,384]{1,0:T(8,128)(2,1)}, bf16[512,384]{1,0:T(8,128)(2,1)}, u32[]{:S(2)}, u32[]{:S(2)}) collective-permute-start(bf16[512,384]{1,0:T(8,128)(2,1)} %get-tuple-element.90), channel_id=1, source_target_pairs={{0,8},{1,9},{2,10},{3,11},{4,12},{5,13},{6,14},{7,15},{8,0},{9,1},... | collective-permute-start | bytes 1179656 | tf_op jit(solution)/shard_map/ppermute | solution.py:809
  327.0 343.8 %reduce-scatter.3.cloned.1.call-start = ((), (), s32[]{:S(2)}) async-start(), calls=%async_computation.4 | async-start | bytes 11354112 | tf_op jit(solution)/shard_map/reduce_scatter | solution.py:1688
  327.0 2.0 collective-permute-start.16
  329.8 39.0 %copy-start.65 = (bf16[768,384]{1,0:T(8,128)(2,1)S(1)}, bf16[768,384]{1,0:T(8,128)(2,1)}, u32[]{:S(2)}) copy-start(bf16[768,384]{1,0:T(8,128)(2,1)} %copy-done.64) | copy-start | bytes 1769476
  329.8 39.0 %copy-start.67 = (bf16[768,384]{1,0:T(8,128)(2,1)S(1)}, bf16[768,384]{1,0:T(8,128)(2,1)}, u32[]{:S(2)}) copy-start(bf16[768,384]{1,0:T(8,128)(2,1)} %copy-done.66) | copy-start | bytes 1769476
  383.7 9.9 %collective-permute-start.17 = (bf16[1536,768]{1,0:T(8,128)(2,1)}, bf16[1536,768]{1,0:T(8,128)(2,1)}, u32[]{:S(2)}, u32[]{:S(2)}) collective-permute-start(bf16[1536,768]{1,0:T(8,128)(2,1)} %pad_maximum_fusion.2), channel_id=1, source_target_pairs={{0,8},{1,9},{2,10},{3,11},{4,12},{5,13},{6,14},{7,15},{8,0},{9,1},... | collective-permute-start | bytes 7077896 | tf_op jit(solution)/shard_map/ppermute | solution.py:809
  384.1 48.3 %collective-permute-start.20 = (bf16[512,768]{1,0:T(8,128)(2,1)}, bf16[512,768]{1,0:T(8,128)(2,1)S(1)}, u32[]{:S(2)}, u32[]{:S(2)}) collective-permute-start(bf16[512,768]{1,0:T(8,128)(2,1)} %get-tuple-element.215), channel_id=1, source_target_pairs={{0,0},{1,8},{2,2},{3,10},{4,4},{5,12},{6,6},{7,14},{8,1},{9,9},{10... | collective-permute-start | bytes 2359304 | tf_op jit(solution)/shard_map/ppermute | solution.py:809
  391.4 19.4 %slice-start = ((s8[4718592]{0:T(1024)(128)(4,1)}), s8[4194304]{0:T(1024)(128)(4,1)S(1)}, s32[]{:S(2)}) async-start(s8[4718592]{0:T(1024)(128)(4,1)} %bitcast.195), calls=%async_computation.6 | async-start | bytes 8388608
  391.4 19.4 %slice-start.2 = ((s8[4718592]{0:T(1024)(128)(4,1)}), s8[4194304]{0:T(1024)(128)(4,1)S(1)}, s32[]{:S(2)}) async-start(s8[4718592]{0:T(1024)(128)(4,1)} %bitcast.216), calls=%async_computation.8 | async-start | bytes 8388608
  393.6 17.2 %slice-start.1 = ((s8[4718592]{0:T(1024)(128)(4,1)}), s8[524288]{0:T(1024)(128)(4,1)S(1)}, s32[]{:S(2)}) async-start(s8[4718592]{0:T(1024)(128)(4,1)} %bitcast.195), calls=%async_computation.7 | async-start | bytes 1048576
  397.7 33.2 %collective-permute-start.18 = (bf16[512,768]{1,0:T(8,128)(2,1)S(1)}, bf16[512,768]{1,0:T(8,128)(2,1)S(1)}, u32[]{:S(2)}, u32[]{:S(2)}) collective-permute-start(bf16[512,768]{1,0:T(8,128)(2,1)S(1)} %get-tuple-element.187), channel_id=1, source_target_pairs={{2,0},{3,1},{4,2},{5,3},{6,4},{7,5},{10,8},{11,9},{12,10},{13,11},... | collective-permute-start | bytes 2359304 | tf_op jit(solution)/shard_map/ppermute | solution.py:809
  399.0 31.9 %collective-permute-start.19 = (bf16[512,768]{1,0:T(8,128)(2,1)S(1)}, bf16[512,768]{1,0:T(8,128)(2,1)S(1)}, u32[]{:S(2)}, u32[]{:S(2)}) collective-permute-start(bf16[512,768]{1,0:T(8,128)(2,1)S(1)} %get-tuple-element.188), channel_id=1, source_target_pairs={{0,2},{1,3},{2,4},{3,5},{4,6},{5,7},{8,10},{9,11},{10,12},{11,13},... | collective-permute-start | bytes 2359304 | tf_op jit(solution)/shard_map/ppermute | solution.py:809
  432.4 20.9 %copy-start.62 = (bf16[512,768]{1,0:T(8,128)(2,1)}, bf16[512,768]{1,0:T(8,128)(2,1)S(1)}, u32[]{:S(2)}) copy-start(bf16[512,768]{1,0:T(8,128)(2,1)S(1)} %collective-permute-done.20) | copy-start | bytes 2359300
  468.5 7.7 %collective-permute-start.21 = (bf16[512,384]{1,0:T(8,128)(2,1)S(1)}, bf16[512,384]{1,0:T(8,128)(2,1)S(1)}, u32[]{:S(2)}, u32[]{:S(2)}) collective-permute-start(bf16[512,384]{1,0:T(8,128)(2,1)S(1)} %get-tuple-element.123), channel_id=1, source_target_pairs={{0,8},{1,9},{2,10},{3,11},{4,12},{5,13},{6,14},{7,15},{8,0},{9,1},... | collective-permute-start | bytes 1179656 | tf_op jit(solution)/shard_map/ppermute | solution.py:809
  475.1 47.0 %collective-permute-start.22 = (bf16[2,4,4,48,384]{4,3,2,1,0:T(8,128)(2,1)S(1)}, bf16[2,4,4,48,384]{4,3,2,1,0:T(8,128)(2,1)}, u32[]{:S(2)}, u32[]{:S(2)}) collective-permute-start(bf16[2,4,4,48,384]{4,3,2,1,0:T(8,128)(2,1)S(1)} %slice_bitcast_fusion.1), channel_id=1, source_target_pairs={{0,1},{1,0},{2,3},{3,2},{4,5},{5,4},{6,7},{7,6},{8,9},{9,8},{10,11... | collective-permute-start | bytes 3538952 | tf_op jit(solution)/shard_map/ppermute | solution.py:809
  537.6 38.6 %collective-permute-start.27 = (bf16[2,4,4,48,384]{4,3,2,1,0:T(8,128)(2,1)S(1)}, bf16[2,4,4,48,384]{4,3,2,1,0:T(8,128)(2,1)S(1)}, u32[]{:S(2)}, u32[]{:S(2)}) collective-permute-start(bf16[2,4,4,48,384]{4,3,2,1,0:T(8,128)(2,1)S(1)} %slice_bitcast_fusion), channel_id=1, source_target_pairs={{0,16},{1,17},{2,18},{3,19},{4,20},{5,21},{6,22},{7,23},{8,24},{9,... | collective-permute-start | bytes 3538952 | tf_op jit(solution)/shard_map/ppermute | solution.py:809
  546.0 30.2 %copy-start.42 = (bf16[2,2,4,4,48,384]{5,4,3,2,1,0:T(8,128)(2,1)S(1)}, bf16[2,2,4,4,48,384]{5,4,3,2,1,0:T(8,128)(2,1)}, u32[]{:S(2)}) copy-start(bf16[2,2,4,4,48,384]{5,4,3,2,1,0:T(8,128)(2,1)} %spread_terms.3) | copy-start | bytes 7077892
  546.1 30.4 %copy-start.41 = (bf16[2,2,4,4,48,384]{5,4,3,2,1,0:T(8,128)(2,1)S(1)}, bf16[2,2,4,4,48,384]{5,4,3,2,1,0:T(8,128)(2,1)}, u32[]{:S(2)}) copy-start(bf16[2,2,4,4,48,384]{5,4,3,2,1,0:T(8,128)(2,1)} %spread_terms.2) | copy-start | bytes 7077892
  546.2 98.7 %collective-permute-start.23 = (bf16[1536,768]{1,0:T(8,128)(2,1)S(1)}, bf16[1536,768]{1,0:T(8,128)(2,1)S(1)}, u32[]{:S(2)}, u32[]{:S(2)}) collective-permute-start(bf16[1536,768]{1,0:T(8,128)(2,1)S(1)} %pad_maximum_fusion.3), channel_id=1, source_target_pairs={{0,8},{1,9},{2,10},{3,11},{4,12},{5,13},{6,14},{7,15},{8,0},{9,1},... | collective-permute-start | bytes 7077896 | tf_op jit(solution)/shard_map/ppermute | solution.py:809
  576.5 21.8 %collective-permute-start.28 = (bf16[4,4,48,384]{3,2,1,0:T(8,128)(2,1)S(1)}, bf16[4,4,48,384]{3,2,1,0:T(8,128)(2,1)S(1)}, u32[]{:S(2)}, u32[]{:S(2)}) collective-permute-start(bf16[4,4,48,384]{3,2,1,0:T(8,128)(2,1)S(1)} %get-tuple-element.177), channel_id=1, source_target_pairs={{0,1},{1,0},{2,3},{3,2},{4,5},{5,4},{6,7},{7,6},{8,9},{9,8},{10,11... | collective-permute-start | bytes 1769480 | tf_op jit(solution)/shard_map/ppermute | solution.py:809
  578.2 20.2 %collective-permute-start.29 = (bf16[4,4,48,384]{3,2,1,0:T(8,128)(2,1)S(1)}, bf16[4,4,48,384]{3,2,1,0:T(8,128)(2,1)S(1)}, u32[]{:S(2)}, u32[]{:S(2)}) collective-permute-start(bf16[4,4,48,384]{3,2,1,0:T(8,128)(2,1)S(1)} %get-tuple-element.179), channel_id=1, source_target_pairs={{0,16},{1,17},{2,18},{3,19},{4,20},{5,21},{6,22},{7,23},{8,24},{9,... | collective-permute-start | bytes 1769480 | tf_op jit(solution)/shard_map/ppermute | solution.py:809
  598.8 45.9 %collective-permute-start.30 = (bf16[2,8,48,384]{3,2,1,0:T(8,128)(2,1)S(1)}, bf16[2,8,48,384]{3,2,1,0:T(8,128)(2,1)S(1)}, u32[]{:S(2)}, u32[]{:S(2)}) collective-permute-start(bf16[2,8,48,384]{3,2,1,0:T(8,128)(2,1)S(1)} %get-tuple-element.184), channel_id=1, source_target_pairs={{0,4},{1,5},{2,6},{3,7},{4,0},{5,1},{6,2},{7,3},{8,12},{9,13},{10,... | collective-permute-start | bytes 1769480 | tf_op jit(solution)/shard_map/ppermute | solution.py:809
  644.8 13.9 %collective-permute-start.31 = (bf16[8,48,384]{2,1,0:T(8,128)(2,1)S(1)}, bf16[8,48,384]{2,1,0:T(8,128)(2,1)S(1)}, u32[]{:S(2)}, u32[]{:S(2)}) collective-permute-start(bf16[8,48,384]{2,1,0:T(8,128)(2,1)S(1)} %fusion.51), channel_id=1, source_target_pairs={{0,2},{1,3},{2,0},{3,1},{4,6},{5,7},{6,4},{7,5},{8,10},{9,11},{10,... | collective-permute-start | bytes 884744 | tf_op jit(solution)/shard_map/ppermute | solution.py:809
  648.6 28.9 %collective-permute-start.24 = (bf16[512,768]{1,0:T(8,128)(2,1)}, bf16[512,768]{1,0:T(8,128)(2,1)}, u32[]{:S(2)}, u32[]{:S(2)}) collective-permute-start(bf16[512,768]{1,0:T(8,128)(2,1)} %get-tuple-element.185), channel_id=1, source_target_pairs={{2,0},{3,1},{4,2},{5,3},{6,4},{7,5},{10,8},{11,9},{12,10},{13,11},... | collective-permute-start | bytes 2359304 | tf_op jit(solution)/shard_map/ppermute | solution.py:809
  649.9 27.7 %collective-permute-start.25 = (bf16[512,768]{1,0:T(8,128)(2,1)S(1)}, bf16[512,768]{1,0:T(8,128)(2,1)}, u32[]{:S(2)}, u32[]{:S(2)}) collective-permute-start(bf16[512,768]{1,0:T(8,128)(2,1)S(1)} %get-tuple-element.186), channel_id=1, source_target_pairs={{0,2},{1,3},{2,4},{3,5},{4,6},{5,7},{8,10},{9,11},{10,12},{11,13},... | collective-permute-start | bytes 2359304 | tf_op jit(solution)/shard_map/ppermute | solution.py:809
  658.8 6.0 collective-permute-start.32
  665.7 21.8 %collective-permute-start.33 = (bf16[2,8,48,384]{3,2,1,0:T(8,128)(2,1)}, bf16[2,8,48,384]{3,2,1,0:T(8,128)(2,1)}, u32[]{:S(2)}, u32[]{:S(2)}) collective-permute-start(bf16[2,8,48,384]{3,2,1,0:T(8,128)(2,1)} %get-tuple-element.197), channel_id=1, source_target_pairs={{0,8},{1,9},{2,10},{3,11},{4,12},{5,13},{6,14},{7,15},{8,0},{9,1},... | collective-permute-start | bytes 1769480 | tf_op jit(solution)/shard_map/ppermute | solution.py:809
  669.2 13.9 %collective-permute-start.36 = (bf16[224,768]{1,0:T(8,128)(2,1)}, bf16[224,768]{1,0:T(8,128)(2,1)S(1)}, u32[]{:S(2)}, u32[]{:S(2)}) collective-permute-start(bf16[224,768]{1,0:T(8,128)(2,1)} %bitcast.204), channel_id=1, source_target_pairs={{0,16},{1,17},{2,18},{3,19},{4,20},{5,21},{6,22},{7,23},{8,24},{9,... | collective-permute-start | bytes 1032200 | tf_op jit(solution)/shard_map/ppermute | solution.py:809
  670.7 15.9 %collective-permute-start.34 = (bf16[224,768]{1,0:T(8,128)(2,1)}, bf16[224,768]{1,0:T(8,128)(2,1)S(1)}, u32[]{:S(2)}, u32[]{:S(2)}) collective-permute-start(bf16[224,768]{1,0:T(8,128)(2,1)} %bitcast.205), channel_id=1, source_target_pairs={{0,16},{1,17},{2,18},{3,19},{4,20},{5,21},{6,22},{7,23},{8,24},{9,... | collective-permute-start | bytes 1032200 | tf_op jit(solution)/shard_map/ppermute | solution.py:809
  679.8 13.3 %collective-permute-start.26 = (bf16[512,768]{1,0:T(8,128)(2,1)S(1)}, bf16[512,768]{1,0:T(8,128)(2,1)S(1)}, u32[]{:S(2)}, u32[]{:S(2)}) collective-permute-start(bf16[512,768]{1,0:T(8,128)(2,1)S(1)} %fusion.2), channel_id=1, source_target_pairs={{0,0},{1,8},{2,2},{3,10},{4,4},{5,12},{6,6},{7,14},{8,1},{9,9},{10... | collective-permute-start | bytes 2359304 | tf_op jit(solution)/shard_map/ppermute | solution.py:809
  683.2 11.2 %collective-permute-start.37 = (bf16[2,224,768]{2,1,0:T(8,128)(2,1)S(1)}, bf16[2,224,768]{2,1,0:T(8,128)(2,1)S(1)}, u32[]{:S(2)}, u32[]{:S(2)}) collective-permute-start(bf16[2,224,768]{2,1,0:T(8,128)(2,1)S(1)} %get-tuple-element.194), channel_id=1, source_target_pairs={{0,8},{1,9},{2,10},{3,11},{4,12},{5,13},{6,14},{7,15},{8,0},{9,1},... | collective-permute-start | bytes 2064392 | tf_op jit(solution)/shard_map/ppermute | solution.py:809
  686.7 7.8 %collective-permute-start.35 = (bf16[2,224,768]{2,1,0:T(8,128)(2,1)S(1)}, bf16[2,224,768]{2,1,0:T(8,128)(2,1)S(1)}, u32[]{:S(2)}, u32[]{:S(2)}) collective-permute-start(bf16[2,224,768]{2,1,0:T(8,128)(2,1)S(1)} %get-tuple-element.196), channel_id=1, source_target_pairs={{0,8},{1,9},{2,10},{3,11},{4,12},{5,13},{6,14},{7,15},{8,0},{9,1},... | collective-permute-start | bytes 2064392 | tf_op jit(solution)/shard_map/ppermute | solution.py:809
  (59 other events, 223.5 us)
Sparse Core Ops, SparseCore 0:
  39.9 122.5 all-gather.2
  165.5 101.0 all-gather.4
  327.1 155.7 reduce-scatter.4
  488.7 174.3 reduce-scatter.2
